TPU v7x, 128 devices: a whole 4x4x4 slice. The times are simulated.
128 devices in a mesh: lat: 8 (over z, core), lon: 16 (over x, y).
Axes of the slice: x: 4, y: 4, z: 4, core: 2. Of those that a mesh axis runs over, the one named last changes fastest.
Arguments:
- surface: float32 [2048, 16384], P('lat', 'lon'), may hold values from -24 to 24
- bathymetry: float32 [2048, 16384], P('lat', 'lon'), may hold values from 0.1 to 1
- land_sea: int32 [2048, 16384], P('lat', 'lon'), may hold values 0 or 1
- flux_lon: float32 [2048, 16384], P('lat', 'lon'), may hold values from -12 to 12
- flux_lat: float32 [2048, 16384], P('lat', 'lon'), may hold values from -12 to 12
Outputs:
- surface_next: float32 [2048, 16384], P('lat', 'lon')
- flux_lon_next: float32 [2048, 16384], P('lat', 'lon')
- flux_lat_next: float32 [2048, 16384], P('lat', 'lon')
All inputs are finite; a program needn't handle non-finite values. No bound on the sum of `land_sea` on one device may be relied on, other than what follows from the above.
Results may differ from a plain program's by a relative error of at most 0.0001.
Values sent between devices are 32-bit elements; how exact they have to be, the bound alone decides.
A program may use at most 64 MiB of HBM per device.

v0:
```python
import jax
import jax.numpy as jnp
from jax import lax
from jax.sharding import PartitionSpec as P

ITERS = 3


courant = -0.4
dispersion = 40.0
continuity = -0.5


def from_behind(value, axis, steps):
    count = lax.axis_size(axis)
    leading, last = (max(0, -steps), min(count, count - steps))
    return lax.ppermute(value, axis, [(source, source + steps) for source in range(leading, last)])


def upper_cells(stacked):
    north_row = from_behind(stacked[:, :1, :], "lat", -1)
    east_col = from_behind(stacked[:, :, :1], "lon", -1)
    eastern = jnp.concatenate([stacked[:, :, 1:], east_col], axis=2)
    northern = jnp.concatenate([stacked[:, 1:, :], north_row], axis=1)
    return (eastern, northern)


def lower_fluxes(field):
    south_row = from_behind(field[:, -1:, :], "lat", 1)
    west_col = from_behind(field[:, :, -1:], "lon", 1)
    western = jnp.concatenate([west_col, field[:, :, :-1]], axis=2)
    southern = jnp.concatenate([south_row, field[:, :-1, :]], axis=1)
    return (western, southern)


def divergence(field):
    western, southern = lower_fluxes(field)
    return field[0] - western[0] + field[1] - southern[1]


def gradient_back(field):
    diverge = divergence(field)
    eastern, northern = upper_cells(diverge[None])
    return jnp.stack([diverge - eastern[0], diverge - northern[0]])


def operate(field, wet, inverse):
    return wet * (inverse * field + gradient_back(field))


def squares(residual):
    return lax.psum(jnp.sum(residual * residual), ("lat", "lon"))


def per_device(surface, bathymetry, land_sea, flux_lon, flux_lat):
    sea = land_sea.astype(jnp.float32)
    cells = jnp.stack([surface, bathymetry, sea])
    eastern, northern = upper_cells(cells)
    wet = jnp.stack([sea * eastern[2], sea * northern[2]])
    depth = jnp.stack([0.5 * (bathymetry + eastern[1]), 0.5 * (bathymetry + northern[1])])
    slope = jnp.stack([eastern[0] - surface, northern[0] - surface])
    start = wet * (jnp.stack([flux_lon, flux_lat]) - courant * depth * slope)
    inverse = 1.0 / (dispersion * depth * depth)
    right_side = wet * inverse * start
    solution = start
    residual = right_side - operate(start, wet, inverse)
    direction = residual
    norm_now = squares(residual)
    for step in range(ITERS):
        image = operate(direction, wet, inverse)
        alpha = norm_now / lax.psum(jnp.sum(direction * image), ("lat", "lon"))
        solution = solution + alpha * direction
        residual = residual - alpha * image
        norm_next = squares(residual)
        direction = residual + norm_next / norm_now * direction
        norm_now = norm_next
    surface_next = surface - continuity * divergence(solution)
    return (surface_next, solution[0], solution[1])


def solution(mesh):
    in_specs = (P("lat", "lon"), P("lat", "lon"), P("lat", "lon"), P("lat", "lon"), P("lat", "lon"))
    out_specs = (P("lat", "lon"), P("lat", "lon"), P("lat", "lon"))
    return jax.shard_map(
        per_device, mesh=mesh, in_specs=in_specs, out_specs=out_specs, check_vma=False
    )
```

profile of v0, /device:TPU:1, one launch (start us, length us, event | category | flops | bytes accessed | tf_op | source)
XLA Modules:
  0.0 493.6 jit_solution(12994027470948280249)
XLA Ops:
  8.7 9.9 %collective-permute-done = f32[3,256,1]{2,1,0:T(8,128)S(1)} collective-permute-done((f32[3,256,1]{2,1,0:T(8,128)S(1)}, f32[3,256,1]{2,1,0:T(8,128)S(1)}, u32[]{:S(2)}, u32[]{:S(2)}) %collective-permute-start) | collective-permute-done | bytes 3104 | tf_op jit(solution)/shard_map/ppermute | solution.py:17
  21.2 4.3 collective-permute-start.3
  28.8 4.8 collective-permute-done.2
  38.0 4.8 collective-permute-done.4
  44.5 5.4 %collective-permute-start.7 = (f32[2,1,1024]{2,1,0:T(1,128)S(1)}, f32[2,1,1024]{2,1,0:T(1,128)S(1)}, u32[]{:S(2)}, u32[]{:S(2)}) collective-permute-start(f32[2,1,1024]{2,1,0:T(1,128)S(1)} %slice.290), channel_id=1, source_target_pairs={{0,16},{16,32},{32,48},{48,64},{64,80},{80,96},{96,112},{1,17},{17... | collective-permute-start | bytes 24584 | tf_op jit(solution)/shard_map/ppermute | solution.py:17
  50.0 4.4 collective-permute-start.6
  54.5 3.3 collective-permute-done.6
  62.1 4.7 collective-permute-done.8
  69.6 74.5 %all-reduce = (f32[]{:T(128)}, f32[]{:T(128)}) all-reduce(f32[]{:T(128)} %get-tuple-element.4, f32[]{:T(128)} %get-tuple-element.3), channel_id=1, replica_groups=mesh['lat'=8,'lon'=16] {'lat','lon'}, use_global_device_ids=true, to_apply=%region_1.0 | all-reduce | flops 2 | bytes 16 | tf_op jit(solution)/shard_map/psum | solution.py:52
  145.4 6.0 %multiply_reduce_fusion.2 = (f32[]{:T(128)}, f32[2,256,1024]{2,1,0:T(8,128)}) fusion(f32[1,256,1024]{2,1,0:T(8,128)} %copy-done.20, f32[1,256,1024]{2,1,0:T(8,128)} %copy-done.19, f32[1,256,1024]{2,1,0:T(8,128)S(1)} %get-tuple-element.19, f32[1,256,1024]{2,1,0:T(8,128)S(1)} %get-tuple-element.20, f32[1,256,1024]{2,1,0:T(8,128)S(1)} %get-tuple-element.17, ...), kind=kLoop, calls=%fused_computation.33 | loop fusion | flops 13631487 | bytes 14680072 | tf_op jit(solution)/shard_map/reduce_sum | solution.py:52
  151.4 63.1 %psum.44 = f32[]{:T(128)} all-reduce(f32[]{:T(128)} %get-tuple-element.12), channel_id=1, replica_groups=mesh['lat'=8,'lon'=16] {'lat','lon'}, use_global_device_ids=true, to_apply=%region_5.0 | all-reduce | flops 1 | bytes 8 | tf_op jit(solution)/shard_map/psum | solution.py:52
  215.8 5.0 %multiply_add_fusion.2 = f32[2,256,1024]{2,1,0:T(8,128)S(1)} fusion(f32[2,256,1024]{2,1,0:T(8,128)} %get-tuple-element.13, f32[]{:T(128)S(6)} %div.24, f32[1,256,1024]{2,1,0:T(8,128)} %copy-done.15, f32[1,256,1024]{2,1,0:T(8,128)} %copy-done.14, f32[1,256,1024]{2,1,0:T(8,128)} %copy-done, f32[1,256,1024]{2,1,0:T(8,128)} %copy-done.3, ...), kind=kLoop, calls=%fused_computation.32 | loop fusion | flops 10485760 | bytes 14680068 | tf_op jit(solution)/shard_map/add | solution.py:75
  220.9 3.5 collective-permute-start.11
  225.8 5.7 %collective-permute-done.10 = f32[2,256,1]{2,1,0:T(8,128)S(1)} collective-permute-done((f32[2,256,1]{2,1,0:T(8,128)S(1)}, f32[2,256,1]{2,1,0:T(8,128)S(1)}, u32[]{:S(2)}, u32[]{:S(2)}) %collective-permute-start.10) | collective-permute-done | bytes 2080 | tf_op jit(solution)/shard_map/ppermute | solution.py:17
  236.6 5.6 %collective-permute-done.12 = f32[1,256,1]{2,1,0:T(8,128)S(1)} collective-permute-done((f32[1,256,1]{2,1,0:T(8,128)S(1)}, f32[1,256,1]{2,1,0:T(8,128)S(1)}, u32[]{:S(2)}, u32[]{:S(2)}) %collective-permute-start.12) | collective-permute-done | bytes 1056 | tf_op jit(solution)/shard_map/ppermute | solution.py:17
  245.6 66.8 %psum.45 = f32[]{:T(128)} all-reduce(f32[]{:T(128)} %get-tuple-element.10), channel_id=1, replica_groups=mesh['lat'=8,'lon'=16] {'lat','lon'}, use_global_device_ids=true, to_apply=%region_7.0 | all-reduce | flops 1 | bytes 8 | tf_op jit(solution)/shard_map/psum | solution.py:71
  313.7 3.4 multiply_reduce_fusion
  317.0 62.7 %psum.46 = f32[]{:T(128)} all-reduce(f32[]{:T(128)} %multiply_reduce_fusion), channel_id=1, replica_groups=mesh['lat'=8,'lon'=16] {'lat','lon'}, use_global_device_ids=true, to_apply=%region_9.0 | all-reduce | flops 1 | bytes 8 | tf_op jit(solution)/shard_map/psum | solution.py:52
  384.0 3.5 collective-permute-start.15
  389.1 5.5 %collective-permute-done.14 = f32[2,256,1]{2,1,0:T(8,128)S(1)} collective-permute-done((f32[2,256,1]{2,1,0:T(8,128)S(1)}, f32[2,256,1]{2,1,0:T(8,128)S(1)}, u32[]{:S(2)}, u32[]{:S(2)}) %collective-permute-start.14) | collective-permute-done | bytes 2080 | tf_op jit(solution)/shard_map/ppermute | solution.py:17
  399.8 5.6 %collective-permute-done.16 = f32[1,256,1]{2,1,0:T(8,128)S(1)} collective-permute-done((f32[1,256,1]{2,1,0:T(8,128)S(1)}, f32[1,256,1]{2,1,0:T(8,128)S(1)}, u32[]{:S(2)}, u32[]{:S(2)}) %collective-permute-start.16) | collective-permute-done | bytes 1056 | tf_op jit(solution)/shard_map/ppermute | solution.py:17
  407.4 66.9 %psum.47 = f32[]{:T(128)} all-reduce(f32[]{:T(128)} %fusion.8), channel_id=1, replica_groups=mesh['lat'=8,'lon'=16] {'lat','lon'}, use_global_device_ids=true, to_apply=%region_11.0 | all-reduce | flops 1 | bytes 8 | tf_op jit(solution)/shard_map/psum | solution.py:71
  475.7 5.3 %multiply_add_fusion = f32[2,256,1024]{2,1,0:T(8,128)S(1)} fusion(f32[2,256,1024]{2,1,0:T(8,128)} %copy-done.9, f32[2,256,1024]{2,1,0:T(8,128)S(1)} %multiply_add_fusion.2, f32[]{:T(128)S(6)} %div.27, f32[]{:T(128)S(6)} %div.25, f32[]{:T(128)S(6)} %div.23, f32[1,256,1024]{2,1,0:T(8,128)} %copy-done.15, f32[1,256,1024]{2,1,0:T(8,128)} %copy-done.14, ...), kind=kLoop, calls=%fused_computation.27 | loop fusion | flops 12582912 | bytes 16777228 | tf_op jit(solution)/shard_map/add | solution.py:72
  486.5 5.0 %collective-permute-done.18 = f32[2,256,1]{2,1,0:T(8,128)S(1)} collective-permute-done((f32[2,256,1]{2,1,0:T(8,128)S(1)}, f32[2,256,1]{2,1,0:T(8,128)S(1)}, u32[]{:S(2)}, u32[]{:S(2)}) %collective-permute-start.18) | collective-permute-done | bytes 2080 | tf_op jit(solution)/shard_map/ppermute | solution.py:17
  (117 shorter events, 56.0 us)
Async XLA Ops:
  2.5 16.1 %collective-permute-start.1 = (f32[3,1,1024]{2,1,0:T(1,128)S(1)}, f32[3,1,1024]{2,1,0:T(1,128)S(1)}, u32[]{:S(2)}, u32[]{:S(2)}) collective-permute-start(f32[3,1,1024]{2,1,0:T(1,128)S(1)} %pad_maximum_fusion.16), channel_id=1, source_target_pairs={{16,0},{32,16},{48,32},{64,48},{80,64},{96,80},{112,96},{17,1},{33... | collective-permute-start | bytes 36872 | tf_op jit(solution)/shard_map/ppermute | solution.py:17
  5.9 12.7 %collective-permute-start = (f32[3,256,1]{2,1,0:T(8,128)S(1)}, f32[3,256,1]{2,1,0:T(8,128)S(1)}, u32[]{:S(2)}, u32[]{:S(2)}) collective-permute-start(f32[3,256,1]{2,1,0:T(8,128)S(1)} %pad_maximum_fusion.15), channel_id=1, source_target_pairs={{1,0},{2,1},{3,2},{4,3},{5,4},{6,5},{7,6},{8,7},{9,8},{10,9},{11,1... | collective-permute-start | bytes 9224 | tf_op jit(solution)/shard_map/ppermute | solution.py:17
  20.1 47.2 %copy-start.6 = (f32[1,256,1024]{2,1,0:T(8,128)}, f32[1,256,1024]{2,1,0:T(8,128)S(1)}, u32[]{:S(2)}) copy-start(f32[1,256,1024]{2,1,0:T(8,128)S(1)} %get-tuple-element.22) | copy-start | bytes 3145732
  20.1 47.2 %copy-start.10 = (f32[1,256,1024]{2,1,0:T(8,128)}, f32[1,256,1024]{2,1,0:T(8,128)S(1)}, u32[]{:S(2)}) copy-start(f32[1,256,1024]{2,1,0:T(8,128)S(1)} %get-tuple-element.18) | copy-start | bytes 3145732
  20.1 125.2 %copy-start = (f32[1,256,1024]{2,1,0:T(8,128)}, f32[1,256,1024]{2,1,0:T(8,128)S(1)}, u32[]{:S(2)}) copy-start(f32[1,256,1024]{2,1,0:T(8,128)S(1)} %get-tuple-element.19) | copy-start | bytes 3145732
  20.1 125.2 %copy-start.3 = (f32[1,256,1024]{2,1,0:T(8,128)}, f32[1,256,1024]{2,1,0:T(8,128)S(1)}, u32[]{:S(2)}) copy-start(f32[1,256,1024]{2,1,0:T(8,128)S(1)} %get-tuple-element.20) | copy-start | bytes 3145732
  21.2 12.5 %collective-permute-start.3 = (f32[2,1,1024]{2,1,0:T(1,128)S(1)}, f32[2,1,1024]{2,1,0:T(1,128)S(1)}, u32[]{:S(2)}, u32[]{:S(2)}) collective-permute-start(f32[2,1,1024]{2,1,0:T(1,128)S(1)} %slice.280), channel_id=1, source_target_pairs={{0,16},{16,32},{32,48},{48,64},{64,80},{80,96},{96,112},{1,17},{17... | collective-permute-start | bytes 24584 | tf_op jit(solution)/shard_map/ppermute | solution.py:17
  25.6 8.0 %collective-permute-start.2 = (f32[2,256,1]{2,1,0:T(8,128)S(1)}, f32[2,256,1]{2,1,0:T(8,128)S(1)}, u32[]{:S(2)}, u32[]{:S(2)}) collective-permute-start(f32[2,256,1]{2,1,0:T(8,128)S(1)} %slice.277), channel_id=1, source_target_pairs={{0,1},{1,2},{2,3},{3,4},{4,5},{5,6},{6,7},{7,8},{8,9},{9,10},{10,1... | collective-permute-start | bytes 6152 | tf_op jit(solution)/shard_map/ppermute | solution.py:17
  34.2 8.5 %collective-permute-start.5 = (f32[1,1,1024]{2,1,0:T(1,128)S(1)}, f32[1,1,1024]{2,1,0:T(1,128)S(1)}, u32[]{:S(2)}, u32[]{:S(2)}) collective-permute-start(f32[1,1,1024]{2,1,0:T(1,128)S(1)} %slice.285), channel_id=1, source_target_pairs={{16,0},{32,16},{48,32},{64,48},{80,64},{96,80},{112,96},{17,1},{33... | collective-permute-start | bytes 12296 | tf_op jit(solution)/shard_map/ppermute | solution.py:17
  36.2 6.5 %collective-permute-start.4 = (f32[1,256,1]{2,1,0:T(8,128)S(1)}, f32[1,256,1]{2,1,0:T(8,128)S(1)}, u32[]{:S(2)}, u32[]{:S(2)}) collective-permute-start(f32[1,256,1]{2,1,0:T(8,128)S(1)} %slice.283), channel_id=1, source_target_pairs={{1,0},{2,1},{3,2},{4,3},{5,4},{6,5},{7,6},{8,7},{9,8},{10,9},{11,1... | collective-permute-start | bytes 3080 | tf_op jit(solution)/shard_map/ppermute | solution.py:17
  44.5 13.3 %collective-permute-start.7 = (f32[2,1,1024]{2,1,0:T(1,128)S(1)}, f32[2,1,1024]{2,1,0:T(1,128)S(1)}, u32[]{:S(2)}, u32[]{:S(2)}) collective-permute-start(f32[2,1,1024]{2,1,0:T(1,128)S(1)} %slice.290), channel_id=1, source_target_pairs={{0,16},{16,32},{32,48},{48,64},{64,80},{80,96},{96,112},{1,17},{17... | collective-permute-start | bytes 24584 | tf_op jit(solution)/shard_map/ppermute | solution.py:17
  50.0 7.7 %collective-permute-start.6 = (f32[2,256,1]{2,1,0:T(8,128)S(1)}, f32[2,256,1]{2,1,0:T(8,128)S(1)}, u32[]{:S(2)}, u32[]{:S(2)}) collective-permute-start(f32[2,256,1]{2,1,0:T(8,128)S(1)} %slice.287), channel_id=1, source_target_pairs={{0,1},{1,2},{2,3},{3,4},{4,5},{5,6},{6,7},{7,8},{8,9},{9,10},{10,1... | collective-permute-start | bytes 6152 | tf_op jit(solution)/shard_map/ppermute | solution.py:17
  58.4 8.4 %collective-permute-start.9 = (f32[1,1,1024]{2,1,0:T(1,128)S(1)}, f32[1,1,1024]{2,1,0:T(1,128)S(1)}, u32[]{:S(2)}, u32[]{:S(2)}) collective-permute-start(f32[1,1,1024]{2,1,0:T(1,128)S(1)} %slice.295), channel_id=1, source_target_pairs={{16,0},{32,16},{48,32},{64,48},{80,64},{96,80},{112,96},{17,1},{33... | collective-permute-start | bytes 12296 | tf_op jit(solution)/shard_map/ppermute | solution.py:17
  60.3 6.5 %collective-permute-start.8 = (f32[1,256,1]{2,1,0:T(8,128)S(1)}, f32[1,256,1]{2,1,0:T(8,128)S(1)}, u32[]{:S(2)}, u32[]{:S(2)}) collective-permute-start(f32[1,256,1]{2,1,0:T(8,128)S(1)} %slice.293), channel_id=1, source_target_pairs={{1,0},{2,1},{3,2},{4,3},{5,4},{6,5},{7,6},{8,7},{9,8},{10,9},{11,1... | collective-permute-start | bytes 3080 | tf_op jit(solution)/shard_map/ppermute | solution.py:17
  220.9 10.7 %collective-permute-start.11 = (f32[2,1,1024]{2,1,0:T(1,128)S(1)}, f32[2,1,1024]{2,1,0:T(1,128)S(1)}, u32[]{:S(2)}, u32[]{:S(2)}) collective-permute-start(f32[2,1,1024]{2,1,0:T(1,128)S(1)} %slice.300), channel_id=1, source_target_pairs={{0,16},{16,32},{32,48},{48,64},{64,80},{80,96},{96,112},{1,17},{17... | collective-permute-start | bytes 24584 | tf_op jit(solution)/shard_map/ppermute | solution.py:17
  224.5 7.0 %collective-permute-start.10 = (f32[2,256,1]{2,1,0:T(8,128)S(1)}, f32[2,256,1]{2,1,0:T(8,128)S(1)}, u32[]{:S(2)}, u32[]{:S(2)}) collective-permute-start(f32[2,256,1]{2,1,0:T(8,128)S(1)} %slice.297), channel_id=1, source_target_pairs={{0,1},{1,2},{2,3},{3,4},{4,5},{5,6},{6,7},{7,8},{8,9},{9,10},{10,1... | collective-permute-start | bytes 6152 | tf_op jit(solution)/shard_map/ppermute | solution.py:17
  232.1 10.1 %collective-permute-start.13 = (f32[1,1,1024]{2,1,0:T(1,128)S(1)}, f32[1,1,1024]{2,1,0:T(1,128)S(1)}, u32[]{:S(2)}, u32[]{:S(2)}) collective-permute-start(f32[1,1,1024]{2,1,0:T(1,128)S(1)} %slice.305), channel_id=1, source_target_pairs={{16,0},{32,16},{48,32},{64,48},{80,64},{96,80},{112,96},{17,1},{33... | collective-permute-start | bytes 12296 | tf_op jit(solution)/shard_map/ppermute | solution.py:17
  234.8 7.4 %collective-permute-start.12 = (f32[1,256,1]{2,1,0:T(8,128)S(1)}, f32[1,256,1]{2,1,0:T(8,128)S(1)}, u32[]{:S(2)}, u32[]{:S(2)}) collective-permute-start(f32[1,256,1]{2,1,0:T(8,128)S(1)} %slice.303), channel_id=1, source_target_pairs={{1,0},{2,1},{3,2},{4,3},{5,4},{6,5},{7,6},{8,7},{9,8},{10,9},{11,1... | collective-permute-start | bytes 3080 | tf_op jit(solution)/shard_map/ppermute | solution.py:17
  384.0 10.5 %collective-permute-start.15 = (f32[2,1,1024]{2,1,0:T(1,128)S(1)}, f32[2,1,1024]{2,1,0:T(1,128)S(1)}, u32[]{:S(2)}, u32[]{:S(2)}) collective-permute-start(f32[2,1,1024]{2,1,0:T(1,128)S(1)} %slice.310), channel_id=1, source_target_pairs={{0,16},{16,32},{32,48},{48,64},{64,80},{80,96},{96,112},{1,17},{17... | collective-permute-start | bytes 24584 | tf_op jit(solution)/shard_map/ppermute | solution.py:17
  387.7 6.8 %collective-permute-start.14 = (f32[2,256,1]{2,1,0:T(8,128)S(1)}, f32[2,256,1]{2,1,0:T(8,128)S(1)}, u32[]{:S(2)}, u32[]{:S(2)}) collective-permute-start(f32[2,256,1]{2,1,0:T(8,128)S(1)} %slice.307), channel_id=1, source_target_pairs={{0,1},{1,2},{2,3},{3,4},{4,5},{5,6},{6,7},{7,8},{8,9},{9,10},{10,1... | collective-permute-start | bytes 6152 | tf_op jit(solution)/shard_map/ppermute | solution.py:17
  395.1 10.4 %collective-permute-start.17 = (f32[1,1,1024]{2,1,0:T(1,128)S(1)}, f32[1,1,1024]{2,1,0:T(1,128)S(1)}, u32[]{:S(2)}, u32[]{:S(2)}) collective-permute-start(f32[1,1,1024]{2,1,0:T(1,128)S(1)} %slice.315), channel_id=1, source_target_pairs={{16,0},{32,16},{48,32},{64,48},{80,64},{96,80},{112,96},{17,1},{33... | collective-permute-start | bytes 12296 | tf_op jit(solution)/shard_map/ppermute | solution.py:17
  398.0 7.4 %collective-permute-start.16 = (f32[1,256,1]{2,1,0:T(8,128)S(1)}, f32[1,256,1]{2,1,0:T(8,128)S(1)}, u32[]{:S(2)}, u32[]{:S(2)}) collective-permute-start(f32[1,256,1]{2,1,0:T(8,128)S(1)} %slice.313), channel_id=1, source_target_pairs={{1,0},{2,1},{3,2},{4,3},{5,4},{6,5},{7,6},{8,7},{9,8},{10,9},{11,1... | collective-permute-start | bytes 3080 | tf_op jit(solution)/shard_map/ppermute | solution.py:17
  481.0 10.5 %collective-permute-start.19 = (f32[2,1,1024]{2,1,0:T(1,128)S(1)}, f32[2,1,1024]{2,1,0:T(1,128)S(1)}, u32[]{:S(2)}, u32[]{:S(2)}) collective-permute-start(f32[2,1,1024]{2,1,0:T(1,128)S(1)} %slice.320), channel_id=1, source_target_pairs={{0,16},{16,32},{32,48},{48,64},{64,80},{80,96},{96,112},{1,17},{17... | collective-permute-start | bytes 24584 | tf_op jit(solution)/shard_map/ppermute | solution.py:17
  483.3 8.1 %collective-permute-start.18 = (f32[2,256,1]{2,1,0:T(8,128)S(1)}, f32[2,256,1]{2,1,0:T(8,128)S(1)}, u32[]{:S(2)}, u32[]{:S(2)}) collective-permute-start(f32[2,256,1]{2,1,0:T(8,128)S(1)} %slice.317), channel_id=1, source_target_pairs={{0,1},{1,2},{2,3},{3,4},{4,5},{5,6},{6,7},{7,8},{8,9},{9,10},{10,1... | collective-permute-start | bytes 6152 | tf_op jit(solution)/shard_map/ppermute | solution.py:17
  (18 other events, 210.9 us)
where the time goes:
time: 498 us; the launch traced here: 494 us
  blocking collectives  334 us (67%)
  waiting for transfers between devices  54.8 us (11%)
  starting transfers between devices  51.5 us (10%)
  other arithmetic  40.9 us (8%)
  between operations  7.92 us (2%)
    psum x3, blocking collectives, squares(): return lax.psum(jnp.sum(residual * residual), ('lat', 'lon'))  200 us
    psum x2, blocking collectives, per_device(): alpha = norm_now / lax.psum(jnp.sum(direction * image), ('lat', 'lon'))  134 us
    ppermute x20, waiting for transfers between devices, from_behind(): lax.ppermute(value, axis, [(source, source + steps) for source in range(l...  54.8 us
    ppermute x20, starting transfers between devices, from_behind(): lax.ppermute(value, axis, [(source, source + steps) for source in range(l...  51.5 us
  transfers between devices with their start and end apart: 20, of which 10 were waited for; matrix products, arithmetic and copies ran while one was open for 1% of the time, Pallas kernels for 0%

commit v1 on v0

--- a/solution.py
+++ b/solution.py
@@ -48,8 +48,9 @@
     return wet * (inverse * field + gradient_back(field))
 
 
-def squares(residual):
-    return lax.psum(jnp.sum(residual * residual), ("lat", "lon"))
+def sums(*pairs):
+    local = jnp.stack([jnp.sum(x * y) for x, y in pairs])
+    return lax.psum(local, ("lat", "lon"))
 
 
 def per_device(surface, bathymetry, land_sea, flux_lon, flux_lat):
@@ -64,15 +65,21 @@
     right_side = wet * inverse * start
     solution = start
     residual = right_side - operate(start, wet, inverse)
-    direction = residual
-    norm_now = squares(residual)
+    applied = operate(residual, wet, inverse)
+    norm_now, curve = sums((residual, residual), (residual, applied))
+    direction, image = residual, applied
     for step in range(ITERS):
-        image = operate(direction, wet, inverse)
-        alpha = norm_now / lax.psum(jnp.sum(direction * image), ("lat", "lon"))
+        alpha = norm_now / curve
         solution = solution + alpha * direction
+        if step == ITERS - 1:
+            break
         residual = residual - alpha * image
-        norm_next = squares(residual)
-        direction = residual + norm_next / norm_now * direction
+        applied = operate(residual, wet, inverse)
+        norm_next, r_ar, r_ap = sums((residual, residual), (residual, applied), (residual, image))
+        beta = norm_next / norm_now
+        curve = r_ar + 2.0 * beta * r_ap + beta * beta * curve
+        direction = residual + beta * direction
+        image = applied + beta * image
         norm_now = norm_next
     surface_next = surface - continuity * divergence(solution)
     return (surface_next, solution[0], solution[1])

time: 498 us -> 373 us (0.75)
  blocking collectives: 334 us -> 209 us
    psum x5 -> x3, blocking collectives: 334 us -> 209 us  [sums(): return lax.psum(local, ('lat', 'lon'))]
    sub x0 -> x2, other arithmetic: none -> 8 us  [per_device(): residual = residual - alpha * image]
    add x2 -> x0, other arithmetic: 7.99 us -> none  [per_device(): direction = residual + norm_next / norm_now * direction]
    reduce_sum x5 -> x3, other arithmetic: 16.2 us -> 8.34 us  [sums(): local = jnp.stack([jnp.sum(x * y) for x, y in pairs])]
    another operation x0 -> x3, other arithmetic: none -> 5.28 us  [sums(): local = jnp.stack([jnp.sum(x * y) for x, y in pairs])]
where the time goes in v1:
time: 373 us; the launch traced here: 369 us
  blocking collectives  209 us (56%)
  waiting for transfers between devices  54.7 us (15%)
  starting transfers between devices  50.6 us (14%)
  other arithmetic  38.4 us (10%)
  between operations  9.97 us (3%)
  local copies, waits for them, and re-layouts  6.32 us (2%)
    psum x3, blocking collectives, sums(): return lax.psum(local, ('lat', 'lon'))  209 us
    ppermute x20, waiting for transfers between devices, from_behind(): lax.ppermute(value, axis, [(source, source + steps) for source in range(l...  54.7 us
    ppermute x20, starting transfers between devices, from_behind(): lax.ppermute(value, axis, [(source, source + steps) for source in range(l...  50.6 us
    reduce_sum x3, other arithmetic, sums(): local = jnp.stack([jnp.sum(x * y) for x, y in pairs])  8.34 us
    sub x2, other arithmetic, per_device(): residual = residual - alpha * image  8 us
  transfers between devices with their start and end apart: 20, of which 10 were waited for; matrix products, arithmetic and copies ran while one was open for 1% of the time, Pallas kernels for 0%

profile of v1, /device:TPU:1, one launch (start us, length us, event | category | flops | bytes accessed | tf_op | source)
XLA Modules:
  0.0 369.0 jit_solution(16811035652455948281)
XLA Ops:
  2.5 3.3 collective-permute-start.1
  8.7 9.9 %collective-permute-done = f32[3,256,1]{2,1,0:T(8,128)S(1)} collective-permute-done((f32[3,256,1]{2,1,0:T(8,128)S(1)}, f32[3,256,1]{2,1,0:T(8,128)S(1)}, u32[]{:S(2)}, u32[]{:S(2)}) %collective-permute-start) | collective-permute-done | bytes 3104 | tf_op jit(solution)/shard_map/ppermute | solution.py:17
  21.5 4.3 %collective-permute-start.3 = (f32[2,1,1024]{2,1,0:T(1,128)S(1)}, f32[2,1,1024]{2,1,0:T(1,128)S(1)}, u32[]{:S(2)}, u32[]{:S(2)}) collective-permute-start(f32[2,1,1024]{2,1,0:T(1,128)S(1)} %slice.280), channel_id=1, source_target_pairs={{0,16},{16,32},{32,48},{48,64},{64,80},{80,96},{96,112},{1,17},{17... | collective-permute-start | bytes 24584 | tf_op jit(solution)/shard_map/ppermute | solution.py:17
  25.9 3.2 collective-permute-start.2
  29.1 4.8 %collective-permute-done.2 = f32[2,256,1]{2,1,0:T(8,128)S(1)} collective-permute-done((f32[2,256,1]{2,1,0:T(8,128)S(1)}, f32[2,256,1]{2,1,0:T(8,128)S(1)}, u32[]{:S(2)}, u32[]{:S(2)}) %collective-permute-start.2) | collective-permute-done | bytes 2080 | tf_op jit(solution)/shard_map/ppermute | solution.py:17
  38.3 4.8 %collective-permute-done.4 = f32[1,256,1]{2,1,0:T(8,128)S(1)} collective-permute-done((f32[1,256,1]{2,1,0:T(8,128)S(1)}, f32[1,256,1]{2,1,0:T(8,128)S(1)}, u32[]{:S(2)}, u32[]{:S(2)}) %collective-permute-start.4) | collective-permute-done | bytes 1056 | tf_op jit(solution)/shard_map/ppermute | solution.py:17
  44.7 5.4 %collective-permute-start.7 = (f32[2,1,1024]{2,1,0:T(1,128)S(1)}, f32[2,1,1024]{2,1,0:T(1,128)S(1)}, u32[]{:S(2)}, u32[]{:S(2)}) collective-permute-start(f32[2,1,1024]{2,1,0:T(1,128)S(1)} %slice.290), channel_id=1, source_target_pairs={{0,16},{16,32},{32,48},{48,64},{64,80},{80,96},{96,112},{1,17},{17... | collective-permute-start | bytes 24584 | tf_op jit(solution)/shard_map/ppermute | solution.py:17
  50.2 4.4 %collective-permute-start.6 = (f32[2,256,1]{2,1,0:T(8,128)S(1)}, f32[2,256,1]{2,1,0:T(8,128)S(1)}, u32[]{:S(2)}, u32[]{:S(2)}) collective-permute-start(f32[2,256,1]{2,1,0:T(8,128)S(1)} %slice.287), channel_id=1, source_target_pairs={{0,1},{1,2},{2,3},{3,4},{4,5},{5,6},{6,7},{7,8},{8,9},{9,10},{10,1... | collective-permute-start | bytes 6152 | tf_op jit(solution)/shard_map/ppermute | solution.py:17
  54.6 3.3 collective-permute-done.6
  62.2 4.7 %collective-permute-done.8 = f32[1,256,1]{2,1,0:T(8,128)S(1)} collective-permute-done((f32[1,256,1]{2,1,0:T(8,128)S(1)}, f32[1,256,1]{2,1,0:T(8,128)S(1)}, u32[]{:S(2)}, u32[]{:S(2)}) %collective-permute-start.8) | collective-permute-done | bytes 1056 | tf_op jit(solution)/shard_map/ppermute | solution.py:17
  67.3 3.2 multiply_reduce_fusion.6
  71.9 74.4 %psum.21 = f32[2]{0:T(128)S(1)} all-reduce(f32[2]{0:T(128)S(1)} %pad_maximum_fusion.17), channel_id=1, replica_groups=mesh['lat'=8,'lon'=16] {'lat','lon'}, use_global_device_ids=true, to_apply=%region_2.0 | all-reduce | flops 2 | bytes 16 | tf_op jit(solution)/shard_map/psum | solution.py:53
  148.2 5.1 %multiply_subtract_fusion.1 = f32[2,256,1024]{2,1,0:T(8,128)S(1)} fusion(f32[2,256,1024]{2,1,0:T(8,128)} %get-tuple-element.15, f32[]{:T(128)S(6)} %div.23, f32[1,256,1024]{2,1,0:T(8,128)} %copy-done.19, f32[1,256,1024]{2,1,0:T(8,128)} %copy-done.18, f32[1,256,1024]{2,1,0:T(8,128)} %copy-done.1, f32[1,256,1024]{2,1,0:T(8,128)} %copy-done.4, ...), kind=kLoop, calls=%fused_computation.35 | loop fusion | flops 10485760 | bytes 14680068 | tf_op jit(solution)/shard_map/sub | solution.py:76
  158.9 5.3 %collective-permute-done.10 = f32[2,256,1]{2,1,0:T(8,128)S(1)} collective-permute-done((f32[2,256,1]{2,1,0:T(8,128)S(1)}, f32[2,256,1]{2,1,0:T(8,128)S(1)}, u32[]{:S(2)}, u32[]{:S(2)}) %collective-permute-start.10) | collective-permute-done | bytes 2080 | tf_op jit(solution)/shard_map/ppermute | solution.py:17
  168.6 5.4 %collective-permute-done.12 = f32[1,256,1]{2,1,0:T(8,128)S(1)} collective-permute-done((f32[1,256,1]{2,1,0:T(8,128)S(1)}, f32[1,256,1]{2,1,0:T(8,128)S(1)}, u32[]{:S(2)}, u32[]{:S(2)}) %collective-permute-start.12) | collective-permute-done | bytes 1056 | tf_op jit(solution)/shard_map/ppermute | solution.py:17
  179.4 67.3 %psum.22 = f32[3]{0:T(128)S(1)} all-reduce(f32[3]{0:T(128)S(1)} %pad_maximum_fusion.18), channel_id=1, replica_groups=mesh['lat'=8,'lon'=16] {'lat','lon'}, use_global_device_ids=true, to_apply=%region_6.0 | all-reduce | flops 3 | bytes 24 | tf_op jit(solution)/shard_map/psum | solution.py:53
  251.3 2.9 multiply_subtract_fusion
  254.3 3.8 %collective-permute-start.15 = (f32[2,1,1024]{2,1,0:T(1,128)S(1)}, f32[2,1,1024]{2,1,0:T(1,128)S(1)}, u32[]{:S(2)}, u32[]{:S(2)}) collective-permute-start(f32[2,1,1024]{2,1,0:T(1,128)S(1)} %slice.310), channel_id=1, source_target_pairs={{0,16},{16,32},{32,48},{48,64},{64,80},{80,96},{96,112},{1,17},{17... | collective-permute-start | bytes 24584 | tf_op jit(solution)/shard_map/ppermute | solution.py:17
  259.5 5.7 %collective-permute-done.14 = f32[2,256,1]{2,1,0:T(8,128)S(1)} collective-permute-done((f32[2,256,1]{2,1,0:T(8,128)S(1)}, f32[2,256,1]{2,1,0:T(8,128)S(1)}, u32[]{:S(2)}, u32[]{:S(2)}) %collective-permute-start.14) | collective-permute-done | bytes 2080 | tf_op jit(solution)/shard_map/ppermute | solution.py:17
  269.5 5.5 %collective-permute-done.16 = f32[1,256,1]{2,1,0:T(8,128)S(1)} collective-permute-done((f32[1,256,1]{2,1,0:T(8,128)S(1)}, f32[1,256,1]{2,1,0:T(8,128)S(1)}, u32[]{:S(2)}, u32[]{:S(2)}) %collective-permute-start.16) | collective-permute-done | bytes 1056 | tf_op jit(solution)/shard_map/ppermute | solution.py:17
  279.6 67.3 %psum.23 = f32[3]{0:T(128)S(1)} all-reduce(f32[3]{0:T(128)S(1)} %pad_maximum_fusion.19), channel_id=1, replica_groups=mesh['lat'=8,'lon'=16] {'lat','lon'}, use_global_device_ids=true, to_apply=%region_10.0 | all-reduce | flops 3 | bytes 24 | tf_op jit(solution)/shard_map/psum | solution.py:53
  350.8 5.3 %multiply_add_fusion = f32[2,256,1024]{2,1,0:T(8,128)S(1)} fusion(f32[2,256,1024]{2,1,0:T(8,128)} %copy-done, f32[2,256,1024]{2,1,0:T(8,128)S(1)} %multiply_subtract_fusion.1, f32[]{:T(128)S(6)} %div.26, f32[]{:T(128)S(6)} %div.27, f32[]{:T(128)S(6)} %div.24, f32[]{:T(128)S(6)} %div.25, f32[]{:T(128)S(6)} %div.23, f32[1,256,1024]{2,1,0:T(8,128)} %copy-done.19, ...), kind=kLoop, calls=%fused_computation.27 | loop fusion | flops 14680064 | bytes 16777236 | tf_op jit(solution)/shard_map/add | solution.py:73
  358.5 3.1 collective-permute-start.18
  361.6 5.2 %collective-permute-done.18 = f32[2,256,1]{2,1,0:T(8,128)S(1)} collective-permute-done((f32[2,256,1]{2,1,0:T(8,128)S(1)}, f32[2,256,1]{2,1,0:T(8,128)S(1)}, u32[]{:S(2)}, u32[]{:S(2)}) %collective-permute-start.18) | collective-permute-done | bytes 2080 | tf_op jit(solution)/shard_map/ppermute | solution.py:17
  (121 shorter events, 51.4 us)
Async XLA Ops:
  2.5 16.1 %collective-permute-start.1 = (f32[3,1,1024]{2,1,0:T(1,128)S(1)}, f32[3,1,1024]{2,1,0:T(1,128)S(1)}, u32[]{:S(2)}, u32[]{:S(2)}) collective-permute-start(f32[3,1,1024]{2,1,0:T(1,128)S(1)} %pad_maximum_fusion.16), channel_id=1, source_target_pairs={{16,0},{32,16},{48,32},{64,48},{80,64},{96,80},{112,96},{17,1},{33... | collective-permute-start | bytes 36872 | tf_op jit(solution)/shard_map/ppermute | solution.py:17
  5.9 12.7 %collective-permute-start = (f32[3,256,1]{2,1,0:T(8,128)S(1)}, f32[3,256,1]{2,1,0:T(8,128)S(1)}, u32[]{:S(2)}, u32[]{:S(2)}) collective-permute-start(f32[3,256,1]{2,1,0:T(8,128)S(1)} %pad_maximum_fusion.15), channel_id=1, source_target_pairs={{1,0},{2,1},{3,2},{4,3},{5,4},{6,5},{7,6},{8,7},{9,8},{10,9},{11,1... | collective-permute-start | bytes 9224 | tf_op jit(solution)/shard_map/ppermute | solution.py:17
  20.3 46.9 %copy-start.1 = (f32[1,256,1024]{2,1,0:T(8,128)}, f32[1,256,1024]{2,1,0:T(8,128)S(1)}, u32[]{:S(2)}) copy-start(f32[1,256,1024]{2,1,0:T(8,128)S(1)} %get-tuple-element.21) | copy-start | bytes 3145732
  20.3 46.9 %copy-start.4 = (f32[1,256,1024]{2,1,0:T(8,128)}, f32[1,256,1024]{2,1,0:T(8,128)S(1)}, u32[]{:S(2)}) copy-start(f32[1,256,1024]{2,1,0:T(8,128)S(1)} %get-tuple-element.22) | copy-start | bytes 3145732
  20.4 46.9 %copy-start.7 = (f32[1,256,1024]{2,1,0:T(8,128)}, f32[1,256,1024]{2,1,0:T(8,128)S(1)}, u32[]{:S(2)}) copy-start(f32[1,256,1024]{2,1,0:T(8,128)S(1)} %get-tuple-element.24) | copy-start | bytes 3145732
  20.4 46.9 %copy-start.12 = (f32[1,256,1024]{2,1,0:T(8,128)}, f32[1,256,1024]{2,1,0:T(8,128)S(1)}, u32[]{:S(2)}) copy-start(f32[1,256,1024]{2,1,0:T(8,128)S(1)} %get-tuple-element.20) | copy-start | bytes 3145732
  21.5 12.5 %collective-permute-start.3 = (f32[2,1,1024]{2,1,0:T(1,128)S(1)}, f32[2,1,1024]{2,1,0:T(1,128)S(1)}, u32[]{:S(2)}, u32[]{:S(2)}) collective-permute-start(f32[2,1,1024]{2,1,0:T(1,128)S(1)} %slice.280), channel_id=1, source_target_pairs={{0,16},{16,32},{32,48},{48,64},{64,80},{80,96},{96,112},{1,17},{17... | collective-permute-start | bytes 24584 | tf_op jit(solution)/shard_map/ppermute | solution.py:17
  25.9 8.0 %collective-permute-start.2 = (f32[2,256,1]{2,1,0:T(8,128)S(1)}, f32[2,256,1]{2,1,0:T(8,128)S(1)}, u32[]{:S(2)}, u32[]{:S(2)}) collective-permute-start(f32[2,256,1]{2,1,0:T(8,128)S(1)} %slice.277), channel_id=1, source_target_pairs={{0,1},{1,2},{2,3},{3,4},{4,5},{5,6},{6,7},{7,8},{8,9},{9,10},{10,1... | collective-permute-start | bytes 6152 | tf_op jit(solution)/shard_map/ppermute | solution.py:17
  34.5 8.5 %collective-permute-start.5 = (f32[1,1,1024]{2,1,0:T(1,128)S(1)}, f32[1,1,1024]{2,1,0:T(1,128)S(1)}, u32[]{:S(2)}, u32[]{:S(2)}) collective-permute-start(f32[1,1,1024]{2,1,0:T(1,128)S(1)} %slice.285), channel_id=1, source_target_pairs={{16,0},{32,16},{48,32},{64,48},{80,64},{96,80},{112,96},{17,1},{33... | collective-permute-start | bytes 12296 | tf_op jit(solution)/shard_map/ppermute | solution.py:17
  36.5 6.5 %collective-permute-start.4 = (f32[1,256,1]{2,1,0:T(8,128)S(1)}, f32[1,256,1]{2,1,0:T(8,128)S(1)}, u32[]{:S(2)}, u32[]{:S(2)}) collective-permute-start(f32[1,256,1]{2,1,0:T(8,128)S(1)} %slice.283), channel_id=1, source_target_pairs={{1,0},{2,1},{3,2},{4,3},{5,4},{6,5},{7,6},{8,7},{9,8},{10,9},{11,1... | collective-permute-start | bytes 3080 | tf_op jit(solution)/shard_map/ppermute | solution.py:17
  44.7 13.3 %collective-permute-start.7 = (f32[2,1,1024]{2,1,0:T(1,128)S(1)}, f32[2,1,1024]{2,1,0:T(1,128)S(1)}, u32[]{:S(2)}, u32[]{:S(2)}) collective-permute-start(f32[2,1,1024]{2,1,0:T(1,128)S(1)} %slice.290), channel_id=1, source_target_pairs={{0,16},{16,32},{32,48},{48,64},{64,80},{80,96},{96,112},{1,17},{17... | collective-permute-start | bytes 24584 | tf_op jit(solution)/shard_map/ppermute | solution.py:17
  50.2 7.7 %collective-permute-start.6 = (f32[2,256,1]{2,1,0:T(8,128)S(1)}, f32[2,256,1]{2,1,0:T(8,128)S(1)}, u32[]{:S(2)}, u32[]{:S(2)}) collective-permute-start(f32[2,256,1]{2,1,0:T(8,128)S(1)} %slice.287), channel_id=1, source_target_pairs={{0,1},{1,2},{2,3},{3,4},{4,5},{5,6},{6,7},{7,8},{8,9},{9,10},{10,1... | collective-permute-start | bytes 6152 | tf_op jit(solution)/shard_map/ppermute | solution.py:17
  58.5 8.4 %collective-permute-start.9 = (f32[1,1,1024]{2,1,0:T(1,128)S(1)}, f32[1,1,1024]{2,1,0:T(1,128)S(1)}, u32[]{:S(2)}, u32[]{:S(2)}) collective-permute-start(f32[1,1,1024]{2,1,0:T(1,128)S(1)} %slice.295), channel_id=1, source_target_pairs={{16,0},{32,16},{48,32},{64,48},{80,64},{96,80},{112,96},{17,1},{33... | collective-permute-start | bytes 12296 | tf_op jit(solution)/shard_map/ppermute | solution.py:17
  60.5 6.5 %collective-permute-start.8 = (f32[1,256,1]{2,1,0:T(8,128)S(1)}, f32[1,256,1]{2,1,0:T(8,128)S(1)}, u32[]{:S(2)}, u32[]{:S(2)}) collective-permute-start(f32[1,256,1]{2,1,0:T(8,128)S(1)} %slice.293), channel_id=1, source_target_pairs={{1,0},{2,1},{3,2},{4,3},{5,4},{6,5},{7,6},{8,7},{9,8},{10,9},{11,1... | collective-permute-start | bytes 3080 | tf_op jit(solution)/shard_map/ppermute | solution.py:17
  153.3 11.0 %collective-permute-start.11 = (f32[2,1,1024]{2,1,0:T(1,128)S(1)}, f32[2,1,1024]{2,1,0:T(1,128)S(1)}, u32[]{:S(2)}, u32[]{:S(2)}) collective-permute-start(f32[2,1,1024]{2,1,0:T(1,128)S(1)} %slice.300), channel_id=1, source_target_pairs={{0,16},{16,32},{32,48},{48,64},{64,80},{80,96},{96,112},{1,17},{17... | collective-permute-start | bytes 24584 | tf_op jit(solution)/shard_map/ppermute | solution.py:17
  156.3 8.0 %collective-permute-start.10 = (f32[2,256,1]{2,1,0:T(8,128)S(1)}, f32[2,256,1]{2,1,0:T(8,128)S(1)}, u32[]{:S(2)}, u32[]{:S(2)}) collective-permute-start(f32[2,256,1]{2,1,0:T(8,128)S(1)} %slice.297), channel_id=1, source_target_pairs={{0,1},{1,2},{2,3},{3,4},{4,5},{5,6},{6,7},{7,8},{8,9},{9,10},{10,1... | collective-permute-start | bytes 6152 | tf_op jit(solution)/shard_map/ppermute | solution.py:17
  164.8 9.2 %collective-permute-start.13 = (f32[1,1,1024]{2,1,0:T(1,128)S(1)}, f32[1,1,1024]{2,1,0:T(1,128)S(1)}, u32[]{:S(2)}, u32[]{:S(2)}) collective-permute-start(f32[1,1,1024]{2,1,0:T(1,128)S(1)} %slice.305), channel_id=1, source_target_pairs={{16,0},{32,16},{48,32},{64,48},{80,64},{96,80},{112,96},{17,1},{33... | collective-permute-start | bytes 12296 | tf_op jit(solution)/shard_map/ppermute | solution.py:17
  166.8 7.2 %collective-permute-start.12 = (f32[1,256,1]{2,1,0:T(8,128)S(1)}, f32[1,256,1]{2,1,0:T(8,128)S(1)}, u32[]{:S(2)}, u32[]{:S(2)}) collective-permute-start(f32[1,256,1]{2,1,0:T(8,128)S(1)} %slice.303), channel_id=1, source_target_pairs={{1,0},{2,1},{3,2},{4,3},{5,4},{6,5},{7,6},{8,7},{9,8},{10,9},{11,1... | collective-permute-start | bytes 3080 | tf_op jit(solution)/shard_map/ppermute | solution.py:17
  254.3 10.9 %collective-permute-start.15 = (f32[2,1,1024]{2,1,0:T(1,128)S(1)}, f32[2,1,1024]{2,1,0:T(1,128)S(1)}, u32[]{:S(2)}, u32[]{:S(2)}) collective-permute-start(f32[2,1,1024]{2,1,0:T(1,128)S(1)} %slice.310), channel_id=1, source_target_pairs={{0,16},{16,32},{32,48},{48,64},{64,80},{80,96},{96,112},{1,17},{17... | collective-permute-start | bytes 24584 | tf_op jit(solution)/shard_map/ppermute | solution.py:17
  258.2 7.0 %collective-permute-start.14 = (f32[2,256,1]{2,1,0:T(8,128)S(1)}, f32[2,256,1]{2,1,0:T(8,128)S(1)}, u32[]{:S(2)}, u32[]{:S(2)}) collective-permute-start(f32[2,256,1]{2,1,0:T(8,128)S(1)} %slice.307), channel_id=1, source_target_pairs={{0,1},{1,2},{2,3},{3,4},{4,5},{5,6},{6,7},{7,8},{8,9},{9,10},{10,1... | collective-permute-start | bytes 6152 | tf_op jit(solution)/shard_map/ppermute | solution.py:17
  265.7 9.3 %collective-permute-start.17 = (f32[1,1,1024]{2,1,0:T(1,128)S(1)}, f32[1,1,1024]{2,1,0:T(1,128)S(1)}, u32[]{:S(2)}, u32[]{:S(2)}) collective-permute-start(f32[1,1,1024]{2,1,0:T(1,128)S(1)} %slice.315), channel_id=1, source_target_pairs={{16,0},{32,16},{48,32},{64,48},{80,64},{96,80},{112,96},{17,1},{33... | collective-permute-start | bytes 12296 | tf_op jit(solution)/shard_map/ppermute | solution.py:17
  267.7 7.4 %collective-permute-start.16 = (f32[1,256,1]{2,1,0:T(8,128)S(1)}, f32[1,256,1]{2,1,0:T(8,128)S(1)}, u32[]{:S(2)}, u32[]{:S(2)}) collective-permute-start(f32[1,256,1]{2,1,0:T(8,128)S(1)} %slice.313), channel_id=1, source_target_pairs={{1,0},{2,1},{3,2},{4,3},{5,4},{6,5},{7,6},{8,7},{9,8},{10,9},{11,1... | collective-permute-start | bytes 3080 | tf_op jit(solution)/shard_map/ppermute | solution.py:17
  356.1 10.7 %collective-permute-start.19 = (f32[2,1,1024]{2,1,0:T(1,128)S(1)}, f32[2,1,1024]{2,1,0:T(1,128)S(1)}, u32[]{:S(2)}, u32[]{:S(2)}) collective-permute-start(f32[2,1,1024]{2,1,0:T(1,128)S(1)} %slice.320), channel_id=1, source_target_pairs={{0,16},{16,32},{32,48},{48,64},{64,80},{80,96},{96,112},{1,17},{17... | collective-permute-start | bytes 24584 | tf_op jit(solution)/shard_map/ppermute | solution.py:17
  358.5 8.3 %collective-permute-start.18 = (f32[2,256,1]{2,1,0:T(8,128)S(1)}, f32[2,256,1]{2,1,0:T(8,128)S(1)}, u32[]{:S(2)}, u32[]{:S(2)}) collective-permute-start(f32[2,256,1]{2,1,0:T(8,128)S(1)} %slice.317), channel_id=1, source_target_pairs={{0,1},{1,2},{2,3},{3,4},{4,5},{5,6},{6,7},{7,8},{8,9},{9,10},{10,1... | collective-permute-start | bytes 6152 | tf_op jit(solution)/shard_map/ppermute | solution.py:17
  (19 other events, 223.3 us)

commit v2 on v1

--- a/solution.py
+++ b/solution.py
@@ -48,9 +48,30 @@
     return wet * (inverse * field + gradient_back(field))
 
 
+def exchange(value, axis, mask):
+    return lax.ppermute(value, axis, [(i, i ^ mask) for i in range(lax.axis_size(axis))])
+
+
+def quad_sum(value, axis, step):
+    first = exchange(value, axis, step)
+    second = exchange(value, axis, 2 * step)
+    third = exchange(value, axis, 3 * step)
+    return (value + first) + (second + third)
+
+
+def total(value, axis):
+    count, step = lax.axis_size(axis), 1
+    while count >= 4:
+        value = quad_sum(value, axis, step)
+        count, step = count // 4, step * 4
+    if count == 2:
+        value = value + exchange(value, axis, step)
+    return value
+
+
 def sums(*pairs):
     local = jnp.stack([jnp.sum(x * y) for x, y in pairs])
-    return lax.psum(local, ("lat", "lon"))
+    return total(total(local, "lon"), "lat")
 
 
 def per_device(surface, bathymetry, land_sea, flux_lon, flux_lat):

time: 373 us -> 253 us (0.68)
  blocking collectives: 209 us -> 0 us
  starting transfers between devices: 50.6 us -> 113 us
  waiting for transfers between devices: 54.7 us -> 76.9 us
  other arithmetic: 38.4 us -> 43.7 us
    psum x3 -> x0, blocking collectives: 209 us -> none  [sums(): return lax.psum(local, ('lat', 'lon'))]
    ppermute x0 -> x30, starting transfers between devices: none -> 59 us  [exchange(): lax.ppermute(value, axis, [(i, i ^ mask) for i in range(lax.axis_size(axi...]
    ppermute x0 -> x30, waiting for transfers between devices: none -> 21.7 us  [exchange(): lax.ppermute(value, axis, [(i, i ^ mask) for i in range(lax.axis_size(axi...]
    add x0 -> x12, other arithmetic: none -> 5.28 us  [the longest x9 5.27 us: quad_sum(): return value + first + (second + third)]
    ppermute x20, starting transfers between devices: 50.6 us -> 54.4 us  [from_behind(): lax.ppermute(value, axis, [(source, source + steps) for source in range(l...]
  transfers between devices with their start and end apart: 20 -> 50, of which waited for: 10 -> 31; matrix products, arithmetic and copies ran while one was open for 1% -> 2% of each run, Pallas kernels for 0% -> 0%
where the time goes in v2:
time: 253 us; the launch traced here: 250 us
  starting transfers between devices  113 us (45%)
  waiting for transfers between devices  76.9 us (30%)
  other arithmetic  43.7 us (17%)
  between operations  10.2 us (4%)
  local copies, waits for them, and re-layouts  6.36 us (3%)
    ppermute x30, starting transfers between devices, exchange(): lax.ppermute(value, axis, [(i, i ^ mask) for i in range(lax.axis_size(axi...  59 us
    ppermute x20, waiting for transfers between devices, from_behind(): lax.ppermute(value, axis, [(source, source + steps) for source in range(l...  55.1 us
    ppermute x20, starting transfers between devices, from_behind(): lax.ppermute(value, axis, [(source, source + steps) for source in range(l...  54.4 us
    ppermute x30, waiting for transfers between devices, exchange(): lax.ppermute(value, axis, [(i, i ^ mask) for i in range(lax.axis_size(axi...  21.7 us
    reduce_sum x3, other arithmetic, sums(): local = jnp.stack([jnp.sum(x * y) for x, y in pairs])  8.41 us
    sub x2, other arithmetic, per_device(): residual = residual - alpha * image  8 us
    add x1, other arithmetic, per_device(): solution = solution + alpha * direction  5.3 us
    add x9, other arithmetic, quad_sum(): return value + first + (second + third)  5.27 us
  transfers between devices with their start and end apart: 50, of which 31 were waited for; matrix products, arithmetic and copies ran while one was open for 2% of the time, Pallas kernels for 0%

profile of v2, /device:TPU:1, one launch (start us, length us, event | category | flops | bytes accessed | tf_op | source)
XLA Modules:
  0.0 250.4 jit_solution(15967228814199173466)
XLA Ops:
  8.7 9.9 %collective-permute-done = f32[3,256,1]{2,1,0:T(8,128)S(1)} collective-permute-done((f32[3,256,1]{2,1,0:T(8,128)S(1)}, f32[3,256,1]{2,1,0:T(8,128)S(1)}, u32[]{:S(2)}, u32[]{:S(2)}) %collective-permute-start) | collective-permute-done | bytes 3104 | tf_op jit(solution)/shard_map/ppermute | solution.py:17
  21.5 4.3 %collective-permute-start.3 = (f32[2,1,1024]{2,1,0:T(1,128)S(1)}, f32[2,1,1024]{2,1,0:T(1,128)S(1)}, u32[]{:S(2)}, u32[]{:S(2)}) collective-permute-start(f32[2,1,1024]{2,1,0:T(1,128)S(1)} %slice.280), channel_id=1, source_target_pairs={{0,16},{16,32},{32,48},{48,64},{64,80},{80,96},{96,112},{1,17},{17... | collective-permute-start | bytes 24584 | tf_op jit(solution)/shard_map/ppermute | solution.py:17
  29.1 4.8 %collective-permute-done.2 = f32[2,256,1]{2,1,0:T(8,128)S(1)} collective-permute-done((f32[2,256,1]{2,1,0:T(8,128)S(1)}, f32[2,256,1]{2,1,0:T(8,128)S(1)}, u32[]{:S(2)}, u32[]{:S(2)}) %collective-permute-start.2) | collective-permute-done | bytes 2080 | tf_op jit(solution)/shard_map/ppermute | solution.py:17
  38.3 4.8 %collective-permute-done.4 = f32[1,256,1]{2,1,0:T(8,128)S(1)} collective-permute-done((f32[1,256,1]{2,1,0:T(8,128)S(1)}, f32[1,256,1]{2,1,0:T(8,128)S(1)}, u32[]{:S(2)}, u32[]{:S(2)}) %collective-permute-start.4) | collective-permute-done | bytes 1056 | tf_op jit(solution)/shard_map/ppermute | solution.py:17
  44.7 5.4 %collective-permute-start.7 = (f32[2,1,1024]{2,1,0:T(1,128)S(1)}, f32[2,1,1024]{2,1,0:T(1,128)S(1)}, u32[]{:S(2)}, u32[]{:S(2)}) collective-permute-start(f32[2,1,1024]{2,1,0:T(1,128)S(1)} %slice.290), channel_id=1, source_target_pairs={{0,16},{16,32},{32,48},{48,64},{64,80},{80,96},{96,112},{1,17},{17... | collective-permute-start | bytes 24584 | tf_op jit(solution)/shard_map/ppermute | solution.py:17
  50.2 4.4 %collective-permute-start.6 = (f32[2,256,1]{2,1,0:T(8,128)S(1)}, f32[2,256,1]{2,1,0:T(8,128)S(1)}, u32[]{:S(2)}, u32[]{:S(2)}) collective-permute-start(f32[2,256,1]{2,1,0:T(8,128)S(1)} %slice.287), channel_id=1, source_target_pairs={{0,1},{1,2},{2,3},{3,4},{4,5},{5,6},{6,7},{7,8},{8,9},{9,10},{10,1... | collective-permute-start | bytes 6152 | tf_op jit(solution)/shard_map/ppermute | solution.py:17
  62.2 4.7 %collective-permute-done.8 = f32[1,256,1]{2,1,0:T(8,128)S(1)} collective-permute-done((f32[1,256,1]{2,1,0:T(8,128)S(1)}, f32[1,256,1]{2,1,0:T(8,128)S(1)}, u32[]{:S(2)}, u32[]{:S(2)}) %collective-permute-start.8) | collective-permute-done | bytes 1056 | tf_op jit(solution)/shard_map/ppermute | solution.py:17
  72.0 6.1 %collective-permute-start.11 = (f32[2]{0:T(128)S(1)}, f32[2]{0:T(128)S(1)}, u32[]{:S(2)}, u32[]{:S(2)}) collective-permute-start(f32[2]{0:T(128)S(1)} %pad_maximum_fusion.17), channel_id=1, source_target_pairs={{0,2},{1,3},{2,0},{3,1},{4,6},{5,7},{6,4},{7,5},{8,10},{9,11},{10,... | collective-permute-start | bytes 32 | tf_op jit(solution)/shard_map/ppermute | solution.py:52
  89.9 7.9 %collective-permute-start.18 = (f32[2]{0:T(128)S(1)}, f32[2]{0:T(128)S(1)}, u32[]{:S(2)}, u32[]{:S(2)}) collective-permute-start(f32[2]{0:T(128)S(1)} %add_add_fusion.7), channel_id=1, source_target_pairs={{0,48},{16,32},{32,16},{48,0},{64,112},{80,96},{96,80},{112,64},{1... | collective-permute-start | bytes 32 | tf_op jit(solution)/shard_map/ppermute | solution.py:52
  106.5 5.1 %multiply_subtract_fusion.1 = f32[2,256,1024]{2,1,0:T(8,128)S(1)} fusion(f32[2,256,1024]{2,1,0:T(8,128)} %get-tuple-element.15, f32[]{:T(128)S(6)} %div.23, f32[1,256,1024]{2,1,0:T(8,128)} %copy-done.19, f32[1,256,1024]{2,1,0:T(8,128)} %copy-done.18, f32[1,256,1024]{2,1,0:T(8,128)} %copy-done.1, f32[1,256,1024]{2,1,0:T(8,128)} %copy-done.4, ...), kind=kLoop, calls=%fused_computation.35 | loop fusion | flops 10485760 | bytes 14680068 | tf_op jit(solution)/shard_map/sub | solution.py:97
  111.6 4.3 %collective-permute-start.21 = (f32[2,1,1024]{2,1,0:T(1,128)S(1)}, f32[2,1,1024]{2,1,0:T(1,128)S(1)}, u32[]{:S(2)}, u32[]{:S(2)}) collective-permute-start(f32[2,1,1024]{2,1,0:T(1,128)S(1)} %slice.300), channel_id=1, source_target_pairs={{0,16},{16,32},{32,48},{48,64},{64,80},{80,96},{96,112},{1,17},{17... | collective-permute-start | bytes 24584 | tf_op jit(solution)/shard_map/ppermute | solution.py:17
  118.4 5.1 %collective-permute-done.20 = f32[2,256,1]{2,1,0:T(8,128)S(1)} collective-permute-done((f32[2,256,1]{2,1,0:T(8,128)S(1)}, f32[2,256,1]{2,1,0:T(8,128)S(1)}, u32[]{:S(2)}, u32[]{:S(2)}) %collective-permute-start.20) | collective-permute-done | bytes 2080 | tf_op jit(solution)/shard_map/ppermute | solution.py:17
  127.9 5.0 %collective-permute-done.22 = f32[1,256,1]{2,1,0:T(8,128)S(1)} collective-permute-done((f32[1,256,1]{2,1,0:T(8,128)S(1)}, f32[1,256,1]{2,1,0:T(8,128)S(1)}, u32[]{:S(2)}, u32[]{:S(2)}) %collective-permute-start.22) | collective-permute-done | bytes 1056 | tf_op jit(solution)/shard_map/ppermute | solution.py:17
  138.2 3.8 %collective-permute-start.25 = (f32[3]{0:T(128)S(1)}, f32[3]{0:T(128)S(1)}, u32[]{:S(2)}, u32[]{:S(2)}) collective-permute-start(f32[3]{0:T(128)S(1)} %pad_maximum_fusion.18), channel_id=1, source_target_pairs={{0,2},{1,3},{2,0},{3,1},{4,6},{5,7},{6,4},{7,5},{8,10},{9,11},{10,... | collective-permute-start | bytes 44 | tf_op jit(solution)/shard_map/ppermute | solution.py:52
  153.7 5.5 %collective-permute-start.32 = (f32[3]{0:T(128)S(1)}, f32[3]{0:T(128)S(1)}, u32[]{:S(2)}, u32[]{:S(2)}) collective-permute-start(f32[3]{0:T(128)S(1)} %add_add_fusion.4), channel_id=1, source_target_pairs={{0,48},{16,32},{32,16},{48,0},{64,112},{80,96},{96,80},{112,64},{1... | collective-permute-start | bytes 44 | tf_op jit(solution)/shard_map/ppermute | solution.py:52
  161.6 3.6 %collective-permute-start.33 = (f32[3]{0:T(128)S(1)}, f32[3]{0:T(128)S(1)}, u32[]{:S(2)}, u32[]{:S(2)}) collective-permute-start(f32[3]{0:T(128)S(1)} %add_add_fusion.3), channel_id=1, source_target_pairs={{0,64},{16,80},{32,96},{48,112},{64,0},{80,16},{96,32},{112,48},{1... | collective-permute-start | bytes 44 | tf_op jit(solution)/shard_map/ppermute | solution.py:52
  173.8 3.8 %collective-permute-start.35 = (f32[2,1,1024]{2,1,0:T(1,128)S(1)}, f32[2,1,1024]{2,1,0:T(1,128)S(1)}, u32[]{:S(2)}, u32[]{:S(2)}) collective-permute-start(f32[2,1,1024]{2,1,0:T(1,128)S(1)} %slice.310), channel_id=1, source_target_pairs={{0,16},{16,32},{32,48},{48,64},{64,80},{80,96},{96,112},{1,17},{17... | collective-permute-start | bytes 24584 | tf_op jit(solution)/shard_map/ppermute | solution.py:17
  180.6 5.8 %collective-permute-done.34 = f32[2,256,1]{2,1,0:T(8,128)S(1)} collective-permute-done((f32[2,256,1]{2,1,0:T(8,128)S(1)}, f32[2,256,1]{2,1,0:T(8,128)S(1)}, u32[]{:S(2)}, u32[]{:S(2)}) %collective-permute-start.34) | collective-permute-done | bytes 2080 | tf_op jit(solution)/shard_map/ppermute | solution.py:17
  190.8 5.6 %collective-permute-done.36 = f32[1,256,1]{2,1,0:T(8,128)S(1)} collective-permute-done((f32[1,256,1]{2,1,0:T(8,128)S(1)}, f32[1,256,1]{2,1,0:T(8,128)S(1)}, u32[]{:S(2)}, u32[]{:S(2)}) %collective-permute-start.36) | collective-permute-done | bytes 1056 | tf_op jit(solution)/shard_map/ppermute | solution.py:17
  215.0 4.7 %collective-permute-start.46 = (f32[3]{0:T(128)S(1)}, f32[3]{0:T(128)S(1)}, u32[]{:S(2)}, u32[]{:S(2)}) collective-permute-start(f32[3]{0:T(128)S(1)} %add_add_fusion.1), channel_id=1, source_target_pairs={{0,48},{16,32},{32,16},{48,0},{64,112},{80,96},{96,80},{112,64},{1... | collective-permute-start | bytes 44 | tf_op jit(solution)/shard_map/ppermute | solution.py:52
  222.1 3.5 %collective-permute-start.47 = (f32[3]{0:T(128)S(1)}, f32[3]{0:T(128)S(1)}, u32[]{:S(2)}, u32[]{:S(2)}) collective-permute-start(f32[3]{0:T(128)S(1)} %add_add_fusion), channel_id=1, source_target_pairs={{0,64},{16,80},{32,96},{48,112},{64,0},{80,16},{96,32},{112,48},{1... | collective-permute-start | bytes 44 | tf_op jit(solution)/shard_map/ppermute | solution.py:52
  230.4 5.3 %multiply_add_fusion = f32[2,256,1024]{2,1,0:T(8,128)S(1)} fusion(f32[2,256,1024]{2,1,0:T(8,128)} %copy-done, f32[2,256,1024]{2,1,0:T(8,128)S(1)} %multiply_subtract_fusion.1, f32[]{:T(128)S(6)} %div.26, f32[]{:T(128)S(6)} %div.27, f32[]{:T(128)S(6)} %div.24, f32[]{:T(128)S(6)} %div.25, f32[]{:T(128)S(6)} %div.23, f32[1,256,1024]{2,1,0:T(8,128)} %copy-done.19, ...), kind=kLoop, calls=%fused_computation.27 | loop fusion | flops 14680064 | bytes 16777236 | tf_op jit(solution)/shard_map/add | solution.py:94
  235.8 3.9 %collective-permute-start.49 = (f32[2,1,1024]{2,1,0:T(1,128)S(1)}, f32[2,1,1024]{2,1,0:T(1,128)S(1)}, u32[]{:S(2)}, u32[]{:S(2)}) collective-permute-start(f32[2,1,1024]{2,1,0:T(1,128)S(1)} %slice.320), channel_id=1, source_target_pairs={{0,16},{16,32},{32,48},{48,64},{64,80},{80,96},{96,112},{1,17},{17... | collective-permute-start | bytes 24584 | tf_op jit(solution)/shard_map/ppermute | solution.py:17
  242.2 6.1 %collective-permute-done.48 = f32[2,256,1]{2,1,0:T(8,128)S(1)} collective-permute-done((f32[2,256,1]{2,1,0:T(8,128)S(1)}, f32[2,256,1]{2,1,0:T(8,128)S(1)}, u32[]{:S(2)}, u32[]{:S(2)}) %collective-permute-start.48) | collective-permute-done | bytes 2080 | tf_op jit(solution)/shard_map/ppermute | solution.py:17
  (190 shorter events, 117.1 us)
Async XLA Ops:
  2.5 16.1 %collective-permute-start.1 = (f32[3,1,1024]{2,1,0:T(1,128)S(1)}, f32[3,1,1024]{2,1,0:T(1,128)S(1)}, u32[]{:S(2)}, u32[]{:S(2)}) collective-permute-start(f32[3,1,1024]{2,1,0:T(1,128)S(1)} %pad_maximum_fusion.16), channel_id=1, source_target_pairs={{16,0},{32,16},{48,32},{64,48},{80,64},{96,80},{112,96},{17,1},{33... | collective-permute-start | bytes 36872 | tf_op jit(solution)/shard_map/ppermute | solution.py:17
  5.9 12.7 %collective-permute-start = (f32[3,256,1]{2,1,0:T(8,128)S(1)}, f32[3,256,1]{2,1,0:T(8,128)S(1)}, u32[]{:S(2)}, u32[]{:S(2)}) collective-permute-start(f32[3,256,1]{2,1,0:T(8,128)S(1)} %pad_maximum_fusion.15), channel_id=1, source_target_pairs={{1,0},{2,1},{3,2},{4,3},{5,4},{6,5},{7,6},{8,7},{9,8},{10,9},{11,1... | collective-permute-start | bytes 9224 | tf_op jit(solution)/shard_map/ppermute | solution.py:17
  21.5 12.5 %collective-permute-start.3 = (f32[2,1,1024]{2,1,0:T(1,128)S(1)}, f32[2,1,1024]{2,1,0:T(1,128)S(1)}, u32[]{:S(2)}, u32[]{:S(2)}) collective-permute-start(f32[2,1,1024]{2,1,0:T(1,128)S(1)} %slice.280), channel_id=1, source_target_pairs={{0,16},{16,32},{32,48},{48,64},{64,80},{80,96},{96,112},{1,17},{17... | collective-permute-start | bytes 24584 | tf_op jit(solution)/shard_map/ppermute | solution.py:17
  25.9 8.0 %collective-permute-start.2 = (f32[2,256,1]{2,1,0:T(8,128)S(1)}, f32[2,256,1]{2,1,0:T(8,128)S(1)}, u32[]{:S(2)}, u32[]{:S(2)}) collective-permute-start(f32[2,256,1]{2,1,0:T(8,128)S(1)} %slice.277), channel_id=1, source_target_pairs={{0,1},{1,2},{2,3},{3,4},{4,5},{5,6},{6,7},{7,8},{8,9},{9,10},{10,1... | collective-permute-start | bytes 6152 | tf_op jit(solution)/shard_map/ppermute | solution.py:17
  34.5 8.5 %collective-permute-start.5 = (f32[1,1,1024]{2,1,0:T(1,128)S(1)}, f32[1,1,1024]{2,1,0:T(1,128)S(1)}, u32[]{:S(2)}, u32[]{:S(2)}) collective-permute-start(f32[1,1,1024]{2,1,0:T(1,128)S(1)} %slice.285), channel_id=1, source_target_pairs={{16,0},{32,16},{48,32},{64,48},{80,64},{96,80},{112,96},{17,1},{33... | collective-permute-start | bytes 12296 | tf_op jit(solution)/shard_map/ppermute | solution.py:17
  36.5 6.5 %collective-permute-start.4 = (f32[1,256,1]{2,1,0:T(8,128)S(1)}, f32[1,256,1]{2,1,0:T(8,128)S(1)}, u32[]{:S(2)}, u32[]{:S(2)}) collective-permute-start(f32[1,256,1]{2,1,0:T(8,128)S(1)} %slice.283), channel_id=1, source_target_pairs={{1,0},{2,1},{3,2},{4,3},{5,4},{6,5},{7,6},{8,7},{9,8},{10,9},{11,1... | collective-permute-start | bytes 3080 | tf_op jit(solution)/shard_map/ppermute | solution.py:17
  44.7 13.3 %collective-permute-start.7 = (f32[2,1,1024]{2,1,0:T(1,128)S(1)}, f32[2,1,1024]{2,1,0:T(1,128)S(1)}, u32[]{:S(2)}, u32[]{:S(2)}) collective-permute-start(f32[2,1,1024]{2,1,0:T(1,128)S(1)} %slice.290), channel_id=1, source_target_pairs={{0,16},{16,32},{32,48},{48,64},{64,80},{80,96},{96,112},{1,17},{17... | collective-permute-start | bytes 24584 | tf_op jit(solution)/shard_map/ppermute | solution.py:17
  50.2 7.7 %collective-permute-start.6 = (f32[2,256,1]{2,1,0:T(8,128)S(1)}, f32[2,256,1]{2,1,0:T(8,128)S(1)}, u32[]{:S(2)}, u32[]{:S(2)}) collective-permute-start(f32[2,256,1]{2,1,0:T(8,128)S(1)} %slice.287), channel_id=1, source_target_pairs={{0,1},{1,2},{2,3},{3,4},{4,5},{5,6},{6,7},{7,8},{8,9},{9,10},{10,1... | collective-permute-start | bytes 6152 | tf_op jit(solution)/shard_map/ppermute | solution.py:17
  58.5 8.4 %collective-permute-start.9 = (f32[1,1,1024]{2,1,0:T(1,128)S(1)}, f32[1,1,1024]{2,1,0:T(1,128)S(1)}, u32[]{:S(2)}, u32[]{:S(2)}) collective-permute-start(f32[1,1,1024]{2,1,0:T(1,128)S(1)} %slice.295), channel_id=1, source_target_pairs={{16,0},{32,16},{48,32},{64,48},{80,64},{96,80},{112,96},{17,1},{33... | collective-permute-start | bytes 12296 | tf_op jit(solution)/shard_map/ppermute | solution.py:17
  60.5 6.5 %collective-permute-start.8 = (f32[1,256,1]{2,1,0:T(8,128)S(1)}, f32[1,256,1]{2,1,0:T(8,128)S(1)}, u32[]{:S(2)}, u32[]{:S(2)}) collective-permute-start(f32[1,256,1]{2,1,0:T(8,128)S(1)} %slice.293), channel_id=1, source_target_pairs={{1,0},{2,1},{3,2},{4,3},{5,4},{6,5},{7,6},{8,7},{9,8},{10,9},{11,1... | collective-permute-start | bytes 3080 | tf_op jit(solution)/shard_map/ppermute | solution.py:17
  72.0 9.1 %collective-permute-start.11 = (f32[2]{0:T(128)S(1)}, f32[2]{0:T(128)S(1)}, u32[]{:S(2)}, u32[]{:S(2)}) collective-permute-start(f32[2]{0:T(128)S(1)} %pad_maximum_fusion.17), channel_id=1, source_target_pairs={{0,2},{1,3},{2,0},{3,1},{4,6},{5,7},{6,4},{7,5},{8,10},{9,11},{10,... | collective-permute-start | bytes 32 | tf_op jit(solution)/shard_map/ppermute | solution.py:52
  89.9 9.2 %collective-permute-start.18 = (f32[2]{0:T(128)S(1)}, f32[2]{0:T(128)S(1)}, u32[]{:S(2)}, u32[]{:S(2)}) collective-permute-start(f32[2]{0:T(128)S(1)} %add_add_fusion.7), channel_id=1, source_target_pairs={{0,48},{16,32},{32,16},{48,0},{64,112},{80,96},{96,80},{112,64},{1... | collective-permute-start | bytes 32 | tf_op jit(solution)/shard_map/ppermute | solution.py:52
  111.6 12.0 %collective-permute-start.21 = (f32[2,1,1024]{2,1,0:T(1,128)S(1)}, f32[2,1,1024]{2,1,0:T(1,128)S(1)}, u32[]{:S(2)}, u32[]{:S(2)}) collective-permute-start(f32[2,1,1024]{2,1,0:T(1,128)S(1)} %slice.300), channel_id=1, source_target_pairs={{0,16},{16,32},{32,48},{48,64},{64,80},{80,96},{96,112},{1,17},{17... | collective-permute-start | bytes 24584 | tf_op jit(solution)/shard_map/ppermute | solution.py:17
  116.0 7.5 %collective-permute-start.20 = (f32[2,256,1]{2,1,0:T(8,128)S(1)}, f32[2,256,1]{2,1,0:T(8,128)S(1)}, u32[]{:S(2)}, u32[]{:S(2)}) collective-permute-start(f32[2,256,1]{2,1,0:T(8,128)S(1)} %slice.297), channel_id=1, source_target_pairs={{0,1},{1,2},{2,3},{3,4},{4,5},{5,6},{6,7},{7,8},{8,9},{9,10},{10,1... | collective-permute-start | bytes 6152 | tf_op jit(solution)/shard_map/ppermute | solution.py:17
  124.1 8.8 %collective-permute-start.23 = (f32[1,1,1024]{2,1,0:T(1,128)S(1)}, f32[1,1,1024]{2,1,0:T(1,128)S(1)}, u32[]{:S(2)}, u32[]{:S(2)}) collective-permute-start(f32[1,1,1024]{2,1,0:T(1,128)S(1)} %slice.305), channel_id=1, source_target_pairs={{16,0},{32,16},{48,32},{64,48},{80,64},{96,80},{112,96},{17,1},{33... | collective-permute-start | bytes 12296 | tf_op jit(solution)/shard_map/ppermute | solution.py:17
  126.1 6.8 %collective-permute-start.22 = (f32[1,256,1]{2,1,0:T(8,128)S(1)}, f32[1,256,1]{2,1,0:T(8,128)S(1)}, u32[]{:S(2)}, u32[]{:S(2)}) collective-permute-start(f32[1,256,1]{2,1,0:T(8,128)S(1)} %slice.303), channel_id=1, source_target_pairs={{1,0},{2,1},{3,2},{4,3},{5,4},{6,5},{7,6},{8,7},{9,8},{10,9},{11,1... | collective-permute-start | bytes 3080 | tf_op jit(solution)/shard_map/ppermute | solution.py:17
  153.7 6.8 %collective-permute-start.32 = (f32[3]{0:T(128)S(1)}, f32[3]{0:T(128)S(1)}, u32[]{:S(2)}, u32[]{:S(2)}) collective-permute-start(f32[3]{0:T(128)S(1)} %add_add_fusion.4), channel_id=1, source_target_pairs={{0,48},{16,32},{32,16},{48,0},{64,112},{80,96},{96,80},{112,64},{1... | collective-permute-start | bytes 44 | tf_op jit(solution)/shard_map/ppermute | solution.py:52
  173.8 12.6 %collective-permute-start.35 = (f32[2,1,1024]{2,1,0:T(1,128)S(1)}, f32[2,1,1024]{2,1,0:T(1,128)S(1)}, u32[]{:S(2)}, u32[]{:S(2)}) collective-permute-start(f32[2,1,1024]{2,1,0:T(1,128)S(1)} %slice.310), channel_id=1, source_target_pairs={{0,16},{16,32},{32,48},{48,64},{64,80},{80,96},{96,112},{1,17},{17... | collective-permute-start | bytes 24584 | tf_op jit(solution)/shard_map/ppermute | solution.py:17
  177.7 8.7 %collective-permute-start.34 = (f32[2,256,1]{2,1,0:T(8,128)S(1)}, f32[2,256,1]{2,1,0:T(8,128)S(1)}, u32[]{:S(2)}, u32[]{:S(2)}) collective-permute-start(f32[2,256,1]{2,1,0:T(8,128)S(1)} %slice.307), channel_id=1, source_target_pairs={{0,1},{1,2},{2,3},{3,4},{4,5},{5,6},{6,7},{7,8},{8,9},{9,10},{10,1... | collective-permute-start | bytes 6152 | tf_op jit(solution)/shard_map/ppermute | solution.py:17
  186.9 9.4 %collective-permute-start.37 = (f32[1,1,1024]{2,1,0:T(1,128)S(1)}, f32[1,1,1024]{2,1,0:T(1,128)S(1)}, u32[]{:S(2)}, u32[]{:S(2)}) collective-permute-start(f32[1,1,1024]{2,1,0:T(1,128)S(1)} %slice.315), channel_id=1, source_target_pairs={{16,0},{32,16},{48,32},{64,48},{80,64},{96,80},{112,96},{17,1},{33... | collective-permute-start | bytes 12296 | tf_op jit(solution)/shard_map/ppermute | solution.py:17
  188.9 7.4 %collective-permute-start.36 = (f32[1,256,1]{2,1,0:T(8,128)S(1)}, f32[1,256,1]{2,1,0:T(8,128)S(1)}, u32[]{:S(2)}, u32[]{:S(2)}) collective-permute-start(f32[1,256,1]{2,1,0:T(8,128)S(1)} %slice.313), channel_id=1, source_target_pairs={{1,0},{2,1},{3,2},{4,3},{5,4},{6,5},{7,6},{8,7},{9,8},{10,9},{11,1... | collective-permute-start | bytes 3080 | tf_op jit(solution)/shard_map/ppermute | solution.py:17
  215.0 5.9 %collective-permute-start.46 = (f32[3]{0:T(128)S(1)}, f32[3]{0:T(128)S(1)}, u32[]{:S(2)}, u32[]{:S(2)}) collective-permute-start(f32[3]{0:T(128)S(1)} %add_add_fusion.1), channel_id=1, source_target_pairs={{0,48},{16,32},{32,16},{48,0},{64,112},{80,96},{96,80},{112,64},{1... | collective-permute-start | bytes 44 | tf_op jit(solution)/shard_map/ppermute | solution.py:52
  235.8 12.5 %collective-permute-start.49 = (f32[2,1,1024]{2,1,0:T(1,128)S(1)}, f32[2,1,1024]{2,1,0:T(1,128)S(1)}, u32[]{:S(2)}, u32[]{:S(2)}) collective-permute-start(f32[2,1,1024]{2,1,0:T(1,128)S(1)} %slice.320), channel_id=1, source_target_pairs={{0,16},{16,32},{32,48},{48,64},{64,80},{80,96},{96,112},{1,17},{17... | collective-permute-start | bytes 24584 | tf_op jit(solution)/shard_map/ppermute | solution.py:17
  239.8 8.5 %collective-permute-start.48 = (f32[2,256,1]{2,1,0:T(8,128)S(1)}, f32[2,256,1]{2,1,0:T(8,128)S(1)}, u32[]{:S(2)}, u32[]{:S(2)}) collective-permute-start(f32[2,256,1]{2,1,0:T(8,128)S(1)} %slice.317), channel_id=1, source_target_pairs={{0,1},{1,2},{2,3},{3,4},{4,5},{5,6},{6,7},{7,8},{8,9},{9,10},{10,1... | collective-permute-start | bytes 6152 | tf_op jit(solution)/shard_map/ppermute | solution.py:17
  (49 other events, 501.1 us)

commit v3 on v2

v3 whole, which is shorter than its diff:
```python
import jax
import jax.numpy as jnp
from jax import lax
from jax.sharding import PartitionSpec as P

ITERS = 3
MARGIN_ROWS = 8
MARGIN_COLS = 8


courant = -0.4
dispersion = 40.0
continuity = -0.5


def from_behind(value, axis, steps):
    count = lax.axis_size(axis)
    leading, last = (max(0, -steps), min(count, count - steps))
    return lax.ppermute(value, axis, [(source, source + steps) for source in range(leading, last)])


def grow(stacked):
    rows, cols = MARGIN_ROWS, MARGIN_COLS
    above = from_behind(stacked[:, :rows, :], "lat", -1)
    below = from_behind(stacked[:, -rows:, :], "lat", 1)
    stacked = jnp.concatenate([below, stacked, above], axis=1)
    right = from_behind(stacked[:, :, :cols], "lon", -1)
    left = from_behind(stacked[:, :, -cols:], "lon", 1)
    return jnp.concatenate([left, stacked, right], axis=2)


def east(field):
    return jnp.pad(field[..., :, 1:], [(0, 0)] * (field.ndim - 1) + [(0, 1)])


def north(field):
    return jnp.pad(field[..., 1:, :], [(0, 0)] * (field.ndim - 2) + [(0, 1), (0, 0)])


def west(field):
    return jnp.pad(field[..., :, :-1], [(0, 0)] * (field.ndim - 1) + [(1, 0)])


def south(field):
    return jnp.pad(field[..., :-1, :], [(0, 0)] * (field.ndim - 2) + [(1, 0), (0, 0)])


def divergence(field):
    return field[0] - west(field[0]) + field[1] - south(field[1])


def operate(field, wet, inverse):
    diverge = divergence(field)
    back = jnp.stack([diverge - east(diverge), diverge - north(diverge)])
    return wet * (inverse * field + back)


def exchange(value, axis, mask):
    return lax.ppermute(value, axis, [(i, i ^ mask) for i in range(lax.axis_size(axis))])


def quad_sum(value, axis, step):
    first = exchange(value, axis, step)
    second = exchange(value, axis, 2 * step)
    third = exchange(value, axis, 3 * step)
    return (value + first) + (second + third)


def total(value, axis):
    count, step = lax.axis_size(axis), 1
    while count >= 4:
        value = quad_sum(value, axis, step)
        count, step = count // 4, step * 4
    if count == 2:
        value = value + exchange(value, axis, step)
    return value


def interior(field):
    rows, cols = MARGIN_ROWS, MARGIN_COLS
    return field[..., rows:-rows, cols:-cols]


def sums(*pairs):
    local = jnp.stack([jnp.sum(interior(x) * interior(y)) for x, y in pairs])
    return total(total(local, "lon"), "lat")


def per_device(surface, bathymetry, land_sea, flux_lon, flux_lat):
    sea = land_sea.astype(jnp.float32)
    grown = grow(jnp.stack([surface, bathymetry, sea, flux_lon, flux_lat]))
    surface_x, bathymetry_x, sea_x = grown[0], grown[1], grown[2]
    wet = jnp.stack([sea_x * east(sea_x), sea_x * north(sea_x)])
    depth = jnp.stack([0.5 * (bathymetry_x + east(bathymetry_x)), 0.5 * (bathymetry_x + north(bathymetry_x))])
    slope = jnp.stack([east(surface_x) - surface_x, north(surface_x) - surface_x])
    start = wet * (grown[3:] - courant * depth * slope)
    inverse = jnp.where(depth > 0, 1.0 / (dispersion * depth * depth), 0.0)
    right_side = wet * inverse * start
    solution = start
    residual = right_side - operate(start, wet, inverse)
    applied = operate(residual, wet, inverse)
    norm_now, curve = sums((residual, residual), (residual, applied))
    direction, image = residual, applied
    for step in range(ITERS):
        alpha = norm_now / curve
        solution = solution + alpha * direction
        if step == ITERS - 1:
            break
        residual = residual - alpha * image
        applied = operate(residual, wet, inverse)
        norm_next, r_ar, r_ap = sums((residual, residual), (residual, applied), (residual, image))
        beta = norm_next / norm_now
        curve = r_ar + 2.0 * beta * r_ap + beta * beta * curve
        direction = residual + beta * direction
        image = applied + beta * image
        norm_now = norm_next
    surface_next = interior(surface_x - continuity * divergence(solution))
    solution = interior(solution)
    return (surface_next, solution[0], solution[1])


def solution(mesh):
    in_specs = (P("lat", "lon"), P("lat", "lon"), P("lat", "lon"), P("lat", "lon"), P("lat", "lon"))
    out_specs = (P("lat", "lon"), P("lat", "lon"), P("lat", "lon"))
    return jax.shard_map(
        per_device, mesh=mesh, in_specs=in_specs, out_specs=out_specs, check_vma=False
    )
```

time: 253 us -> 187 us (0.74)
  starting transfers between devices: 113 us -> 62.5 us
  waiting for transfers between devices: 76.9 us -> 27.7 us
  local copies, waits for them, and re-layouts: 6.36 us -> 38.9 us
  other arithmetic: 43.7 us -> 47.5 us
    ppermute x20 -> x4, waiting for transfers between devices: 55.1 us -> 5.72 us  [from_behind(): lax.ppermute(value, axis, [(source, source + steps) for source in range(l...]
    ppermute x20 -> x4, starting transfers between devices: 54.4 us -> 12.2 us  [from_behind(): lax.ppermute(value, axis, [(source, source + steps) for source in range(l...]
    unnamed x46 -> x63, local copies, waits for them, and re-layouts: 0.47 us -> 14.2 us
    ppermute x30, starting transfers between devices: 59 us -> 50.4 us  [exchange(): lax.ppermute(value, axis, [(i, i ^ mask) for i in range(lax.axis_size(axi...]
    concatenate x0 -> x1, local copies, waits for them, and re-layouts: none -> 8.4 us  [grow(): return jnp.concatenate([left, stacked, right], axis=2)]
    slice x28 -> x21, local copies, waits for them, and re-layouts: 3.9 us -> 11.2 us  [the longest x7 6 us: east(): return jnp.pad(field[..., :, 1:], [(0, 0)] * (field.ndim - 1) + [(0, 1)])]
    squeeze x0 -> x7, local copies, waits for them, and re-layouts: none -> 2.66 us  [the longest x1 1.92 us: per_device(): return (surface_next, solution[0], solution[1])]
    sub x10 -> x5, other arithmetic: 6.88 us -> 4.24 us  [the longest x1 2.42 us: per_device(): surface_next = interior(surface_x - continuity * divergence(solution))]
  transfers between devices with their start and end apart: 50 -> 34, of which waited for: 31 -> 24; matrix products, arithmetic and copies ran while one was open for 2% -> 0% of each run, Pallas kernels for 0% -> 0%
where the time goes in v3:
time: 187 us; the launch traced here: 186 us
  starting transfers between devices  62.5 us (33%)
  other arithmetic  47.5 us (25%)
  local copies, waits for them, and re-layouts  38.9 us (21%)
  waiting for transfers between devices  27.7 us (15%)
  between operations  9.86 us (5%)
    ppermute x30, starting transfers between devices, exchange(): lax.ppermute(value, axis, [(i, i ^ mask) for i in range(lax.axis_size(axi...  50.4 us
    ppermute x30, waiting for transfers between devices, exchange(): lax.ppermute(value, axis, [(i, i ^ mask) for i in range(lax.axis_size(axi...  22 us
    unnamed x63, local copies, waits for them, and re-layouts  14.2 us
    ppermute x4, starting transfers between devices, from_behind(): lax.ppermute(value, axis, [(source, source + steps) for source in range(l...  12.2 us
    sub x2, other arithmetic, per_device(): residual = residual - alpha * image  8.87 us
    concatenate x1, local copies, waits for them, and re-layouts, grow(): return jnp.concatenate([left, stacked, right], axis=2)  8.4 us
    reduce_sum x3, other arithmetic, sums(): local = jnp.stack([jnp.sum(interior(x) * interior(y)) for x, y in pairs])  7.84 us
    add x1, other arithmetic, per_device(): solution = solution + alpha * direction  6.06 us
  transfers between devices with their start and end apart: 34, of which 24 were waited for; matrix products, arithmetic and copies ran while one was open for 0% of the time, Pallas kernels for 0%

profile of v3, /device:TPU:1, one launch (start us, length us, event | category | flops | bytes accessed | tf_op | source)
XLA Modules:
  0.0 186.4 jit_solution(6858381054557308470)
XLA Ops:
  3.9 4.9 %collective-permute-start = (f32[5,8,1024]{2,1,0:T(8,128)S(1)}, f32[5,8,1024]{2,1,0:T(8,128)S(1)}, u32[]{:S(2)}, u32[]{:S(2)}) collective-permute-start(f32[5,8,1024]{2,1,0:T(8,128)S(1)} %get-tuple-element.30), channel_id=1, source_target_pairs={{0,16},{16,32},{32,48},{48,64},{64,80},{80,96},{96,112},{1,17},{17... | collective-permute-start | bytes 491528 | tf_op jit(solution)/shard_map/ppermute | solution.py:19
  11.1 4.4 %collective-permute-done.1 = f32[5,8,1024]{2,1,0:T(8,128)S(1)} collective-permute-done((f32[5,8,1024]{2,1,0:T(8,128)S(1)}, f32[5,8,1024]{2,1,0:T(8,128)S(1)}, u32[]{:S(2)}, u32[]{:S(2)}) %collective-permute-start.1) | collective-permute-done | bytes 163872 | tf_op jit(solution)/shard_map/ppermute | solution.py:19
  16.4 2.5 %copy-done.12 = f32[5,272,1024]{2,1,0:T(8,128)} copy-done((f32[5,272,1024]{2,1,0:T(8,128)}, f32[5,272,1024]{2,1,0:T(8,128)S(1)}, u32[]{:S(2)}) %copy-start.12) | copy-done | bytes 5570584
  21.0 4.0 %collective-permute-start.2 = (f32[5,272,8]{1,2,0:T(8,128)S(1)}, f32[5,272,8]{1,2,0:T(8,128)S(1)}, u32[]{:S(2)}, u32[]{:S(2)}) collective-permute-start(f32[5,272,8]{1,2,0:T(8,128)S(1)} %copy.16), channel_id=1, source_target_pairs={{0,1},{1,2},{2,3},{3,4},{4,5},{5,6},{6,7},{7,8},{8,9},{9,10},{10,1... | collective-permute-start | bytes 130568 | tf_op jit(solution)/shard_map/ppermute | solution.py:19
  26.6 8.4 %concatenate.7 = f32[5,272,1040]{2,1,0:T(8,128)} concatenate(f32[5,272,8]{2,1,0:T(8,128)S(1)} %copy.18, f32[5,272,1024]{2,1,0:T(8,128)} %copy-done.12, f32[5,272,8]{2,1,0:T(8,128)S(1)} %copy.19), dimensions={2} | concatenate | bytes 11315200 | tf_op jit(solution)/shard_map/concatenate | solution.py:29
  35.0 3.6 %slice_bitcast_fusion.18 = (f32[271,1040]{1,0:T(8,128)S(1)}, f32[271,1040]{1,0:T(8,128)S(1)}, f32[271,1040]{1,0:T(8,128)}) fusion(f32[5,272,1040]{2,1,0:T(8,128)} %concatenate.7), kind=kLoop, calls=%fused_computation.64 | loop fusion | bytes 6764160 | tf_op jit(solution)/shard_map/slice | solution.py:37
  44.0 2.8 %multiply_bitcast_fusion.3 = (f32[1,272,1040]{2,1,0:T(8,128)S(1)}, f32[1,272,1040]{2,1,0:T(8,128)S(1)}, f32[1,272,1040]{2,1,0:T(8,128)S(1)}, f32[1,272,1040]{2,1...) fusion(f32[272,1039]{1,0:T(8,128)} %slice.276, f32[5,272,1040]{2,1,0:T(8,128)S(1)} %copy-done.7, ...), kind=kLoop, calls=%fused_computation.80 | loop fusion | flops 2263040 | bytes 16957056 | tf_op jit(solution)/shard_map/stack | solution.py:93
  49.1 2.5 %fusion.1 = (f32[2,272,1040]{2,1,0:T(8,128)}, f32[2,272,1040]{2,1,0:T(8,128)S(1)}) fusion(f32[1,272,1040]{2,1,0:T(8,128)S(1)} %get-tuple-element.18, f32[1,272,1040]{2,1,0:T(8,128)S(1)} %get-tuple-element.17, f32[1,272,1040]{2,1,0:T(8,128)S(1)} %get-tuple-element.45, f32[1,272,1040]{2,1,0:T(8,128)S(1)} %get-tuple-element.44, ...), kind=kLoop, calls=%fused_computation.6 | loop fusion | flops 10749440 | bytes 15841280 | tf_op jit(solution)/shard_map/jit(_where)/select_n | solution.py:97
  57.5 3.4 %collective-permute-start.5 = (f32[2]{0:T(128)S(1)}, f32[2]{0:T(128)S(1)}, u32[]{:S(2)}, u32[]{:S(2)}) collective-permute-start(f32[2]{0:T(128)S(1)} %pad_maximum_fusion.4), channel_id=1, source_target_pairs={{0,2},{1,3},{2,0},{3,1},{4,6},{5,7},{6,4},{7,5},{8,10},{9,11},{10,... | collective-permute-start | bytes 32 | tf_op jit(solution)/shard_map/ppermute | solution.py:59
  66.3 4.5 %collective-permute-start.9 = (f32[2]{0:T(128)S(1)}, f32[2]{0:T(128)S(1)}, u32[]{:S(2)}, u32[]{:S(2)}) collective-permute-start(f32[2]{0:T(128)S(1)} %add_add_fusion.8), channel_id=1, source_target_pairs={{0,12},{1,13},{2,14},{3,15},{4,8},{5,9},{6,10},{7,11},{8,4},{9,5},... | collective-permute-start | bytes 32 | tf_op jit(solution)/shard_map/ppermute | solution.py:59
  71.7 3.0 %collective-permute-done.8 = f32[2]{0:T(128)S(1)} collective-permute-done((f32[2]{0:T(128)S(1)}, f32[2]{0:T(128)S(1)}, u32[]{:S(2)}, u32[]{:S(2)}) %collective-permute-start.8) | collective-permute-done | bytes 40 | tf_op jit(solution)/shard_map/ppermute | solution.py:59
  74.7 3.9 %collective-permute-start.12 = (f32[2]{0:T(128)S(1)}, f32[2]{0:T(128)S(1)}, u32[]{:S(2)}, u32[]{:S(2)}) collective-permute-start(f32[2]{0:T(128)S(1)} %add_add_fusion.7), channel_id=1, source_target_pairs={{0,48},{16,32},{32,16},{48,0},{64,112},{80,96},{96,80},{112,64},{1... | collective-permute-start | bytes 32 | tf_op jit(solution)/shard_map/ppermute | solution.py:59
  81.0 3.4 %collective-permute-start.13 = (f32[2]{0:T(128)S(1)}, f32[2]{0:T(128)S(1)}, u32[]{:S(2)}, u32[]{:S(2)}) collective-permute-start(f32[2]{0:T(128)S(1)} %add_add_fusion.6), channel_id=1, source_target_pairs={{0,64},{16,80},{32,96},{48,112},{64,0},{80,16},{96,32},{112,48},{1... | collective-permute-start | bytes 32 | tf_op jit(solution)/shard_map/ppermute | solution.py:59
  87.3 3.6 %multiply_subtract_fusion.1 = f32[2,272,1040]{2,1,0:T(8,128)S(1)} fusion(f32[2,272,1040]{2,1,0:T(8,128)S(1)} %get-tuple-element.37, f32[]{:T(128)S(6)} %div.23, f32[1,272,1040]{2,1,0:T(8,128)} %copy-done.15, f32[1,272,1040]{2,1,0:T(8,128)} %copy-done.14, f32[1,272,1040]{2,1,0:T(8,128)} %copy-done.10, f32[1,272,1040]{2,1,0:T(8,128)} %copy-done.8, ...), kind=kLoop, calls=%fused_computation.21 | loop fusion | flops 7354880 | bytes 11315204 | tf_op jit(solution)/shard_map/sub | solution.py:109
  97.1 2.4 %multiply_reduce_fusion.2 = (f32[]{:T(128)}, f32[]{:T(128)}, f32[]{:T(128)}) fusion(f32[2,272,1040]{2,1,0:T(8,128)S(1)} %multiply_subtract_fusion.1, f32[2,272,1040]{2,1,0:T(8,128)S(1)} %fusion.6, f32[2,272,1040]{2,1,0:T(8,128)S(1)} %copy-done.19), kind=kLoop, calls=%fused_computation.35 | loop fusion | flops 3145725 | bytes 6291468 | tf_op jit(solution)/shard_map/reduce_sum | solution.py:85
  103.2 2.3 %collective-permute-start.16 = (f32[3]{0:T(128)S(1)}, f32[3]{0:T(128)S(1)}, u32[]{:S(2)}, u32[]{:S(2)}) collective-permute-start(f32[3]{0:T(128)S(1)} %pad_maximum_fusion.5), channel_id=1, source_target_pairs={{0,3},{1,2},{2,1},{3,0},{4,7},{5,6},{6,5},{7,4},{8,11},{9,10},{10,... | collective-permute-start | bytes 44 | tf_op jit(solution)/shard_map/ppermute | solution.py:59
  114.7 5.4 %collective-permute-start.22 = (f32[3]{0:T(128)S(1)}, f32[3]{0:T(128)S(1)}, u32[]{:S(2)}, u32[]{:S(2)}) collective-permute-start(f32[3]{0:T(128)S(1)} %add_add_fusion.4), channel_id=1, source_target_pairs={{0,48},{16,32},{32,16},{48,0},{64,112},{80,96},{96,80},{112,64},{1... | collective-permute-start | bytes 44 | tf_op jit(solution)/shard_map/ppermute | solution.py:59
  122.6 3.4 %collective-permute-start.23 = (f32[3]{0:T(128)S(1)}, f32[3]{0:T(128)S(1)}, u32[]{:S(2)}, u32[]{:S(2)}) collective-permute-start(f32[3]{0:T(128)S(1)} %add_add_fusion.3), channel_id=1, source_target_pairs={{0,64},{16,80},{32,96},{48,112},{64,0},{80,16},{96,32},{112,48},{1... | collective-permute-start | bytes 44 | tf_op jit(solution)/shard_map/ppermute | solution.py:59
  131.5 5.3 %multiply_subtract_fusion = (f32[2,272,1040]{2,1,0:T(8,128)S(1)}, f32[2,272,1040]{2,1,0:T(8,128)S(1)}) fusion(f32[2,272,1040]{2,1,0:T(8,128)} %copy-done, f32[]{:T(128)S(6)} %div.25, f32[]{:T(128)S(6)} %div.24, f32[1,272,1040]{2,1,0:T(8,128)} %copy-done.21, f32[1,272,1040]{2,1,0:T(8,128)} %copy-done.20, f32[1,272,1040]{2,1,0:T(8,128)} %copy-done.10, ...), kind=kLoop, calls=%fused_computation.19 | loop fusion | flops 10749440 | bytes 18104328 | tf_op jit(solution)/shard_map/sub | solution.py:109
  140.4 3.7 %multiply_reduce_fusion = (f32[]{:T(128)}, f32[]{:T(128)}, f32[]{:T(128)}) fusion(f32[2,272,1040]{2,1,0:T(8,128)S(1)} %get-tuple-element.14, f32[2,272,1040]{2,1,0:T(8,128)S(1)} %get-tuple-element.15, f32[1,272,1040]{2,1,0:T(8,128)S(1)} %get-tuple-element.39, f32[1,272,1040]{2,1,0:T(8,128)S(1)} %get-tuple-element.38, f32[2,272,1040]{2,1,0:T(8,128)S(1)} %copy-done.24, ...), kind=kLoop, calls=%fused_computation.33 | loop fusion | flops 5767165 | bytes 10817548 | tf_op jit(solution)/shard_map/reduce_sum | solution.py:85
  158.7 5.3 %collective-permute-start.32 = (f32[3]{0:T(128)S(1)}, f32[3]{0:T(128)S(1)}, u32[]{:S(2)}, u32[]{:S(2)}) collective-permute-start(f32[3]{0:T(128)S(1)} %add_add_fusion.1), channel_id=1, source_target_pairs={{0,48},{16,32},{32,16},{48,0},{64,112},{80,96},{96,80},{112,64},{1... | collective-permute-start | bytes 44 | tf_op jit(solution)/shard_map/ppermute | solution.py:59
  166.4 3.4 %collective-permute-start.33 = (f32[3]{0:T(128)S(1)}, f32[3]{0:T(128)S(1)}, u32[]{:S(2)}, u32[]{:S(2)}) collective-permute-start(f32[3]{0:T(128)S(1)} %add_add_fusion), channel_id=1, source_target_pairs={{0,64},{16,80},{32,96},{48,112},{64,0},{80,16},{96,32},{112,48},{1... | collective-permute-start | bytes 44 | tf_op jit(solution)/shard_map/ppermute | solution.py:59
  174.6 6.1 %multiply_add_fusion = f32[2,272,1040]{2,1,0:T(8,128)S(1)} fusion(f32[2,272,1040]{2,1,0:T(8,128)} %copy-done, f32[2,272,1040]{2,1,0:T(8,128)S(1)} %get-tuple-element.37, f32[]{:T(128)S(6)} %div.26, f32[]{:T(128)S(6)} %div.27, f32[]{:T(128)S(6)} %div.24, f32[]{:T(128)S(6)} %div.25, f32[]{:T(128)S(6)} %div.23, f32[2,272,1040]{2,1,0:T(8,128)} %copy-done.13, ...), kind=kLoop, calls=%fused_computation.18 | loop fusion | flops 10749440 | bytes 18104340 | tf_op jit(solution)/shard_map/add | solution.py:106
  184.0 2.4 %slice_subtract_fusion.1 = f32[256,1024]{1,0:T(8,128)} fusion(f32[272,1040]{1,0:T(8,128)S(1)} %copy-done.23, f32[271,1040]{1,0:T(8,128)S(1)} %slice_bitcast_fusion, f32[272,1040]{1,0:T(8,128)S(1)} %get-tuple-element.35, f32[272,1039]{1,0:T(8,128)S(1)} %bitcast.141, f32[272,1040]{1,0:T(8,128)S(1)} %get-tuple-element.34), kind=kLoop, calls=%fused_computation.83 | loop fusion | flops 1310720 | bytes 6452096 | tf_op jit(solution)/shard_map/sub | solution.py:117
  (179 shorter events, 82.0 us)
Async XLA Ops:
  3.9 7.2 %collective-permute-start = (f32[5,8,1024]{2,1,0:T(8,128)S(1)}, f32[5,8,1024]{2,1,0:T(8,128)S(1)}, u32[]{:S(2)}, u32[]{:S(2)}) collective-permute-start(f32[5,8,1024]{2,1,0:T(8,128)S(1)} %get-tuple-element.30), channel_id=1, source_target_pairs={{0,16},{16,32},{32,48},{48,64},{64,80},{80,96},{96,112},{1,17},{17... | collective-permute-start | bytes 491528 | tf_op jit(solution)/shard_map/ppermute | solution.py:19
  8.8 6.6 %collective-permute-start.1 = (f32[5,8,1024]{2,1,0:T(8,128)S(1)}, f32[5,8,1024]{2,1,0:T(8,128)S(1)}, u32[]{:S(2)}, u32[]{:S(2)}) collective-permute-start(f32[5,8,1024]{2,1,0:T(8,128)S(1)} %get-tuple-element.31), channel_id=1, source_target_pairs={{16,0},{32,16},{48,32},{64,48},{80,64},{96,80},{112,96},{17,1},{33... | collective-permute-start | bytes 491528 | tf_op jit(solution)/shard_map/ppermute | solution.py:19
  19.4 5.6 %collective-permute-start.3 = (f32[5,272,8]{1,2,0:T(8,128)S(1)}, f32[5,272,8]{1,2,0:T(8,128)S(1)}, u32[]{:S(2)}, u32[]{:S(2)}) collective-permute-start(f32[5,272,8]{1,2,0:T(8,128)S(1)} %copy.17), channel_id=1, source_target_pairs={{1,0},{2,1},{3,2},{4,3},{5,4},{6,5},{7,6},{8,7},{9,8},{10,9},{11,1... | collective-permute-start | bytes 130568 | tf_op jit(solution)/shard_map/ppermute | solution.py:19
  21.0 5.3 %collective-permute-start.2 = (f32[5,272,8]{1,2,0:T(8,128)S(1)}, f32[5,272,8]{1,2,0:T(8,128)S(1)}, u32[]{:S(2)}, u32[]{:S(2)}) collective-permute-start(f32[5,272,8]{1,2,0:T(8,128)S(1)} %copy.16), channel_id=1, source_target_pairs={{0,1},{1,2},{2,3},{3,4},{4,5},{5,6},{6,7},{7,8},{8,9},{9,10},{10,1... | collective-permute-start | bytes 130568 | tf_op jit(solution)/shard_map/ppermute | solution.py:19
  57.5 5.4 %collective-permute-start.5 = (f32[2]{0:T(128)S(1)}, f32[2]{0:T(128)S(1)}, u32[]{:S(2)}, u32[]{:S(2)}) collective-permute-start(f32[2]{0:T(128)S(1)} %pad_maximum_fusion.4), channel_id=1, source_target_pairs={{0,2},{1,3},{2,0},{3,1},{4,6},{5,7},{6,4},{7,5},{8,10},{9,11},{10,... | collective-permute-start | bytes 32 | tf_op jit(solution)/shard_map/ppermute | solution.py:59
  60.9 3.6 %collective-permute-start.6 = (f32[2]{0:T(128)S(1)}, f32[2]{0:T(128)S(1)}, u32[]{:S(2)}, u32[]{:S(2)}) collective-permute-start(f32[2]{0:T(128)S(1)} %pad_maximum_fusion.4), channel_id=1, source_target_pairs={{0,3},{1,2},{2,1},{3,0},{4,7},{5,6},{6,5},{7,4},{8,11},{9,10},{10,... | collective-permute-start | bytes 32 | tf_op jit(solution)/shard_map/ppermute | solution.py:59
  66.3 5.5 %collective-permute-start.9 = (f32[2]{0:T(128)S(1)}, f32[2]{0:T(128)S(1)}, u32[]{:S(2)}, u32[]{:S(2)}) collective-permute-start(f32[2]{0:T(128)S(1)} %add_add_fusion.8), channel_id=1, source_target_pairs={{0,12},{1,13},{2,14},{3,15},{4,8},{5,9},{6,10},{7,11},{8,4},{9,5},... | collective-permute-start | bytes 32 | tf_op jit(solution)/shard_map/ppermute | solution.py:59
  70.8 3.9 %collective-permute-start.8 = (f32[2]{0:T(128)S(1)}, f32[2]{0:T(128)S(1)}, u32[]{:S(2)}, u32[]{:S(2)}) collective-permute-start(f32[2]{0:T(128)S(1)} %add_add_fusion.8), channel_id=1, source_target_pairs={{0,8},{1,9},{2,10},{3,11},{4,12},{5,13},{6,14},{7,15},{8,0},{9,1},... | collective-permute-start | bytes 32 | tf_op jit(solution)/shard_map/ppermute | solution.py:59
  71.0 3.7 %collective-permute-start.7 = (f32[2]{0:T(128)S(1)}, f32[2]{0:T(128)S(1)}, u32[]{:S(2)}, u32[]{:S(2)}) collective-permute-start(f32[2]{0:T(128)S(1)} %add_add_fusion.8), channel_id=1, source_target_pairs={{0,4},{1,5},{2,6},{3,7},{4,0},{5,1},{6,2},{7,3},{8,12},{9,13},{10,... | collective-permute-start | bytes 32 | tf_op jit(solution)/shard_map/ppermute | solution.py:59
  74.7 5.2 %collective-permute-start.12 = (f32[2]{0:T(128)S(1)}, f32[2]{0:T(128)S(1)}, u32[]{:S(2)}, u32[]{:S(2)}) collective-permute-start(f32[2]{0:T(128)S(1)} %add_add_fusion.7), channel_id=1, source_target_pairs={{0,48},{16,32},{32,16},{48,0},{64,112},{80,96},{96,80},{112,64},{1... | collective-permute-start | bytes 32 | tf_op jit(solution)/shard_map/ppermute | solution.py:59
  81.0 4.3 %collective-permute-start.13 = (f32[2]{0:T(128)S(1)}, f32[2]{0:T(128)S(1)}, u32[]{:S(2)}, u32[]{:S(2)}) collective-permute-start(f32[2]{0:T(128)S(1)} %add_add_fusion.6), channel_id=1, source_target_pairs={{0,64},{16,80},{32,96},{48,112},{64,0},{80,16},{96,32},{112,48},{1... | collective-permute-start | bytes 32 | tf_op jit(solution)/shard_map/ppermute | solution.py:59
  101.5 4.1 %collective-permute-start.15 = (f32[3]{0:T(128)S(1)}, f32[3]{0:T(128)S(1)}, u32[]{:S(2)}, u32[]{:S(2)}) collective-permute-start(f32[3]{0:T(128)S(1)} %pad_maximum_fusion.5), channel_id=1, source_target_pairs={{0,2},{1,3},{2,0},{3,1},{4,6},{5,7},{6,4},{7,5},{8,10},{9,11},{10,... | collective-permute-start | bytes 44 | tf_op jit(solution)/shard_map/ppermute | solution.py:59
  103.2 3.6 %collective-permute-start.16 = (f32[3]{0:T(128)S(1)}, f32[3]{0:T(128)S(1)}, u32[]{:S(2)}, u32[]{:S(2)}) collective-permute-start(f32[3]{0:T(128)S(1)} %pad_maximum_fusion.5), channel_id=1, source_target_pairs={{0,3},{1,2},{2,1},{3,0},{4,7},{5,6},{6,5},{7,4},{8,11},{9,10},{10,... | collective-permute-start | bytes 44 | tf_op jit(solution)/shard_map/ppermute | solution.py:59
  110.0 3.6 %collective-permute-start.19 = (f32[3]{0:T(128)S(1)}, f32[3]{0:T(128)S(1)}, u32[]{:S(2)}, u32[]{:S(2)}) collective-permute-start(f32[3]{0:T(128)S(1)} %add_add_fusion.5), channel_id=1, source_target_pairs={{0,12},{1,13},{2,14},{3,15},{4,8},{5,9},{6,10},{7,11},{8,4},{9,5},... | collective-permute-start | bytes 44 | tf_op jit(solution)/shard_map/ppermute | solution.py:59
  110.8 3.9 %collective-permute-start.18 = (f32[3]{0:T(128)S(1)}, f32[3]{0:T(128)S(1)}, u32[]{:S(2)}, u32[]{:S(2)}) collective-permute-start(f32[3]{0:T(128)S(1)} %add_add_fusion.5), channel_id=1, source_target_pairs={{0,8},{1,9},{2,10},{3,11},{4,12},{5,13},{6,14},{7,15},{8,0},{9,1},... | collective-permute-start | bytes 44 | tf_op jit(solution)/shard_map/ppermute | solution.py:59
  111.8 2.9 %collective-permute-start.17 = (f32[3]{0:T(128)S(1)}, f32[3]{0:T(128)S(1)}, u32[]{:S(2)}, u32[]{:S(2)}) collective-permute-start(f32[3]{0:T(128)S(1)} %add_add_fusion.5), channel_id=1, source_target_pairs={{0,4},{1,5},{2,6},{3,7},{4,0},{5,1},{6,2},{7,3},{8,12},{9,13},{10,... | collective-permute-start | bytes 44 | tf_op jit(solution)/shard_map/ppermute | solution.py:59
  114.7 6.7 %collective-permute-start.22 = (f32[3]{0:T(128)S(1)}, f32[3]{0:T(128)S(1)}, u32[]{:S(2)}, u32[]{:S(2)}) collective-permute-start(f32[3]{0:T(128)S(1)} %add_add_fusion.4), channel_id=1, source_target_pairs={{0,48},{16,32},{32,16},{48,0},{64,112},{80,96},{96,80},{112,64},{1... | collective-permute-start | bytes 44 | tf_op jit(solution)/shard_map/ppermute | solution.py:59
  122.6 4.3 %collective-permute-start.23 = (f32[3]{0:T(128)S(1)}, f32[3]{0:T(128)S(1)}, u32[]{:S(2)}, u32[]{:S(2)}) collective-permute-start(f32[3]{0:T(128)S(1)} %add_add_fusion.3), channel_id=1, source_target_pairs={{0,64},{16,80},{32,96},{48,112},{64,0},{80,16},{96,32},{112,48},{1... | collective-permute-start | bytes 44 | tf_op jit(solution)/shard_map/ppermute | solution.py:59
  146.2 3.9 %collective-permute-start.25 = (f32[3]{0:T(128)S(1)}, f32[3]{0:T(128)S(1)}, u32[]{:S(2)}, u32[]{:S(2)}) collective-permute-start(f32[3]{0:T(128)S(1)} %pad_maximum_fusion.6), channel_id=1, source_target_pairs={{0,2},{1,3},{2,0},{3,1},{4,6},{5,7},{6,4},{7,5},{8,10},{9,11},{10,... | collective-permute-start | bytes 44 | tf_op jit(solution)/shard_map/ppermute | solution.py:59
  146.2 3.9 %collective-permute-start.26 = (f32[3]{0:T(128)S(1)}, f32[3]{0:T(128)S(1)}, u32[]{:S(2)}, u32[]{:S(2)}) collective-permute-start(f32[3]{0:T(128)S(1)} %pad_maximum_fusion.6), channel_id=1, source_target_pairs={{0,3},{1,2},{2,1},{3,0},{4,7},{5,6},{6,5},{7,4},{8,11},{9,10},{10,... | collective-permute-start | bytes 44 | tf_op jit(solution)/shard_map/ppermute | solution.py:59
  152.8 3.6 %collective-permute-start.29 = (f32[3]{0:T(128)S(1)}, f32[3]{0:T(128)S(1)}, u32[]{:S(2)}, u32[]{:S(2)}) collective-permute-start(f32[3]{0:T(128)S(1)} %add_add_fusion.2), channel_id=1, source_target_pairs={{0,12},{1,13},{2,14},{3,15},{4,8},{5,9},{6,10},{7,11},{8,4},{9,5},... | collective-permute-start | bytes 44 | tf_op jit(solution)/shard_map/ppermute | solution.py:59
  154.7 3.9 %collective-permute-start.28 = (f32[3]{0:T(128)S(1)}, f32[3]{0:T(128)S(1)}, u32[]{:S(2)}, u32[]{:S(2)}) collective-permute-start(f32[3]{0:T(128)S(1)} %add_add_fusion.2), channel_id=1, source_target_pairs={{0,8},{1,9},{2,10},{3,11},{4,12},{5,13},{6,14},{7,15},{8,0},{9,1},... | collective-permute-start | bytes 44 | tf_op jit(solution)/shard_map/ppermute | solution.py:59
  158.7 6.5 %collective-permute-start.32 = (f32[3]{0:T(128)S(1)}, f32[3]{0:T(128)S(1)}, u32[]{:S(2)}, u32[]{:S(2)}) collective-permute-start(f32[3]{0:T(128)S(1)} %add_add_fusion.1), channel_id=1, source_target_pairs={{0,48},{16,32},{32,16},{48,0},{64,112},{80,96},{96,80},{112,64},{1... | collective-permute-start | bytes 44 | tf_op jit(solution)/shard_map/ppermute | solution.py:59
  166.4 4.3 %collective-permute-start.33 = (f32[3]{0:T(128)S(1)}, f32[3]{0:T(128)S(1)}, u32[]{:S(2)}, u32[]{:S(2)}) collective-permute-start(f32[3]{0:T(128)S(1)} %add_add_fusion), channel_id=1, source_target_pairs={{0,64},{16,80},{32,96},{48,112},{64,0},{80,16},{96,32},{112,48},{1... | collective-permute-start | bytes 44 | tf_op jit(solution)/shard_map/ppermute | solution.py:59
  (40 other events, 107.8 us)

commit v4 on v3

--- a/solution.py
+++ b/solution.py
@@ -1,7 +1,13 @@
+import functools
+
 import jax
 import jax.numpy as jnp
 from jax import lax
+from jax.experimental import pallas as pl
+from jax.experimental.pallas import tpu as pltpu
 from jax.sharding import PartitionSpec as P
+
+MESH = pl.DeviceIdType.MESH
 
 ITERS = 3
 MARGIN_ROWS = 8
@@ -55,25 +61,79 @@
     return wet * (inverse * field + back)
 
 
-def exchange(value, axis, mask):
-    return lax.ppermute(value, axis, [(i, i ^ mask) for i in range(lax.axis_size(axis))])
+def stages_of(sizes):
+    stages = []
+    for axis in ("lon", "lat"):
+        count, stride = sizes[axis], 1
+        while count > 1:
+            members = 4 if count % 4 == 0 else count
+            stages.append((axis, stride, members))
+            count, stride = count // members, stride * members
+    return tuple(stages)
 
 
-def quad_sum(value, axis, step):
-    first = exchange(value, axis, step)
-    second = exchange(value, axis, 2 * step)
-    third = exchange(value, axis, 3 * step)
-    return (value + first) + (second + third)
+def reduce_kernel(stages, local_ref, out_ref, parts, got, send_sem, recv_sem):
+    me = {"lat": lax.axis_index("lat"), "lon": lax.axis_index("lon")}
+
+    def partner(axis, stride, members, offset):
+        own = me[axis]
+        digit = (own // stride) % members
+        other = own - digit * stride + ((digit + offset) % members) * stride
+        return tuple(other if name == axis else me[name] for name in ("lat", "lon"))
+
+    barrier = pltpu.get_barrier_semaphore()
+    greeted = 0
+    for axis, stride, members in stages:
+        for offset in range(1, members):
+            pl.semaphore_signal(barrier, inc=1, device_id=partner(axis, stride, members, offset), device_id_type=MESH)
+            greeted += 1
+    pl.semaphore_wait(barrier, greeted)
+
+    value = local_ref[...]
+    for stage, (axis, stride, members) in enumerate(stages):
+        parts[stage] = value
+        got[stage, 0] = value
+        copies = []
+        for offset in range(1, members):
+            slot = members - offset
+            copy = pltpu.make_async_remote_copy(
+                src_ref=parts.at[stage],
+                dst_ref=got.at[stage, slot],
+                send_sem=send_sem.at[stage, offset],
+                recv_sem=recv_sem.at[stage, slot],
+                device_id=partner(axis, stride, members, offset),
+                device_id_type=MESH,
+            )
+            copy.start()
+            copies.append(copy)
+        for copy in copies:
+            copy.wait()
+        digit = (me[axis] // stride) % members
+        ordered = [got[stage, (member - digit) % members] for member in range(members)]
+        while len(ordered) > 1:
+            ordered = [ordered[k] + ordered[k + 1] for k in range(0, len(ordered), 2)]
+        value = ordered[0]
+    out_ref[...] = value
 
 
-def total(value, axis):
-    count, step = lax.axis_size(axis), 1
-    while count >= 4:
-        value = quad_sum(value, axis, step)
-        count, step = count // 4, step * 4
-    if count == 2:
-        value = value + exchange(value, axis, step)
-    return value
+def all_sum(local):
+    sizes = {"lat": lax.axis_size("lat"), "lon": lax.axis_size("lon")}
+    stages = stages_of(sizes)
+    tile = jnp.zeros((8, 128), jnp.float32).at[0, : local.shape[0]].set(local)
+    summed = pl.pallas_call(
+        functools.partial(reduce_kernel, stages),
+        out_shape=jax.ShapeDtypeStruct((8, 128), jnp.float32),
+        in_specs=[pl.BlockSpec(memory_space=pltpu.VMEM)],
+        out_specs=pl.BlockSpec(memory_space=pltpu.VMEM),
+        scratch_shapes=[
+            pltpu.VMEM((len(stages), 8, 128), jnp.float32),
+            pltpu.VMEM((len(stages), 4, 8, 128), jnp.float32),
+            pltpu.SemaphoreType.DMA((len(stages), 4)),
+            pltpu.SemaphoreType.DMA((len(stages), 4)),
+        ],
+        compiler_params=pltpu.CompilerParams(collective_id=0, has_side_effects=True),
+    )(tile)
+    return summed[0, : local.shape[0]]
 
 
 def interior(field):
@@ -83,7 +143,7 @@
 
 def sums(*pairs):
     local = jnp.stack([jnp.sum(interior(x) * interior(y)) for x, y in pairs])
-    return total(total(local, "lon"), "lat")
+    return all_sum(local)
 
 
 def per_device(surface, bathymetry, land_sea, flux_lon, flux_lat):

time: 187 us -> 170 us (0.909)
  Pallas kernels: 0 us -> 56.5 us
  starting transfers between devices: 62.5 us -> 12.2 us
  waiting for transfers between devices: 27.7 us -> 5.72 us
  other arithmetic: 47.5 us -> 42.2 us
  local copies, waits for them, and re-layouts: 38.9 us -> 42.8 us
    pallas_call x0 -> x3, Pallas kernels: none -> 56.5 us  [all_sum(): pl.pallas_call(functools.partial(reduce_kernel, stages), out_shape=jax.Sh...]
    ppermute x30 -> x0, starting transfers between devices: 50.4 us -> none  [exchange(): lax.ppermute(value, axis, [(i, i ^ mask) for i in range(lax.axis_size(axi...]
    ppermute x30 -> x0, waiting for transfers between devices: 22 us -> none  [exchange(): lax.ppermute(value, axis, [(i, i ^ mask) for i in range(lax.axis_size(axi...]
    add x12 -> x0, other arithmetic: 5.43 us -> none  [the longest x9 5.42 us: quad_sum(): return value + first + (second + third)]
  transfers between devices with their start and end apart: 34 -> 4, of which waited for: 24 -> 3; matrix products, arithmetic and copies ran while one was open for 0% -> 0% of each run, Pallas kernels for 0% -> 0%
where the time goes in v4:
time: 170 us; the launch traced here: 169 us
  Pallas kernels  56.5 us (33%)
  local copies, waits for them, and re-layouts  42.8 us (25%)
  other arithmetic  42.2 us (25%)
  starting transfers between devices  12.2 us (7%)
  between operations  9.48 us (6%)
  waiting for transfers between devices  5.72 us (3%)
    pallas_call x3, Pallas kernels, all_sum(): pl.pallas_call(functools.partial(reduce_kernel, stages), out_shape=jax.Sh...  56.5 us
    unnamed x63, local copies, waits for them, and re-layouts  14.2 us
    ppermute x4, starting transfers between devices, from_behind(): lax.ppermute(value, axis, [(source, source + steps) for source in range(l...  12.2 us
    sub x2, other arithmetic, per_device(): residual = residual - alpha * image  9.06 us
    concatenate x1, local copies, waits for them, and re-layouts, grow(): return jnp.concatenate([left, stacked, right], axis=2)  8.35 us
    reduce_sum x3, other arithmetic, sums(): local = jnp.stack([jnp.sum(interior(x) * interior(y)) for x, y in pairs])  7.86 us
    add x1, other arithmetic, per_device(): solution = solution + alpha * direction  6.06 us
    slice x7, local copies, waits for them, and re-layouts, east(): return jnp.pad(field[..., :, 1:], [(0, 0)] * (field.ndim - 1) + [(0, 1)])  5.89 us
  transfers between devices with their start and end apart: 4, of which 3 were waited for; matrix products, arithmetic and copies ran while one was open for 0% of the time, Pallas kernels for 0%

profile of v4, /device:TPU:1, one launch (start us, length us, event | category | flops | bytes accessed | tf_op | source)
XLA Modules:
  0.0 168.8 jit_solution(9766554380283173617)
XLA Ops:
  3.9 4.9 %collective-permute-start = (f32[5,8,1024]{2,1,0:T(8,128)S(1)}, f32[5,8,1024]{2,1,0:T(8,128)S(1)}, u32[]{:S(2)}, u32[]{:S(2)}) collective-permute-start(f32[5,8,1024]{2,1,0:T(8,128)S(1)} %get-tuple-element.66), channel_id=1, source_target_pairs={{0,16},{16,32},{32,48},{48,64},{64,80},{80,96},{96,112},{1,17},{17... | collective-permute-start | bytes 491528 | tf_op jit(solution)/shard_map/ppermute | solution.py:25
  8.8 1.9 %collective-permute-start.1 = (f32[5,8,1024]{2,1,0:T(8,128)S(1)}, f32[5,8,1024]{2,1,0:T(8,128)S(1)}, u32[]{:S(2)}, u32[]{:S(2)}) collective-permute-start(f32[5,8,1024]{2,1,0:T(8,128)S(1)} %get-tuple-element.67), channel_id=1, source_target_pairs={{16,0},{32,16},{48,32},{64,48},{80,64},{96,80},{112,96},{17,1},{33... | collective-permute-start | bytes 491528 | tf_op jit(solution)/shard_map/ppermute | solution.py:25
  11.1 4.4 %collective-permute-done.1 = f32[5,8,1024]{2,1,0:T(8,128)S(1)} collective-permute-done((f32[5,8,1024]{2,1,0:T(8,128)S(1)}, f32[5,8,1024]{2,1,0:T(8,128)S(1)}, u32[]{:S(2)}, u32[]{:S(2)}) %collective-permute-start.1) | collective-permute-done | bytes 163872 | tf_op jit(solution)/shard_map/ppermute | solution.py:25
  16.4 2.5 %copy-done.12 = f32[5,272,1024]{2,1,0:T(8,128)} copy-done((f32[5,272,1024]{2,1,0:T(8,128)}, f32[5,272,1024]{2,1,0:T(8,128)S(1)}, u32[]{:S(2)}) %copy-start.12) | copy-done | bytes 5570584
  21.0 4.0 %collective-permute-start.2 = (f32[5,272,8]{1,2,0:T(8,128)S(1)}, f32[5,272,8]{1,2,0:T(8,128)S(1)}, u32[]{:S(2)}, u32[]{:S(2)}) collective-permute-start(f32[5,272,8]{1,2,0:T(8,128)S(1)} %copy.16), channel_id=1, source_target_pairs={{0,1},{1,2},{2,3},{3,4},{4,5},{5,6},{6,7},{7,8},{8,9},{9,10},{10,1... | collective-permute-start | bytes 130568 | tf_op jit(solution)/shard_map/ppermute | solution.py:25
  26.5 8.3 %concatenate.13 = f32[5,272,1040]{2,1,0:T(8,128)} concatenate(f32[5,272,8]{2,1,0:T(8,128)S(1)} %copy.18, f32[5,272,1024]{2,1,0:T(8,128)} %copy-done.12, f32[5,272,8]{2,1,0:T(8,128)S(1)} %copy.19), dimensions={2} | concatenate | bytes 11315200 | tf_op jit(solution)/shard_map/concatenate | solution.py:35
  34.9 3.6 %slice_bitcast_fusion.18 = (f32[271,1040]{1,0:T(8,128)S(1)}, f32[271,1040]{1,0:T(8,128)S(1)}, f32[271,1040]{1,0:T(8,128)}) fusion(f32[5,272,1040]{2,1,0:T(8,128)} %concatenate.13), kind=kLoop, calls=%fused_computation.64 | loop fusion | bytes 6764160 | tf_op jit(solution)/shard_map/slice | solution.py:43
  40.9 1.4 slice.347
  42.4 1.5 slice.349
  43.8 2.8 %multiply_bitcast_fusion.3 = (f32[1,272,1040]{2,1,0:T(8,128)S(1)}, f32[1,272,1040]{2,1,0:T(8,128)S(1)}, f32[1,272,1040]{2,1,0:T(8,128)S(1)}, f32[1,272,1040]{2,1...) fusion(f32[272,1039]{1,0:T(8,128)} %slice.343, f32[5,272,1040]{2,1,0:T(8,128)S(1)} %copy-done.7, ...), kind=kLoop, calls=%fused_computation.80 | loop fusion | flops 2263040 | bytes 16957056 | tf_op jit(solution)/shard_map/stack | solution.py:153
  48.9 2.5 %fusion.1 = (f32[2,272,1040]{2,1,0:T(8,128)}, f32[2,272,1040]{2,1,0:T(8,128)S(1)}) fusion(f32[1,272,1040]{2,1,0:T(8,128)S(1)} %get-tuple-element.54, f32[1,272,1040]{2,1,0:T(8,128)S(1)} %get-tuple-element.53, f32[1,272,1040]{2,1,0:T(8,128)S(1)} %get-tuple-element.81, f32[1,272,1040]{2,1,0:T(8,128)S(1)} %get-tuple-element.80, ...), kind=kLoop, calls=%fused_computation.6 | loop fusion | flops 10749440 | bytes 15841280 | tf_op jit(solution)/shard_map/jit(_where)/select_n | solution.py:157
  54.2 1.7 %multiply_reduce_fusion.4 = (f32[]{:T(128)}, f32[]{:T(128)}) fusion(f32[2,272,1040]{2,1,0:T(8,128)S(1)} %get-tuple-element.73, f32[2,272,1040]{2,1,0:T(8,128)S(1)} %fusion.5), kind=kLoop, calls=%fused_computation.37 | loop fusion | flops 2097150 | bytes 4194312 | tf_op jit(solution)/shard_map/reduce_sum | solution.py:145
  57.9 23.7 %shard_map.76 = f32[8,128]{1,0:T(8,128)} custom-call(f32[8,128]{1,0:T(8,128)} %scatter.10.local_ref), custom_call_target="tpu_custom_call" | custom-call | tf_op jit(solution)/shard_map/pallas_call | solution.py:123
  84.3 3.8 %multiply_subtract_fusion.1 = f32[2,272,1040]{2,1,0:T(8,128)S(1)} fusion(f32[2,272,1040]{2,1,0:T(8,128)S(1)} %get-tuple-element.73, f32[]{:T(128)S(6)} %div.23, f32[1,272,1040]{2,1,0:T(8,128)} %copy-done.15, f32[1,272,1040]{2,1,0:T(8,128)} %copy-done.14, f32[1,272,1040]{2,1,0:T(8,128)} %copy-done.10, f32[1,272,1040]{2,1,0:T(8,128)} %copy-done.8, ...), kind=kLoop, calls=%fused_computation.21 | loop fusion | flops 7354880 | bytes 11315204 | tf_op jit(solution)/shard_map/sub | solution.py:169
  94.3 2.4 %multiply_reduce_fusion.2 = (f32[]{:T(128)}, f32[]{:T(128)}, f32[]{:T(128)}) fusion(f32[2,272,1040]{2,1,0:T(8,128)S(1)} %multiply_subtract_fusion.1, f32[2,272,1040]{2,1,0:T(8,128)S(1)} %fusion.6, f32[2,272,1040]{2,1,0:T(8,128)S(1)} %copy-done.19), kind=kLoop, calls=%fused_computation.35 | loop fusion | flops 3145725 | bytes 6291468 | tf_op jit(solution)/shard_map/reduce_sum | solution.py:145
  96.6 2.0 %maximum_bitcast_fusion.1 = f32[1,3]{1,0:T(1,128)S(1)} fusion(f32[1]{0:T(128)} %bitcast.39, f32[1]{0:T(128)} %bitcast.38, f32[1]{0:T(128)} %bitcast.32), kind=kLoop, calls=%fused_computation.94 | loop fusion | flops 6 | bytes 24 | tf_op jit(solution)/shard_map/reshape.101
  99.2 16.1 %shard_map.77 = f32[8,128]{1,0:T(8,128)} custom-call(f32[8,128]{1,0:T(8,128)} %scatter.11.local_ref), custom_call_target="tpu_custom_call" | custom-call | tf_op jit(solution)/shard_map/pallas_call | solution.py:123
  120.4 5.3 %multiply_subtract_fusion = (f32[2,272,1040]{2,1,0:T(8,128)S(1)}, f32[2,272,1040]{2,1,0:T(8,128)S(1)}) fusion(f32[2,272,1040]{2,1,0:T(8,128)} %copy-done, f32[]{:T(128)S(6)} %div.25, f32[]{:T(128)S(6)} %div.24, f32[1,272,1040]{2,1,0:T(8,128)} %copy-done.21, f32[1,272,1040]{2,1,0:T(8,128)} %copy-done.20, f32[1,272,1040]{2,1,0:T(8,128)} %copy-done.10, ...), kind=kLoop, calls=%fused_computation.19 | loop fusion | flops 10749440 | bytes 18104328 | tf_op jit(solution)/shard_map/sub | solution.py:169
  129.3 3.7 %multiply_reduce_fusion = (f32[]{:T(128)}, f32[]{:T(128)}, f32[]{:T(128)}) fusion(f32[2,272,1040]{2,1,0:T(8,128)S(1)} %get-tuple-element.50, f32[2,272,1040]{2,1,0:T(8,128)S(1)} %get-tuple-element.51, f32[1,272,1040]{2,1,0:T(8,128)S(1)} %get-tuple-element.75, f32[1,272,1040]{2,1,0:T(8,128)S(1)} %get-tuple-element.74, f32[2,272,1040]{2,1,0:T(8,128)S(1)} %copy-done.24, ...), kind=kLoop, calls=%fused_computation.33 | loop fusion | flops 5767165 | bytes 10817548 | tf_op jit(solution)/shard_map/reduce_sum | solution.py:145
  133.1 2.0 %maximum_bitcast_fusion.2 = f32[1,3]{1,0:T(1,128)S(1)} fusion(f32[1]{0:T(128)} %bitcast.51, f32[1]{0:T(128)} %bitcast.50, f32[1]{0:T(128)} %bitcast.44), kind=kLoop, calls=%fused_computation.95 | loop fusion | flops 6 | bytes 24 | tf_op jit(solution)/shard_map/reshape.102
  135.7 16.7 %shard_map.78 = f32[8,128]{1,0:T(8,128)} custom-call(f32[8,128]{1,0:T(8,128)} %scatter.14.local_ref), custom_call_target="tpu_custom_call" | custom-call | tf_op jit(solution)/shard_map/pallas_call | solution.py:123
  157.0 6.1 %multiply_add_fusion = f32[2,272,1040]{2,1,0:T(8,128)S(1)} fusion(f32[2,272,1040]{2,1,0:T(8,128)} %copy-done, f32[2,272,1040]{2,1,0:T(8,128)S(1)} %get-tuple-element.73, f32[]{:T(128)S(6)} %div.26, f32[]{:T(128)S(6)} %div.27, f32[]{:T(128)S(6)} %div.24, f32[]{:T(128)S(6)} %div.25, f32[]{:T(128)S(6)} %div.23, f32[2,272,1040]{2,1,0:T(8,128)} %copy-done.13, ...), kind=kLoop, calls=%fused_computation.18 | loop fusion | flops 10749440 | bytes 18104340 | tf_op jit(solution)/shard_map/add | solution.py:166
  163.1 1.9 %slice_bitcast_fusion.21 = (f32[256,1024]{1,0:T(8,128)}, f32[256,1024]{1,0:T(8,128)}) fusion(f32[2,272,1040]{2,1,0:T(8,128)S(1)} %multiply_add_fusion), kind=kLoop, calls=%fused_computation.81 | loop fusion | bytes 4194304 | tf_op jit(solution)/shard_map/squeeze | solution.py:179
  166.3 2.4 %slice_subtract_fusion.1 = f32[256,1024]{1,0:T(8,128)} fusion(f32[272,1040]{1,0:T(8,128)S(1)} %copy-done.23, f32[271,1040]{1,0:T(8,128)S(1)} %slice_bitcast_fusion, f32[272,1040]{1,0:T(8,128)S(1)} %get-tuple-element.71, f32[272,1039]{1,0:T(8,128)S(1)} %bitcast.147, f32[272,1040]{1,0:T(8,128)S(1)} %get-tuple-element.70), kind=kLoop, calls=%fused_computation.83 | loop fusion | flops 1310720 | bytes 6452096 | tf_op jit(solution)/shard_map/sub | solution.py:177
  (113 shorter events, 33.7 us)
Async XLA Ops:
  0.6 1.8 %copy-start.27 = (s32[256,1024]{1,0:T(8,128)S(1)}, s32[256,1024]{1,0:T(8,128)}, u32[]{:S(2)}) copy-start(s32[256,1024]{1,0:T(8,128)} %param.13) | copy-start | bytes 3145732
  3.9 7.2 %collective-permute-start = (f32[5,8,1024]{2,1,0:T(8,128)S(1)}, f32[5,8,1024]{2,1,0:T(8,128)S(1)}, u32[]{:S(2)}, u32[]{:S(2)}) collective-permute-start(f32[5,8,1024]{2,1,0:T(8,128)S(1)} %get-tuple-element.66), channel_id=1, source_target_pairs={{0,16},{16,32},{32,48},{48,64},{64,80},{80,96},{96,112},{1,17},{17... | collective-permute-start | bytes 491528 | tf_op jit(solution)/shard_map/ppermute | solution.py:25
  8.8 6.6 %collective-permute-start.1 = (f32[5,8,1024]{2,1,0:T(8,128)S(1)}, f32[5,8,1024]{2,1,0:T(8,128)S(1)}, u32[]{:S(2)}, u32[]{:S(2)}) collective-permute-start(f32[5,8,1024]{2,1,0:T(8,128)S(1)} %get-tuple-element.67), channel_id=1, source_target_pairs={{16,0},{32,16},{48,32},{64,48},{80,64},{96,80},{112,96},{17,1},{33... | collective-permute-start | bytes 491528 | tf_op jit(solution)/shard_map/ppermute | solution.py:25
  16.4 2.5 %copy-start.12 = (f32[5,272,1024]{2,1,0:T(8,128)}, f32[5,272,1024]{2,1,0:T(8,128)S(1)}, u32[]{:S(2)}) copy-start(f32[5,272,1024]{2,1,0:T(8,128)S(1)} %pad_maximum_fusion) | copy-start | bytes 16711684
  19.4 5.6 %collective-permute-start.3 = (f32[5,272,8]{1,2,0:T(8,128)S(1)}, f32[5,272,8]{1,2,0:T(8,128)S(1)}, u32[]{:S(2)}, u32[]{:S(2)}) collective-permute-start(f32[5,272,8]{1,2,0:T(8,128)S(1)} %copy.17), channel_id=1, source_target_pairs={{1,0},{2,1},{3,2},{4,3},{5,4},{6,5},{7,6},{8,7},{9,8},{10,9},{11,1... | collective-permute-start | bytes 130568 | tf_op jit(solution)/shard_map/ppermute | solution.py:25
  21.0 5.3 %collective-permute-start.2 = (f32[5,272,8]{1,2,0:T(8,128)S(1)}, f32[5,272,8]{1,2,0:T(8,128)S(1)}, u32[]{:S(2)}, u32[]{:S(2)}) collective-permute-start(f32[5,272,8]{1,2,0:T(8,128)S(1)} %copy.16), channel_id=1, source_target_pairs={{0,1},{1,2},{2,3},{3,4},{4,5},{5,6},{6,7},{7,8},{8,9},{9,10},{10,1... | collective-permute-start | bytes 130568 | tf_op jit(solution)/shard_map/ppermute | solution.py:25
  34.9 4.4 %copy-start.7 = (f32[5,272,1040]{2,1,0:T(8,128)S(1)}, f32[5,272,1040]{2,1,0:T(8,128)}, u32[]{:S(2)}) copy-start(f32[5,272,1040]{2,1,0:T(8,128)} %concatenate.13) | copy-start | bytes 16972804
  39.5 2.9 %copy-start.22 = (f32[272,1040]{1,0:T(8,128)}, f32[272,1040]{1,0:T(8,128)S(1)}, u32[]{:S(2)}) copy-start(f32[272,1040]{1,0:T(8,128)S(1)} %get-tuple-element.60) | copy-start | bytes 3394564
  46.7 2.2 %copy-start.16 = (f32[1,272,1040]{2,1,0:T(8,128)}, f32[1,272,1040]{2,1,0:T(8,128)S(1)}, u32[]{:S(2)}) copy-start(f32[1,272,1040]{2,1,0:T(8,128)S(1)} %get-tuple-element.56) | copy-start | bytes 3394564
  46.7 2.2 %copy-start.17 = (f32[1,272,1040]{2,1,0:T(8,128)}, f32[1,272,1040]{2,1,0:T(8,128)S(1)}, u32[]{:S(2)}) copy-start(f32[1,272,1040]{2,1,0:T(8,128)S(1)} %get-tuple-element.57) | copy-start | bytes 3394564
  46.7 6.1 %copy-start.1 = (f32[1,272,1040]{2,1,0:T(8,128)}, f32[1,272,1040]{2,1,0:T(8,128)S(1)}, u32[]{:S(2)}) copy-start(f32[1,272,1040]{2,1,0:T(8,128)S(1)} %get-tuple-element.52) | copy-start | bytes 3394564
  46.7 6.1 %copy-start.4 = (f32[1,272,1040]{2,1,0:T(8,128)}, f32[1,272,1040]{2,1,0:T(8,128)S(1)}, u32[]{:S(2)}) copy-start(f32[1,272,1040]{2,1,0:T(8,128)S(1)} %get-tuple-element.55) | copy-start | bytes 3394564
  46.7 6.1 %copy-start.8 = (f32[1,272,1040]{2,1,0:T(8,128)}, f32[1,272,1040]{2,1,0:T(8,128)S(1)}, u32[]{:S(2)}) copy-start(f32[1,272,1040]{2,1,0:T(8,128)S(1)} %get-tuple-element.53) | copy-start | bytes 3394564
  46.7 6.1 %copy-start.10 = (f32[1,272,1040]{2,1,0:T(8,128)}, f32[1,272,1040]{2,1,0:T(8,128)S(1)}, u32[]{:S(2)}) copy-start(f32[1,272,1040]{2,1,0:T(8,128)S(1)} %get-tuple-element.54) | copy-start | bytes 3394564
  54.2 1.8 %copy-start.18 = (f32[2,272,1040]{2,1,0:T(8,128)}, f32[2,272,1040]{2,1,0:T(8,128)S(1)}, u32[]{:S(2)}) copy-start(f32[2,272,1040]{2,1,0:T(8,128)S(1)} %fusion.5) | copy-start | bytes 6789124
  88.1 5.3 %copy-start = (f32[2,272,1040]{2,1,0:T(8,128)}, f32[2,272,1040]{2,1,0:T(8,128)S(1)}, u32[]{:S(2)}) copy-start(f32[2,272,1040]{2,1,0:T(8,128)S(1)} %multiply_subtract_fusion.1) | copy-start | bytes 6789124
  89.2 2.6 %copy-start.5 = (f32[1,272,1040]{2,1,0:T(8,128)S(1)}, f32[1,272,1040]{2,1,0:T(8,128)}, u32[]{:S(2)}) copy-start(f32[1,272,1040]{2,1,0:T(8,128)} %copy-done.4) | copy-start | bytes 3394564
  89.2 2.9 %copy-start.9 = (f32[1,272,1040]{2,1,0:T(8,128)S(1)}, f32[1,272,1040]{2,1,0:T(8,128)}, u32[]{:S(2)}) copy-start(f32[1,272,1040]{2,1,0:T(8,128)} %copy-done.8) | copy-start | bytes 3394564
  89.2 3.3 %copy-start.11 = (f32[1,272,1040]{2,1,0:T(8,128)S(1)}, f32[1,272,1040]{2,1,0:T(8,128)}, u32[]{:S(2)}) copy-start(f32[1,272,1040]{2,1,0:T(8,128)} %copy-done.10) | copy-start | bytes 3394564
  89.5 3.8 %copy-start.20 = (f32[1,272,1040]{2,1,0:T(8,128)}, f32[1,272,1040]{2,1,0:T(8,128)S(1)}, u32[]{:S(2)}) copy-start(f32[1,272,1040]{2,1,0:T(8,128)S(1)} %get-tuple-element.76) | copy-start | bytes 3394564
  89.5 3.8 %copy-start.21 = (f32[1,272,1040]{2,1,0:T(8,128)}, f32[1,272,1040]{2,1,0:T(8,128)S(1)}, u32[]{:S(2)}) copy-start(f32[1,272,1040]{2,1,0:T(8,128)S(1)} %get-tuple-element.77) | copy-start | bytes 3394564
  92.6 1.7 %copy-start.19 = (f32[2,272,1040]{2,1,0:T(8,128)S(1)}, f32[2,272,1040]{2,1,0:T(8,128)}, u32[]{:S(2)}) copy-start(f32[2,272,1040]{2,1,0:T(8,128)} %copy-done.18) | copy-start | bytes 6789124
  126.9 1.7 copy-start.6
  126.9 2.5 %copy-start.24 = (f32[2,272,1040]{2,1,0:T(8,128)S(1)}, f32[2,272,1040]{2,1,0:T(8,128)}, u32[]{:S(2)}) copy-start(f32[2,272,1040]{2,1,0:T(8,128)} %get-tuple-element.72) | copy-start | bytes 6789124
  (10 other events, 13.6 us)

commit v5 on v4

--- a/solution.py
+++ b/solution.py
@@ -62,14 +62,7 @@
 
 
 def stages_of(sizes):
-    stages = []
-    for axis in ("lon", "lat"):
-        count, stride = sizes[axis], 1
-        while count > 1:
-            members = 4 if count % 4 == 0 else count
-            stages.append((axis, stride, members))
-            count, stride = count // members, stride * members
-    return tuple(stages)
+    return tuple((axis, 1, sizes[axis]) for axis in ("lon", "lat") if sizes[axis] > 1)
 
 
 def reduce_kernel(stages, local_ref, out_ref, parts, got, send_sem, recv_sem):
@@ -119,6 +112,7 @@
 def all_sum(local):
     sizes = {"lat": lax.axis_size("lat"), "lon": lax.axis_size("lon")}
     stages = stages_of(sizes)
+    widest = max(members for _, _, members in stages)
     tile = jnp.zeros((8, 128), jnp.float32).at[0, : local.shape[0]].set(local)
     summed = pl.pallas_call(
         functools.partial(reduce_kernel, stages),
@@ -127,9 +121,9 @@
         out_specs=pl.BlockSpec(memory_space=pltpu.VMEM),
         scratch_shapes=[
             pltpu.VMEM((len(stages), 8, 128), jnp.float32),
-            pltpu.VMEM((len(stages), 4, 8, 128), jnp.float32),
-            pltpu.SemaphoreType.DMA((len(stages), 4)),
-            pltpu.SemaphoreType.DMA((len(stages), 4)),
+            pltpu.VMEM((len(stages), widest, 8, 128), jnp.float32),
+            pltpu.SemaphoreType.DMA((len(stages), widest)),
+            pltpu.SemaphoreType.DMA((len(stages), widest)),
         ],
         compiler_params=pltpu.CompilerParams(collective_id=0, has_side_effects=True),
     )(tile)

time: 170 us -> 160 us (0.941)
  Pallas kernels: 56.5 us -> 46.9 us
    pallas_call x3, Pallas kernels: 56.5 us -> 46.9 us  [all_sum(): pl.pallas_call(functools.partial(reduce_kernel, stages), out_shape=jax.Sh...]
where the time goes in v5:
time: 160 us; the launch traced here: 159 us
  Pallas kernels  46.9 us (29%)
  local copies, waits for them, and re-layouts  42.8 us (27%)
  other arithmetic  42.2 us (26%)
  starting transfers between devices  12.2 us (8%)
  between operations  9.48 us (6%)
  waiting for transfers between devices  5.72 us (4%)
    pallas_call x3, Pallas kernels, all_sum(): pl.pallas_call(functools.partial(reduce_kernel, stages), out_shape=jax.Sh...  46.9 us
    unnamed x63, local copies, waits for them, and re-layouts  14.2 us
    ppermute x4, starting transfers between devices, from_behind(): lax.ppermute(value, axis, [(source, source + steps) for source in range(l...  12.2 us
    sub x2, other arithmetic, per_device(): residual = residual - alpha * image  9.06 us
    concatenate x1, local copies, waits for them, and re-layouts, grow(): return jnp.concatenate([left, stacked, right], axis=2)  8.35 us
    reduce_sum x3, other arithmetic, sums(): local = jnp.stack([jnp.sum(interior(x) * interior(y)) for x, y in pairs])  7.86 us
    add x1, other arithmetic, per_device(): solution = solution + alpha * direction  6.06 us
    slice x7, local copies, waits for them, and re-layouts, east(): return jnp.pad(field[..., :, 1:], [(0, 0)] * (field.ndim - 1) + [(0, 1)])  5.89 us
  transfers between devices with their start and end apart: 4, of which 3 were waited for; matrix products, arithmetic and copies ran while one was open for 0% of the time, Pallas kernels for 0%

profile of v5, /device:TPU:1, one launch (start us, length us, event | category | flops | bytes accessed | tf_op | source)
XLA Modules:
  0.0 159.2 jit_solution(7882599243898243623)
XLA Ops:
  3.9 4.9 %collective-permute-start = (f32[5,8,1024]{2,1,0:T(8,128)S(1)}, f32[5,8,1024]{2,1,0:T(8,128)S(1)}, u32[]{:S(2)}, u32[]{:S(2)}) collective-permute-start(f32[5,8,1024]{2,1,0:T(8,128)S(1)} %get-tuple-element.66), channel_id=1, source_target_pairs={{0,16},{16,32},{32,48},{48,64},{64,80},{80,96},{96,112},{1,17},{17... | collective-permute-start | bytes 491528 | tf_op jit(solution)/shard_map/ppermute | solution.py:25
  8.8 1.9 %collective-permute-start.1 = (f32[5,8,1024]{2,1,0:T(8,128)S(1)}, f32[5,8,1024]{2,1,0:T(8,128)S(1)}, u32[]{:S(2)}, u32[]{:S(2)}) collective-permute-start(f32[5,8,1024]{2,1,0:T(8,128)S(1)} %get-tuple-element.67), channel_id=1, source_target_pairs={{16,0},{32,16},{48,32},{64,48},{80,64},{96,80},{112,96},{17,1},{33... | collective-permute-start | bytes 491528 | tf_op jit(solution)/shard_map/ppermute | solution.py:25
  11.1 4.4 %collective-permute-done.1 = f32[5,8,1024]{2,1,0:T(8,128)S(1)} collective-permute-done((f32[5,8,1024]{2,1,0:T(8,128)S(1)}, f32[5,8,1024]{2,1,0:T(8,128)S(1)}, u32[]{:S(2)}, u32[]{:S(2)}) %collective-permute-start.1) | collective-permute-done | bytes 163872 | tf_op jit(solution)/shard_map/ppermute | solution.py:25
  16.4 2.5 %copy-done.12 = f32[5,272,1024]{2,1,0:T(8,128)} copy-done((f32[5,272,1024]{2,1,0:T(8,128)}, f32[5,272,1024]{2,1,0:T(8,128)S(1)}, u32[]{:S(2)}) %copy-start.12) | copy-done | bytes 5570584
  21.0 4.0 %collective-permute-start.2 = (f32[5,272,8]{1,2,0:T(8,128)S(1)}, f32[5,272,8]{1,2,0:T(8,128)S(1)}, u32[]{:S(2)}, u32[]{:S(2)}) collective-permute-start(f32[5,272,8]{1,2,0:T(8,128)S(1)} %copy.16), channel_id=1, source_target_pairs={{0,1},{1,2},{2,3},{3,4},{4,5},{5,6},{6,7},{7,8},{8,9},{9,10},{10,1... | collective-permute-start | bytes 130568 | tf_op jit(solution)/shard_map/ppermute | solution.py:25
  26.5 8.3 %concatenate.13 = f32[5,272,1040]{2,1,0:T(8,128)} concatenate(f32[5,272,8]{2,1,0:T(8,128)S(1)} %copy.18, f32[5,272,1024]{2,1,0:T(8,128)} %copy-done.12, f32[5,272,8]{2,1,0:T(8,128)S(1)} %copy.19), dimensions={2} | concatenate | bytes 11315200 | tf_op jit(solution)/shard_map/concatenate | solution.py:35
  34.9 3.6 %slice_bitcast_fusion.18 = (f32[271,1040]{1,0:T(8,128)S(1)}, f32[271,1040]{1,0:T(8,128)S(1)}, f32[271,1040]{1,0:T(8,128)}) fusion(f32[5,272,1040]{2,1,0:T(8,128)} %concatenate.13), kind=kLoop, calls=%fused_computation.64 | loop fusion | bytes 6764160 | tf_op jit(solution)/shard_map/slice | solution.py:43
  40.9 1.4 slice.347
  42.4 1.5 slice.349
  43.8 2.8 %multiply_bitcast_fusion.3 = (f32[1,272,1040]{2,1,0:T(8,128)S(1)}, f32[1,272,1040]{2,1,0:T(8,128)S(1)}, f32[1,272,1040]{2,1,0:T(8,128)S(1)}, f32[1,272,1040]{2,1...) fusion(f32[272,1039]{1,0:T(8,128)} %slice.343, f32[5,272,1040]{2,1,0:T(8,128)S(1)} %copy-done.7, ...), kind=kLoop, calls=%fused_computation.80 | loop fusion | flops 2263040 | bytes 16957056 | tf_op jit(solution)/shard_map/stack | solution.py:147
  48.9 2.5 %fusion.1 = (f32[2,272,1040]{2,1,0:T(8,128)}, f32[2,272,1040]{2,1,0:T(8,128)S(1)}) fusion(f32[1,272,1040]{2,1,0:T(8,128)S(1)} %get-tuple-element.54, f32[1,272,1040]{2,1,0:T(8,128)S(1)} %get-tuple-element.53, f32[1,272,1040]{2,1,0:T(8,128)S(1)} %get-tuple-element.81, f32[1,272,1040]{2,1,0:T(8,128)S(1)} %get-tuple-element.80, ...), kind=kLoop, calls=%fused_computation.6 | loop fusion | flops 10749440 | bytes 15841280 | tf_op jit(solution)/shard_map/jit(_where)/select_n | solution.py:151
  54.2 1.7 %multiply_reduce_fusion.4 = (f32[]{:T(128)}, f32[]{:T(128)}) fusion(f32[2,272,1040]{2,1,0:T(8,128)S(1)} %get-tuple-element.73, f32[2,272,1040]{2,1,0:T(8,128)S(1)} %fusion.5), kind=kLoop, calls=%fused_computation.37 | loop fusion | flops 2097150 | bytes 4194312 | tf_op jit(solution)/shard_map/reduce_sum | solution.py:139
  57.9 20.8 %shard_map.76 = f32[8,128]{1,0:T(8,128)} custom-call(f32[8,128]{1,0:T(8,128)} %scatter.10.local_ref), custom_call_target="tpu_custom_call" | custom-call | tf_op jit(solution)/shard_map/pallas_call | solution.py:117
  81.4 3.8 %multiply_subtract_fusion.1 = f32[2,272,1040]{2,1,0:T(8,128)S(1)} fusion(f32[2,272,1040]{2,1,0:T(8,128)S(1)} %get-tuple-element.73, f32[]{:T(128)S(6)} %div.23, f32[1,272,1040]{2,1,0:T(8,128)} %copy-done.15, f32[1,272,1040]{2,1,0:T(8,128)} %copy-done.14, f32[1,272,1040]{2,1,0:T(8,128)} %copy-done.10, f32[1,272,1040]{2,1,0:T(8,128)} %copy-done.8, ...), kind=kLoop, calls=%fused_computation.21 | loop fusion | flops 7354880 | bytes 11315204 | tf_op jit(solution)/shard_map/sub | solution.py:163
  91.3 2.4 %multiply_reduce_fusion.2 = (f32[]{:T(128)}, f32[]{:T(128)}, f32[]{:T(128)}) fusion(f32[2,272,1040]{2,1,0:T(8,128)S(1)} %multiply_subtract_fusion.1, f32[2,272,1040]{2,1,0:T(8,128)S(1)} %fusion.6, f32[2,272,1040]{2,1,0:T(8,128)S(1)} %copy-done.19), kind=kLoop, calls=%fused_computation.35 | loop fusion | flops 3145725 | bytes 6291468 | tf_op jit(solution)/shard_map/reduce_sum | solution.py:139
  93.7 2.0 %maximum_bitcast_fusion.1 = f32[1,3]{1,0:T(1,128)S(1)} fusion(f32[1]{0:T(128)} %bitcast.39, f32[1]{0:T(128)} %bitcast.38, f32[1]{0:T(128)} %bitcast.32), kind=kLoop, calls=%fused_computation.94 | loop fusion | flops 6 | bytes 24 | tf_op jit(solution)/shard_map/reshape.101
  96.3 12.8 %shard_map.77 = f32[8,128]{1,0:T(8,128)} custom-call(f32[8,128]{1,0:T(8,128)} %scatter.11.local_ref), custom_call_target="tpu_custom_call" | custom-call | tf_op jit(solution)/shard_map/pallas_call | solution.py:117
  114.3 5.3 %multiply_subtract_fusion = (f32[2,272,1040]{2,1,0:T(8,128)S(1)}, f32[2,272,1040]{2,1,0:T(8,128)S(1)}) fusion(f32[2,272,1040]{2,1,0:T(8,128)} %copy-done, f32[]{:T(128)S(6)} %div.25, f32[]{:T(128)S(6)} %div.24, f32[1,272,1040]{2,1,0:T(8,128)} %copy-done.21, f32[1,272,1040]{2,1,0:T(8,128)} %copy-done.20, f32[1,272,1040]{2,1,0:T(8,128)} %copy-done.10, ...), kind=kLoop, calls=%fused_computation.19 | loop fusion | flops 10749440 | bytes 18104328 | tf_op jit(solution)/shard_map/sub | solution.py:163
  123.2 3.7 %multiply_reduce_fusion = (f32[]{:T(128)}, f32[]{:T(128)}, f32[]{:T(128)}) fusion(f32[2,272,1040]{2,1,0:T(8,128)S(1)} %get-tuple-element.50, f32[2,272,1040]{2,1,0:T(8,128)S(1)} %get-tuple-element.51, f32[1,272,1040]{2,1,0:T(8,128)S(1)} %get-tuple-element.75, f32[1,272,1040]{2,1,0:T(8,128)S(1)} %get-tuple-element.74, f32[2,272,1040]{2,1,0:T(8,128)S(1)} %copy-done.24, ...), kind=kLoop, calls=%fused_computation.33 | loop fusion | flops 5767165 | bytes 10817548 | tf_op jit(solution)/shard_map/reduce_sum | solution.py:139
  126.9 2.0 %maximum_bitcast_fusion.2 = f32[1,3]{1,0:T(1,128)S(1)} fusion(f32[1]{0:T(128)} %bitcast.51, f32[1]{0:T(128)} %bitcast.50, f32[1]{0:T(128)} %bitcast.44), kind=kLoop, calls=%fused_computation.95 | loop fusion | flops 6 | bytes 24 | tf_op jit(solution)/shard_map/reshape.102
  129.5 13.3 %shard_map.78 = f32[8,128]{1,0:T(8,128)} custom-call(f32[8,128]{1,0:T(8,128)} %scatter.14.local_ref), custom_call_target="tpu_custom_call" | custom-call | tf_op jit(solution)/shard_map/pallas_call | solution.py:117
  147.4 6.1 %multiply_add_fusion = f32[2,272,1040]{2,1,0:T(8,128)S(1)} fusion(f32[2,272,1040]{2,1,0:T(8,128)} %copy-done, f32[2,272,1040]{2,1,0:T(8,128)S(1)} %get-tuple-element.73, f32[]{:T(128)S(6)} %div.26, f32[]{:T(128)S(6)} %div.27, f32[]{:T(128)S(6)} %div.24, f32[]{:T(128)S(6)} %div.25, f32[]{:T(128)S(6)} %div.23, f32[2,272,1040]{2,1,0:T(8,128)} %copy-done.13, ...), kind=kLoop, calls=%fused_computation.18 | loop fusion | flops 10749440 | bytes 18104340 | tf_op jit(solution)/shard_map/add | solution.py:160
  153.6 1.9 %slice_bitcast_fusion.21 = (f32[256,1024]{1,0:T(8,128)}, f32[256,1024]{1,0:T(8,128)}) fusion(f32[2,272,1040]{2,1,0:T(8,128)S(1)} %multiply_add_fusion), kind=kLoop, calls=%fused_computation.81 | loop fusion | bytes 4194304 | tf_op jit(solution)/shard_map/squeeze | solution.py:173
  156.8 2.4 %slice_subtract_fusion.1 = f32[256,1024]{1,0:T(8,128)} fusion(f32[272,1040]{1,0:T(8,128)S(1)} %copy-done.23, f32[271,1040]{1,0:T(8,128)S(1)} %slice_bitcast_fusion, f32[272,1040]{1,0:T(8,128)S(1)} %get-tuple-element.71, f32[272,1039]{1,0:T(8,128)S(1)} %bitcast.147, f32[272,1040]{1,0:T(8,128)S(1)} %get-tuple-element.70), kind=kLoop, calls=%fused_computation.83 | loop fusion | flops 1310720 | bytes 6452096 | tf_op jit(solution)/shard_map/sub | solution.py:171
  (113 shorter events, 33.7 us)
Async XLA Ops:
  0.6 1.8 %copy-start.27 = (s32[256,1024]{1,0:T(8,128)S(1)}, s32[256,1024]{1,0:T(8,128)}, u32[]{:S(2)}) copy-start(s32[256,1024]{1,0:T(8,128)} %param.13) | copy-start | bytes 3145732
  3.9 7.2 %collective-permute-start = (f32[5,8,1024]{2,1,0:T(8,128)S(1)}, f32[5,8,1024]{2,1,0:T(8,128)S(1)}, u32[]{:S(2)}, u32[]{:S(2)}) collective-permute-start(f32[5,8,1024]{2,1,0:T(8,128)S(1)} %get-tuple-element.66), channel_id=1, source_target_pairs={{0,16},{16,32},{32,48},{48,64},{64,80},{80,96},{96,112},{1,17},{17... | collective-permute-start | bytes 491528 | tf_op jit(solution)/shard_map/ppermute | solution.py:25
  8.8 6.6 %collective-permute-start.1 = (f32[5,8,1024]{2,1,0:T(8,128)S(1)}, f32[5,8,1024]{2,1,0:T(8,128)S(1)}, u32[]{:S(2)}, u32[]{:S(2)}) collective-permute-start(f32[5,8,1024]{2,1,0:T(8,128)S(1)} %get-tuple-element.67), channel_id=1, source_target_pairs={{16,0},{32,16},{48,32},{64,48},{80,64},{96,80},{112,96},{17,1},{33... | collective-permute-start | bytes 491528 | tf_op jit(solution)/shard_map/ppermute | solution.py:25
  16.4 2.5 %copy-start.12 = (f32[5,272,1024]{2,1,0:T(8,128)}, f32[5,272,1024]{2,1,0:T(8,128)S(1)}, u32[]{:S(2)}) copy-start(f32[5,272,1024]{2,1,0:T(8,128)S(1)} %pad_maximum_fusion) | copy-start | bytes 16711684
  19.4 5.6 %collective-permute-start.3 = (f32[5,272,8]{1,2,0:T(8,128)S(1)}, f32[5,272,8]{1,2,0:T(8,128)S(1)}, u32[]{:S(2)}, u32[]{:S(2)}) collective-permute-start(f32[5,272,8]{1,2,0:T(8,128)S(1)} %copy.17), channel_id=1, source_target_pairs={{1,0},{2,1},{3,2},{4,3},{5,4},{6,5},{7,6},{8,7},{9,8},{10,9},{11,1... | collective-permute-start | bytes 130568 | tf_op jit(solution)/shard_map/ppermute | solution.py:25
  21.0 5.3 %collective-permute-start.2 = (f32[5,272,8]{1,2,0:T(8,128)S(1)}, f32[5,272,8]{1,2,0:T(8,128)S(1)}, u32[]{:S(2)}, u32[]{:S(2)}) collective-permute-start(f32[5,272,8]{1,2,0:T(8,128)S(1)} %copy.16), channel_id=1, source_target_pairs={{0,1},{1,2},{2,3},{3,4},{4,5},{5,6},{6,7},{7,8},{8,9},{9,10},{10,1... | collective-permute-start | bytes 130568 | tf_op jit(solution)/shard_map/ppermute | solution.py:25
  34.9 4.4 %copy-start.7 = (f32[5,272,1040]{2,1,0:T(8,128)S(1)}, f32[5,272,1040]{2,1,0:T(8,128)}, u32[]{:S(2)}) copy-start(f32[5,272,1040]{2,1,0:T(8,128)} %concatenate.13) | copy-start | bytes 16972804
  39.5 2.9 %copy-start.22 = (f32[272,1040]{1,0:T(8,128)}, f32[272,1040]{1,0:T(8,128)S(1)}, u32[]{:S(2)}) copy-start(f32[272,1040]{1,0:T(8,128)S(1)} %get-tuple-element.60) | copy-start | bytes 3394564
  46.7 2.2 %copy-start.16 = (f32[1,272,1040]{2,1,0:T(8,128)}, f32[1,272,1040]{2,1,0:T(8,128)S(1)}, u32[]{:S(2)}) copy-start(f32[1,272,1040]{2,1,0:T(8,128)S(1)} %get-tuple-element.56) | copy-start | bytes 3394564
  46.7 2.2 %copy-start.17 = (f32[1,272,1040]{2,1,0:T(8,128)}, f32[1,272,1040]{2,1,0:T(8,128)S(1)}, u32[]{:S(2)}) copy-start(f32[1,272,1040]{2,1,0:T(8,128)S(1)} %get-tuple-element.57) | copy-start | bytes 3394564
  46.7 6.1 %copy-start.1 = (f32[1,272,1040]{2,1,0:T(8,128)}, f32[1,272,1040]{2,1,0:T(8,128)S(1)}, u32[]{:S(2)}) copy-start(f32[1,272,1040]{2,1,0:T(8,128)S(1)} %get-tuple-element.52) | copy-start | bytes 3394564
  46.7 6.1 %copy-start.4 = (f32[1,272,1040]{2,1,0:T(8,128)}, f32[1,272,1040]{2,1,0:T(8,128)S(1)}, u32[]{:S(2)}) copy-start(f32[1,272,1040]{2,1,0:T(8,128)S(1)} %get-tuple-element.55) | copy-start | bytes 3394564
  46.7 6.1 %copy-start.8 = (f32[1,272,1040]{2,1,0:T(8,128)}, f32[1,272,1040]{2,1,0:T(8,128)S(1)}, u32[]{:S(2)}) copy-start(f32[1,272,1040]{2,1,0:T(8,128)S(1)} %get-tuple-element.53) | copy-start | bytes 3394564
  46.7 6.1 %copy-start.10 = (f32[1,272,1040]{2,1,0:T(8,128)}, f32[1,272,1040]{2,1,0:T(8,128)S(1)}, u32[]{:S(2)}) copy-start(f32[1,272,1040]{2,1,0:T(8,128)S(1)} %get-tuple-element.54) | copy-start | bytes 3394564
  54.2 1.8 %copy-start.18 = (f32[2,272,1040]{2,1,0:T(8,128)}, f32[2,272,1040]{2,1,0:T(8,128)S(1)}, u32[]{:S(2)}) copy-start(f32[2,272,1040]{2,1,0:T(8,128)S(1)} %fusion.5) | copy-start | bytes 6789124
  85.1 5.3 %copy-start = (f32[2,272,1040]{2,1,0:T(8,128)}, f32[2,272,1040]{2,1,0:T(8,128)S(1)}, u32[]{:S(2)}) copy-start(f32[2,272,1040]{2,1,0:T(8,128)S(1)} %multiply_subtract_fusion.1) | copy-start | bytes 6789124
  86.3 2.6 %copy-start.5 = (f32[1,272,1040]{2,1,0:T(8,128)S(1)}, f32[1,272,1040]{2,1,0:T(8,128)}, u32[]{:S(2)}) copy-start(f32[1,272,1040]{2,1,0:T(8,128)} %copy-done.4) | copy-start | bytes 3394564
  86.3 2.9 %copy-start.9 = (f32[1,272,1040]{2,1,0:T(8,128)S(1)}, f32[1,272,1040]{2,1,0:T(8,128)}, u32[]{:S(2)}) copy-start(f32[1,272,1040]{2,1,0:T(8,128)} %copy-done.8) | copy-start | bytes 3394564
  86.3 3.3 %copy-start.11 = (f32[1,272,1040]{2,1,0:T(8,128)S(1)}, f32[1,272,1040]{2,1,0:T(8,128)}, u32[]{:S(2)}) copy-start(f32[1,272,1040]{2,1,0:T(8,128)} %copy-done.10) | copy-start | bytes 3394564
  86.6 3.8 %copy-start.20 = (f32[1,272,1040]{2,1,0:T(8,128)}, f32[1,272,1040]{2,1,0:T(8,128)S(1)}, u32[]{:S(2)}) copy-start(f32[1,272,1040]{2,1,0:T(8,128)S(1)} %get-tuple-element.76) | copy-start | bytes 3394564
  86.6 3.8 %copy-start.21 = (f32[1,272,1040]{2,1,0:T(8,128)}, f32[1,272,1040]{2,1,0:T(8,128)S(1)}, u32[]{:S(2)}) copy-start(f32[1,272,1040]{2,1,0:T(8,128)S(1)} %get-tuple-element.77) | copy-start | bytes 3394564
  89.6 1.7 %copy-start.19 = (f32[2,272,1040]{2,1,0:T(8,128)S(1)}, f32[2,272,1040]{2,1,0:T(8,128)}, u32[]{:S(2)}) copy-start(f32[2,272,1040]{2,1,0:T(8,128)} %copy-done.18) | copy-start | bytes 6789124
  120.7 1.7 %copy-start.6 = (f32[1,272,1040]{2,1,0:T(8,128)S(1)}, f32[1,272,1040]{2,1,0:T(8,128)}, u32[]{:S(2)}) copy-start(f32[1,272,1040]{2,1,0:T(8,128)} %copy-done.4) | copy-start | bytes 3394564
  120.7 2.5 %copy-start.24 = (f32[2,272,1040]{2,1,0:T(8,128)S(1)}, f32[2,272,1040]{2,1,0:T(8,128)}, u32[]{:S(2)}) copy-start(f32[2,272,1040]{2,1,0:T(8,128)} %get-tuple-element.72) | copy-start | bytes 6789124
  (10 other events, 13.6 us)

commit v6 on v5

--- a/solution.py
+++ b/solution.py
@@ -25,30 +25,30 @@
     return lax.ppermute(value, axis, [(source, source + steps) for source in range(leading, last)])
 
 
-def grow(stacked):
+def grow(fields):
     rows, cols = MARGIN_ROWS, MARGIN_COLS
-    above = from_behind(stacked[:, :rows, :], "lat", -1)
-    below = from_behind(stacked[:, -rows:, :], "lat", 1)
-    stacked = jnp.concatenate([below, stacked, above], axis=1)
-    right = from_behind(stacked[:, :, :cols], "lon", -1)
-    left = from_behind(stacked[:, :, -cols:], "lon", 1)
-    return jnp.concatenate([left, stacked, right], axis=2)
+    above = from_behind(jnp.stack([f[:rows] for f in fields]), "lat", -1)
+    below = from_behind(jnp.stack([f[-rows:] for f in fields]), "lat", 1)
+    tall = [jnp.concatenate([f, above[k], below[k]], axis=0) for k, f in enumerate(fields)]
+    right = from_behind(jnp.stack([f[:, :cols] for f in tall]), "lon", -1)
+    left = from_behind(jnp.stack([f[:, -cols:] for f in tall]), "lon", 1)
+    return [jnp.concatenate([f, right[k], left[k]], axis=1) for k, f in enumerate(tall)]
 
 
 def east(field):
-    return jnp.pad(field[..., :, 1:], [(0, 0)] * (field.ndim - 1) + [(0, 1)])
+    return jnp.roll(field, -1, axis=-1)
 
 
 def north(field):
-    return jnp.pad(field[..., 1:, :], [(0, 0)] * (field.ndim - 2) + [(0, 1), (0, 0)])
+    return jnp.roll(field, -1, axis=-2)
 
 
 def west(field):
-    return jnp.pad(field[..., :, :-1], [(0, 0)] * (field.ndim - 1) + [(1, 0)])
+    return jnp.roll(field, 1, axis=-1)
 
 
 def south(field):
-    return jnp.pad(field[..., :-1, :], [(0, 0)] * (field.ndim - 2) + [(1, 0), (0, 0)])
+    return jnp.roll(field, 1, axis=-2)
 
 
 def divergence(field):
@@ -132,7 +132,7 @@
 
 def interior(field):
     rows, cols = MARGIN_ROWS, MARGIN_COLS
-    return field[..., rows:-rows, cols:-cols]
+    return field[..., : -2 * rows, : -2 * cols]
 
 
 def sums(*pairs):
@@ -142,12 +142,11 @@
 
 def per_device(surface, bathymetry, land_sea, flux_lon, flux_lat):
     sea = land_sea.astype(jnp.float32)
-    grown = grow(jnp.stack([surface, bathymetry, sea, flux_lon, flux_lat]))
-    surface_x, bathymetry_x, sea_x = grown[0], grown[1], grown[2]
+    surface_x, bathymetry_x, sea_x, flux_lon_x, flux_lat_x = grow([surface, bathymetry, sea, flux_lon, flux_lat])
     wet = jnp.stack([sea_x * east(sea_x), sea_x * north(sea_x)])
     depth = jnp.stack([0.5 * (bathymetry_x + east(bathymetry_x)), 0.5 * (bathymetry_x + north(bathymetry_x))])
     slope = jnp.stack([east(surface_x) - surface_x, north(surface_x) - surface_x])
-    start = wet * (grown[3:] - courant * depth * slope)
+    start = wet * (jnp.stack([flux_lon_x, flux_lat_x]) - courant * depth * slope)
     inverse = jnp.where(depth > 0, 1.0 / (dispersion * depth * depth), 0.0)
     right_side = wet * inverse * start
     solution = start

time: 160 us -> 198 us (1.24)
  local copies, waits for them, and re-layouts: 42.8 us -> 78.8 us
  other arithmetic: 42.2 us -> 44.7 us
    concatenate x1 -> x44, local copies, waits for them, and re-layouts: 8.35 us -> 27.4 us  [the longest x8 12.7 us: grow(): jnp.concatenate([f, right[k], left[k]], axis=1)]
    another operation x1 -> x18, local copies, waits for them, and re-layouts: 0.07 us -> 13.8 us  [the longest x11 7.09 us: grow(): left = from_behind(jnp.stack([f[:, -cols:] for f in tall]), 'lon', 1)]
    slice x21 -> x17, local copies, waits for them, and re-layouts: 11 us -> 1.6 us  [the longest x10 0.78 us: south(): return jnp.roll(field, 1, axis=-2)]
    squeeze x1 -> x14, local copies, waits for them, and re-layouts: 0.24 us -> 7.13 us  [the longest x6 3.91 us: grow(): right[k]]
    unnamed x63 -> x128, local copies, waits for them, and re-layouts: 14.2 us -> 20.8 us
    concatenate x1 -> x3, other arithmetic: 0.93 us -> 4.88 us  [the longest x2 3.16 us: grow(): jnp.concatenate([f, right[k], left[k]], axis=1)]
    another operation x8 -> x3, other arithmetic: 9.25 us -> 5.36 us
    reduce_sum x3, other arithmetic: 7.86 us -> 4.3 us  [sums(): local = jnp.stack([jnp.sum(interior(x) * interior(y)) for x, y in pairs])]
  transfers between devices with their start and end apart: 4 -> 4, of which waited for: 3 -> 3; matrix products, arithmetic and copies ran while one was open for 0% -> 6% of each run, Pallas kernels for 0% -> 0%
where the time goes in v6:
time: 198 us; the launch traced here: 196 us
  local copies, waits for them, and re-layouts  78.8 us (40%)
  Pallas kernels  46.8 us (24%)
  other arithmetic  44.7 us (23%)
  starting transfers between devices  11.3 us (6%)
  between operations  10.1 us (5%)
  waiting for transfers between devices  4.66 us (2%)
    pallas_call x3, Pallas kernels, all_sum(): pl.pallas_call(functools.partial(reduce_kernel, stages), out_shape=jax.Sh...  46.8 us
    unnamed x128, local copies, waits for them, and re-layouts  20.8 us
    concatenate x8, local copies, waits for them, and re-layouts, grow(): jnp.concatenate([f, right[k], left[k]], axis=1)  12.7 us
    ppermute x4, starting transfers between devices, from_behind(): lax.ppermute(value, axis, [(source, source + steps) for source in range(l...  11.3 us
    sub x2, other arithmetic, per_device(): residual = residual - alpha * image  9.06 us
    concatenate x14, local copies, waits for them, and re-layouts, east(): return jnp.roll(field, -1, axis=-1)  7.93 us
    another operation x11, local copies, waits for them, and re-layouts, grow(): left = from_behind(jnp.stack([f[:, -cols:] for f in tall]), 'lon', 1)  7.09 us
    add x1, other arithmetic, per_device(): solution = solution + alpha * direction  6.01 us
  transfers between devices with their start and end apart: 4, of which 3 were waited for; matrix products, arithmetic and copies ran while one was open for 6% of the time, Pallas kernels for 0%

profile of v6, /device:TPU:1, one launch (start us, length us, event | category | flops | bytes accessed | tf_op | source)
XLA Modules:
  0.0 196.4 jit_solution(3253259917806298821)
XLA Ops:
  4.4 3.3 %collective-permute-start = (f32[5,8,1024]{2,1,0:T(8,128)S(1)}, f32[5,8,1024]{2,1,0:T(8,128)S(1)}, u32[]{:S(2)}, u32[]{:S(2)}) collective-permute-start(f32[5,8,1024]{2,1,0:T(8,128)S(1)} %get-tuple-element.120), channel_id=1, source_target_pairs={{16,0},{32,16},{48,32},{64,48},{80,64},{96,80},{112,96},{17,1},{33... | collective-permute-start | bytes 491528 | tf_op jit(solution)/shard_map/ppermute | solution.py:25
  7.7 3.6 %collective-permute-start.1 = (f32[5,8,1024]{2,1,0:T(8,128)S(1)}, f32[5,8,1024]{2,1,0:T(8,128)S(1)}, u32[]{:S(2)}, u32[]{:S(2)}) collective-permute-start(f32[5,8,1024]{2,1,0:T(8,128)S(1)} %get-tuple-element.121), channel_id=1, source_target_pairs={{0,16},{16,32},{32,48},{48,64},{64,80},{80,96},{96,112},{1,17},{17... | collective-permute-start | bytes 491528 | tf_op jit(solution)/shard_map/ppermute | solution.py:25
  14.1 1.9 fusion.34
  23.3 1.7 pad_maximum_fusion.6
  31.9 3.2 %collective-permute-start.3 = (f32[5,272,8]{1,2,0:T(8,128)}, f32[5,272,8]{1,2,0:T(8,128)S(1)}, u32[]{:S(2)}, u32[]{:S(2)}) collective-permute-start(f32[5,272,8]{1,2,0:T(8,128)} %constant_dynamic-update-slice_fusion.15), channel_id=1, source_target_pairs={{0,1},{1,2},{2,3},{3,4},{4,5},{5,6},{6,7},{7,8},{8,9},{9,10},{10,1... | collective-permute-start | bytes 130568 | tf_op jit(solution)/shard_map/ppermute | solution.py:25
  36.1 1.6 copy.24
  47.6 2.4 %collective-permute-done.2 = f32[5,272,8]{1,2,0:T(8,128)S(1)} collective-permute-done((f32[5,272,8]{1,2,0:T(8,128)}, f32[5,272,8]{1,2,0:T(8,128)S(1)}, u32[]{:S(2)}, u32[]{:S(2)}) %collective-permute-start.2) | collective-permute-done | bytes 43552 | tf_op jit(solution)/shard_map/ppermute | solution.py:25
  69.6 1.8 concatenate.336
  71.4 2.6 %concatenate.327 = f32[1,272,1040]{2,1,0:T(8,128)} concatenate(f32[1,272,1024]{2,1,0:T(8,128)} %get-tuple-element.104, f32[1,272,8]{2,1,0:T(8,128)S(1)} %copy.36, f32[1,272,8]{2,1,0:T(8,128)S(1)} %copy.37), dimensions={2} | concatenate | bytes 2263040 | tf_op jit(solution)/shard_map/concatenate | solution.py:35
  74.0 2.2 %concatenate.350 = f32[1,272,1040]{2,1,0:T(8,128)} concatenate(f32[1,272,1024]{2,1,0:T(8,128)} %get-tuple-element.108, f32[1,272,8]{2,1,0:T(8,128)S(1)} %copy.48, f32[1,272,8]{2,1,0:T(8,128)S(1)} %copy.49), dimensions={2} | concatenate | bytes 2263040 | tf_op jit(solution)/shard_map/concatenate | solution.py:35
  76.2 2.3 %concatenate.338 = f32[1,272,1040]{2,1,0:T(8,128)} concatenate(f32[1,272,1024]{2,1,0:T(8,128)} %get-tuple-element.167, f32[1,272,8]{2,1,0:T(8,128)S(1)} %copy.44, f32[1,272,8]{2,1,0:T(8,128)S(1)} %copy.45), dimensions={2} | concatenate | bytes 2263040 | tf_op jit(solution)/shard_map/concatenate | solution.py:35
  78.5 2.4 %maximum_multiply_fusion.1 = (f32[1,272,1040]{2,1,0:T(8,128)S(1)}, f32[1,272,1040]{2,1,0:T(8,128)S(1)}) fusion(f32[1,272,1040]{2,1,0:T(8,128)} %concatenate.327, f32[1,272,1]{2,1,0:T(8,128)S(1)} %copy-done.41, f32[1,272,1039]{2,1,0:T(8,128)} %slice_bitcast_fusion.16, f32[1,1,1040]{2,1,0:T(1,128)S(1)} %copy-done.55, f32[1,271,1040]{2,1,0:T(8,128)} %slice_bitcast_fusion.15), kind=kLoop, calls=%fused_computation.54 | loop fusion | flops 1131520 | bytes 5657600 | tf_op jit(solution)/shard_map/mul | solution.py:146
  82.0 1.8 copy-done.34
  89.4 2.5 %fusion.1 = (f32[2,272,1040]{2,1,0:T(8,128)}, f32[2,272,1040]{2,1,0:T(8,128)S(1)}) fusion(f32[1,272,1040]{2,1,0:T(8,128)S(1)} %get-tuple-element.101, f32[1,272,1040]{2,1,0:T(8,128)S(1)} %get-tuple-element.100, f32[1,272,1040]{2,1,0:T(8,128)S(1)} %maximum_subtract_fusion.6, f32[1,272,1040]{2,1,0:T(8,128)S(1)} %get-tuple-element.58, ...), kind=kLoop, calls=%fused_computation.5 | loop fusion | flops 11315200 | bytes 15841280 | tf_op jit(solution)/shard_map/jit(_where)/select_n | solution.py:150
  99.3 20.4 %shard_map.76 = f32[8,128]{1,0:T(8,128)} custom-call(f32[8,128]{1,0:T(8,128)} %scatter.10.local_ref), custom_call_target="tpu_custom_call" | custom-call | tf_op jit(solution)/shard_map/pallas_call | solution.py:117
  122.4 3.8 %multiply_subtract_fusion.1 = f32[2,272,1040]{2,1,0:T(8,128)S(1)} fusion(f32[2,272,1040]{2,1,0:T(8,128)S(1)} %get-tuple-element.65, f32[]{:T(128)S(6)} %div.23, f32[1,272,1040]{2,1,0:T(8,128)} %copy-done.13, f32[1,272,1040]{2,1,0:T(8,128)} %copy-done.12, f32[1,272,1040]{2,1,0:T(8,128)} %copy-done.9, f32[1,272,1040]{2,1,0:T(8,128)} %copy-done.7, ...), kind=kLoop, calls=%fused_computation.20 | loop fusion | flops 7354880 | bytes 11315204 | tf_op jit(solution)/shard_map/sub | solution.py:162
  133.1 1.5 multiply_reduce_fusion.2
  134.6 2.0 %maximum_bitcast_fusion.1 = f32[1,3]{1,0:T(1,128)S(1)} fusion(f32[1]{0:T(128)} %bitcast.94, f32[1]{0:T(128)} %bitcast.93, f32[1]{0:T(128)} %bitcast.82), kind=kLoop, calls=%fused_computation.174 | loop fusion | flops 6 | bytes 24 | tf_op jit(solution)/shard_map/reshape.103
  137.2 13.0 %shard_map.77 = f32[8,128]{1,0:T(8,128)} custom-call(f32[8,128]{1,0:T(8,128)} %scatter.11.local_ref), custom_call_target="tpu_custom_call" | custom-call | tf_op jit(solution)/shard_map/pallas_call | solution.py:117
  155.4 5.3 %multiply_subtract_fusion = (f32[2,272,1040]{2,1,0:T(8,128)S(1)}, f32[2,272,1040]{2,1,0:T(8,128)S(1)}) fusion(f32[2,272,1040]{2,1,0:T(8,128)} %copy-done, f32[]{:T(128)S(6)} %div.25, f32[]{:T(128)S(6)} %div.24, f32[1,272,1040]{2,1,0:T(8,128)} %copy-done.25, f32[1,272,1040]{2,1,0:T(8,128)} %copy-done.24, f32[1,272,1040]{2,1,0:T(8,128)} %copy-done.9, ...), kind=kLoop, calls=%fused_computation.18 | loop fusion | flops 10749440 | bytes 18104328 | tf_op jit(solution)/shard_map/sub | solution.py:162
  166.2 2.0 %maximum_bitcast_fusion.2 = f32[1,3]{1,0:T(1,128)S(1)} fusion(f32[1]{0:T(128)} %bitcast.111, f32[1]{0:T(128)} %bitcast.110, f32[1]{0:T(128)} %bitcast.99), kind=kLoop, calls=%fused_computation.175 | loop fusion | flops 6 | bytes 24 | tf_op jit(solution)/shard_map/reshape.104
  168.9 13.4 %shard_map.78 = f32[8,128]{1,0:T(8,128)} custom-call(f32[8,128]{1,0:T(8,128)} %scatter.14.local_ref), custom_call_target="tpu_custom_call" | custom-call | tf_op jit(solution)/shard_map/pallas_call | solution.py:117
  186.9 6.0 %multiply_add_fusion = f32[2,272,1040]{2,1,0:T(8,128)S(1)} fusion(f32[2,272,1040]{2,1,0:T(8,128)} %copy-done, f32[2,272,1040]{2,1,0:T(8,128)S(1)} %get-tuple-element.65, f32[]{:T(128)S(6)} %div.26, f32[]{:T(128)S(6)} %div.27, f32[]{:T(128)S(6)} %div.24, f32[]{:T(128)S(6)} %div.25, f32[]{:T(128)S(6)} %div.23, f32[2,272,1040]{2,1,0:T(8,128)} %copy-done.11, ...), kind=kLoop, calls=%fused_computation.17 | loop fusion | flops 11315200 | bytes 18104340 | tf_op jit(solution)/shard_map/add | solution.py:159
  193.2 1.6 slice_bitcast_fusion.21
  (253 shorter events, 83.9 us)
Async XLA Ops:
  4.4 7.9 %collective-permute-start = (f32[5,8,1024]{2,1,0:T(8,128)S(1)}, f32[5,8,1024]{2,1,0:T(8,128)S(1)}, u32[]{:S(2)}, u32[]{:S(2)}) collective-permute-start(f32[5,8,1024]{2,1,0:T(8,128)S(1)} %get-tuple-element.120), channel_id=1, source_target_pairs={{16,0},{32,16},{48,32},{64,48},{80,64},{96,80},{112,96},{17,1},{33... | collective-permute-start | bytes 491528 | tf_op jit(solution)/shard_map/ppermute | solution.py:25
  7.7 5.8 %collective-permute-start.1 = (f32[5,8,1024]{2,1,0:T(8,128)S(1)}, f32[5,8,1024]{2,1,0:T(8,128)S(1)}, u32[]{:S(2)}, u32[]{:S(2)}) collective-permute-start(f32[5,8,1024]{2,1,0:T(8,128)S(1)} %get-tuple-element.121), channel_id=1, source_target_pairs={{0,16},{16,32},{32,48},{48,64},{64,80},{80,96},{96,112},{1,17},{17... | collective-permute-start | bytes 491528 | tf_op jit(solution)/shard_map/ppermute | solution.py:25
  25.0 21.8 %copy-start.29 = (f32[272,1024]{1,0:T(8,128)}, f32[272,1024]{1,0:T(8,128)S(1)}, u32[]{:S(2)}) copy-start(f32[272,1024]{1,0:T(8,128)S(1)} %get-tuple-element.165) | copy-start | bytes 3342340
  25.0 4.5 %copy-start.53 = (f32[1,272,8]{1,2,0:T(8,128)S(1)}, f32[1,272,8]{1,2,0:T(8,128)}, u32[]{:S(2)}) copy-start(f32[1,272,8]{1,2,0:T(8,128)} %copy.30) | copy-start | bytes 26116
  25.0 5.1 %copy-start.54 = (f32[1,272,8]{1,2,0:T(8,128)S(1)}, f32[1,272,8]{1,2,0:T(8,128)}, u32[]{:S(2)}) copy-start(f32[1,272,8]{1,2,0:T(8,128)} %copy.31) | copy-start | bytes 26116
  31.9 14.2 %collective-permute-start.3 = (f32[5,272,8]{1,2,0:T(8,128)}, f32[5,272,8]{1,2,0:T(8,128)S(1)}, u32[]{:S(2)}, u32[]{:S(2)}) collective-permute-start(f32[5,272,8]{1,2,0:T(8,128)} %constant_dynamic-update-slice_fusion.15), channel_id=1, source_target_pairs={{0,1},{1,2},{2,3},{3,4},{4,5},{5,6},{6,7},{7,8},{8,9},{9,10},{10,1... | collective-permute-start | bytes 130568 | tf_op jit(solution)/shard_map/ppermute | solution.py:25
  44.9 5.2 %collective-permute-start.2 = (f32[5,272,8]{1,2,0:T(8,128)}, f32[5,272,8]{1,2,0:T(8,128)S(1)}, u32[]{:S(2)}, u32[]{:S(2)}) collective-permute-start(f32[5,272,8]{1,2,0:T(8,128)} %constant_dynamic-update-slice_fusion.10), channel_id=1, source_target_pairs={{1,0},{2,1},{3,2},{4,3},{5,4},{6,5},{7,6},{8,7},{9,8},{10,9},{11,1... | collective-permute-start | bytes 130568 | tf_op jit(solution)/shard_map/ppermute | solution.py:25
  53.8 3.6 %copy-start.28 = (f32[272,1024]{1,0:T(8,128)S(1)}, f32[272,1024]{1,0:T(8,128)}, u32[]{:S(2)}) copy-start(f32[272,1024]{1,0:T(8,128)} %copy-done.27) | copy-start | bytes 3342340
  63.7 3.5 %copy-start.43 = (f32[272,8]{0,1:T(8,128)S(1)}, f32[272,8]{0,1:T(8,128)}, u32[]{:S(2)}) copy-start(f32[272,8]{0,1:T(8,128)} %get-tuple-element.144) | copy-start | bytes 26116
  63.7 3.7 %copy-start.47 = (f32[272,8]{0,1:T(8,128)S(1)}, f32[272,8]{0,1:T(8,128)}, u32[]{:S(2)}) copy-start(f32[272,8]{0,1:T(8,128)} %get-tuple-element.152) | copy-start | bytes 26116
  65.1 3.3 %copy-start.31 = (f32[272,1024]{1,0:T(8,128)S(1)}, f32[272,1024]{1,0:T(8,128)}, u32[]{:S(2)}) copy-start(f32[272,1024]{1,0:T(8,128)} %copy-done.30) | copy-start | bytes 3342340
  69.6 15.5 %copy-start.14 = (f32[272,1040]{1,0:T(8,128)}, f32[272,1040]{1,0:T(8,128)S(1)}, u32[]{:S(2)}) copy-start(f32[272,1040]{1,0:T(8,128)S(1)} %concatenate.335) | copy-start | bytes 3394564
  71.4 13.7 %copy-start.16 = (f32[272,1040]{1,0:T(8,128)}, f32[272,1040]{1,0:T(8,128)S(1)}, u32[]{:S(2)}) copy-start(f32[272,1040]{1,0:T(8,128)S(1)} %concatenate.336) | copy-start | bytes 3394564
  78.5 3.2 %copy-start.37 = (f32[1,272,1040]{2,1,0:T(8,128)S(1)}, f32[1,272,1040]{2,1,0:T(8,128)}, u32[]{:S(2)}) copy-start(f32[1,272,1040]{2,1,0:T(8,128)} %concatenate.350) | copy-start | bytes 3394564
  78.5 3.2 %copy-start.42 = (f32[1,272,1]{2,1,0:T(8,128)S(1)}, f32[1,272,1]{2,1,0:T(8,128)}, u32[]{:S(2)}) copy-start(f32[1,272,1]{2,1,0:T(8,128)} %slice_bitcast_fusion.27) | copy-start | bytes 3268
  78.5 3.2 %copy-start.56 = (f32[1,1,1040]{2,1,0:T(1,128)S(1)}, f32[1,1,1040]{2,1,0:T(1,128)}, u32[]{:S(2)}) copy-start(f32[1,1,1040]{2,1,0:T(1,128)} %slice_bitcast_fusion.61) | copy-start | bytes 12484
  81.7 12.4 %copy-start.1 = (f32[1,272,1040]{2,1,0:T(8,128)}, f32[1,272,1040]{2,1,0:T(8,128)S(1)}, u32[]{:S(2)}) copy-start(f32[1,272,1040]{2,1,0:T(8,128)S(1)} %get-tuple-element.98) | copy-start | bytes 3394564
  81.7 12.4 %copy-start.4 = (f32[1,272,1040]{2,1,0:T(8,128)}, f32[1,272,1040]{2,1,0:T(8,128)S(1)}, u32[]{:S(2)}) copy-start(f32[1,272,1040]{2,1,0:T(8,128)S(1)} %get-tuple-element.99) | copy-start | bytes 3394564
  84.6 3.2 %copy-start.18 = (f32[1,272,1040]{2,1,0:T(8,128)}, f32[1,272,1040]{2,1,0:T(8,128)S(1)}, u32[]{:S(2)}) copy-start(f32[1,272,1040]{2,1,0:T(8,128)S(1)} %get-tuple-element.102) | copy-start | bytes 3394564
  84.7 3.2 %copy-start.19 = (f32[1,272,1040]{2,1,0:T(8,128)}, f32[1,272,1040]{2,1,0:T(8,128)S(1)}, u32[]{:S(2)}) copy-start(f32[1,272,1040]{2,1,0:T(8,128)S(1)} %get-tuple-element.103) | copy-start | bytes 3394564
  85.0 9.1 %copy-start.7 = (f32[1,272,1040]{2,1,0:T(8,128)}, f32[1,272,1040]{2,1,0:T(8,128)S(1)}, u32[]{:S(2)}) copy-start(f32[1,272,1040]{2,1,0:T(8,128)S(1)} %get-tuple-element.100) | copy-start | bytes 3394564
  85.0 9.1 %copy-start.9 = (f32[1,272,1040]{2,1,0:T(8,128)}, f32[1,272,1040]{2,1,0:T(8,128)S(1)}, u32[]{:S(2)}) copy-start(f32[1,272,1040]{2,1,0:T(8,128)S(1)} %get-tuple-element.101) | copy-start | bytes 3394564
  126.2 6.0 %copy-start = (f32[2,272,1040]{2,1,0:T(8,128)}, f32[2,272,1040]{2,1,0:T(8,128)S(1)}, u32[]{:S(2)}) copy-start(f32[2,272,1040]{2,1,0:T(8,128)S(1)} %multiply_subtract_fusion.1) | copy-start | bytes 6789124
  128.5 3.6 %copy-start.25 = (f32[1,272,1040]{2,1,0:T(8,128)}, f32[1,272,1040]{2,1,0:T(8,128)S(1)}, u32[]{:S(2)}) copy-start(f32[1,272,1040]{2,1,0:T(8,128)S(1)} %maximum_subtract_fusion.14) | copy-start | bytes 3394564
  (38 other events, 80.7 us)

commit v7 on v5

--- a/solution.py
+++ b/solution.py
@@ -74,14 +74,6 @@
         other = own - digit * stride + ((digit + offset) % members) * stride
         return tuple(other if name == axis else me[name] for name in ("lat", "lon"))
 
-    barrier = pltpu.get_barrier_semaphore()
-    greeted = 0
-    for axis, stride, members in stages:
-        for offset in range(1, members):
-            pl.semaphore_signal(barrier, inc=1, device_id=partner(axis, stride, members, offset), device_id_type=MESH)
-            greeted += 1
-    pl.semaphore_wait(barrier, greeted)
-
     value = local_ref[...]
     for stage, (axis, stride, members) in enumerate(stages):
         parts[stage] = value
@@ -125,7 +117,7 @@
             pltpu.SemaphoreType.DMA((len(stages), widest)),
             pltpu.SemaphoreType.DMA((len(stages), widest)),
         ],
-        compiler_params=pltpu.CompilerParams(collective_id=0, has_side_effects=True),
+        compiler_params=pltpu.CompilerParams(has_side_effects=True),
     )(tile)
     return summed[0, : local.shape[0]]
 

time: 160 us -> 174 us (1.087)
  Pallas kernels: 46.9 us -> 61.1 us
    pallas_call x3, Pallas kernels: 46.9 us -> 61.1 us  [all_sum(): pl.pallas_call(functools.partial(reduce_kernel, stages), out_shape=jax.Sh...]
where the time goes in v7:
time: 174 us; the launch traced here: 173 us
  Pallas kernels  61.1 us (35%)
  local copies, waits for them, and re-layouts  42.8 us (25%)
  other arithmetic  42 us (24%)
  starting transfers between devices  12.2 us (7%)
  between operations  9.48 us (5%)
  waiting for transfers between devices  5.72 us (3%)
    pallas_call x3, Pallas kernels, all_sum(): pl.pallas_call(functools.partial(reduce_kernel, stages), out_shape=jax.Sh...  61.1 us
    unnamed x63, local copies, waits for them, and re-layouts  14.2 us
    ppermute x4, starting transfers between devices, from_behind(): lax.ppermute(value, axis, [(source, source + steps) for source in range(l...  12.2 us
    sub x2, other arithmetic, per_device(): residual = residual - alpha * image  8.87 us
    concatenate x1, local copies, waits for them, and re-layouts, grow(): return jnp.concatenate([left, stacked, right], axis=2)  8.35 us
    reduce_sum x3, other arithmetic, sums(): local = jnp.stack([jnp.sum(interior(x) * interior(y)) for x, y in pairs])  7.86 us
    add x1, other arithmetic, per_device(): solution = solution + alpha * direction  6.06 us
    slice x7, local copies, waits for them, and re-layouts, east(): return jnp.pad(field[..., :, 1:], [(0, 0)] * (field.ndim - 1) + [(0, 1)])  5.89 us
  transfers between devices with their start and end apart: 4, of which 3 were waited for; matrix products, arithmetic and copies ran while one was open for 0% of the time, Pallas kernels for 0%

profile of v7, /device:TPU:1, one launch (start us, length us, event | category | flops | bytes accessed | tf_op | source)
XLA Modules:
  0.0 173.2 jit_solution(7678571750374094990)
XLA Ops:
  3.9 4.9 %collective-permute-start = (f32[5,8,1024]{2,1,0:T(8,128)S(1)}, f32[5,8,1024]{2,1,0:T(8,128)S(1)}, u32[]{:S(2)}, u32[]{:S(2)}) collective-permute-start(f32[5,8,1024]{2,1,0:T(8,128)S(1)} %get-tuple-element.66), channel_id=1, source_target_pairs={{0,16},{16,32},{32,48},{48,64},{64,80},{80,96},{96,112},{1,17},{17... | collective-permute-start | bytes 491528 | tf_op jit(solution)/shard_map/ppermute | solution.py:25
  8.8 1.9 %collective-permute-start.1 = (f32[5,8,1024]{2,1,0:T(8,128)S(1)}, f32[5,8,1024]{2,1,0:T(8,128)S(1)}, u32[]{:S(2)}, u32[]{:S(2)}) collective-permute-start(f32[5,8,1024]{2,1,0:T(8,128)S(1)} %get-tuple-element.67), channel_id=1, source_target_pairs={{16,0},{32,16},{48,32},{64,48},{80,64},{96,80},{112,96},{17,1},{33... | collective-permute-start | bytes 491528 | tf_op jit(solution)/shard_map/ppermute | solution.py:25
  11.1 4.4 %collective-permute-done.1 = f32[5,8,1024]{2,1,0:T(8,128)S(1)} collective-permute-done((f32[5,8,1024]{2,1,0:T(8,128)S(1)}, f32[5,8,1024]{2,1,0:T(8,128)S(1)}, u32[]{:S(2)}, u32[]{:S(2)}) %collective-permute-start.1) | collective-permute-done | bytes 163872 | tf_op jit(solution)/shard_map/ppermute | solution.py:25
  16.4 2.5 %copy-done.12 = f32[5,272,1024]{2,1,0:T(8,128)} copy-done((f32[5,272,1024]{2,1,0:T(8,128)}, f32[5,272,1024]{2,1,0:T(8,128)S(1)}, u32[]{:S(2)}) %copy-start.12) | copy-done | bytes 5570584
  21.0 4.0 %collective-permute-start.2 = (f32[5,272,8]{1,2,0:T(8,128)S(1)}, f32[5,272,8]{1,2,0:T(8,128)S(1)}, u32[]{:S(2)}, u32[]{:S(2)}) collective-permute-start(f32[5,272,8]{1,2,0:T(8,128)S(1)} %copy.16), channel_id=1, source_target_pairs={{0,1},{1,2},{2,3},{3,4},{4,5},{5,6},{6,7},{7,8},{8,9},{9,10},{10,1... | collective-permute-start | bytes 130568 | tf_op jit(solution)/shard_map/ppermute | solution.py:25
  26.5 8.3 %concatenate.13 = f32[5,272,1040]{2,1,0:T(8,128)} concatenate(f32[5,272,8]{2,1,0:T(8,128)S(1)} %copy.18, f32[5,272,1024]{2,1,0:T(8,128)} %copy-done.12, f32[5,272,8]{2,1,0:T(8,128)S(1)} %copy.19), dimensions={2} | concatenate | bytes 11315200 | tf_op jit(solution)/shard_map/concatenate | solution.py:35
  34.9 3.6 %slice_bitcast_fusion.18 = (f32[271,1040]{1,0:T(8,128)S(1)}, f32[271,1040]{1,0:T(8,128)S(1)}, f32[271,1040]{1,0:T(8,128)}) fusion(f32[5,272,1040]{2,1,0:T(8,128)} %concatenate.13), kind=kLoop, calls=%fused_computation.64 | loop fusion | bytes 6764160 | tf_op jit(solution)/shard_map/slice | solution.py:43
  40.9 1.4 slice.347
  42.4 1.5 slice.349
  43.8 2.8 %multiply_bitcast_fusion.3 = (f32[1,272,1040]{2,1,0:T(8,128)S(1)}, f32[1,272,1040]{2,1,0:T(8,128)S(1)}, f32[1,272,1040]{2,1,0:T(8,128)S(1)}, f32[1,272,1040]{2,1...) fusion(f32[272,1039]{1,0:T(8,128)} %slice.343, f32[5,272,1040]{2,1,0:T(8,128)S(1)} %copy-done.7, ...), kind=kLoop, calls=%fused_computation.80 | loop fusion | flops 2263040 | bytes 16957056 | tf_op jit(solution)/shard_map/stack | solution.py:139
  48.9 2.5 %fusion.1 = (f32[2,272,1040]{2,1,0:T(8,128)}, f32[2,272,1040]{2,1,0:T(8,128)S(1)}) fusion(f32[1,272,1040]{2,1,0:T(8,128)S(1)} %get-tuple-element.54, f32[1,272,1040]{2,1,0:T(8,128)S(1)} %get-tuple-element.53, f32[1,272,1040]{2,1,0:T(8,128)S(1)} %get-tuple-element.81, f32[1,272,1040]{2,1,0:T(8,128)S(1)} %get-tuple-element.80, ...), kind=kLoop, calls=%fused_computation.6 | loop fusion | flops 10749440 | bytes 15841280 | tf_op jit(solution)/shard_map/jit(_where)/select_n | solution.py:143
  54.2 1.7 %multiply_reduce_fusion.4 = (f32[]{:T(128)}, f32[]{:T(128)}) fusion(f32[2,272,1040]{2,1,0:T(8,128)S(1)} %get-tuple-element.73, f32[2,272,1040]{2,1,0:T(8,128)S(1)} %fusion.5), kind=kLoop, calls=%fused_computation.37 | loop fusion | flops 2097150 | bytes 4194312 | tf_op jit(solution)/shard_map/reduce_sum | solution.py:131
  57.9 25.8 %shard_map.76 = f32[8,128]{1,0:T(8,128)} custom-call(f32[8,128]{1,0:T(8,128)} %scatter.10.local_ref), custom_call_target="tpu_custom_call" | custom-call | tf_op jit(solution)/shard_map/pallas_call | solution.py:109
  86.4 3.6 %multiply_subtract_fusion.1 = f32[2,272,1040]{2,1,0:T(8,128)S(1)} fusion(f32[2,272,1040]{2,1,0:T(8,128)S(1)} %get-tuple-element.73, f32[]{:T(128)S(6)} %div.23, f32[1,272,1040]{2,1,0:T(8,128)} %copy-done.15, f32[1,272,1040]{2,1,0:T(8,128)} %copy-done.14, f32[1,272,1040]{2,1,0:T(8,128)} %copy-done.10, f32[1,272,1040]{2,1,0:T(8,128)} %copy-done.8, ...), kind=kLoop, calls=%fused_computation.21 | loop fusion | flops 7354880 | bytes 11315204 | tf_op jit(solution)/shard_map/sub | solution.py:155
  96.2 2.4 %multiply_reduce_fusion.2 = (f32[]{:T(128)}, f32[]{:T(128)}, f32[]{:T(128)}) fusion(f32[2,272,1040]{2,1,0:T(8,128)S(1)} %multiply_subtract_fusion.1, f32[2,272,1040]{2,1,0:T(8,128)S(1)} %fusion.6, f32[2,272,1040]{2,1,0:T(8,128)S(1)} %copy-done.19), kind=kLoop, calls=%fused_computation.35 | loop fusion | flops 3145725 | bytes 6291468 | tf_op jit(solution)/shard_map/reduce_sum | solution.py:131
  98.6 2.0 %maximum_bitcast_fusion.1 = f32[1,3]{1,0:T(1,128)S(1)} fusion(f32[1]{0:T(128)} %bitcast.39, f32[1]{0:T(128)} %bitcast.38, f32[1]{0:T(128)} %bitcast.32), kind=kLoop, calls=%fused_computation.94 | loop fusion | flops 6 | bytes 24 | tf_op jit(solution)/shard_map/reshape.101
  101.2 17.6 %shard_map.77 = f32[8,128]{1,0:T(8,128)} custom-call(f32[8,128]{1,0:T(8,128)} %scatter.11.local_ref), custom_call_target="tpu_custom_call" | custom-call | tf_op jit(solution)/shard_map/pallas_call | solution.py:109
  124.0 5.3 %multiply_subtract_fusion = (f32[2,272,1040]{2,1,0:T(8,128)S(1)}, f32[2,272,1040]{2,1,0:T(8,128)S(1)}) fusion(f32[2,272,1040]{2,1,0:T(8,128)} %copy-done, f32[]{:T(128)S(6)} %div.25, f32[]{:T(128)S(6)} %div.24, f32[1,272,1040]{2,1,0:T(8,128)} %copy-done.21, f32[1,272,1040]{2,1,0:T(8,128)} %copy-done.20, f32[1,272,1040]{2,1,0:T(8,128)} %copy-done.10, ...), kind=kLoop, calls=%fused_computation.19 | loop fusion | flops 10749440 | bytes 18104328 | tf_op jit(solution)/shard_map/sub | solution.py:155
  132.8 3.7 %multiply_reduce_fusion = (f32[]{:T(128)}, f32[]{:T(128)}, f32[]{:T(128)}) fusion(f32[2,272,1040]{2,1,0:T(8,128)S(1)} %get-tuple-element.50, f32[2,272,1040]{2,1,0:T(8,128)S(1)} %get-tuple-element.51, f32[1,272,1040]{2,1,0:T(8,128)S(1)} %get-tuple-element.75, f32[1,272,1040]{2,1,0:T(8,128)S(1)} %get-tuple-element.74, f32[2,272,1040]{2,1,0:T(8,128)S(1)} %copy-done.24, ...), kind=kLoop, calls=%fused_computation.33 | loop fusion | flops 5767165 | bytes 10817548 | tf_op jit(solution)/shard_map/reduce_sum | solution.py:131
  136.6 2.0 %maximum_bitcast_fusion.2 = f32[1,3]{1,0:T(1,128)S(1)} fusion(f32[1]{0:T(128)} %bitcast.51, f32[1]{0:T(128)} %bitcast.50, f32[1]{0:T(128)} %bitcast.44), kind=kLoop, calls=%fused_computation.95 | loop fusion | flops 6 | bytes 24 | tf_op jit(solution)/shard_map/reshape.102
  139.2 17.6 %shard_map.78 = f32[8,128]{1,0:T(8,128)} custom-call(f32[8,128]{1,0:T(8,128)} %scatter.14.local_ref), custom_call_target="tpu_custom_call" | custom-call | tf_op jit(solution)/shard_map/pallas_call | solution.py:109
  161.4 6.1 %multiply_add_fusion = f32[2,272,1040]{2,1,0:T(8,128)S(1)} fusion(f32[2,272,1040]{2,1,0:T(8,128)} %copy-done, f32[2,272,1040]{2,1,0:T(8,128)S(1)} %get-tuple-element.73, f32[]{:T(128)S(6)} %div.26, f32[]{:T(128)S(6)} %div.27, f32[]{:T(128)S(6)} %div.24, f32[]{:T(128)S(6)} %div.25, f32[]{:T(128)S(6)} %div.23, f32[2,272,1040]{2,1,0:T(8,128)} %copy-done.13, ...), kind=kLoop, calls=%fused_computation.18 | loop fusion | flops 10749440 | bytes 18104340 | tf_op jit(solution)/shard_map/add | solution.py:152
  167.6 1.9 %slice_bitcast_fusion.21 = (f32[256,1024]{1,0:T(8,128)}, f32[256,1024]{1,0:T(8,128)}) fusion(f32[2,272,1040]{2,1,0:T(8,128)S(1)} %multiply_add_fusion), kind=kLoop, calls=%fused_computation.81 | loop fusion | bytes 4194304 | tf_op jit(solution)/shard_map/squeeze | solution.py:165
  170.8 2.4 %slice_subtract_fusion.1 = f32[256,1024]{1,0:T(8,128)} fusion(f32[272,1040]{1,0:T(8,128)S(1)} %copy-done.23, f32[271,1040]{1,0:T(8,128)S(1)} %slice_bitcast_fusion, f32[272,1040]{1,0:T(8,128)S(1)} %get-tuple-element.71, f32[272,1039]{1,0:T(8,128)S(1)} %bitcast.147, f32[272,1040]{1,0:T(8,128)S(1)} %get-tuple-element.70), kind=kLoop, calls=%fused_computation.83 | loop fusion | flops 1310720 | bytes 6452096 | tf_op jit(solution)/shard_map/sub | solution.py:163
  (113 shorter events, 33.7 us)
Async XLA Ops:
  0.6 1.8 %copy-start.27 = (s32[256,1024]{1,0:T(8,128)S(1)}, s32[256,1024]{1,0:T(8,128)}, u32[]{:S(2)}) copy-start(s32[256,1024]{1,0:T(8,128)} %param.13) | copy-start | bytes 3145732
  3.9 7.2 %collective-permute-start = (f32[5,8,1024]{2,1,0:T(8,128)S(1)}, f32[5,8,1024]{2,1,0:T(8,128)S(1)}, u32[]{:S(2)}, u32[]{:S(2)}) collective-permute-start(f32[5,8,1024]{2,1,0:T(8,128)S(1)} %get-tuple-element.66), channel_id=1, source_target_pairs={{0,16},{16,32},{32,48},{48,64},{64,80},{80,96},{96,112},{1,17},{17... | collective-permute-start | bytes 491528 | tf_op jit(solution)/shard_map/ppermute | solution.py:25
  8.8 6.6 %collective-permute-start.1 = (f32[5,8,1024]{2,1,0:T(8,128)S(1)}, f32[5,8,1024]{2,1,0:T(8,128)S(1)}, u32[]{:S(2)}, u32[]{:S(2)}) collective-permute-start(f32[5,8,1024]{2,1,0:T(8,128)S(1)} %get-tuple-element.67), channel_id=1, source_target_pairs={{16,0},{32,16},{48,32},{64,48},{80,64},{96,80},{112,96},{17,1},{33... | collective-permute-start | bytes 491528 | tf_op jit(solution)/shard_map/ppermute | solution.py:25
  16.4 2.5 %copy-start.12 = (f32[5,272,1024]{2,1,0:T(8,128)}, f32[5,272,1024]{2,1,0:T(8,128)S(1)}, u32[]{:S(2)}) copy-start(f32[5,272,1024]{2,1,0:T(8,128)S(1)} %pad_maximum_fusion) | copy-start | bytes 16711684
  19.4 5.6 %collective-permute-start.3 = (f32[5,272,8]{1,2,0:T(8,128)S(1)}, f32[5,272,8]{1,2,0:T(8,128)S(1)}, u32[]{:S(2)}, u32[]{:S(2)}) collective-permute-start(f32[5,272,8]{1,2,0:T(8,128)S(1)} %copy.17), channel_id=1, source_target_pairs={{1,0},{2,1},{3,2},{4,3},{5,4},{6,5},{7,6},{8,7},{9,8},{10,9},{11,1... | collective-permute-start | bytes 130568 | tf_op jit(solution)/shard_map/ppermute | solution.py:25
  21.0 5.3 %collective-permute-start.2 = (f32[5,272,8]{1,2,0:T(8,128)S(1)}, f32[5,272,8]{1,2,0:T(8,128)S(1)}, u32[]{:S(2)}, u32[]{:S(2)}) collective-permute-start(f32[5,272,8]{1,2,0:T(8,128)S(1)} %copy.16), channel_id=1, source_target_pairs={{0,1},{1,2},{2,3},{3,4},{4,5},{5,6},{6,7},{7,8},{8,9},{9,10},{10,1... | collective-permute-start | bytes 130568 | tf_op jit(solution)/shard_map/ppermute | solution.py:25
  34.9 4.4 %copy-start.7 = (f32[5,272,1040]{2,1,0:T(8,128)S(1)}, f32[5,272,1040]{2,1,0:T(8,128)}, u32[]{:S(2)}) copy-start(f32[5,272,1040]{2,1,0:T(8,128)} %concatenate.13) | copy-start | bytes 16972804
  39.5 2.9 %copy-start.22 = (f32[272,1040]{1,0:T(8,128)}, f32[272,1040]{1,0:T(8,128)S(1)}, u32[]{:S(2)}) copy-start(f32[272,1040]{1,0:T(8,128)S(1)} %get-tuple-element.60) | copy-start | bytes 3394564
  46.7 2.2 %copy-start.16 = (f32[1,272,1040]{2,1,0:T(8,128)}, f32[1,272,1040]{2,1,0:T(8,128)S(1)}, u32[]{:S(2)}) copy-start(f32[1,272,1040]{2,1,0:T(8,128)S(1)} %get-tuple-element.56) | copy-start | bytes 3394564
  46.7 2.2 %copy-start.17 = (f32[1,272,1040]{2,1,0:T(8,128)}, f32[1,272,1040]{2,1,0:T(8,128)S(1)}, u32[]{:S(2)}) copy-start(f32[1,272,1040]{2,1,0:T(8,128)S(1)} %get-tuple-element.57) | copy-start | bytes 3394564
  46.7 6.1 %copy-start.1 = (f32[1,272,1040]{2,1,0:T(8,128)}, f32[1,272,1040]{2,1,0:T(8,128)S(1)}, u32[]{:S(2)}) copy-start(f32[1,272,1040]{2,1,0:T(8,128)S(1)} %get-tuple-element.52) | copy-start | bytes 3394564
  46.7 6.1 %copy-start.4 = (f32[1,272,1040]{2,1,0:T(8,128)}, f32[1,272,1040]{2,1,0:T(8,128)S(1)}, u32[]{:S(2)}) copy-start(f32[1,272,1040]{2,1,0:T(8,128)S(1)} %get-tuple-element.55) | copy-start | bytes 3394564
  46.7 6.1 %copy-start.8 = (f32[1,272,1040]{2,1,0:T(8,128)}, f32[1,272,1040]{2,1,0:T(8,128)S(1)}, u32[]{:S(2)}) copy-start(f32[1,272,1040]{2,1,0:T(8,128)S(1)} %get-tuple-element.53) | copy-start | bytes 3394564
  46.7 6.1 %copy-start.10 = (f32[1,272,1040]{2,1,0:T(8,128)}, f32[1,272,1040]{2,1,0:T(8,128)S(1)}, u32[]{:S(2)}) copy-start(f32[1,272,1040]{2,1,0:T(8,128)S(1)} %get-tuple-element.54) | copy-start | bytes 3394564
  54.2 1.8 %copy-start.18 = (f32[2,272,1040]{2,1,0:T(8,128)}, f32[2,272,1040]{2,1,0:T(8,128)S(1)}, u32[]{:S(2)}) copy-start(f32[2,272,1040]{2,1,0:T(8,128)S(1)} %fusion.5) | copy-start | bytes 6789124
  90.1 5.3 %copy-start = (f32[2,272,1040]{2,1,0:T(8,128)}, f32[2,272,1040]{2,1,0:T(8,128)S(1)}, u32[]{:S(2)}) copy-start(f32[2,272,1040]{2,1,0:T(8,128)S(1)} %multiply_subtract_fusion.1) | copy-start | bytes 6789124
  91.2 2.6 %copy-start.5 = (f32[1,272,1040]{2,1,0:T(8,128)S(1)}, f32[1,272,1040]{2,1,0:T(8,128)}, u32[]{:S(2)}) copy-start(f32[1,272,1040]{2,1,0:T(8,128)} %copy-done.4) | copy-start | bytes 3394564
  91.2 2.9 %copy-start.9 = (f32[1,272,1040]{2,1,0:T(8,128)S(1)}, f32[1,272,1040]{2,1,0:T(8,128)}, u32[]{:S(2)}) copy-start(f32[1,272,1040]{2,1,0:T(8,128)} %copy-done.8) | copy-start | bytes 3394564
  91.2 3.3 %copy-start.11 = (f32[1,272,1040]{2,1,0:T(8,128)S(1)}, f32[1,272,1040]{2,1,0:T(8,128)}, u32[]{:S(2)}) copy-start(f32[1,272,1040]{2,1,0:T(8,128)} %copy-done.10) | copy-start | bytes 3394564
  91.5 3.8 %copy-start.20 = (f32[1,272,1040]{2,1,0:T(8,128)}, f32[1,272,1040]{2,1,0:T(8,128)S(1)}, u32[]{:S(2)}) copy-start(f32[1,272,1040]{2,1,0:T(8,128)S(1)} %get-tuple-element.76) | copy-start | bytes 3394564
  91.5 3.8 %copy-start.21 = (f32[1,272,1040]{2,1,0:T(8,128)}, f32[1,272,1040]{2,1,0:T(8,128)S(1)}, u32[]{:S(2)}) copy-start(f32[1,272,1040]{2,1,0:T(8,128)S(1)} %get-tuple-element.77) | copy-start | bytes 3394564
  94.5 1.7 copy-start.19
  130.4 1.7 copy-start.6
  130.4 2.5 %copy-start.24 = (f32[2,272,1040]{2,1,0:T(8,128)S(1)}, f32[2,272,1040]{2,1,0:T(8,128)}, u32[]{:S(2)}) copy-start(f32[2,272,1040]{2,1,0:T(8,128)} %get-tuple-element.72) | copy-start | bytes 6789124
  (10 other events, 13.6 us)

commit v8 on v5

--- a/solution.py
+++ b/solution.py
@@ -65,7 +65,7 @@
     return tuple((axis, 1, sizes[axis]) for axis in ("lon", "lat") if sizes[axis] > 1)
 
 
-def reduce_kernel(stages, local_ref, out_ref, parts, got, send_sem, recv_sem):
+def reduce_kernel(stages, local_ref, prev_ref, out_ref, parts, got, send_sem, recv_sem):
     me = {"lat": lax.axis_index("lat"), "lon": lax.axis_index("lon")}
 
     def partner(axis, stride, members, offset):
@@ -106,18 +106,28 @@
         while len(ordered) > 1:
             ordered = [ordered[k] + ordered[k + 1] for k in range(0, len(ordered), 2)]
         value = ordered[0]
-    out_ref[...] = value
+    norm, r_ar, r_ap = value[0:1], value[1:2], value[2:3]
+    beta = norm / prev_ref[2:3]
+    curve = r_ar + 2.0 * beta * r_ap + beta * beta * prev_ref[3:4]
+    out_ref[...] = jnp.zeros_like(value)
+    out_ref[0:1] = norm / curve
+    out_ref[1:2] = beta
+    out_ref[2:3] = norm
+    out_ref[3:4] = curve
 
 
-def all_sum(local):
+def cg_scalars(local, previous):
     sizes = {"lat": lax.axis_size("lat"), "lon": lax.axis_size("lon")}
     stages = stages_of(sizes)
     widest = max(members for _, _, members in stages)
-    tile = jnp.zeros((8, 128), jnp.float32).at[0, : local.shape[0]].set(local)
-    summed = pl.pallas_call(
+    rows = lax.broadcasted_iota(jnp.int32, (8, 128), 0)
+    tile = jnp.zeros((8, 128), jnp.float32)
+    for k in range(local.shape[0]):
+        tile = jnp.where(rows == k, local[k], tile)
+    return pl.pallas_call(
         functools.partial(reduce_kernel, stages),
         out_shape=jax.ShapeDtypeStruct((8, 128), jnp.float32),
-        in_specs=[pl.BlockSpec(memory_space=pltpu.VMEM)],
+        in_specs=[pl.BlockSpec(memory_space=pltpu.VMEM)] * 2,
         out_specs=pl.BlockSpec(memory_space=pltpu.VMEM),
         scratch_shapes=[
             pltpu.VMEM((len(stages), 8, 128), jnp.float32),
@@ -126,8 +136,7 @@
             pltpu.SemaphoreType.DMA((len(stages), widest)),
         ],
         compiler_params=pltpu.CompilerParams(collective_id=0, has_side_effects=True),
-    )(tile)
-    return summed[0, : local.shape[0]]
+    )(tile, previous)
 
 
 def interior(field):
@@ -135,9 +144,8 @@
     return field[..., rows:-rows, cols:-cols]
 
 
-def sums(*pairs):
-    local = jnp.stack([jnp.sum(interior(x) * interior(y)) for x, y in pairs])
-    return all_sum(local)
+def dots(*pairs):
+    return jnp.stack([jnp.sum(interior(x) * interior(y)) for x, y in pairs])
 
 
 def per_device(surface, bathymetry, land_sea, flux_lon, flux_lat):
@@ -153,21 +161,21 @@
     solution = start
     residual = right_side - operate(start, wet, inverse)
     applied = operate(residual, wet, inverse)
-    norm_now, curve = sums((residual, residual), (residual, applied))
+    rows = lax.broadcasted_iota(jnp.int32, (8, 128), 0)
+    previous = jnp.where(rows == 2, jnp.inf, 0.0).astype(jnp.float32)
+    stats = cg_scalars(dots((residual, residual), (residual, applied)), previous)
     direction, image = residual, applied
     for step in range(ITERS):
-        alpha = norm_now / curve
+        alpha = stats[0, 0]
         solution = solution + alpha * direction
         if step == ITERS - 1:
             break
         residual = residual - alpha * image
         applied = operate(residual, wet, inverse)
-        norm_next, r_ar, r_ap = sums((residual, residual), (residual, applied), (residual, image))
-        beta = norm_next / norm_now
-        curve = r_ar + 2.0 * beta * r_ap + beta * beta * curve
+        stats = cg_scalars(dots((residual, residual), (residual, applied), (residual, image)), stats)
+        beta = stats[1, 0]
         direction = residual + beta * direction
         image = applied + beta * image
-        norm_now = norm_next
     surface_next = interior(surface_x - continuity * divergence(solution))
     solution = interior(solution)
     return (surface_next, solution[0], solution[1])

time: 160 us -> 156 us (0.975)
  between operations: 9.48 us -> 1.25 us
  other arithmetic: 42.2 us -> 49.1 us
  Pallas kernels: 46.9 us -> 44.2 us
  waiting for transfers between devices: 5.72 us -> 8.35 us
    select_n x0 -> x7, other arithmetic: none -> 7.13 us  [the longest x6 7.13 us: cg_scalars(): tile = jnp.where(rows == k, local[k], tile)]
    another operation x3 -> x0, other arithmetic: 5.33 us -> none
    another operation x3 -> x0, local copies, waits for them, and re-layouts: 4.15 us -> none  [the longest x2 2.81 us: per_device(): norm_next, r_ar, r_ap = sums((residual, residual), (residual, applied), (...]
    slice x0 -> x3, local copies, waits for them, and re-layouts: none -> 3.82 us  [the longest x2 2.49 us: per_device(): alpha = stats[0, 0]]
    add x1, other arithmetic: 6.06 us -> 9.23 us  [per_device(): solution = solution + alpha * direction]
    pallas_call x3, Pallas kernels: 46.9 us -> 44.2 us  [cg_scalars(): pl.pallas_call(functools.partial(reduce_kernel, stages), out_shape=jax.Sh...]
    ppermute x4, waiting for transfers between devices: 5.72 us -> 8.35 us  [from_behind(): lax.ppermute(value, axis, [(source, source + steps) for source in range(l...]
    sub x2, other arithmetic: 9.06 us -> 11 us  [per_device(): residual = residual - alpha * image]
where the time goes in v8:
time: 156 us
  other arithmetic  49.1 us (31%)
  Pallas kernels  44.2 us (28%)
  local copies, waits for them, and re-layouts  41.4 us (27%)
  starting transfers between devices  11.4 us (7%)
  waiting for transfers between devices  8.35 us (5%)
    pallas_call x3, Pallas kernels, cg_scalars(): pl.pallas_call(functools.partial(reduce_kernel, stages), out_shape=jax.Sh...  44.2 us
    unnamed x63, local copies, waits for them, and re-layouts  14.3 us
    ppermute x4, starting transfers between devices, from_behind(): lax.ppermute(value, axis, [(source, source + steps) for source in range(l...  11.4 us
    sub x2, other arithmetic, per_device(): residual = residual - alpha * image  11 us
    add x1, other arithmetic, per_device(): solution = solution + alpha * direction  9.23 us
    concatenate x1, local copies, waits for them, and re-layouts, grow(): return jnp.concatenate([left, stacked, right], axis=2)  8.37 us
    ppermute x4, waiting for transfers between devices, from_behind(): lax.ppermute(value, axis, [(source, source + steps) for source in range(l...  8.35 us
    reduce_sum x3, other arithmetic, dots(): return jnp.stack([jnp.sum(interior(x) * interior(y)) for x, y in pairs])  7.88 us
  transfers between devices with their start and end apart: 4, of which 3 were waited for; matrix products, arithmetic and copies ran while one was open for 0% of the time, Pallas kernels for 0%

profile of v8, /device:TPU:1, one launch (start us, length us, event | category | flops | bytes accessed | tf_op | source)
XLA Modules:
  0.0 155.7 jit_solution(8852891226974344258)
XLA Ops:
  3.9 4.9 %collective-permute-start = (f32[5,8,1024]{2,1,0:T(8,128)S(1)}, f32[5,8,1024]{2,1,0:T(8,128)S(1)}, u32[]{:S(2)}, u32[]{:S(2)}) collective-permute-start(f32[5,8,1024]{2,1,0:T(8,128)S(1)} %get-tuple-element.30), channel_id=1, source_target_pairs={{0,16},{16,32},{32,48},{48,64},{64,80},{80,96},{96,112},{1,17},{17... | collective-permute-start | bytes 491528 | tf_op jit(solution)/shard_map/ppermute | solution.py:25
  8.8 1.9 %collective-permute-start.1 = (f32[5,8,1024]{2,1,0:T(8,128)S(1)}, f32[5,8,1024]{2,1,0:T(8,128)S(1)}, u32[]{:S(2)}, u32[]{:S(2)}) collective-permute-start(f32[5,8,1024]{2,1,0:T(8,128)S(1)} %get-tuple-element.31), channel_id=1, source_target_pairs={{16,0},{32,16},{48,32},{64,48},{80,64},{96,80},{112,96},{17,1},{33... | collective-permute-start | bytes 491528 | tf_op jit(solution)/shard_map/ppermute | solution.py:25
  11.1 4.4 %collective-permute-done.1 = f32[5,8,1024]{2,1,0:T(8,128)S(1)} collective-permute-done((f32[5,8,1024]{2,1,0:T(8,128)S(1)}, f32[5,8,1024]{2,1,0:T(8,128)S(1)}, u32[]{:S(2)}, u32[]{:S(2)}) %collective-permute-start.1) | collective-permute-done | bytes 163872 | tf_op jit(solution)/shard_map/ppermute | solution.py:25
  16.4 2.4 %copy-done.12 = f32[5,272,1024]{2,1,0:T(8,128)} copy-done((f32[5,272,1024]{2,1,0:T(8,128)}, f32[5,272,1024]{2,1,0:T(8,128)S(1)}, u32[]{:S(2)}) %copy-start.12) | copy-done | bytes 5570584
  19.6 3.2 %collective-permute-start.2 = (f32[5,272,8]{1,2,0:T(8,128)S(1)}, f32[5,272,8]{1,2,0:T(8,128)S(1)}, u32[]{:S(2)}, u32[]{:S(2)}) collective-permute-start(f32[5,272,8]{1,2,0:T(8,128)S(1)} %copy.16), channel_id=1, source_target_pairs={{0,1},{1,2},{2,3},{3,4},{4,5},{5,6},{6,7},{7,8},{8,9},{9,10},{10,1... | collective-permute-start | bytes 130568 | tf_op jit(solution)/shard_map/ppermute | solution.py:25
  24.2 3.7 %collective-permute-done.3 = f32[5,272,8]{1,2,0:T(8,128)S(1)} collective-permute-done((f32[5,272,8]{1,2,0:T(8,128)S(1)}, f32[5,272,8]{1,2,0:T(8,128)S(1)}, u32[]{:S(2)}, u32[]{:S(2)}) %collective-permute-start.3) | collective-permute-done | bytes 43552 | tf_op jit(solution)/shard_map/ppermute | solution.py:25
  28.3 8.4 %concatenate.7 = f32[5,272,1040]{2,1,0:T(8,128)} concatenate(f32[5,272,8]{2,1,0:T(8,128)S(1)} %copy.18, f32[5,272,1024]{2,1,0:T(8,128)} %copy-done.12, f32[5,272,8]{2,1,0:T(8,128)S(1)} %copy.19), dimensions={2} | concatenate | bytes 11315200 | tf_op jit(solution)/shard_map/concatenate | solution.py:35
  36.7 3.5 %slice_bitcast_fusion.18 = (f32[271,1040]{1,0:T(8,128)S(1)}, f32[271,1040]{1,0:T(8,128)S(1)}, f32[271,1040]{1,0:T(8,128)}) fusion(f32[5,272,1040]{2,1,0:T(8,128)} %concatenate.7), kind=kLoop, calls=%fused_computation.64 | loop fusion | bytes 6764160 | tf_op jit(solution)/shard_map/slice | solution.py:43
  41.3 1.5 slice.296
  45.7 2.8 %multiply_bitcast_fusion.3 = (f32[1,272,1040]{2,1,0:T(8,128)S(1)}, f32[1,272,1040]{2,1,0:T(8,128)S(1)}, f32[1,272,1040]{2,1,0:T(8,128)S(1)}, f32[1,272,1040]{2,1...) fusion(f32[272,1039]{1,0:T(8,128)} %slice.296, f32[5,272,1040]{2,1,0:T(8,128)S(1)} %copy-done.7, ...), kind=kLoop, calls=%fused_computation.80 | loop fusion | flops 2263040 | bytes 16957056 | tf_op jit(solution)/shard_map/stack | solution.py:155
  50.8 2.5 %fusion.1 = (f32[2,272,1040]{2,1,0:T(8,128)}, f32[2,272,1040]{2,1,0:T(8,128)S(1)}) fusion(f32[1,272,1040]{2,1,0:T(8,128)S(1)} %get-tuple-element.18, f32[1,272,1040]{2,1,0:T(8,128)S(1)} %get-tuple-element.17, f32[1,272,1040]{2,1,0:T(8,128)S(1)} %get-tuple-element.45, f32[1,272,1040]{2,1,0:T(8,128)S(1)} %get-tuple-element.44, ...), kind=kLoop, calls=%fused_computation.6 | loop fusion | flops 10749440 | bytes 15841280 | tf_op jit(solution)/shard_map/jit(_where)/select_n | solution.py:159
  56.1 1.7 %multiply_reduce_fusion.4 = (f32[]{:T(128)}, f32[]{:T(128)}) fusion(f32[2,272,1040]{2,1,0:T(8,128)S(1)} %fusion.5, f32[2,272,1040]{2,1,0:T(8,128)S(1)} %get-tuple-element.37), kind=kLoop, calls=%fused_computation.37 | loop fusion | flops 2097150 | bytes 4194312 | tf_op jit(solution)/shard_map/reduce_sum | solution.py:148
  60.5 17.8 %shard_map.76.prev_ref = f32[8,128]{1,0:T(8,128)} custom-call(f32[8,128]{1,0:T(8,128)} %broadcast_select_fusion.local_ref, f32[8,128]{1,0:T(8,128)} %iota.49.prev_ref), custom_call_target="tpu_custom_call" | custom-call | tf_op jit(solution)/shard_map/pallas_call | solution.py:127
  79.5 4.4 %multiply_subtract_fusion.1 = f32[2,272,1040]{2,1,0:T(8,128)S(1)} fusion(f32[2,272,1040]{2,1,0:T(8,128)S(1)} %get-tuple-element.37, f32[]{:T(128)} %bitcast.27, f32[1,272,1040]{2,1,0:T(8,128)} %copy-done.15, f32[1,272,1040]{2,1,0:T(8,128)} %copy-done.14, f32[1,272,1040]{2,1,0:T(8,128)} %copy-done.10, f32[1,272,1040]{2,1,0:T(8,128)} %copy-done.8, ...), kind=kLoop, calls=%fused_computation.21 | loop fusion | flops 7354880 | bytes 11315204 | tf_op jit(solution)/shard_map/sub | solution.py:173
  90.1 2.3 %multiply_reduce_fusion.2 = (f32[]{:T(128)}, f32[]{:T(128)}, f32[]{:T(128)}) fusion(f32[2,272,1040]{2,1,0:T(8,128)S(1)} %copy-done.19, f32[2,272,1040]{2,1,0:T(8,128)S(1)} %multiply_subtract_fusion.1, f32[2,272,1040]{2,1,0:T(8,128)S(1)} %fusion.6), kind=kLoop, calls=%fused_computation.35 | loop fusion | flops 3145725 | bytes 6291468 | tf_op jit(solution)/shard_map/reduce_sum | solution.py:148
  93.1 1.9 %select_select_fusion.1.local_ref = f32[8,128]{1,0:T(8,128)} fusion(f32[8]{0:T(128)S(1)} %fusion.24, f32[]{:T(128)} %get-tuple-element.10, f32[]{:T(128)} %get-tuple-element.9, pred[8]{0:T(512)(128)(4,1)S(1)} %get-tuple-element.50, pred[8]{0:T(512)(128)(4,1)S(1)} %get-tuple-element.51), kind=kLoop, calls=%fused_computation.94 | loop fusion | flops 2048 | bytes 4152 | tf_op jit(solution)/shard_map/jit(_where)/select_n | solution.py:126
  95.0 13.0 %shard_map.77.prev_ref = f32[8,128]{1,0:T(8,128)} custom-call(f32[8,128]{1,0:T(8,128)} %select_select_fusion.1.local_ref, f32[8,128]{1,0:T(8,128)} %shard_map.76.prev_ref), custom_call_target="tpu_custom_call" | custom-call | tf_op jit(solution)/shard_map/pallas_call | solution.py:127
  109.3 6.6 %multiply_subtract_fusion = (f32[2,272,1040]{2,1,0:T(8,128)S(1)}, f32[2,272,1040]{2,1,0:T(8,128)S(1)}) fusion(f32[2,272,1040]{2,1,0:T(8,128)} %copy-done, f32[]{:T(128)} %bitcast.33, f32[]{:T(128)} %bitcast.34, f32[1,272,1040]{2,1,0:T(8,128)} %copy-done.21, f32[1,272,1040]{2,1,0:T(8,128)} %copy-done.20, f32[1,272,1040]{2,1,0:T(8,128)} %copy-done.10, ...), kind=kLoop, calls=%fused_computation.19 | loop fusion | flops 10749440 | bytes 18104328 | tf_op jit(solution)/shard_map/sub | solution.py:173
  119.5 3.8 %fusion.12 = (f32[]{:T(128)}, f32[]{:T(128)}, f32[]{:T(128)}) fusion(f32[2,272,1040]{2,1,0:T(8,128)S(1)} %get-tuple-element.15, f32[2,272,1040]{2,1,0:T(8,128)S(1)} %get-tuple-element.14, f32[1,272,1040]{2,1,0:T(8,128)S(1)} %get-tuple-element.39, f32[1,272,1040]{2,1,0:T(8,128)S(1)} %get-tuple-element.38, f32[2,272,1040]{2,1,0:T(8,128)S(1)} %copy-done.24, ...), kind=kLoop, calls=%fused_computation.30 | loop fusion | flops 5767165 | bytes 10817548 | tf_op jit(solution)/shard_map/reduce_sum | solution.py:148
  124.0 2.0 %select_select_fusion.local_ref = f32[8,128]{1,0:T(8,128)} fusion(f32[8]{0:T(128)S(1)} %fusion.23, f32[]{:T(128)} %get-tuple-element.8, f32[]{:T(128)} %get-tuple-element.6, pred[8]{0:T(512)(128)(4,1)S(1)} %get-tuple-element.50, pred[8]{0:T(512)(128)(4,1)S(1)} %get-tuple-element.51), kind=kLoop, calls=%fused_computation.93 | loop fusion | flops 2048 | bytes 4152 | tf_op jit(solution)/shard_map/jit(_where)/select_n | solution.py:126
  125.9 13.5 %shard_map.78 = f32[8,128]{1,0:T(8,128)} custom-call(f32[8,128]{1,0:T(8,128)} %select_select_fusion.local_ref, f32[8,128]{1,0:T(8,128)} %shard_map.77.prev_ref), custom_call_target="tpu_custom_call" | custom-call | tf_op jit(solution)/shard_map/pallas_call | solution.py:127
  140.7 9.2 %multiply_add_fusion = f32[2,272,1040]{2,1,0:T(8,128)S(1)} fusion(f32[2,272,1040]{2,1,0:T(8,128)} %copy-done, f32[2,272,1040]{2,1,0:T(8,128)S(1)} %get-tuple-element.37, f32[]{:T(128)} %bitcast.41, f32[]{:T(128)} %bitcast.40, f32[]{:T(128)} %bitcast.34, f32[]{:T(128)} %bitcast.33, f32[]{:T(128)} %bitcast.27, f32[2,272,1040]{2,1,0:T(8,128)} %copy-done.13, ...), kind=kLoop, calls=%fused_computation.18 | loop fusion | flops 10749440 | bytes 18104340 | tf_op jit(solution)/shard_map/add | solution.py:170
  150.1 1.9 %slice_bitcast_fusion.21 = (f32[256,1024]{1,0:T(8,128)}, f32[256,1024]{1,0:T(8,128)}) fusion(f32[2,272,1040]{2,1,0:T(8,128)S(1)} %multiply_add_fusion), kind=kLoop, calls=%fused_computation.81 | loop fusion | bytes 4194304 | tf_op jit(solution)/shard_map/squeeze | solution.py:181
  153.3 2.4 %slice_subtract_fusion.1 = f32[256,1024]{1,0:T(8,128)} fusion(f32[272,1040]{1,0:T(8,128)S(1)} %copy-done.23, f32[271,1040]{1,0:T(8,128)S(1)} %slice_bitcast_fusion, f32[272,1040]{1,0:T(8,128)S(1)} %get-tuple-element.35, f32[272,1039]{1,0:T(8,128)S(1)} %bitcast.130, f32[272,1040]{1,0:T(8,128)S(1)} %get-tuple-element.34), kind=kLoop, calls=%fused_computation.83 | loop fusion | flops 1310720 | bytes 6452096 | tf_op jit(solution)/shard_map/sub | solution.py:179
  (116 shorter events, 34.7 us)
Async XLA Ops:
  0.6 1.8 %copy-start.27 = (s32[256,1024]{1,0:T(8,128)S(1)}, s32[256,1024]{1,0:T(8,128)}, u32[]{:S(2)}) copy-start(s32[256,1024]{1,0:T(8,128)} %param.7) | copy-start | bytes 3145732
  3.9 7.2 %collective-permute-start = (f32[5,8,1024]{2,1,0:T(8,128)S(1)}, f32[5,8,1024]{2,1,0:T(8,128)S(1)}, u32[]{:S(2)}, u32[]{:S(2)}) collective-permute-start(f32[5,8,1024]{2,1,0:T(8,128)S(1)} %get-tuple-element.30), channel_id=1, source_target_pairs={{0,16},{16,32},{32,48},{48,64},{64,80},{80,96},{96,112},{1,17},{17... | collective-permute-start | bytes 491528 | tf_op jit(solution)/shard_map/ppermute | solution.py:25
  8.8 6.6 %collective-permute-start.1 = (f32[5,8,1024]{2,1,0:T(8,128)S(1)}, f32[5,8,1024]{2,1,0:T(8,128)S(1)}, u32[]{:S(2)}, u32[]{:S(2)}) collective-permute-start(f32[5,8,1024]{2,1,0:T(8,128)S(1)} %get-tuple-element.31), channel_id=1, source_target_pairs={{16,0},{32,16},{48,32},{64,48},{80,64},{96,80},{112,96},{17,1},{33... | collective-permute-start | bytes 491528 | tf_op jit(solution)/shard_map/ppermute | solution.py:25
  16.4 2.4 %copy-start.12 = (f32[5,272,1024]{2,1,0:T(8,128)}, f32[5,272,1024]{2,1,0:T(8,128)S(1)}, u32[]{:S(2)}) copy-start(f32[5,272,1024]{2,1,0:T(8,128)S(1)} %pad_maximum_fusion) | copy-start | bytes 16711684
  19.6 8.4 %collective-permute-start.2 = (f32[5,272,8]{1,2,0:T(8,128)S(1)}, f32[5,272,8]{1,2,0:T(8,128)S(1)}, u32[]{:S(2)}, u32[]{:S(2)}) collective-permute-start(f32[5,272,8]{1,2,0:T(8,128)S(1)} %copy.16), channel_id=1, source_target_pairs={{0,1},{1,2},{2,3},{3,4},{4,5},{5,6},{6,7},{7,8},{8,9},{9,10},{10,1... | collective-permute-start | bytes 130568 | tf_op jit(solution)/shard_map/ppermute | solution.py:25
  22.9 5.0 %collective-permute-start.3 = (f32[5,272,8]{1,2,0:T(8,128)S(1)}, f32[5,272,8]{1,2,0:T(8,128)S(1)}, u32[]{:S(2)}, u32[]{:S(2)}) collective-permute-start(f32[5,272,8]{1,2,0:T(8,128)S(1)} %copy.17), channel_id=1, source_target_pairs={{1,0},{2,1},{3,2},{4,3},{5,4},{6,5},{7,6},{8,7},{9,8},{10,9},{11,1... | collective-permute-start | bytes 130568 | tf_op jit(solution)/shard_map/ppermute | solution.py:25
  36.7 4.4 %copy-start.7 = (f32[5,272,1040]{2,1,0:T(8,128)S(1)}, f32[5,272,1040]{2,1,0:T(8,128)}, u32[]{:S(2)}) copy-start(f32[5,272,1040]{2,1,0:T(8,128)} %concatenate.7) | copy-start | bytes 16972804
  41.3 3.0 %copy-start.22 = (f32[272,1040]{1,0:T(8,128)}, f32[272,1040]{1,0:T(8,128)S(1)}, u32[]{:S(2)}) copy-start(f32[272,1040]{1,0:T(8,128)S(1)} %get-tuple-element.24) | copy-start | bytes 3394564
  48.6 2.2 %copy-start.16 = (f32[1,272,1040]{2,1,0:T(8,128)}, f32[1,272,1040]{2,1,0:T(8,128)S(1)}, u32[]{:S(2)}) copy-start(f32[1,272,1040]{2,1,0:T(8,128)S(1)} %get-tuple-element.20) | copy-start | bytes 3394564
  48.6 2.2 %copy-start.17 = (f32[1,272,1040]{2,1,0:T(8,128)}, f32[1,272,1040]{2,1,0:T(8,128)S(1)}, u32[]{:S(2)}) copy-start(f32[1,272,1040]{2,1,0:T(8,128)S(1)} %get-tuple-element.21) | copy-start | bytes 3394564
  48.6 6.1 %copy-start.1 = (f32[1,272,1040]{2,1,0:T(8,128)}, f32[1,272,1040]{2,1,0:T(8,128)S(1)}, u32[]{:S(2)}) copy-start(f32[1,272,1040]{2,1,0:T(8,128)S(1)} %get-tuple-element.16) | copy-start | bytes 3394564
  48.6 6.1 %copy-start.4 = (f32[1,272,1040]{2,1,0:T(8,128)}, f32[1,272,1040]{2,1,0:T(8,128)S(1)}, u32[]{:S(2)}) copy-start(f32[1,272,1040]{2,1,0:T(8,128)S(1)} %get-tuple-element.19) | copy-start | bytes 3394564
  48.6 6.1 %copy-start.8 = (f32[1,272,1040]{2,1,0:T(8,128)}, f32[1,272,1040]{2,1,0:T(8,128)S(1)}, u32[]{:S(2)}) copy-start(f32[1,272,1040]{2,1,0:T(8,128)S(1)} %get-tuple-element.17) | copy-start | bytes 3394564
  48.6 6.1 %copy-start.10 = (f32[1,272,1040]{2,1,0:T(8,128)}, f32[1,272,1040]{2,1,0:T(8,128)S(1)}, u32[]{:S(2)}) copy-start(f32[1,272,1040]{2,1,0:T(8,128)S(1)} %get-tuple-element.18) | copy-start | bytes 3394564
  56.1 1.8 %copy-start.18 = (f32[2,272,1040]{2,1,0:T(8,128)}, f32[2,272,1040]{2,1,0:T(8,128)S(1)}, u32[]{:S(2)}) copy-start(f32[2,272,1040]{2,1,0:T(8,128)S(1)} %fusion.5) | copy-start | bytes 6789124
  83.9 5.3 %copy-start = (f32[2,272,1040]{2,1,0:T(8,128)}, f32[2,272,1040]{2,1,0:T(8,128)S(1)}, u32[]{:S(2)}) copy-start(f32[2,272,1040]{2,1,0:T(8,128)S(1)} %multiply_subtract_fusion.1) | copy-start | bytes 6789124
  85.1 2.6 %copy-start.5 = (f32[1,272,1040]{2,1,0:T(8,128)S(1)}, f32[1,272,1040]{2,1,0:T(8,128)}, u32[]{:S(2)}) copy-start(f32[1,272,1040]{2,1,0:T(8,128)} %copy-done.4) | copy-start | bytes 3394564
  85.1 2.9 %copy-start.9 = (f32[1,272,1040]{2,1,0:T(8,128)S(1)}, f32[1,272,1040]{2,1,0:T(8,128)}, u32[]{:S(2)}) copy-start(f32[1,272,1040]{2,1,0:T(8,128)} %copy-done.8) | copy-start | bytes 3394564
  85.1 3.3 %copy-start.11 = (f32[1,272,1040]{2,1,0:T(8,128)S(1)}, f32[1,272,1040]{2,1,0:T(8,128)}, u32[]{:S(2)}) copy-start(f32[1,272,1040]{2,1,0:T(8,128)} %copy-done.10) | copy-start | bytes 3394564
  85.4 3.8 %copy-start.20 = (f32[1,272,1040]{2,1,0:T(8,128)}, f32[1,272,1040]{2,1,0:T(8,128)S(1)}, u32[]{:S(2)}) copy-start(f32[1,272,1040]{2,1,0:T(8,128)S(1)} %get-tuple-element.40) | copy-start | bytes 3394564
  85.4 3.8 %copy-start.21 = (f32[1,272,1040]{2,1,0:T(8,128)}, f32[1,272,1040]{2,1,0:T(8,128)S(1)}, u32[]{:S(2)}) copy-start(f32[1,272,1040]{2,1,0:T(8,128)S(1)} %get-tuple-element.41) | copy-start | bytes 3394564
  88.4 1.7 %copy-start.19 = (f32[2,272,1040]{2,1,0:T(8,128)S(1)}, f32[2,272,1040]{2,1,0:T(8,128)}, u32[]{:S(2)}) copy-start(f32[2,272,1040]{2,1,0:T(8,128)} %copy-done.18) | copy-start | bytes 6789124
  117.0 1.7 %copy-start.6 = (f32[1,272,1040]{2,1,0:T(8,128)S(1)}, f32[1,272,1040]{2,1,0:T(8,128)}, u32[]{:S(2)}) copy-start(f32[1,272,1040]{2,1,0:T(8,128)} %copy-done.4) | copy-start | bytes 3394564
  117.1 2.5 %copy-start.24 = (f32[2,272,1040]{2,1,0:T(8,128)S(1)}, f32[2,272,1040]{2,1,0:T(8,128)}, u32[]{:S(2)}) copy-start(f32[2,272,1040]{2,1,0:T(8,128)} %get-tuple-element.36) | copy-start | bytes 6789124
  (10 other events, 13.8 us)

commit v9 on v8

--- a/solution.py
+++ b/solution.py
@@ -25,14 +25,35 @@
     return lax.ppermute(value, axis, [(source, source + steps) for source in range(leading, last)])
 
 
+def from_corner(value, lat_steps, lon_steps):
+    lats, lons = lax.axis_size("lat"), lax.axis_size("lon")
+    pairs = [
+        (lat * lons + lon, (lat + lat_steps) * lons + lon + lon_steps)
+        for lat in range(lats)
+        for lon in range(lons)
+        if 0 <= lat + lat_steps < lats and 0 <= lon + lon_steps < lons
+    ]
+    return lax.ppermute(value, ("lat", "lon"), pairs)
+
+
 def grow(stacked):
     rows, cols = MARGIN_ROWS, MARGIN_COLS
     above = from_behind(stacked[:, :rows, :], "lat", -1)
     below = from_behind(stacked[:, -rows:, :], "lat", 1)
-    stacked = jnp.concatenate([below, stacked, above], axis=1)
     right = from_behind(stacked[:, :, :cols], "lon", -1)
     left = from_behind(stacked[:, :, -cols:], "lon", 1)
-    return jnp.concatenate([left, stacked, right], axis=2)
+    north_east = from_corner(stacked[:, :rows, :cols], -1, -1)
+    north_west = from_corner(stacked[:, :rows, -cols:], -1, 1)
+    south_east = from_corner(stacked[:, -rows:, :cols], 1, -1)
+    south_west = from_corner(stacked[:, -rows:, -cols:], 1, 1)
+    return jnp.concatenate(
+        [
+            jnp.concatenate([south_west, below, south_east], axis=2),
+            jnp.concatenate([left, stacked, right], axis=2),
+            jnp.concatenate([north_west, above, north_east], axis=2),
+        ],
+        axis=1,
+    )
 
 
 def east(field):

time: 156 us -> 158 us (1.013)
  starting transfers between devices: 11.4 us -> 23.9 us
  waiting for transfers between devices: 8.35 us -> 0.02 us
  local copies, waits for them, and re-layouts: 41.4 us -> 34.3 us
  Pallas kernels: 44.2 us -> 46.5 us
  other arithmetic: 49.1 us -> 51.2 us
    ppermute x0 -> x4, starting transfers between devices: none -> 11.6 us  [from_corner(): return lax.ppermute(value, ('lat', 'lon'), pairs)]
    ppermute x4, waiting for transfers between devices: 8.35 us -> 0.01 us  [from_behind(): lax.ppermute(value, axis, [(source, source + steps) for source in range(l...]
    unnamed x63 -> x61, local copies, waits for them, and re-layouts: 14.3 us -> 10.9 us
    slice x5, local copies, waits for them, and re-layouts: 3.82 us -> 0.59 us  [north(): field[..., 1:, :]]
    pallas_call x3, Pallas kernels: 44.2 us -> 46.5 us  [cg_scalars(): pl.pallas_call(functools.partial(reduce_kernel, stages), out_shape=jax.Sh...]
    concatenate x1, other arithmetic: 0.93 us -> 3.1 us  [grow(): jnp.concatenate([jnp.concatenate([south_west, below, south_east], axis=2)...]
    concatenate x1 -> x3, local copies, waits for them, and re-layouts: 8.37 us -> 8.42 us  [the longest x1 8.14 us: grow(): jnp.concatenate([left, stacked, right], axis=2)]
  transfers between devices with their start and end apart: 4 -> 8, of which waited for: 3 -> 0; matrix products, arithmetic and copies ran while one was open for 0% -> 6% of each run, Pallas kernels for 0% -> 0%
where the time goes in v9:
time: 158 us; the launch traced here: 157 us
  other arithmetic  51.2 us (32%)
  Pallas kernels  46.5 us (29%)
  local copies, waits for them, and re-layouts  34.3 us (22%)
  starting transfers between devices  23.9 us (15%)
    pallas_call x3, Pallas kernels, cg_scalars(): pl.pallas_call(functools.partial(reduce_kernel, stages), out_shape=jax.Sh...  46.5 us
    ppermute x4, starting transfers between devices, from_behind(): lax.ppermute(value, axis, [(source, source + steps) for source in range(l...  12.3 us
    ppermute x4, starting transfers between devices, from_corner(): return lax.ppermute(value, ('lat', 'lon'), pairs)  11.6 us
    sub x2, other arithmetic, per_device(): residual = residual - alpha * image  11.1 us
    unnamed x61, local copies, waits for them, and re-layouts  10.9 us
    add x1, other arithmetic, per_device(): solution = solution + alpha * direction  9.38 us
    concatenate x1, local copies, waits for them, and re-layouts, grow(): jnp.concatenate([left, stacked, right], axis=2)  8.14 us
    reduce_sum x3, other arithmetic, dots(): return jnp.stack([jnp.sum(interior(x) * interior(y)) for x, y in pairs])  7.94 us
  transfers between devices with their start and end apart: 8, of which 0 were waited for; matrix products, arithmetic and copies ran while one was open for 6% of the time, Pallas kernels for 0%

profile of v9, /device:TPU:1, one launch (start us, length us, event | category | flops | bytes accessed | tf_op | source)
XLA Modules:
  0.0 157.3 jit_solution(16930871031065037668)
XLA Ops:
  5.3 4.9 %collective-permute-start.1 = (f32[5,8,1024]{2,1,0:T(8,128)S(1)}, f32[5,8,1024]{2,1,0:T(8,128)S(1)}, u32[]{:S(2)}, u32[]{:S(2)}) collective-permute-start(f32[5,8,1024]{2,1,0:T(8,128)S(1)} %get-tuple-element.32), channel_id=1, source_target_pairs={{0,16},{16,32},{32,48},{48,64},{64,80},{80,96},{96,112},{1,17},{17... | collective-permute-start | bytes 491528 | tf_op jit(solution)/shard_map/ppermute | solution.py:25
  10.2 1.9 %collective-permute-start.6 = (f32[5,8,1024]{2,1,0:T(8,128)S(1)}, f32[5,8,1024]{2,1,0:T(8,128)S(1)}, u32[]{:S(2)}, u32[]{:S(2)}) collective-permute-start(f32[5,8,1024]{2,1,0:T(8,128)S(1)} %get-tuple-element.33), channel_id=1, source_target_pairs={{16,0},{32,16},{48,32},{64,48},{80,64},{96,80},{112,96},{17,1},{33... | collective-permute-start | bytes 491528 | tf_op jit(solution)/shard_map/ppermute | solution.py:25
  12.6 4.2 %collective-permute-start.3 = (f32[5,256,8]{1,2,0:T(8,128)S(1)}, f32[5,256,8]{1,2,0:T(8,128)S(1)}, u32[]{:S(2)}, u32[]{:S(2)}) collective-permute-start(f32[5,256,8]{1,2,0:T(8,128)S(1)} %copy.16), channel_id=1, source_target_pairs={{0,1},{1,2},{2,3},{3,4},{4,5},{5,6},{6,7},{7,8},{8,9},{9,10},{10,1... | collective-permute-start | bytes 122888 | tf_op jit(solution)/shard_map/ppermute | solution.py:25
  19.6 3.8 %collective-permute-start.5 = (f32[5,8,8]{2,1,0:T(8,128)S(1)}, f32[5,8,8]{2,1,0:T(8,128)S(1)}, u32[]{:S(2)}, u32[]{:S(2)}) collective-permute-start(f32[5,8,8]{2,1,0:T(8,128)S(1)} %get-tuple-element.30), channel_id=1, source_target_pairs={{16,1},{17,2},{18,3},{19,4},{20,5},{21,6},{22,7},{23,8},{24,9},{25... | collective-permute-start | bytes 3848 | tf_op jit(solution)/shard_map/ppermute | solution.py:36
  23.5 5.2 %collective-permute-start = (f32[5,8,8]{2,1,0:T(8,128)S(1)}, f32[5,8,8]{2,1,0:T(8,128)S(1)}, u32[]{:S(2)}, u32[]{:S(2)}) collective-permute-start(f32[5,8,8]{2,1,0:T(8,128)S(1)} %get-tuple-element.31), channel_id=1, source_target_pairs={{0,17},{1,18},{2,19},{3,20},{4,21},{5,22},{6,23},{7,24},{8,25},{9,... | collective-permute-start | bytes 3848 | tf_op jit(solution)/shard_map/ppermute | solution.py:36
  29.1 8.1 %concatenate.13 = f32[5,256,1040]{2,1,0:T(8,128)} concatenate(f32[5,256,8]{2,1,0:T(8,128)S(1)} %copy.18, f32[5,256,1024]{2,1,0:T(8,128)} %copy-done.19, f32[5,256,8]{2,1,0:T(8,128)S(1)} %copy.19), dimensions={2} | concatenate | bytes 10649600 | tf_op jit(solution)/shard_map/concatenate | solution.py:52
  37.6 3.1 %pad_maximum_fusion = f32[5,272,1040]{2,1,0:T(8,128)S(1)} fusion(f32[5,8,1040]{2,1,0:T(8,128)S(1)} %concatenate.14, f32[5,256,1040]{2,1,0:T(8,128)} %concatenate.13, f32[5,8,1040]{2,1,0:T(8,128)S(1)} %concatenate.12), kind=kLoop, calls=%fused_computation | loop fusion | flops 2828800 | bytes 11315200 | tf_op jit(solution)/shard_map/concatenate | solution.py:49
  41.6 2.0 %slice.320 = f32[272,1039]{1,0:T(8,128)} slice(f32[272,1040]{1,0:T(8,128)S(1)} %get-tuple-element.23), slice={[0:272], [1:1040]} | slice | bytes 2260864 | tf_op jit(solution)/shard_map/slice | solution.py:60
  43.6 1.5 slice.322
  45.1 2.4 %multiply_bitcast_fusion.3 = (f32[1,272,1040]{2,1,0:T(8,128)S(1)}, f32[1,272,1040]{2,1,0:T(8,128)S(1)}, f32[1,272,1040]{2,1,0:T(8,128)S(1)}, f32[1,272,1040]{2,1...) fusion(f32[272,1039]{1,0:T(8,128)S(1)} %slice.316, f32[5,272,1040]{2,1,0:T(8,128)S(1)} %pad_maximum_fusion, ...), kind=kLoop, calls=%fused_computation.80 | loop fusion | flops 2263040 | bytes 16957056 | tf_op jit(solution)/shard_map/stack | solution.py:176
  49.7 2.4 %fusion.1 = (f32[2,272,1040]{2,1,0:T(8,128)}, f32[2,272,1040]{2,1,0:T(8,128)S(1)}) fusion(f32[1,272,1040]{2,1,0:T(8,128)S(1)} %get-tuple-element.18, f32[1,272,1040]{2,1,0:T(8,128)S(1)} %get-tuple-element.17, f32[1,272,1040]{2,1,0:T(8,128)S(1)} %get-tuple-element.49, f32[1,272,1040]{2,1,0:T(8,128)S(1)} %get-tuple-element.48, ...), kind=kLoop, calls=%fused_computation.6 | loop fusion | flops 10749440 | bytes 15841280 | tf_op jit(solution)/shard_map/jit(_where)/select_n | solution.py:180
  55.0 1.8 %multiply_reduce_fusion.4 = (f32[]{:T(128)}, f32[]{:T(128)}) fusion(f32[2,272,1040]{2,1,0:T(8,128)S(1)} %fusion.5, f32[2,272,1040]{2,1,0:T(8,128)S(1)} %get-tuple-element.41), kind=kLoop, calls=%fused_computation.37 | loop fusion | flops 2097150 | bytes 4194312 | tf_op jit(solution)/shard_map/reduce_sum | solution.py:169
  59.4 20.0 %shard_map.76.prev_ref = f32[8,128]{1,0:T(8,128)} custom-call(f32[8,128]{1,0:T(8,128)} %broadcast_select_fusion.local_ref, f32[8,128]{1,0:T(8,128)} %iota.49.prev_ref), custom_call_target="tpu_custom_call" | custom-call | tf_op jit(solution)/shard_map/pallas_call | solution.py:148
  80.6 4.4 %multiply_subtract_fusion.1 = f32[2,272,1040]{2,1,0:T(8,128)S(1)} fusion(f32[2,272,1040]{2,1,0:T(8,128)S(1)} %get-tuple-element.41, f32[]{:T(128)} %bitcast.27, f32[1,272,1040]{2,1,0:T(8,128)} %copy-done.14, f32[1,272,1040]{2,1,0:T(8,128)} %copy-done.13, f32[1,272,1040]{2,1,0:T(8,128)} %copy-done.10, f32[1,272,1040]{2,1,0:T(8,128)} %copy-done.8, ...), kind=kLoop, calls=%fused_computation.21 | loop fusion | flops 7354880 | bytes 11315204 | tf_op jit(solution)/shard_map/sub | solution.py:194
  91.2 2.4 %multiply_reduce_fusion.2 = (f32[]{:T(128)}, f32[]{:T(128)}, f32[]{:T(128)}) fusion(f32[2,272,1040]{2,1,0:T(8,128)S(1)} %copy-done.18, f32[2,272,1040]{2,1,0:T(8,128)S(1)} %multiply_subtract_fusion.1, f32[2,272,1040]{2,1,0:T(8,128)S(1)} %fusion.6), kind=kLoop, calls=%fused_computation.35 | loop fusion | flops 3145725 | bytes 6291468 | tf_op jit(solution)/shard_map/reduce_sum | solution.py:169
  94.2 2.0 %select_select_fusion.1.local_ref = f32[8,128]{1,0:T(8,128)} fusion(f32[8]{0:T(128)S(1)} %fusion.24, f32[]{:T(128)} %get-tuple-element.10, f32[]{:T(128)} %get-tuple-element.9, pred[8]{0:T(512)(128)(4,1)S(1)} %get-tuple-element.54, pred[8]{0:T(512)(128)(4,1)S(1)} %get-tuple-element.55), kind=kLoop, calls=%fused_computation.94 | loop fusion | flops 2048 | bytes 4152 | tf_op jit(solution)/shard_map/jit(_where)/select_n | solution.py:147
  96.2 14.0 %shard_map.77.prev_ref = f32[8,128]{1,0:T(8,128)} custom-call(f32[8,128]{1,0:T(8,128)} %select_select_fusion.1.local_ref, f32[8,128]{1,0:T(8,128)} %shard_map.76.prev_ref), custom_call_target="tpu_custom_call" | custom-call | tf_op jit(solution)/shard_map/pallas_call | solution.py:148
  111.6 6.7 %multiply_subtract_fusion = (f32[2,272,1040]{2,1,0:T(8,128)S(1)}, f32[2,272,1040]{2,1,0:T(8,128)S(1)}) fusion(f32[2,272,1040]{2,1,0:T(8,128)} %copy-done, f32[]{:T(128)} %bitcast.33, f32[]{:T(128)} %bitcast.34, f32[1,272,1040]{2,1,0:T(8,128)} %copy-done.21, f32[1,272,1040]{2,1,0:T(8,128)} %copy-done.20, f32[1,272,1040]{2,1,0:T(8,128)} %copy-done.10, ...), kind=kLoop, calls=%fused_computation.19 | loop fusion | flops 10749440 | bytes 18104328 | tf_op jit(solution)/shard_map/sub | solution.py:194
  121.9 3.8 %fusion.12 = (f32[]{:T(128)}, f32[]{:T(128)}, f32[]{:T(128)}) fusion(f32[2,272,1040]{2,1,0:T(8,128)S(1)} %get-tuple-element.15, f32[2,272,1040]{2,1,0:T(8,128)S(1)} %get-tuple-element.14, f32[1,272,1040]{2,1,0:T(8,128)S(1)} %get-tuple-element.43, f32[1,272,1040]{2,1,0:T(8,128)S(1)} %get-tuple-element.42, f32[2,272,1040]{2,1,0:T(8,128)S(1)} %copy-done.24, ...), kind=kLoop, calls=%fused_computation.30 | loop fusion | flops 5767165 | bytes 10817548 | tf_op jit(solution)/shard_map/reduce_sum | solution.py:169
  126.3 1.9 %select_select_fusion.local_ref = f32[8,128]{1,0:T(8,128)} fusion(f32[8]{0:T(128)S(1)} %fusion.23, f32[]{:T(128)} %get-tuple-element.8, f32[]{:T(128)} %get-tuple-element.6, pred[8]{0:T(512)(128)(4,1)S(1)} %get-tuple-element.54, pred[8]{0:T(512)(128)(4,1)S(1)} %get-tuple-element.55), kind=kLoop, calls=%fused_computation.93 | loop fusion | flops 2048 | bytes 4152 | tf_op jit(solution)/shard_map/jit(_where)/select_n | solution.py:147
  128.3 12.5 %shard_map.78 = f32[8,128]{1,0:T(8,128)} custom-call(f32[8,128]{1,0:T(8,128)} %select_select_fusion.local_ref, f32[8,128]{1,0:T(8,128)} %shard_map.77.prev_ref), custom_call_target="tpu_custom_call" | custom-call | tf_op jit(solution)/shard_map/pallas_call | solution.py:148
  142.1 9.4 %multiply_add_fusion = f32[2,272,1040]{2,1,0:T(8,128)S(1)} fusion(f32[2,272,1040]{2,1,0:T(8,128)} %copy-done, f32[2,272,1040]{2,1,0:T(8,128)S(1)} %get-tuple-element.41, f32[]{:T(128)} %bitcast.41, f32[]{:T(128)} %bitcast.40, f32[]{:T(128)} %bitcast.34, f32[]{:T(128)} %bitcast.33, f32[]{:T(128)} %bitcast.27, f32[2,272,1040]{2,1,0:T(8,128)} %copy-done.12, ...), kind=kLoop, calls=%fused_computation.18 | loop fusion | flops 10749440 | bytes 18104340 | tf_op jit(solution)/shard_map/add | solution.py:191
  151.6 1.9 %slice_bitcast_fusion.21 = (f32[256,1024]{1,0:T(8,128)}, f32[256,1024]{1,0:T(8,128)}) fusion(f32[2,272,1040]{2,1,0:T(8,128)S(1)} %multiply_add_fusion), kind=kLoop, calls=%fused_computation.81 | loop fusion | bytes 4194304 | tf_op jit(solution)/shard_map/squeeze | solution.py:202
  154.8 2.5 %slice_subtract_fusion.1 = f32[256,1024]{1,0:T(8,128)} fusion(f32[272,1040]{1,0:T(8,128)S(1)} %copy-done.23, f32[271,1040]{1,0:T(8,128)S(1)} %slice_bitcast_fusion, f32[272,1040]{1,0:T(8,128)S(1)} %get-tuple-element.39, f32[272,1039]{1,0:T(8,128)S(1)} %bitcast.130, f32[272,1040]{1,0:T(8,128)S(1)} %get-tuple-element.38), kind=kLoop, calls=%fused_computation.83 | loop fusion | flops 1310720 | bytes 6452096 | tf_op jit(solution)/shard_map/sub | solution.py:200
  (125 shorter events, 33.1 us)
Async XLA Ops:
  3.8 8.3 %copy-start.19 = (f32[5,256,1024]{2,1,0:T(8,128)}, f32[5,256,1024]{2,1,0:T(8,128)S(1)}, u32[]{:S(2)}) copy-start(f32[5,256,1024]{2,1,0:T(8,128)S(1)} %bitcast_dynamic-update-slice_fusion) | copy-start | bytes 15728644
  3.9 14.4 %collective-permute-start.2 = (f32[5,8,8]{2,1,0:T(8,128)S(1)}, f32[5,8,8]{2,1,0:T(8,128)S(1)}, u32[]{:S(2)}, u32[]{:S(2)}) collective-permute-start(f32[5,8,8]{2,1,0:T(8,128)S(1)} %get-tuple-element.28), channel_id=1, source_target_pairs={{1,16},{2,17},{3,18},{4,19},{5,20},{6,21},{7,22},{8,23},{9,24},{10... | collective-permute-start | bytes 3848 | tf_op jit(solution)/shard_map/ppermute | solution.py:36
  5.3 32.0 %collective-permute-start.1 = (f32[5,8,1024]{2,1,0:T(8,128)S(1)}, f32[5,8,1024]{2,1,0:T(8,128)S(1)}, u32[]{:S(2)}, u32[]{:S(2)}) collective-permute-start(f32[5,8,1024]{2,1,0:T(8,128)S(1)} %get-tuple-element.32), channel_id=1, source_target_pairs={{0,16},{16,32},{32,48},{48,64},{64,80},{80,96},{96,112},{1,17},{17... | collective-permute-start | bytes 491528 | tf_op jit(solution)/shard_map/ppermute | solution.py:25
  10.2 27.3 %collective-permute-start.6 = (f32[5,8,1024]{2,1,0:T(8,128)S(1)}, f32[5,8,1024]{2,1,0:T(8,128)S(1)}, u32[]{:S(2)}, u32[]{:S(2)}) collective-permute-start(f32[5,8,1024]{2,1,0:T(8,128)S(1)} %get-tuple-element.33), channel_id=1, source_target_pairs={{16,0},{32,16},{48,32},{64,48},{80,64},{96,80},{112,96},{17,1},{33... | collective-permute-start | bytes 491528 | tf_op jit(solution)/shard_map/ppermute | solution.py:25
  12.6 7.0 %collective-permute-start.3 = (f32[5,256,8]{1,2,0:T(8,128)S(1)}, f32[5,256,8]{1,2,0:T(8,128)S(1)}, u32[]{:S(2)}, u32[]{:S(2)}) collective-permute-start(f32[5,256,8]{1,2,0:T(8,128)S(1)} %copy.16), channel_id=1, source_target_pairs={{0,1},{1,2},{2,3},{3,4},{4,5},{5,6},{6,7},{7,8},{8,9},{9,10},{10,1... | collective-permute-start | bytes 122888 | tf_op jit(solution)/shard_map/ppermute | solution.py:25
  17.0 6.5 %collective-permute-start.4 = (f32[5,256,8]{1,2,0:T(8,128)S(1)}, f32[5,256,8]{1,2,0:T(8,128)S(1)}, u32[]{:S(2)}, u32[]{:S(2)}) collective-permute-start(f32[5,256,8]{1,2,0:T(8,128)S(1)} %copy.17), channel_id=1, source_target_pairs={{1,0},{2,1},{3,2},{4,3},{5,4},{6,5},{7,6},{8,7},{9,8},{10,9},{11,1... | collective-permute-start | bytes 122888 | tf_op jit(solution)/shard_map/ppermute | solution.py:25
  18.3 19.1 %collective-permute-start.7 = (f32[5,8,8]{2,1,0:T(8,128)S(1)}, f32[5,8,8]{2,1,0:T(8,128)S(1)}, u32[]{:S(2)}, u32[]{:S(2)}) collective-permute-start(f32[5,8,8]{2,1,0:T(8,128)S(1)} %get-tuple-element.29), channel_id=1, source_target_pairs={{17,0},{18,1},{19,2},{20,3},{21,4},{22,5},{23,6},{24,7},{25,8},{26... | collective-permute-start | bytes 3848 | tf_op jit(solution)/shard_map/ppermute | solution.py:36
  19.6 17.8 %collective-permute-start.5 = (f32[5,8,8]{2,1,0:T(8,128)S(1)}, f32[5,8,8]{2,1,0:T(8,128)S(1)}, u32[]{:S(2)}, u32[]{:S(2)}) collective-permute-start(f32[5,8,8]{2,1,0:T(8,128)S(1)} %get-tuple-element.30), channel_id=1, source_target_pairs={{16,1},{17,2},{18,3},{19,4},{20,5},{21,6},{22,7},{23,8},{24,9},{25... | collective-permute-start | bytes 3848 | tf_op jit(solution)/shard_map/ppermute | solution.py:36
  23.5 13.8 %collective-permute-start = (f32[5,8,8]{2,1,0:T(8,128)S(1)}, f32[5,8,8]{2,1,0:T(8,128)S(1)}, u32[]{:S(2)}, u32[]{:S(2)}) collective-permute-start(f32[5,8,8]{2,1,0:T(8,128)S(1)} %get-tuple-element.31), channel_id=1, source_target_pairs={{0,17},{1,18},{2,19},{3,20},{4,21},{5,22},{6,23},{7,24},{8,25},{9,... | collective-permute-start | bytes 3848 | tf_op jit(solution)/shard_map/ppermute | solution.py:36
  40.7 9.0 %copy-start.7 = (f32[5,272,1040]{2,1,0:T(8,128)}, f32[5,272,1040]{2,1,0:T(8,128)S(1)}, u32[]{:S(2)}) copy-start(f32[5,272,1040]{2,1,0:T(8,128)S(1)} %pad_maximum_fusion) | copy-start | bytes 16972804
  41.2 2.4 %copy-start.22 = (f32[272,1040]{1,0:T(8,128)}, f32[272,1040]{1,0:T(8,128)S(1)}, u32[]{:S(2)}) copy-start(f32[272,1040]{1,0:T(8,128)S(1)} %get-tuple-element.24) | copy-start | bytes 3394564
  47.5 2.2 %copy-start.15 = (f32[1,272,1040]{2,1,0:T(8,128)}, f32[1,272,1040]{2,1,0:T(8,128)S(1)}, u32[]{:S(2)}) copy-start(f32[1,272,1040]{2,1,0:T(8,128)S(1)} %get-tuple-element.20) | copy-start | bytes 3394564
  47.5 2.2 %copy-start.16 = (f32[1,272,1040]{2,1,0:T(8,128)}, f32[1,272,1040]{2,1,0:T(8,128)S(1)}, u32[]{:S(2)}) copy-start(f32[1,272,1040]{2,1,0:T(8,128)S(1)} %get-tuple-element.21) | copy-start | bytes 3394564
  47.5 6.0 %copy-start.1 = (f32[1,272,1040]{2,1,0:T(8,128)}, f32[1,272,1040]{2,1,0:T(8,128)S(1)}, u32[]{:S(2)}) copy-start(f32[1,272,1040]{2,1,0:T(8,128)S(1)} %get-tuple-element.16) | copy-start | bytes 3394564
  47.6 6.0 %copy-start.4 = (f32[1,272,1040]{2,1,0:T(8,128)}, f32[1,272,1040]{2,1,0:T(8,128)S(1)}, u32[]{:S(2)}) copy-start(f32[1,272,1040]{2,1,0:T(8,128)S(1)} %get-tuple-element.19) | copy-start | bytes 3394564
  47.6 6.0 %copy-start.8 = (f32[1,272,1040]{2,1,0:T(8,128)}, f32[1,272,1040]{2,1,0:T(8,128)S(1)}, u32[]{:S(2)}) copy-start(f32[1,272,1040]{2,1,0:T(8,128)S(1)} %get-tuple-element.17) | copy-start | bytes 3394564
  47.6 6.0 %copy-start.10 = (f32[1,272,1040]{2,1,0:T(8,128)}, f32[1,272,1040]{2,1,0:T(8,128)S(1)}, u32[]{:S(2)}) copy-start(f32[1,272,1040]{2,1,0:T(8,128)S(1)} %get-tuple-element.18) | copy-start | bytes 3394564
  85.0 5.3 %copy-start = (f32[2,272,1040]{2,1,0:T(8,128)}, f32[2,272,1040]{2,1,0:T(8,128)S(1)}, u32[]{:S(2)}) copy-start(f32[2,272,1040]{2,1,0:T(8,128)S(1)} %multiply_subtract_fusion.1) | copy-start | bytes 6789124
  86.1 2.6 %copy-start.5 = (f32[1,272,1040]{2,1,0:T(8,128)S(1)}, f32[1,272,1040]{2,1,0:T(8,128)}, u32[]{:S(2)}) copy-start(f32[1,272,1040]{2,1,0:T(8,128)} %copy-done.4) | copy-start | bytes 3394564
  86.2 2.9 %copy-start.9 = (f32[1,272,1040]{2,1,0:T(8,128)S(1)}, f32[1,272,1040]{2,1,0:T(8,128)}, u32[]{:S(2)}) copy-start(f32[1,272,1040]{2,1,0:T(8,128)} %copy-done.8) | copy-start | bytes 3394564
  86.2 3.3 %copy-start.11 = (f32[1,272,1040]{2,1,0:T(8,128)S(1)}, f32[1,272,1040]{2,1,0:T(8,128)}, u32[]{:S(2)}) copy-start(f32[1,272,1040]{2,1,0:T(8,128)} %copy-done.10) | copy-start | bytes 3394564
  86.4 3.8 %copy-start.20 = (f32[1,272,1040]{2,1,0:T(8,128)}, f32[1,272,1040]{2,1,0:T(8,128)S(1)}, u32[]{:S(2)}) copy-start(f32[1,272,1040]{2,1,0:T(8,128)S(1)} %get-tuple-element.44) | copy-start | bytes 3394564
  86.5 3.8 %copy-start.21 = (f32[1,272,1040]{2,1,0:T(8,128)}, f32[1,272,1040]{2,1,0:T(8,128)S(1)}, u32[]{:S(2)}) copy-start(f32[1,272,1040]{2,1,0:T(8,128)S(1)} %get-tuple-element.45) | copy-start | bytes 3394564
  119.4 2.5 %copy-start.24 = (f32[2,272,1040]{2,1,0:T(8,128)S(1)}, f32[2,272,1040]{2,1,0:T(8,128)}, u32[]{:S(2)}) copy-start(f32[2,272,1040]{2,1,0:T(8,128)} %get-tuple-element.40) | copy-start | bytes 6789124
  (13 other events, 19.3 us)

commit v10 on v8

--- a/solution.py
+++ b/solution.py
@@ -1,4 +1,6 @@
 import functools
+
+import numpy as np
 
 import jax
 import jax.numpy as jnp
@@ -55,10 +57,13 @@
     return field[0] - west(field[0]) + field[1] - south(field[1])
 
 
+def gradient_back(field):
+    diverge = divergence(field)
+    return jnp.stack([diverge - east(diverge), diverge - north(diverge)])
+
+
 def operate(field, wet, inverse):
-    diverge = divergence(field)
-    back = jnp.stack([diverge - east(diverge), diverge - north(diverge)])
-    return wet * (inverse * field + back)
+    return wet * (inverse * field + gradient_back(field))
 
 
 def stages_of(sizes):
@@ -152,17 +157,18 @@
     sea = land_sea.astype(jnp.float32)
     grown = grow(jnp.stack([surface, bathymetry, sea, flux_lon, flux_lat]))
     surface_x, bathymetry_x, sea_x = grown[0], grown[1], grown[2]
-    wet = jnp.stack([sea_x * east(sea_x), sea_x * north(sea_x)])
-    depth = jnp.stack([0.5 * (bathymetry_x + east(bathymetry_x)), 0.5 * (bathymetry_x + north(bathymetry_x))])
-    slope = jnp.stack([east(surface_x) - surface_x, north(surface_x) - surface_x])
+    eastern, northern = east(grown[:3]), north(grown[:3])
+    wet = jnp.stack([sea_x * eastern[2], sea_x * northern[2]])
+    depth = jnp.stack([0.5 * (bathymetry_x + eastern[1]), 0.5 * (bathymetry_x + northern[1])])
+    slope = jnp.stack([eastern[0] - surface_x, northern[0] - surface_x])
     start = wet * (grown[3:] - courant * depth * slope)
     inverse = jnp.where(depth > 0, 1.0 / (dispersion * depth * depth), 0.0)
-    right_side = wet * inverse * start
     solution = start
-    residual = right_side - operate(start, wet, inverse)
+    residual = -(wet * gradient_back(start))
     applied = operate(residual, wet, inverse)
-    rows = lax.broadcasted_iota(jnp.int32, (8, 128), 0)
-    previous = jnp.where(rows == 2, jnp.inf, 0.0).astype(jnp.float32)
+    previous = np.zeros((8, 128), np.float32)
+    previous[2] = np.inf
+    previous = jnp.asarray(previous)
     stats = cg_scalars(dots((residual, residual), (residual, applied)), previous)
     direction, image = residual, applied
     for step in range(ITERS):

time: 156 us -> 157 us (level)
  other arithmetic: 49.1 us -> 51.9 us
  local copies, waits for them, and re-layouts: 41.4 us -> 39.3 us
    mul x2, other arithmetic: 1.52 us -> 4.95 us  [the longest x1 4.16 us: per_device(): wet = jnp.stack([sea_x * eastern[2], sea_x * northern[2]])]
    mul x1, other arithmetic: 0.73 us -> 4.08 us  [per_device(): start = wet * (grown[3:] - courant * depth * slope)]
    another operation x5 -> x4, other arithmetic: 3.92 us -> 1.11 us  [gradient_back(): return jnp.stack([diverge - east(diverge), diverge - north(diverge)])]
    slice x7 -> x5, local copies, waits for them, and re-layouts: 5.94 us -> 4.47 us  [east(): return jnp.pad(field[..., :, 1:], [(0, 0)] * (field.ndim - 1) + [(0, 1)])]
    unnamed x63 -> x53, local copies, waits for them, and re-layouts: 14.3 us -> 15.7 us
where the time goes in v10:
time: 157 us; the launch traced here: 156 us
  other arithmetic  51.9 us (33%)
  Pallas kernels  44.2 us (28%)
  local copies, waits for them, and re-layouts  39.3 us (25%)
  starting transfers between devices  11.4 us (7%)
  waiting for transfers between devices  8.37 us (5%)
    pallas_call x3, Pallas kernels, cg_scalars(): pl.pallas_call(functools.partial(reduce_kernel, stages), out_shape=jax.Sh...  44.2 us
    unnamed x53, local copies, waits for them, and re-layouts  15.7 us
    ppermute x4, starting transfers between devices, from_behind(): lax.ppermute(value, axis, [(source, source + steps) for source in range(l...  11.4 us
    sub x2, other arithmetic, per_device(): residual = residual - alpha * image  9.77 us
    add x1, other arithmetic, per_device(): solution = solution + alpha * direction  9.22 us
    concatenate x1, local copies, waits for them, and re-layouts, grow(): return jnp.concatenate([left, stacked, right], axis=2)  8.37 us
    ppermute x4, waiting for transfers between devices, from_behind(): lax.ppermute(value, axis, [(source, source + steps) for source in range(l...  8.37 us
    reduce_sum x3, other arithmetic, dots(): return jnp.stack([jnp.sum(interior(x) * interior(y)) for x, y in pairs])  8 us
  transfers between devices with their start and end apart: 4, of which 3 were waited for; matrix products, arithmetic and copies ran while one was open for 0% of the time, Pallas kernels for 0%

profile of v10, /device:TPU:1, one launch (start us, length us, event | category | flops | bytes accessed | tf_op | source)
XLA Modules:
  0.0 156.4 jit_solution(2565663277918579156)
XLA Ops:
  3.9 4.9 %collective-permute-start = (f32[5,8,1024]{2,1,0:T(8,128)S(1)}, f32[5,8,1024]{2,1,0:T(8,128)S(1)}, u32[]{:S(2)}, u32[]{:S(2)}) collective-permute-start(f32[5,8,1024]{2,1,0:T(8,128)S(1)} %get-tuple-element.28), channel_id=1, source_target_pairs={{0,16},{16,32},{32,48},{48,64},{64,80},{80,96},{96,112},{1,17},{17... | collective-permute-start | bytes 491528 | tf_op jit(solution)/shard_map/ppermute | solution.py:27
  8.8 1.9 %collective-permute-start.1 = (f32[5,8,1024]{2,1,0:T(8,128)S(1)}, f32[5,8,1024]{2,1,0:T(8,128)S(1)}, u32[]{:S(2)}, u32[]{:S(2)}) collective-permute-start(f32[5,8,1024]{2,1,0:T(8,128)S(1)} %get-tuple-element.29), channel_id=1, source_target_pairs={{16,0},{32,16},{48,32},{64,48},{80,64},{96,80},{112,96},{17,1},{33... | collective-permute-start | bytes 491528 | tf_op jit(solution)/shard_map/ppermute | solution.py:27
  11.1 4.4 %collective-permute-done.1 = f32[5,8,1024]{2,1,0:T(8,128)S(1)} collective-permute-done((f32[5,8,1024]{2,1,0:T(8,128)S(1)}, f32[5,8,1024]{2,1,0:T(8,128)S(1)}, u32[]{:S(2)}, u32[]{:S(2)}) %collective-permute-start.1) | collective-permute-done | bytes 163872 | tf_op jit(solution)/shard_map/ppermute | solution.py:27
  16.4 2.4 %copy-done.15 = f32[5,272,1024]{2,1,0:T(8,128)} copy-done((f32[5,272,1024]{2,1,0:T(8,128)}, f32[5,272,1024]{2,1,0:T(8,128)S(1)}, u32[]{:S(2)}) %copy-start.15) | copy-done | bytes 5570584
  19.7 3.2 %collective-permute-start.2 = (f32[5,272,8]{1,2,0:T(8,128)S(1)}, f32[5,272,8]{1,2,0:T(8,128)S(1)}, u32[]{:S(2)}, u32[]{:S(2)}) collective-permute-start(f32[5,272,8]{1,2,0:T(8,128)S(1)} %copy.17), channel_id=1, source_target_pairs={{0,1},{1,2},{2,3},{3,4},{4,5},{5,6},{6,7},{7,8},{8,9},{9,10},{10,1... | collective-permute-start | bytes 130568 | tf_op jit(solution)/shard_map/ppermute | solution.py:27
  24.2 3.7 %collective-permute-done.3 = f32[5,272,8]{1,2,0:T(8,128)S(1)} collective-permute-done((f32[5,272,8]{1,2,0:T(8,128)S(1)}, f32[5,272,8]{1,2,0:T(8,128)S(1)}, u32[]{:S(2)}, u32[]{:S(2)}) %collective-permute-start.3) | collective-permute-done | bytes 43552 | tf_op jit(solution)/shard_map/ppermute | solution.py:27
  28.4 8.4 %concatenate.7 = f32[5,272,1040]{2,1,0:T(8,128)} concatenate(f32[5,272,8]{2,1,0:T(8,128)S(1)} %copy.19, f32[5,272,1024]{2,1,0:T(8,128)} %copy-done.15, f32[5,272,8]{2,1,0:T(8,128)S(1)} %copy.20), dimensions={2} | concatenate | bytes 11315200 | tf_op jit(solution)/shard_map/concatenate | solution.py:37
  36.7 2.5 %slice.294 = f32[3,271,1040]{2,1,0:T(8,128)S(1)} slice(f32[5,272,1040]{2,1,0:T(8,128)} %concatenate.7), slice={[0:3], [1:272], [0:1040]} | slice | bytes 6764160 | tf_op jit(solution)/shard_map/slice | solution.py:45
  40.6 2.9 %slice.293 = f32[3,272,1039]{2,1,0:T(8,128)} slice(f32[5,272,1040]{2,1,0:T(8,128)S(1)} %copy-done.6), slice={[0:3], [0:272], [1:1040]} | slice | bytes 6782592 | tf_op jit(solution)/shard_map/slice | solution.py:41
  43.6 4.2 %fusion.13 = (f32[1,272,1040]{2,1,0:T(8,128)S(1)}, f32[1,272,1040]{2,1,0:T(8,128)S(1)}, f32[1,272,1040]{2,1,0:T(8,128)}, f32[1,272,1040]{2,1,0:T(8,128)}, f32[1,...) fusion(f32[3,272,1039]{2,1,0:T(8,128)} %slice.293, f32[5,272,1040]{2,1,0:T(8,128)S(1)} %copy-done.6, ...), kind=kLoop, calls=%fused_computation.43 | loop fusion | flops 2263040 | bytes 18088576 | tf_op jit(solution)/shard_map/mul | solution.py:161
  47.7 4.1 %fusion.2 = f32[2,272,1040]{2,1,0:T(8,128)S(1)} fusion(f32[5,272,1040]{2,1,0:T(8,128)S(1)} %copy-done.6, f32[1,272,1040]{2,1,0:T(8,128)} %get-tuple-element.22, f32[1,272,1040]{2,1,0:T(8,128)} %get-tuple-element.18, f32[1,272,1040]{2,1,0:T(8,128)S(1)} %get-tuple-element.23, f32[1,272,1040]{2,1,0:T(8,128)S(1)} %get-tuple-element.17, ...), kind=kLoop, calls=%fused_computation.14 | loop fusion | flops 3960320 | bytes 11315200 | tf_op jit(solution)/shard_map/mul | solution.py:164
  55.1 2.1 %fusion.1 = (f32[2,272,1040]{2,1,0:T(8,128)}, f32[2,272,1040]{2,1,0:T(8,128)S(1)}) fusion(f32[1,272,1040]{2,1,0:T(8,128)S(1)} %get-tuple-element.23, f32[1,272,1040]{2,1,0:T(8,128)S(1)} %get-tuple-element.17, f32[1,272,1040]{2,1,0:T(8,128)S(1)} %get-tuple-element.41, f32[1,272,1040]{2,1,0:T(8,128)S(1)} %get-tuple-element.40, ...), kind=kLoop, calls=%fused_computation.12 | loop fusion | flops 7920640 | bytes 13578240 | tf_op jit(solution)/shard_map/jit(_where)/select_n | solution.py:165
  62.4 17.8 %shard_map.85.prev_ref = f32[8,128]{1,0:T(8,128)} custom-call(f32[8,128]{1,0:T(8,128)} %broadcast_select_fusion.local_ref, f32[8,128]{1,0:T(8,128)} %constant.8.clone.prev_ref), custom_call_target="tpu_custom_call" | custom-call | tf_op jit(solution)/shard_map/pallas_call | solution.py:132
  81.4 4.2 %multiply_subtract_fusion.1 = f32[2,272,1040]{2,1,0:T(8,128)S(1)} fusion(f32[2,272,1040]{2,1,0:T(8,128)} %copy-done.7, f32[]{:T(128)} %bitcast.16, f32[1,272,1040]{2,1,0:T(8,128)} %copy-done.14, f32[1,272,1040]{2,1,0:T(8,128)} %copy-done.13, f32[1,272,1040]{2,1,0:T(8,128)} %copy-done.3, f32[1,272,1040]{2,1,0:T(8,128)} %copy-done), kind=kLoop, calls=%fused_computation.26 | loop fusion | flops 3394560 | bytes 9052164 | tf_op jit(solution)/shard_map/sub | solution.py:179
  91.7 2.5 %multiply_reduce_fusion.2 = (f32[]{:T(128)}, f32[]{:T(128)}, f32[]{:T(128)}) fusion(f32[2,272,1040]{2,1,0:T(8,128)S(1)} %copy-done.8, f32[2,272,1040]{2,1,0:T(8,128)S(1)} %multiply_subtract_fusion.1, f32[2,272,1040]{2,1,0:T(8,128)S(1)} %fusion.5), kind=kLoop, calls=%fused_computation.40 | loop fusion | flops 3145725 | bytes 6291468 | tf_op jit(solution)/shard_map/reduce_sum | solution.py:153
  94.8 2.0 %select_select_fusion.1.local_ref = f32[8,128]{1,0:T(8,128)} fusion(f32[8]{0:T(128)S(1)} %fusion.31, f32[]{:T(128)} %get-tuple-element.10, f32[]{:T(128)} %get-tuple-element.9, pred[8]{0:T(512)(128)(4,1)S(1)} %get-tuple-element.48, pred[8]{0:T(512)(128)(4,1)S(1)} %get-tuple-element.49), kind=kLoop, calls=%fused_computation.96 | loop fusion | flops 2048 | bytes 4152 | tf_op jit(solution)/shard_map/jit(_where)/select_n | solution.py:131
  96.8 13.0 %shard_map.86.prev_ref = f32[8,128]{1,0:T(8,128)} custom-call(f32[8,128]{1,0:T(8,128)} %select_select_fusion.1.local_ref, f32[8,128]{1,0:T(8,128)} %shard_map.85.prev_ref), custom_call_target="tpu_custom_call" | custom-call | tf_op jit(solution)/shard_map/pallas_call | solution.py:132
  111.1 5.6 %multiply_subtract_fusion = (f32[2,272,1040]{2,1,0:T(8,128)S(1)}, f32[2,272,1040]{2,1,0:T(8,128)S(1)}) fusion(f32[2,272,1040]{2,1,0:T(8,128)S(1)} %multiply_subtract_fusion.1, f32[]{:T(128)} %bitcast.22, f32[2,272,1040]{2,1,0:T(8,128)} %copy-done.7, f32[]{:T(128)} %bitcast.23, f32[1,272,1040]{2,1,0:T(8,128)} %copy-done.18, f32[1,272,1040]{2,1,0:T(8,128)} %copy-done.17, ...), kind=kLoop, calls=%fused_computation.24 | loop fusion | flops 8486400 | bytes 15841288 | tf_op jit(solution)/shard_map/sub | solution.py:179
  120.3 3.8 %fusion.11 = (f32[]{:T(128)}, f32[]{:T(128)}, f32[]{:T(128)}) fusion(f32[2,272,1040]{2,1,0:T(8,128)S(1)} %get-tuple-element.15, f32[2,272,1040]{2,1,0:T(8,128)S(1)} %get-tuple-element.14, f32[1,272,1040]{2,1,0:T(8,128)S(1)} %get-tuple-element.37, f32[1,272,1040]{2,1,0:T(8,128)S(1)} %get-tuple-element.36, f32[2,272,1040]{2,1,0:T(8,128)S(1)} %copy-done.19, ...), kind=kLoop, calls=%fused_computation.35 | loop fusion | flops 5767165 | bytes 10817548 | tf_op jit(solution)/shard_map/reduce_sum | solution.py:153
  124.8 1.9 %select_select_fusion.local_ref = f32[8,128]{1,0:T(8,128)} fusion(f32[8]{0:T(128)S(1)} %fusion.30, f32[]{:T(128)} %get-tuple-element.8, f32[]{:T(128)} %get-tuple-element.6, pred[8]{0:T(512)(128)(4,1)S(1)} %get-tuple-element.48, pred[8]{0:T(512)(128)(4,1)S(1)} %get-tuple-element.49), kind=kLoop, calls=%fused_computation.95 | loop fusion | flops 2048 | bytes 4152 | tf_op jit(solution)/shard_map/jit(_where)/select_n | solution.py:131
  126.6 13.5 %shard_map.87 = f32[8,128]{1,0:T(8,128)} custom-call(f32[8,128]{1,0:T(8,128)} %select_select_fusion.local_ref, f32[8,128]{1,0:T(8,128)} %shard_map.86.prev_ref), custom_call_target="tpu_custom_call" | custom-call | tf_op jit(solution)/shard_map/pallas_call | solution.py:132
  141.4 9.2 %multiply_add_fusion = f32[2,272,1040]{2,1,0:T(8,128)S(1)} fusion(f32[2,272,1040]{2,1,0:T(8,128)S(1)} %multiply_subtract_fusion.1, f32[]{:T(128)} %bitcast.30, f32[]{:T(128)} %bitcast.29, f32[]{:T(128)} %bitcast.23, f32[]{:T(128)} %bitcast.22, f32[]{:T(128)} %bitcast.16, f32[2,272,1040]{2,1,0:T(8,128)} %copy-done.16, f32[1,272,1040]{2,1,0:T(8,128)} %copy-done.14, ...), kind=kLoop, calls=%fused_computation.23 | loop fusion | flops 12446720 | bytes 18104340 | tf_op jit(solution)/shard_map/add | solution.py:176
  150.7 1.9 %slice_bitcast_fusion.16 = (f32[256,1024]{1,0:T(8,128)}, f32[256,1024]{1,0:T(8,128)}) fusion(f32[2,272,1040]{2,1,0:T(8,128)S(1)} %multiply_add_fusion), kind=kLoop, calls=%fused_computation.83 | loop fusion | bytes 4194304 | tf_op jit(solution)/shard_map/squeeze | solution.py:187
  153.9 2.5 %slice_subtract_fusion.1 = f32[256,1024]{1,0:T(8,128)} fusion(f32[272,1040]{1,0:T(8,128)S(1)} %copy-done.20, f32[271,1040]{1,0:T(8,128)S(1)} %slice_bitcast_fusion, f32[272,1040]{1,0:T(8,128)S(1)} %get-tuple-element.33, f32[272,1039]{1,0:T(8,128)S(1)} %bitcast.96, f32[272,1040]{1,0:T(8,128)S(1)} %get-tuple-element.32), kind=kLoop, calls=%fused_computation.85 | loop fusion | flops 1310720 | bytes 6452096 | tf_op jit(solution)/shard_map/sub | solution.py:185
  (101 shorter events, 32.9 us)
Async XLA Ops:
  0.6 1.5 copy-start.21
  0.6 1.8 %copy-start.22 = (s32[256,1024]{1,0:T(8,128)S(1)}, s32[256,1024]{1,0:T(8,128)}, u32[]{:S(2)}) copy-start(s32[256,1024]{1,0:T(8,128)} %param.8) | copy-start | bytes 3145732
  3.9 7.2 %collective-permute-start = (f32[5,8,1024]{2,1,0:T(8,128)S(1)}, f32[5,8,1024]{2,1,0:T(8,128)S(1)}, u32[]{:S(2)}, u32[]{:S(2)}) collective-permute-start(f32[5,8,1024]{2,1,0:T(8,128)S(1)} %get-tuple-element.28), channel_id=1, source_target_pairs={{0,16},{16,32},{32,48},{48,64},{64,80},{80,96},{96,112},{1,17},{17... | collective-permute-start | bytes 491528 | tf_op jit(solution)/shard_map/ppermute | solution.py:27
  8.8 6.6 %collective-permute-start.1 = (f32[5,8,1024]{2,1,0:T(8,128)S(1)}, f32[5,8,1024]{2,1,0:T(8,128)S(1)}, u32[]{:S(2)}, u32[]{:S(2)}) collective-permute-start(f32[5,8,1024]{2,1,0:T(8,128)S(1)} %get-tuple-element.29), channel_id=1, source_target_pairs={{16,0},{32,16},{48,32},{64,48},{80,64},{96,80},{112,96},{17,1},{33... | collective-permute-start | bytes 491528 | tf_op jit(solution)/shard_map/ppermute | solution.py:27
  16.4 2.4 %copy-start.15 = (f32[5,272,1024]{2,1,0:T(8,128)}, f32[5,272,1024]{2,1,0:T(8,128)S(1)}, u32[]{:S(2)}) copy-start(f32[5,272,1024]{2,1,0:T(8,128)S(1)} %pad_maximum_fusion) | copy-start | bytes 16711684
  19.7 8.4 %collective-permute-start.2 = (f32[5,272,8]{1,2,0:T(8,128)S(1)}, f32[5,272,8]{1,2,0:T(8,128)S(1)}, u32[]{:S(2)}, u32[]{:S(2)}) collective-permute-start(f32[5,272,8]{1,2,0:T(8,128)S(1)} %copy.17), channel_id=1, source_target_pairs={{0,1},{1,2},{2,3},{3,4},{4,5},{5,6},{6,7},{7,8},{8,9},{9,10},{10,1... | collective-permute-start | bytes 130568 | tf_op jit(solution)/shard_map/ppermute | solution.py:27
  22.9 5.0 %collective-permute-start.3 = (f32[5,272,8]{1,2,0:T(8,128)S(1)}, f32[5,272,8]{1,2,0:T(8,128)S(1)}, u32[]{:S(2)}, u32[]{:S(2)}) collective-permute-start(f32[5,272,8]{1,2,0:T(8,128)S(1)} %copy.18), channel_id=1, source_target_pairs={{1,0},{2,1},{3,2},{4,3},{5,4},{6,5},{7,6},{8,7},{9,8},{10,9},{11,1... | collective-permute-start | bytes 130568 | tf_op jit(solution)/shard_map/ppermute | solution.py:27
  36.7 3.9 %copy-start.6 = (f32[5,272,1040]{2,1,0:T(8,128)S(1)}, f32[5,272,1040]{2,1,0:T(8,128)}, u32[]{:S(2)}) copy-start(f32[5,272,1040]{2,1,0:T(8,128)} %concatenate.7) | copy-start | bytes 16972804
  47.7 7.3 %copy-start = (f32[1,272,1040]{2,1,0:T(8,128)}, f32[1,272,1040]{2,1,0:T(8,128)S(1)}, u32[]{:S(2)}) copy-start(f32[1,272,1040]{2,1,0:T(8,128)S(1)} %get-tuple-element.16) | copy-start | bytes 3394564
  47.7 7.3 %copy-start.3 = (f32[1,272,1040]{2,1,0:T(8,128)}, f32[1,272,1040]{2,1,0:T(8,128)S(1)}, u32[]{:S(2)}) copy-start(f32[1,272,1040]{2,1,0:T(8,128)S(1)} %get-tuple-element.24) | copy-start | bytes 3394564
  47.7 7.3 %copy-start.9 = (f32[1,272,1040]{2,1,0:T(8,128)}, f32[1,272,1040]{2,1,0:T(8,128)S(1)}, u32[]{:S(2)}) copy-start(f32[1,272,1040]{2,1,0:T(8,128)S(1)} %get-tuple-element.17) | copy-start | bytes 3394564
  47.7 7.3 %copy-start.11 = (f32[1,272,1040]{2,1,0:T(8,128)}, f32[1,272,1040]{2,1,0:T(8,128)S(1)}, u32[]{:S(2)}) copy-start(f32[1,272,1040]{2,1,0:T(8,128)S(1)} %get-tuple-element.23) | copy-start | bytes 3394564
  53.2 1.8 %copy-start.13 = (f32[1,272,1040]{2,1,0:T(8,128)}, f32[1,272,1040]{2,1,0:T(8,128)S(1)}, u32[]{:S(2)}) copy-start(f32[1,272,1040]{2,1,0:T(8,128)S(1)} %get-tuple-element.42) | copy-start | bytes 3394564
  53.2 1.8 %copy-start.14 = (f32[1,272,1040]{2,1,0:T(8,128)}, f32[1,272,1040]{2,1,0:T(8,128)S(1)}, u32[]{:S(2)}) copy-start(f32[1,272,1040]{2,1,0:T(8,128)S(1)} %get-tuple-element.43) | copy-start | bytes 3394564
  86.7 1.5 copy-start.1
  86.7 2.6 %copy-start.4 = (f32[1,272,1040]{2,1,0:T(8,128)S(1)}, f32[1,272,1040]{2,1,0:T(8,128)}, u32[]{:S(2)}) copy-start(f32[1,272,1040]{2,1,0:T(8,128)} %copy-done.3) | copy-start | bytes 3394564
  86.7 2.9 %copy-start.10 = (f32[1,272,1040]{2,1,0:T(8,128)S(1)}, f32[1,272,1040]{2,1,0:T(8,128)}, u32[]{:S(2)}) copy-start(f32[1,272,1040]{2,1,0:T(8,128)} %copy-done.9) | copy-start | bytes 3394564
  86.7 3.3 %copy-start.12 = (f32[1,272,1040]{2,1,0:T(8,128)S(1)}, f32[1,272,1040]{2,1,0:T(8,128)}, u32[]{:S(2)}) copy-start(f32[1,272,1040]{2,1,0:T(8,128)} %copy-done.11) | copy-start | bytes 3394564
  86.9 3.9 %copy-start.17 = (f32[1,272,1040]{2,1,0:T(8,128)}, f32[1,272,1040]{2,1,0:T(8,128)S(1)}, u32[]{:S(2)}) copy-start(f32[1,272,1040]{2,1,0:T(8,128)S(1)} %get-tuple-element.38) | copy-start | bytes 3394564
  86.9 3.9 %copy-start.18 = (f32[1,272,1040]{2,1,0:T(8,128)}, f32[1,272,1040]{2,1,0:T(8,128)S(1)}, u32[]{:S(2)}) copy-start(f32[1,272,1040]{2,1,0:T(8,128)S(1)} %get-tuple-element.39) | copy-start | bytes 3394564
  90.0 1.7 %copy-start.8 = (f32[2,272,1040]{2,1,0:T(8,128)S(1)}, f32[2,272,1040]{2,1,0:T(8,128)}, u32[]{:S(2)}) copy-start(f32[2,272,1040]{2,1,0:T(8,128)} %copy-done.7) | copy-start | bytes 6789124
  116.7 1.5 copy-start.16
  117.9 1.7 %copy-start.5 = (f32[1,272,1040]{2,1,0:T(8,128)S(1)}, f32[1,272,1040]{2,1,0:T(8,128)}, u32[]{:S(2)}) copy-start(f32[1,272,1040]{2,1,0:T(8,128)} %copy-done.3) | copy-start | bytes 3394564
  117.9 2.5 %copy-start.19 = (f32[2,272,1040]{2,1,0:T(8,128)S(1)}, f32[2,272,1040]{2,1,0:T(8,128)}, u32[]{:S(2)}) copy-start(f32[2,272,1040]{2,1,0:T(8,128)} %get-tuple-element.34) | copy-start | bytes 6789124
  (5 other events, 6.7 us)

commit v11 on v8

--- a/solution.py
+++ b/solution.py
@@ -32,11 +32,11 @@
     stacked = jnp.concatenate([below, stacked, above], axis=1)
     right = from_behind(stacked[:, :, :cols], "lon", -1)
     left = from_behind(stacked[:, :, -cols:], "lon", 1)
-    return jnp.concatenate([left, stacked, right], axis=2)
+    return jnp.concatenate([stacked, right, left], axis=2)
 
 
 def east(field):
-    return jnp.pad(field[..., :, 1:], [(0, 0)] * (field.ndim - 1) + [(0, 1)])
+    return jnp.roll(field, -1, axis=-1)
 
 
 def north(field):
@@ -44,7 +44,7 @@
 
 
 def west(field):
-    return jnp.pad(field[..., :, :-1], [(0, 0)] * (field.ndim - 1) + [(1, 0)])
+    return jnp.roll(field, 1, axis=-1)
 
 
 def south(field):
@@ -141,7 +141,7 @@
 
 def interior(field):
     rows, cols = MARGIN_ROWS, MARGIN_COLS
-    return field[..., rows:-rows, cols:-cols]
+    return field[..., rows:-rows, : -2 * cols]
 
 
 def dots(*pairs):

time: 156 us -> 147 us (0.942)
  other arithmetic: 49.1 us -> 42.8 us
  local copies, waits for them, and re-layouts: 41.4 us -> 36.9 us
  Pallas kernels: 44.2 us -> 47 us
  waiting for transfers between devices: 8.35 us -> 5.96 us
    slice x7 -> x13, local copies, waits for them, and re-layouts: 5.94 us -> 2.06 us  [the longest x8 1.6 us: east(): return jnp.roll(field, -1, axis=-1)]
    reduce_sum x3, other arithmetic: 7.88 us -> 4.22 us  [dots(): return jnp.stack([jnp.sum(interior(x) * interior(y)) for x, y in pairs])]
    pallas_call x3, Pallas kernels: 44.2 us -> 47 us  [cg_scalars(): pl.pallas_call(functools.partial(reduce_kernel, stages), out_shape=jax.Sh...]
    ppermute x4, waiting for transfers between devices: 8.35 us -> 5.96 us  [from_behind(): lax.ppermute(value, axis, [(source, source + steps) for source in range(l...]
    another operation x1, other arithmetic: 2.83 us -> 0.46 us  [per_device(): wet = jnp.stack([sea_x * east(sea_x), sea_x * north(sea_x)])]
    concatenate x1 -> x5, local copies, waits for them, and re-layouts: 8.37 us -> 8.76 us  [the longest x1 7.63 us: grow(): return jnp.concatenate([stacked, right, left], axis=2)]
    unnamed x63 -> x61, local copies, waits for them, and re-layouts: 14.3 us -> 14.6 us
where the time goes in v11:
time: 147 us; the launch traced here: 146 us
  Pallas kernels  47 us (32%)
  other arithmetic  42.8 us (29%)
  local copies, waits for them, and re-layouts  36.9 us (25%)
  starting transfers between devices  12.1 us (8%)
  waiting for transfers between devices  5.96 us (4%)
    pallas_call x3, Pallas kernels, cg_scalars(): pl.pallas_call(functools.partial(reduce_kernel, stages), out_shape=jax.Sh...  47 us
    unnamed x61, local copies, waits for them, and re-layouts  14.6 us
    ppermute x4, starting transfers between devices, from_behind(): lax.ppermute(value, axis, [(source, source + steps) for source in range(l...  12.1 us
    sub x2, other arithmetic, per_device(): residual = residual - alpha * image  11 us
    add x1, other arithmetic, per_device(): solution = solution + alpha * direction  9.23 us
    concatenate x1, local copies, waits for them, and re-layouts, grow(): return jnp.concatenate([stacked, right, left], axis=2)  7.63 us
    select_n x6, other arithmetic, cg_scalars(): tile = jnp.where(rows == k, local[k], tile)  7.2 us
    ppermute x4, waiting for transfers between devices, from_behind(): lax.ppermute(value, axis, [(source, source + steps) for source in range(l...  5.96 us
  transfers between devices with their start and end apart: 4, of which 3 were waited for; matrix products, arithmetic and copies ran while one was open for 0% of the time, Pallas kernels for 0%

profile of v11, /device:TPU:1, one launch (start us, length us, event | category | flops | bytes accessed | tf_op | source)
XLA Modules:
  0.0 146.1 jit_solution(2980554190675457509)
XLA Ops:
  0.7 1.4 bitcast_dynamic-update-slice_fusion.4
  3.9 4.9 %collective-permute-start = (f32[5,8,1024]{2,1,0:T(8,128)S(1)}, f32[5,8,1024]{2,1,0:T(8,128)S(1)}, u32[]{:S(2)}, u32[]{:S(2)}) collective-permute-start(f32[5,8,1024]{2,1,0:T(8,128)S(1)} %get-tuple-element.30), channel_id=1, source_target_pairs={{0,16},{16,32},{32,48},{48,64},{64,80},{80,96},{96,112},{1,17},{17... | collective-permute-start | bytes 491528 | tf_op jit(solution)/shard_map/ppermute | solution.py:25
  8.8 1.9 %collective-permute-start.1 = (f32[5,8,1024]{2,1,0:T(8,128)S(1)}, f32[5,8,1024]{2,1,0:T(8,128)S(1)}, u32[]{:S(2)}, u32[]{:S(2)}) collective-permute-start(f32[5,8,1024]{2,1,0:T(8,128)S(1)} %get-tuple-element.31), channel_id=1, source_target_pairs={{16,0},{32,16},{48,32},{64,48},{80,64},{96,80},{112,96},{17,1},{33... | collective-permute-start | bytes 491528 | tf_op jit(solution)/shard_map/ppermute | solution.py:25
  11.1 4.4 %collective-permute-done.1 = f32[5,8,1024]{2,1,0:T(8,128)S(1)} collective-permute-done((f32[5,8,1024]{2,1,0:T(8,128)S(1)}, f32[5,8,1024]{2,1,0:T(8,128)S(1)}, u32[]{:S(2)}, u32[]{:S(2)}) %collective-permute-start.1) | collective-permute-done | bytes 163872 | tf_op jit(solution)/shard_map/ppermute | solution.py:25
  16.4 2.4 %copy-done.12 = f32[5,272,1024]{2,1,0:T(8,128)} copy-done((f32[5,272,1024]{2,1,0:T(8,128)}, f32[5,272,1024]{2,1,0:T(8,128)S(1)}, u32[]{:S(2)}) %copy-start.12) | copy-done | bytes 5570584
  21.0 4.0 %collective-permute-start.3 = (f32[5,272,8]{1,2,0:T(8,128)S(1)}, f32[5,272,8]{1,2,0:T(8,128)S(1)}, u32[]{:S(2)}, u32[]{:S(2)}) collective-permute-start(f32[5,272,8]{1,2,0:T(8,128)S(1)} %copy.17), channel_id=1, source_target_pairs={{0,1},{1,2},{2,3},{3,4},{4,5},{5,6},{6,7},{7,8},{8,9},{9,10},{10,1... | collective-permute-start | bytes 130568 | tf_op jit(solution)/shard_map/ppermute | solution.py:25
  26.7 7.6 %concatenate.60 = f32[5,272,1040]{2,1,0:T(8,128)} concatenate(f32[5,272,1024]{2,1,0:T(8,128)} %copy-done.12, f32[5,272,8]{2,1,0:T(8,128)S(1)} %copy.18, f32[5,272,8]{2,1,0:T(8,128)S(1)} %copy.19), dimensions={2} | concatenate | bytes 11315200 | tf_op jit(solution)/shard_map/concatenate | solution.py:35
  34.4 2.4 %slice_bitcast_fusion.19 = (f32[271,1040]{1,0:T(8,128)S(1)}, f32[271,1040]{1,0:T(8,128)S(1)}, f32[271,1040]{1,0:T(8,128)S(1)}) fusion(f32[5,272,1040]{2,1,0:T(8,128)} %concatenate.60), kind=kLoop, calls=%fused_computation.65 | loop fusion | bytes 6764160 | tf_op jit(solution)/shard_map/slice | solution.py:43
  36.8 1.5 copy-done
  43.0 2.4 %fusion.1 = (f32[2,272,1040]{2,1,0:T(8,128)}, f32[2,272,1040]{2,1,0:T(8,128)S(1)}) fusion(f32[1,272,1040]{2,1,0:T(8,128)S(1)} %get-tuple-element.23, f32[1,272,1040]{2,1,0:T(8,128)S(1)} %get-tuple-element.18, f32[1,272,1040]{2,1,0:T(8,128)S(1)} %get-tuple-element.45, f32[1,272,1040]{2,1,0:T(8,128)S(1)} %get-tuple-element.44, ...), kind=kLoop, calls=%fused_computation.6 | loop fusion | flops 10749440 | bytes 15841280 | tf_op jit(solution)/shard_map/jit(_where)/select_n | solution.py:159
  48.4 1.4 multiply_reduce_fusion.4
  50.6 1.3 broadcast_select_fusion.local_ref
  52.6 20.8 %shard_map.76.prev_ref = f32[8,128]{1,0:T(8,128)} custom-call(f32[8,128]{1,0:T(8,128)} %broadcast_select_fusion.local_ref, f32[8,128]{1,0:T(8,128)} %iota.49.prev_ref), custom_call_target="tpu_custom_call" | custom-call | tf_op jit(solution)/shard_map/pallas_call | solution.py:127
  74.6 4.4 %multiply_subtract_fusion.1 = f32[2,272,1040]{2,1,0:T(8,128)S(1)} fusion(f32[2,272,1040]{2,1,0:T(8,128)S(1)} %get-tuple-element.37, f32[]{:T(128)} %bitcast.30, f32[1,272,1040]{2,1,0:T(8,128)} %copy-done.15, f32[1,272,1040]{2,1,0:T(8,128)} %copy-done.14, f32[1,272,1040]{2,1,0:T(8,128)} %copy-done.8, f32[1,272,1040]{2,1,0:T(8,128)} %copy-done.10, ...), kind=kLoop, calls=%fused_computation.21 | loop fusion | flops 7354880 | bytes 11315204 | tf_op jit(solution)/shard_map/sub | solution.py:173
  87.2 2.0 %select_select_fusion.1.local_ref = f32[8,128]{1,0:T(8,128)} fusion(f32[8]{0:T(128)S(1)} %fusion.29, f32[]{:T(128)} %get-tuple-element.10, f32[]{:T(128)} %get-tuple-element.9, pred[8]{0:T(512)(128)(4,1)S(1)} %get-tuple-element.54, pred[8]{0:T(512)(128)(4,1)S(1)} %get-tuple-element.55), kind=kLoop, calls=%fused_computation.110 | loop fusion | flops 2048 | bytes 4152 | tf_op jit(solution)/shard_map/jit(_where)/select_n | solution.py:126
  89.2 12.9 %shard_map.77.prev_ref = f32[8,128]{1,0:T(8,128)} custom-call(f32[8,128]{1,0:T(8,128)} %select_select_fusion.1.local_ref, f32[8,128]{1,0:T(8,128)} %shard_map.76.prev_ref), custom_call_target="tpu_custom_call" | custom-call | tf_op jit(solution)/shard_map/pallas_call | solution.py:127
  102.1 1.3 fusion.34
  103.4 6.5 %multiply_subtract_fusion = (f32[2,272,1040]{2,1,0:T(8,128)S(1)}, f32[2,272,1040]{2,1,0:T(8,128)S(1)}) fusion(f32[2,272,1040]{2,1,0:T(8,128)} %copy-done.1, f32[]{:T(128)} %bitcast.36, f32[]{:T(128)} %bitcast.37, f32[1,272,1040]{2,1,0:T(8,128)} %copy-done.21, f32[1,272,1040]{2,1,0:T(8,128)} %copy-done.20, f32[1,272,1040]{2,1,0:T(8,128)} %copy-done.8, ...), kind=kLoop, calls=%fused_computation.19 | loop fusion | flops 10749440 | bytes 18104328 | tf_op jit(solution)/shard_map/sub | solution.py:173
  113.7 1.5 %fusion.12 = (f32[]{:T(128)}, f32[]{:T(128)}, f32[]{:T(128)}) fusion(f32[2,272,1040]{2,1,0:T(8,128)S(1)} %get-tuple-element.15, f32[2,272,1040]{2,1,0:T(8,128)S(1)} %get-tuple-element.14, f32[1,272,1040]{2,1,0:T(8,128)S(1)} %get-tuple-element.39, f32[1,272,1040]{2,1,0:T(8,128)S(1)} %get-tuple-element.38, f32[2,272,1040]{2,1,0:T(8,128)S(1)} %copy-done.24, ...), kind=kLoop, calls=%fused_computation.30 | loop fusion | flops 5767165 | bytes 10817548 | tf_op jit(solution)/shard_map/reduce_sum | solution.py:148
  115.8 2.0 %select_select_fusion.local_ref = f32[8,128]{1,0:T(8,128)} fusion(f32[8]{0:T(128)S(1)} %fusion.28, f32[]{:T(128)} %get-tuple-element.8, f32[]{:T(128)} %get-tuple-element.6, pred[8]{0:T(512)(128)(4,1)S(1)} %get-tuple-element.54, pred[8]{0:T(512)(128)(4,1)S(1)} %get-tuple-element.55), kind=kLoop, calls=%fused_computation.109 | loop fusion | flops 2048 | bytes 4152 | tf_op jit(solution)/shard_map/jit(_where)/select_n | solution.py:126
  117.8 13.4 %shard_map.78 = f32[8,128]{1,0:T(8,128)} custom-call(f32[8,128]{1,0:T(8,128)} %select_select_fusion.local_ref, f32[8,128]{1,0:T(8,128)} %shard_map.77.prev_ref), custom_call_target="tpu_custom_call" | custom-call | tf_op jit(solution)/shard_map/pallas_call | solution.py:127
  132.5 9.2 %multiply_add_fusion = f32[2,272,1040]{2,1,0:T(8,128)S(1)} fusion(f32[2,272,1040]{2,1,0:T(8,128)} %copy-done.1, f32[2,272,1040]{2,1,0:T(8,128)S(1)} %get-tuple-element.37, f32[]{:T(128)} %bitcast.44, f32[]{:T(128)} %bitcast.43, f32[]{:T(128)} %bitcast.37, f32[]{:T(128)} %bitcast.36, f32[]{:T(128)} %bitcast.30, f32[2,272,1040]{2,1,0:T(8,128)} %copy-done.13, ...), kind=kLoop, calls=%fused_computation.18 | loop fusion | flops 10749440 | bytes 18104340 | tf_op jit(solution)/shard_map/add | solution.py:170
  141.8 1.6 %slice_bitcast_fusion.24 = (f32[256,1024]{1,0:T(8,128)}, f32[256,1024]{1,0:T(8,128)}) fusion(f32[2,272,1040]{2,1,0:T(8,128)S(1)} %multiply_add_fusion), kind=kLoop, calls=%fused_computation.93 | loop fusion | bytes 4194304 | tf_op jit(solution)/shard_map/squeeze | solution.py:181
  144.7 1.4 slice_subtract_fusion.1
  (125 shorter events, 32.0 us)
Async XLA Ops:
  0.6 1.5 %copy-start.25 = (f32[256,1024]{1,0:T(8,128)S(1)}, f32[256,1024]{1,0:T(8,128)}, u32[]{:S(2)}) copy-start(f32[256,1024]{1,0:T(8,128)} %param.6) | copy-start | bytes 3145732
  0.6 1.8 %copy-start.26 = (s32[256,1024]{1,0:T(8,128)S(1)}, s32[256,1024]{1,0:T(8,128)}, u32[]{:S(2)}) copy-start(s32[256,1024]{1,0:T(8,128)} %param.7) | copy-start | bytes 3145732
  3.9 7.2 %collective-permute-start = (f32[5,8,1024]{2,1,0:T(8,128)S(1)}, f32[5,8,1024]{2,1,0:T(8,128)S(1)}, u32[]{:S(2)}, u32[]{:S(2)}) collective-permute-start(f32[5,8,1024]{2,1,0:T(8,128)S(1)} %get-tuple-element.30), channel_id=1, source_target_pairs={{0,16},{16,32},{32,48},{48,64},{64,80},{80,96},{96,112},{1,17},{17... | collective-permute-start | bytes 491528 | tf_op jit(solution)/shard_map/ppermute | solution.py:25
  8.8 6.6 %collective-permute-start.1 = (f32[5,8,1024]{2,1,0:T(8,128)S(1)}, f32[5,8,1024]{2,1,0:T(8,128)S(1)}, u32[]{:S(2)}, u32[]{:S(2)}) collective-permute-start(f32[5,8,1024]{2,1,0:T(8,128)S(1)} %get-tuple-element.31), channel_id=1, source_target_pairs={{16,0},{32,16},{48,32},{64,48},{80,64},{96,80},{112,96},{17,1},{33... | collective-permute-start | bytes 491528 | tf_op jit(solution)/shard_map/ppermute | solution.py:25
  16.4 2.4 %copy-start.12 = (f32[5,272,1024]{2,1,0:T(8,128)}, f32[5,272,1024]{2,1,0:T(8,128)S(1)}, u32[]{:S(2)}) copy-start(f32[5,272,1024]{2,1,0:T(8,128)S(1)} %pad_maximum_fusion) | copy-start | bytes 16711684
  19.6 6.8 %collective-permute-start.2 = (f32[5,272,8]{1,2,0:T(8,128)S(1)}, f32[5,272,8]{1,2,0:T(8,128)S(1)}, u32[]{:S(2)}, u32[]{:S(2)}) collective-permute-start(f32[5,272,8]{1,2,0:T(8,128)S(1)} %copy.16), channel_id=1, source_target_pairs={{1,0},{2,1},{3,2},{4,3},{5,4},{6,5},{7,6},{8,7},{9,8},{10,9},{11,1... | collective-permute-start | bytes 130568 | tf_op jit(solution)/shard_map/ppermute | solution.py:25
  21.0 5.3 %collective-permute-start.3 = (f32[5,272,8]{1,2,0:T(8,128)S(1)}, f32[5,272,8]{1,2,0:T(8,128)S(1)}, u32[]{:S(2)}, u32[]{:S(2)}) collective-permute-start(f32[5,272,8]{1,2,0:T(8,128)S(1)} %copy.17), channel_id=1, source_target_pairs={{0,1},{1,2},{2,3},{3,4},{4,5},{5,6},{6,7},{7,8},{8,9},{9,10},{10,1... | collective-permute-start | bytes 130568 | tf_op jit(solution)/shard_map/ppermute | solution.py:25
  34.4 3.9 %copy-start = (f32[5,272,1040]{2,1,0:T(8,128)S(1)}, f32[5,272,1040]{2,1,0:T(8,128)}, u32[]{:S(2)}) copy-start(f32[5,272,1040]{2,1,0:T(8,128)} %concatenate.60) | copy-start | bytes 16972804
  40.2 2.9 %copy-start.16 = (f32[1,272,1040]{2,1,0:T(8,128)}, f32[1,272,1040]{2,1,0:T(8,128)S(1)}, u32[]{:S(2)}) copy-start(f32[1,272,1040]{2,1,0:T(8,128)S(1)} %get-tuple-element.24) | copy-start | bytes 3394564
  40.2 6.8 %copy-start.2 = (f32[1,272,1040]{2,1,0:T(8,128)}, f32[1,272,1040]{2,1,0:T(8,128)S(1)}, u32[]{:S(2)}) copy-start(f32[1,272,1040]{2,1,0:T(8,128)S(1)} %get-tuple-element.22) | copy-start | bytes 3394564
  40.2 6.8 %copy-start.8 = (f32[1,272,1040]{2,1,0:T(8,128)}, f32[1,272,1040]{2,1,0:T(8,128)S(1)}, u32[]{:S(2)}) copy-start(f32[1,272,1040]{2,1,0:T(8,128)S(1)} %get-tuple-element.23) | copy-start | bytes 3394564
  40.7 2.3 %copy-start.17 = (f32[1,272,1040]{2,1,0:T(8,128)}, f32[1,272,1040]{2,1,0:T(8,128)S(1)}, u32[]{:S(2)}) copy-start(f32[1,272,1040]{2,1,0:T(8,128)S(1)} %get-tuple-element.17) | copy-start | bytes 3394564
  40.7 6.3 %copy-start.5 = (f32[1,272,1040]{2,1,0:T(8,128)}, f32[1,272,1040]{2,1,0:T(8,128)S(1)}, u32[]{:S(2)}) copy-start(f32[1,272,1040]{2,1,0:T(8,128)S(1)} %get-tuple-element.16) | copy-start | bytes 3394564
  40.7 6.3 %copy-start.10 = (f32[1,272,1040]{2,1,0:T(8,128)}, f32[1,272,1040]{2,1,0:T(8,128)S(1)}, u32[]{:S(2)}) copy-start(f32[1,272,1040]{2,1,0:T(8,128)S(1)} %get-tuple-element.18) | copy-start | bytes 3394564
  79.0 5.4 %copy-start.1 = (f32[2,272,1040]{2,1,0:T(8,128)}, f32[2,272,1040]{2,1,0:T(8,128)S(1)}, u32[]{:S(2)}) copy-start(f32[2,272,1040]{2,1,0:T(8,128)S(1)} %multiply_subtract_fusion.1) | copy-start | bytes 6789124
  80.3 2.4 %copy-start.6 = (f32[1,272,1040]{2,1,0:T(8,128)S(1)}, f32[1,272,1040]{2,1,0:T(8,128)}, u32[]{:S(2)}) copy-start(f32[1,272,1040]{2,1,0:T(8,128)} %copy-done.5) | copy-start | bytes 3394564
  80.3 2.9 %copy-start.9 = (f32[1,272,1040]{2,1,0:T(8,128)S(1)}, f32[1,272,1040]{2,1,0:T(8,128)}, u32[]{:S(2)}) copy-start(f32[1,272,1040]{2,1,0:T(8,128)} %copy-done.8) | copy-start | bytes 3394564
  80.3 3.3 %copy-start.11 = (f32[1,272,1040]{2,1,0:T(8,128)S(1)}, f32[1,272,1040]{2,1,0:T(8,128)}, u32[]{:S(2)}) copy-start(f32[1,272,1040]{2,1,0:T(8,128)} %copy-done.10) | copy-start | bytes 3394564
  80.7 3.7 %copy-start.20 = (f32[1,272,1040]{2,1,0:T(8,128)}, f32[1,272,1040]{2,1,0:T(8,128)S(1)}, u32[]{:S(2)}) copy-start(f32[1,272,1040]{2,1,0:T(8,128)S(1)} %get-tuple-element.40) | copy-start | bytes 3394564
  80.7 3.7 %copy-start.21 = (f32[1,272,1040]{2,1,0:T(8,128)}, f32[1,272,1040]{2,1,0:T(8,128)S(1)}, u32[]{:S(2)}) copy-start(f32[1,272,1040]{2,1,0:T(8,128)S(1)} %get-tuple-element.41) | copy-start | bytes 3394564
  83.6 1.7 %copy-start.19 = (f32[2,272,1040]{2,1,0:T(8,128)S(1)}, f32[2,272,1040]{2,1,0:T(8,128)}, u32[]{:S(2)}) copy-start(f32[2,272,1040]{2,1,0:T(8,128)} %copy-done.18) | copy-start | bytes 6789124
  110.0 1.6 %copy-start.13 = (f32[2,272,1040]{2,1,0:T(8,128)}, f32[2,272,1040]{2,1,0:T(8,128)S(1)}, u32[]{:S(2)}) copy-start(f32[2,272,1040]{2,1,0:T(8,128)S(1)} %get-tuple-element.15) | copy-start | bytes 6789124
  111.2 1.7 %copy-start.7 = (f32[1,272,1040]{2,1,0:T(8,128)S(1)}, f32[1,272,1040]{2,1,0:T(8,128)}, u32[]{:S(2)}) copy-start(f32[1,272,1040]{2,1,0:T(8,128)} %copy-done.5) | copy-start | bytes 3394564
  111.2 2.5 %copy-start.24 = (f32[2,272,1040]{2,1,0:T(8,128)S(1)}, f32[2,272,1040]{2,1,0:T(8,128)}, u32[]{:S(2)}) copy-start(f32[2,272,1040]{2,1,0:T(8,128)} %get-tuple-element.36) | copy-start | bytes 6789124
  (9 other events, 11.8 us)

commit v12 on v11

--- a/solution.py
+++ b/solution.py
@@ -29,10 +29,11 @@
     rows, cols = MARGIN_ROWS, MARGIN_COLS
     above = from_behind(stacked[:, :rows, :], "lat", -1)
     below = from_behind(stacked[:, -rows:, :], "lat", 1)
-    stacked = jnp.concatenate([below, stacked, above], axis=1)
-    right = from_behind(stacked[:, :, :cols], "lon", -1)
-    left = from_behind(stacked[:, :, -cols:], "lon", 1)
-    return jnp.concatenate([stacked, right, left], axis=2)
+    width = stacked.shape[2]
+    wide = lax.optimization_barrier(jnp.pad(jnp.concatenate([below, stacked, above], axis=1), ((0, 0), (0, 0), (0, 2 * cols))))
+    right = from_behind(wide[:, :, :cols], "lon", -1)
+    left = from_behind(wide[:, :, width - cols : width], "lon", 1)
+    return lax.dynamic_update_slice(wide, jnp.concatenate([right, left], axis=2), (0, 0, width))
 
 
 def east(field):

time: 147 us -> 139 us (0.946)
  local copies, waits for them, and re-layouts: 36.9 us -> 30.2 us
  Pallas kernels: 47 us -> 44.3 us
  waiting for transfers between devices: 5.96 us -> 8.34 us
    concatenate x1, local copies, waits for them, and re-layouts: 7.63 us -> 0.24 us  [grow(): jnp.concatenate([right, left], axis=2)]
    pallas_call x3, Pallas kernels: 47 us -> 44.3 us  [cg_scalars(): pl.pallas_call(functools.partial(reduce_kernel, stages), out_shape=jax.Sh...]
    ppermute x4, waiting for transfers between devices: 5.96 us -> 8.34 us  [from_behind(): lax.ppermute(value, axis, [(source, source + steps) for source in range(l...]
where the time goes in v12:
time: 139 us; the launch traced here: 138 us
  Pallas kernels  44.3 us (32%)
  other arithmetic  42.7 us (31%)
  local copies, waits for them, and re-layouts  30.2 us (22%)
  starting transfers between devices  11.4 us (8%)
  waiting for transfers between devices  8.34 us (6%)
    pallas_call x3, Pallas kernels, cg_scalars(): pl.pallas_call(functools.partial(reduce_kernel, stages), out_shape=jax.Sh...  44.3 us
    unnamed x61, local copies, waits for them, and re-layouts  14.8 us
    ppermute x4, starting transfers between devices, from_behind(): lax.ppermute(value, axis, [(source, source + steps) for source in range(l...  11.4 us
    sub x2, other arithmetic, per_device(): residual = residual - alpha * image  10.8 us
    add x1, other arithmetic, per_device(): solution = solution + alpha * direction  9.23 us
    ppermute x4, waiting for transfers between devices, from_behind(): lax.ppermute(value, axis, [(source, source + steps) for source in range(l...  8.34 us
    select_n x6, other arithmetic, cg_scalars(): tile = jnp.where(rows == k, local[k], tile)  7.2 us
    reduce_sum x3, other arithmetic, dots(): return jnp.stack([jnp.sum(interior(x) * interior(y)) for x, y in pairs])  4.22 us
  transfers between devices with their start and end apart: 4, of which 3 were waited for; matrix products, arithmetic and copies ran while one was open for 0% of the time, Pallas kernels for 0%

profile of v12, /device:TPU:1, one launch (start us, length us, event | category | flops | bytes accessed | tf_op | source)
XLA Modules:
  0.0 138.2 jit_solution(11969329785166982625)
XLA Ops:
  0.7 1.4 %bitcast_dynamic-update-slice_fusion.4 = f32[5,256,1024]{2,1,0:T(8,128)S(1)} fusion(f32[256,1024]{1,0:T(8,128)} %param.5), kind=kLoop, calls=%fused_computation.107 | loop fusion | bytes 2097152
  3.9 4.9 %collective-permute-start = (f32[5,8,1024]{2,1,0:T(8,128)S(1)}, f32[5,8,1024]{2,1,0:T(8,128)S(1)}, u32[]{:S(2)}, u32[]{:S(2)}) collective-permute-start(f32[5,8,1024]{2,1,0:T(8,128)S(1)} %get-tuple-element.30), channel_id=1, source_target_pairs={{0,16},{16,32},{32,48},{48,64},{64,80},{80,96},{96,112},{1,17},{17... | collective-permute-start | bytes 491528 | tf_op jit(solution)/shard_map/ppermute | solution.py:25
  8.8 1.9 %collective-permute-start.1 = (f32[5,8,1024]{2,1,0:T(8,128)S(1)}, f32[5,8,1024]{2,1,0:T(8,128)S(1)}, u32[]{:S(2)}, u32[]{:S(2)}) collective-permute-start(f32[5,8,1024]{2,1,0:T(8,128)S(1)} %get-tuple-element.31), channel_id=1, source_target_pairs={{16,0},{32,16},{48,32},{64,48},{80,64},{96,80},{112,96},{17,1},{33... | collective-permute-start | bytes 491528 | tf_op jit(solution)/shard_map/ppermute | solution.py:25
  11.1 4.4 %collective-permute-done.1 = f32[5,8,1024]{2,1,0:T(8,128)S(1)} collective-permute-done((f32[5,8,1024]{2,1,0:T(8,128)S(1)}, f32[5,8,1024]{2,1,0:T(8,128)S(1)}, u32[]{:S(2)}, u32[]{:S(2)}) %collective-permute-start.1) | collective-permute-done | bytes 163872 | tf_op jit(solution)/shard_map/ppermute | solution.py:25
  16.3 2.6 %copy-done = f32[5,272,1040]{2,1,0:T(8,128)} copy-done((f32[5,272,1040]{2,1,0:T(8,128)}, f32[5,272,1040]{2,1,0:T(8,128)S(1)}, u32[]{:S(2)}) %copy-start) | copy-done | bytes 5657624
  19.8 3.2 %collective-permute-start.3 = (f32[5,272,8]{1,2,0:T(8,128)S(1)}, f32[5,272,8]{1,2,0:T(8,128)S(1)}, u32[]{:S(2)}, u32[]{:S(2)}) collective-permute-start(f32[5,272,8]{1,2,0:T(8,128)S(1)} %copy.17), channel_id=1, source_target_pairs={{0,1},{1,2},{2,3},{3,4},{4,5},{5,6},{6,7},{7,8},{8,9},{9,10},{10,1... | collective-permute-start | bytes 130568 | tf_op jit(solution)/shard_map/ppermute | solution.py:25
  24.3 3.6 %collective-permute-done.2 = f32[5,272,8]{1,2,0:T(8,128)S(1)} collective-permute-done((f32[5,272,8]{1,2,0:T(8,128)S(1)}, f32[5,272,8]{1,2,0:T(8,128)S(1)}, u32[]{:S(2)}, u32[]{:S(2)}) %collective-permute-start.2) | collective-permute-done | bytes 43552 | tf_op jit(solution)/shard_map/ppermute | solution.py:25
  29.2 2.4 %slice_bitcast_fusion.19 = (f32[271,1040]{1,0:T(8,128)S(1)}, f32[271,1040]{1,0:T(8,128)S(1)}, f32[271,1040]{1,0:T(8,128)S(1)}) fusion(f32[5,272,1040]{2,1,0:T(8,128)} %constant_dynamic-update-slice_fusion), kind=kLoop, calls=%fused_computation.67 | loop fusion | bytes 6764160 | tf_op jit(solution)/shard_map/slice | solution.py:44
  31.7 1.5 %copy-done.1 = f32[5,272,1040]{2,1,0:T(8,128)S(1)} copy-done((f32[5,272,1040]{2,1,0:T(8,128)S(1)}, f32[5,272,1040]{2,1,0:T(8,128)}, u32[]{:S(2)}) %copy-start.1) | copy-done | bytes 5657624
  37.9 2.6 %fusion.1 = (f32[2,272,1040]{2,1,0:T(8,128)}, f32[2,272,1040]{2,1,0:T(8,128)S(1)}) fusion(f32[1,272,1040]{2,1,0:T(8,128)S(1)} %get-tuple-element.23, f32[1,272,1040]{2,1,0:T(8,128)S(1)} %get-tuple-element.18, f32[1,272,1040]{2,1,0:T(8,128)S(1)} %get-tuple-element.45, f32[1,272,1040]{2,1,0:T(8,128)S(1)} %get-tuple-element.44, ...), kind=kLoop, calls=%fused_computation.8 | loop fusion | flops 10749440 | bytes 15841280 | tf_op jit(solution)/shard_map/jit(_where)/select_n | solution.py:160
  43.4 1.4 %multiply_reduce_fusion.4 = (f32[]{:T(128)}, f32[]{:T(128)}) fusion(f32[2,272,1040]{2,1,0:T(8,128)S(1)} %fusion.5, f32[2,272,1040]{2,1,0:T(8,128)S(1)} %get-tuple-element.37), kind=kLoop, calls=%fused_computation.39 | loop fusion | flops 2097150 | bytes 4194312 | tf_op jit(solution)/shard_map/reduce_sum | solution.py:149
  45.6 1.3 broadcast_select_fusion.local_ref
  47.6 17.8 %shard_map.76.prev_ref = f32[8,128]{1,0:T(8,128)} custom-call(f32[8,128]{1,0:T(8,128)} %broadcast_select_fusion.local_ref, f32[8,128]{1,0:T(8,128)} %iota.49.prev_ref), custom_call_target="tpu_custom_call" | custom-call | tf_op jit(solution)/shard_map/pallas_call | solution.py:128
  66.6 4.2 %multiply_subtract_fusion.1 = f32[2,272,1040]{2,1,0:T(8,128)S(1)} fusion(f32[2,272,1040]{2,1,0:T(8,128)S(1)} %get-tuple-element.37, f32[]{:T(128)} %bitcast.30, f32[1,272,1040]{2,1,0:T(8,128)} %copy-done.15, f32[1,272,1040]{2,1,0:T(8,128)} %copy-done.14, f32[1,272,1040]{2,1,0:T(8,128)} %copy-done.9, f32[1,272,1040]{2,1,0:T(8,128)} %copy-done.11, ...), kind=kLoop, calls=%fused_computation.23 | loop fusion | flops 7354880 | bytes 11315204 | tf_op jit(solution)/shard_map/sub | solution.py:174
  79.0 2.0 %select_select_fusion.1.local_ref = f32[8,128]{1,0:T(8,128)} fusion(f32[8]{0:T(128)S(1)} %fusion.29, f32[]{:T(128)} %get-tuple-element.10, f32[]{:T(128)} %get-tuple-element.9, pred[8]{0:T(512)(128)(4,1)S(1)} %get-tuple-element.54, pred[8]{0:T(512)(128)(4,1)S(1)} %get-tuple-element.55), kind=kLoop, calls=%fused_computation.113 | loop fusion | flops 2048 | bytes 4152 | tf_op jit(solution)/shard_map/jit(_where)/select_n | solution.py:127
  81.0 13.0 %shard_map.77.prev_ref = f32[8,128]{1,0:T(8,128)} custom-call(f32[8,128]{1,0:T(8,128)} %select_select_fusion.1.local_ref, f32[8,128]{1,0:T(8,128)} %shard_map.76.prev_ref), custom_call_target="tpu_custom_call" | custom-call | tf_op jit(solution)/shard_map/pallas_call | solution.py:128
  94.0 1.3 fusion.34
  95.4 6.5 %multiply_subtract_fusion = (f32[2,272,1040]{2,1,0:T(8,128)S(1)}, f32[2,272,1040]{2,1,0:T(8,128)S(1)}) fusion(f32[2,272,1040]{2,1,0:T(8,128)} %copy-done.2, f32[]{:T(128)} %bitcast.36, f32[]{:T(128)} %bitcast.37, f32[1,272,1040]{2,1,0:T(8,128)} %copy-done.21, f32[1,272,1040]{2,1,0:T(8,128)} %copy-done.20, f32[1,272,1040]{2,1,0:T(8,128)} %copy-done.9, ...), kind=kLoop, calls=%fused_computation.21 | loop fusion | flops 10749440 | bytes 18104328 | tf_op jit(solution)/shard_map/sub | solution.py:174
  105.6 1.5 %fusion.12 = (f32[]{:T(128)}, f32[]{:T(128)}, f32[]{:T(128)}) fusion(f32[2,272,1040]{2,1,0:T(8,128)S(1)} %get-tuple-element.15, f32[2,272,1040]{2,1,0:T(8,128)S(1)} %get-tuple-element.14, f32[1,272,1040]{2,1,0:T(8,128)S(1)} %get-tuple-element.39, f32[1,272,1040]{2,1,0:T(8,128)S(1)} %get-tuple-element.38, f32[2,272,1040]{2,1,0:T(8,128)S(1)} %copy-done.24, ...), kind=kLoop, calls=%fused_computation.32 | loop fusion | flops 5767165 | bytes 10817548 | tf_op jit(solution)/shard_map/reduce_sum | solution.py:149
  107.8 2.0 %select_select_fusion.local_ref = f32[8,128]{1,0:T(8,128)} fusion(f32[8]{0:T(128)S(1)} %fusion.28, f32[]{:T(128)} %get-tuple-element.8, f32[]{:T(128)} %get-tuple-element.6, pred[8]{0:T(512)(128)(4,1)S(1)} %get-tuple-element.54, pred[8]{0:T(512)(128)(4,1)S(1)} %get-tuple-element.55), kind=kLoop, calls=%fused_computation.112 | loop fusion | flops 2048 | bytes 4152 | tf_op jit(solution)/shard_map/jit(_where)/select_n | solution.py:127
  109.7 13.5 %shard_map.78 = f32[8,128]{1,0:T(8,128)} custom-call(f32[8,128]{1,0:T(8,128)} %select_select_fusion.local_ref, f32[8,128]{1,0:T(8,128)} %shard_map.77.prev_ref), custom_call_target="tpu_custom_call" | custom-call | tf_op jit(solution)/shard_map/pallas_call | solution.py:128
  124.5 9.2 %multiply_add_fusion = f32[2,272,1040]{2,1,0:T(8,128)S(1)} fusion(f32[2,272,1040]{2,1,0:T(8,128)} %copy-done.2, f32[2,272,1040]{2,1,0:T(8,128)S(1)} %get-tuple-element.37, f32[]{:T(128)} %bitcast.44, f32[]{:T(128)} %bitcast.43, f32[]{:T(128)} %bitcast.37, f32[]{:T(128)} %bitcast.36, f32[]{:T(128)} %bitcast.30, f32[2,272,1040]{2,1,0:T(8,128)} %copy-done.13, ...), kind=kLoop, calls=%fused_computation.20 | loop fusion | flops 10749440 | bytes 18104340 | tf_op jit(solution)/shard_map/add | solution.py:171
  133.9 1.6 %slice_bitcast_fusion.24 = (f32[256,1024]{1,0:T(8,128)}, f32[256,1024]{1,0:T(8,128)}) fusion(f32[2,272,1040]{2,1,0:T(8,128)S(1)} %multiply_add_fusion), kind=kLoop, calls=%fused_computation.95 | loop fusion | bytes 4194304 | tf_op jit(solution)/shard_map/squeeze | solution.py:182
  136.7 1.4 %slice_subtract_fusion.1 = f32[256,1024]{1,0:T(8,128)} fusion(f32[272,1040]{1,0:T(8,128)S(1)} %copy-done.23, f32[271,1040]{1,0:T(8,128)S(1)} %slice_bitcast_fusion, f32[272,1040]{1,0:T(8,128)S(1)} %get-tuple-element.35, f32[272,1040]{1,0:T(8,128)S(1)} %get-tuple-element.34, f32[272,1039]{1,0:T(8,128)S(1)} %bitcast.130, f32[272,1]{1,0:T(8,128)S(1)} %slice.402), kind=kLoop, calls=%fused_computation.97 | loop fusion | flops 1572864 | bytes 6453184 | tf_op jit(solution)/shard_map/sub | solution.py:180
  (125 shorter events, 31.4 us)
Async XLA Ops:
  0.6 1.5 %copy-start.25 = (f32[256,1024]{1,0:T(8,128)S(1)}, f32[256,1024]{1,0:T(8,128)}, u32[]{:S(2)}) copy-start(f32[256,1024]{1,0:T(8,128)} %param.6) | copy-start | bytes 3145732
  0.6 1.8 %copy-start.26 = (s32[256,1024]{1,0:T(8,128)S(1)}, s32[256,1024]{1,0:T(8,128)}, u32[]{:S(2)}) copy-start(s32[256,1024]{1,0:T(8,128)} %param.7) | copy-start | bytes 3145732
  3.9 7.2 %collective-permute-start = (f32[5,8,1024]{2,1,0:T(8,128)S(1)}, f32[5,8,1024]{2,1,0:T(8,128)S(1)}, u32[]{:S(2)}, u32[]{:S(2)}) collective-permute-start(f32[5,8,1024]{2,1,0:T(8,128)S(1)} %get-tuple-element.30), channel_id=1, source_target_pairs={{0,16},{16,32},{32,48},{48,64},{64,80},{80,96},{96,112},{1,17},{17... | collective-permute-start | bytes 491528 | tf_op jit(solution)/shard_map/ppermute | solution.py:25
  8.8 6.6 %collective-permute-start.1 = (f32[5,8,1024]{2,1,0:T(8,128)S(1)}, f32[5,8,1024]{2,1,0:T(8,128)S(1)}, u32[]{:S(2)}, u32[]{:S(2)}) collective-permute-start(f32[5,8,1024]{2,1,0:T(8,128)S(1)} %get-tuple-element.31), channel_id=1, source_target_pairs={{16,0},{32,16},{48,32},{64,48},{80,64},{96,80},{112,96},{17,1},{33... | collective-permute-start | bytes 491528 | tf_op jit(solution)/shard_map/ppermute | solution.py:25
  16.3 2.6 %copy-start = (f32[5,272,1040]{2,1,0:T(8,128)}, f32[5,272,1040]{2,1,0:T(8,128)S(1)}, u32[]{:S(2)}) copy-start(f32[5,272,1040]{2,1,0:T(8,128)S(1)} %select_maximum_fusion) | copy-start | bytes 16972804
  19.8 4.5 %collective-permute-start.3 = (f32[5,272,8]{1,2,0:T(8,128)S(1)}, f32[5,272,8]{1,2,0:T(8,128)S(1)}, u32[]{:S(2)}, u32[]{:S(2)}) collective-permute-start(f32[5,272,8]{1,2,0:T(8,128)S(1)} %copy.17), channel_id=1, source_target_pairs={{0,1},{1,2},{2,3},{3,4},{4,5},{5,6},{6,7},{7,8},{8,9},{9,10},{10,1... | collective-permute-start | bytes 130568 | tf_op jit(solution)/shard_map/ppermute | solution.py:25
  23.0 5.0 %collective-permute-start.2 = (f32[5,272,8]{1,2,0:T(8,128)S(1)}, f32[5,272,8]{1,2,0:T(8,128)S(1)}, u32[]{:S(2)}, u32[]{:S(2)}) collective-permute-start(f32[5,272,8]{1,2,0:T(8,128)S(1)} %copy.16), channel_id=1, source_target_pairs={{1,0},{2,1},{3,2},{4,3},{5,4},{6,5},{7,6},{8,7},{9,8},{10,9},{11,1... | collective-permute-start | bytes 130568 | tf_op jit(solution)/shard_map/ppermute | solution.py:25
  29.2 3.9 %copy-start.1 = (f32[5,272,1040]{2,1,0:T(8,128)S(1)}, f32[5,272,1040]{2,1,0:T(8,128)}, u32[]{:S(2)}) copy-start(f32[5,272,1040]{2,1,0:T(8,128)} %constant_dynamic-update-slice_fusion) | copy-start | bytes 16972804
  35.0 2.9 %copy-start.16 = (f32[1,272,1040]{2,1,0:T(8,128)}, f32[1,272,1040]{2,1,0:T(8,128)S(1)}, u32[]{:S(2)}) copy-start(f32[1,272,1040]{2,1,0:T(8,128)S(1)} %get-tuple-element.24) | copy-start | bytes 3394564
  35.0 7.0 %copy-start.3 = (f32[1,272,1040]{2,1,0:T(8,128)}, f32[1,272,1040]{2,1,0:T(8,128)S(1)}, u32[]{:S(2)}) copy-start(f32[1,272,1040]{2,1,0:T(8,128)S(1)} %get-tuple-element.22) | copy-start | bytes 3394564
  35.0 7.0 %copy-start.9 = (f32[1,272,1040]{2,1,0:T(8,128)}, f32[1,272,1040]{2,1,0:T(8,128)S(1)}, u32[]{:S(2)}) copy-start(f32[1,272,1040]{2,1,0:T(8,128)S(1)} %get-tuple-element.23) | copy-start | bytes 3394564
  35.5 2.3 %copy-start.17 = (f32[1,272,1040]{2,1,0:T(8,128)}, f32[1,272,1040]{2,1,0:T(8,128)S(1)}, u32[]{:S(2)}) copy-start(f32[1,272,1040]{2,1,0:T(8,128)S(1)} %get-tuple-element.17) | copy-start | bytes 3394564
  35.5 6.5 %copy-start.6 = (f32[1,272,1040]{2,1,0:T(8,128)}, f32[1,272,1040]{2,1,0:T(8,128)S(1)}, u32[]{:S(2)}) copy-start(f32[1,272,1040]{2,1,0:T(8,128)S(1)} %get-tuple-element.16) | copy-start | bytes 3394564
  35.5 6.5 %copy-start.11 = (f32[1,272,1040]{2,1,0:T(8,128)}, f32[1,272,1040]{2,1,0:T(8,128)S(1)}, u32[]{:S(2)}) copy-start(f32[1,272,1040]{2,1,0:T(8,128)S(1)} %get-tuple-element.18) | copy-start | bytes 3394564
  70.8 5.4 %copy-start.2 = (f32[2,272,1040]{2,1,0:T(8,128)}, f32[2,272,1040]{2,1,0:T(8,128)S(1)}, u32[]{:S(2)}) copy-start(f32[2,272,1040]{2,1,0:T(8,128)S(1)} %multiply_subtract_fusion.1) | copy-start | bytes 6789124
  72.1 2.4 %copy-start.7 = (f32[1,272,1040]{2,1,0:T(8,128)S(1)}, f32[1,272,1040]{2,1,0:T(8,128)}, u32[]{:S(2)}) copy-start(f32[1,272,1040]{2,1,0:T(8,128)} %copy-done.6) | copy-start | bytes 3394564
  72.1 2.9 %copy-start.10 = (f32[1,272,1040]{2,1,0:T(8,128)S(1)}, f32[1,272,1040]{2,1,0:T(8,128)}, u32[]{:S(2)}) copy-start(f32[1,272,1040]{2,1,0:T(8,128)} %copy-done.9) | copy-start | bytes 3394564
  72.1 3.3 %copy-start.12 = (f32[1,272,1040]{2,1,0:T(8,128)S(1)}, f32[1,272,1040]{2,1,0:T(8,128)}, u32[]{:S(2)}) copy-start(f32[1,272,1040]{2,1,0:T(8,128)} %copy-done.11) | copy-start | bytes 3394564
  72.5 3.7 %copy-start.20 = (f32[1,272,1040]{2,1,0:T(8,128)}, f32[1,272,1040]{2,1,0:T(8,128)S(1)}, u32[]{:S(2)}) copy-start(f32[1,272,1040]{2,1,0:T(8,128)S(1)} %get-tuple-element.40) | copy-start | bytes 3394564
  72.5 3.7 %copy-start.21 = (f32[1,272,1040]{2,1,0:T(8,128)}, f32[1,272,1040]{2,1,0:T(8,128)S(1)}, u32[]{:S(2)}) copy-start(f32[1,272,1040]{2,1,0:T(8,128)S(1)} %get-tuple-element.41) | copy-start | bytes 3394564
  75.4 1.7 %copy-start.19 = (f32[2,272,1040]{2,1,0:T(8,128)S(1)}, f32[2,272,1040]{2,1,0:T(8,128)}, u32[]{:S(2)}) copy-start(f32[2,272,1040]{2,1,0:T(8,128)} %copy-done.18) | copy-start | bytes 6789124
  101.9 1.6 %copy-start.13 = (f32[2,272,1040]{2,1,0:T(8,128)}, f32[2,272,1040]{2,1,0:T(8,128)S(1)}, u32[]{:S(2)}) copy-start(f32[2,272,1040]{2,1,0:T(8,128)S(1)} %get-tuple-element.15) | copy-start | bytes 6789124
  103.2 1.7 %copy-start.8 = (f32[1,272,1040]{2,1,0:T(8,128)S(1)}, f32[1,272,1040]{2,1,0:T(8,128)}, u32[]{:S(2)}) copy-start(f32[1,272,1040]{2,1,0:T(8,128)} %copy-done.6) | copy-start | bytes 3394564
  103.2 2.5 %copy-start.24 = (f32[2,272,1040]{2,1,0:T(8,128)S(1)}, f32[2,272,1040]{2,1,0:T(8,128)}, u32[]{:S(2)}) copy-start(f32[2,272,1040]{2,1,0:T(8,128)} %get-tuple-element.36) | copy-start | bytes 6789124
  (9 other events, 11.8 us)

commit v13 on v12

--- a/solution.py
+++ b/solution.py
@@ -66,7 +66,8 @@
     return tuple((axis, 1, sizes[axis]) for axis in ("lon", "lat") if sizes[axis] > 1)
 
 
-def reduce_kernel(stages, local_ref, prev_ref, out_ref, parts, got, send_sem, recv_sem):
+def reduce_kernel(stages, count, *refs):
+    partial_refs, (prev_ref, out_ref, parts, got, send_sem, recv_sem) = refs[:count], refs[count:]
     me = {"lat": lax.axis_index("lat"), "lon": lax.axis_index("lon")}
 
     def partner(axis, stride, members, offset):
@@ -83,7 +84,11 @@
             greeted += 1
     pl.semaphore_wait(barrier, greeted)
 
-    value = local_ref[...]
+    rows = lax.broadcasted_iota(jnp.int32, (8, 128), 0)
+    value = jnp.zeros((8, 128), jnp.float32)
+    for k, partial_ref in enumerate(partial_refs):
+        total = jnp.sum(jnp.sum(partial_ref[...], axis=1, keepdims=True), axis=0, keepdims=True)
+        value = jnp.where(rows == k, total, value)
     for stage, (axis, stride, members) in enumerate(stages):
         parts[stage] = value
         got[stage, 0] = value
@@ -117,18 +122,14 @@
     out_ref[3:4] = curve
 
 
-def cg_scalars(local, previous):
+def cg_scalars(partials, previous):
     sizes = {"lat": lax.axis_size("lat"), "lon": lax.axis_size("lon")}
     stages = stages_of(sizes)
     widest = max(members for _, _, members in stages)
-    rows = lax.broadcasted_iota(jnp.int32, (8, 128), 0)
-    tile = jnp.zeros((8, 128), jnp.float32)
-    for k in range(local.shape[0]):
-        tile = jnp.where(rows == k, local[k], tile)
     return pl.pallas_call(
-        functools.partial(reduce_kernel, stages),
+        functools.partial(reduce_kernel, stages, len(partials)),
         out_shape=jax.ShapeDtypeStruct((8, 128), jnp.float32),
-        in_specs=[pl.BlockSpec(memory_space=pltpu.VMEM)] * 2,
+        in_specs=[pl.BlockSpec(memory_space=pltpu.VMEM)] * (len(partials) + 1),
         out_specs=pl.BlockSpec(memory_space=pltpu.VMEM),
         scratch_shapes=[
             pltpu.VMEM((len(stages), 8, 128), jnp.float32),
@@ -137,7 +138,7 @@
             pltpu.SemaphoreType.DMA((len(stages), widest)),
         ],
         compiler_params=pltpu.CompilerParams(collective_id=0, has_side_effects=True),
-    )(tile, previous)
+    )(*partials, previous)
 
 
 def interior(field):
@@ -146,7 +147,11 @@
 
 
 def dots(*pairs):
-    return jnp.stack([jnp.sum(interior(x) * interior(y)) for x, y in pairs])
+    def fold(x, y):
+        product = interior(x) * interior(y)
+        return jnp.sum(product.reshape(-1, 8, product.shape[-1] // 128, 128), axis=(0, 2))
+
+    return [fold(x, y) for x, y in pairs]
 
 
 def per_device(surface, bathymetry, land_sea, flux_lon, flux_lat):
@@ -164,7 +169,7 @@
     applied = operate(residual, wet, inverse)
     rows = lax.broadcasted_iota(jnp.int32, (8, 128), 0)
     previous = jnp.where(rows == 2, jnp.inf, 0.0).astype(jnp.float32)
-    stats = cg_scalars(dots((residual, residual), (residual, applied)), previous)
+    stats = cg_scalars(dots((residual, residual), (residual, applied)) + [jnp.zeros((8, 128), jnp.float32)], previous)
     direction, image = residual, applied
     for step in range(ITERS):
         alpha = stats[0, 0]

time: 139 us -> 139 us (level)
  local copies, waits for them, and re-layouts: 30.2 us -> 31.7 us
  other arithmetic: 42.7 us -> 41.3 us
    select_n x6 -> x0, other arithmetic: 7.2 us -> none  [cg_scalars(): tile = jnp.where(rows == k, local[k], tile)]
    reduce_sum x3 -> x8, other arithmetic: 4.22 us -> 7.12 us  [fold(): jnp.sum(product.reshape(-1, 8, product.shape[-1] // 128, 128), axis=(0, 2))]
    mul x0 -> x3, other arithmetic: none -> 2.39 us  [fold(): product = interior(x) * interior(y)]
where the time goes in v13:
time: 139 us
  Pallas kernels  44.6 us (32%)
  other arithmetic  41.3 us (30%)
  local copies, waits for them, and re-layouts  31.7 us (23%)
  starting transfers between devices  11.4 us (8%)
  waiting for transfers between devices  8.36 us (6%)
    pallas_call x3, Pallas kernels, cg_scalars(): pl.pallas_call(functools.partial(reduce_kernel, stages, len(partials)), o...  44.6 us
    unnamed x61, local copies, waits for them, and re-layouts  15.7 us
    ppermute x4, starting transfers between devices, from_behind(): lax.ppermute(value, axis, [(source, source + steps) for source in range(l...  11.4 us
    sub x2, other arithmetic, per_device(): residual = residual - alpha * image  11.1 us
    add x1, other arithmetic, per_device(): solution = solution + alpha * direction  9.32 us
    ppermute x4, waiting for transfers between devices, from_behind(): lax.ppermute(value, axis, [(source, source + steps) for source in range(l...  8.36 us
    reduce_sum x8, other arithmetic, fold(): jnp.sum(product.reshape(-1, 8, product.shape[-1] // 128, 128), axis=(0, 2))  7.12 us
    slice x5, local copies, waits for them, and re-layouts, north(): field[..., 1:, :]  2.79 us
  transfers between devices with their start and end apart: 4, of which 3 were waited for; matrix products, arithmetic and copies ran while one was open for 0% of the time, Pallas kernels for 0%

profile of v13, /device:TPU:1, one launch (start us, length us, event | category | flops | bytes accessed | tf_op | source)
XLA Modules:
  0.0 138.6 jit_solution(16817328978146928621)
XLA Ops:
  0.7 1.4 %bitcast_dynamic-update-slice_fusion.4 = f32[5,256,1024]{2,1,0:T(8,128)S(1)} fusion(f32[256,1024]{1,0:T(8,128)} %param.5), kind=kLoop, calls=%fused_computation.112 | loop fusion | bytes 2097152
  3.9 4.9 %collective-permute-start = (f32[5,8,1024]{2,1,0:T(8,128)S(1)}, f32[5,8,1024]{2,1,0:T(8,128)S(1)}, u32[]{:S(2)}, u32[]{:S(2)}) collective-permute-start(f32[5,8,1024]{2,1,0:T(8,128)S(1)} %get-tuple-element.25), channel_id=1, source_target_pairs={{0,16},{16,32},{32,48},{48,64},{64,80},{80,96},{96,112},{1,17},{17... | collective-permute-start | bytes 491528 | tf_op jit(solution)/shard_map/ppermute | solution.py:25
  8.8 1.9 %collective-permute-start.1 = (f32[5,8,1024]{2,1,0:T(8,128)S(1)}, f32[5,8,1024]{2,1,0:T(8,128)S(1)}, u32[]{:S(2)}, u32[]{:S(2)}) collective-permute-start(f32[5,8,1024]{2,1,0:T(8,128)S(1)} %get-tuple-element.26), channel_id=1, source_target_pairs={{16,0},{32,16},{48,32},{64,48},{80,64},{96,80},{112,96},{17,1},{33... | collective-permute-start | bytes 491528 | tf_op jit(solution)/shard_map/ppermute | solution.py:25
  11.1 4.4 %collective-permute-done.1 = f32[5,8,1024]{2,1,0:T(8,128)S(1)} collective-permute-done((f32[5,8,1024]{2,1,0:T(8,128)S(1)}, f32[5,8,1024]{2,1,0:T(8,128)S(1)}, u32[]{:S(2)}, u32[]{:S(2)}) %collective-permute-start.1) | collective-permute-done | bytes 163872 | tf_op jit(solution)/shard_map/ppermute | solution.py:25
  16.3 2.6 %copy-done = f32[5,272,1040]{2,1,0:T(8,128)} copy-done((f32[5,272,1040]{2,1,0:T(8,128)}, f32[5,272,1040]{2,1,0:T(8,128)S(1)}, u32[]{:S(2)}) %copy-start) | copy-done | bytes 5657624
  19.8 3.2 %collective-permute-start.3 = (f32[5,272,8]{1,2,0:T(8,128)S(1)}, f32[5,272,8]{1,2,0:T(8,128)S(1)}, u32[]{:S(2)}, u32[]{:S(2)}) collective-permute-start(f32[5,272,8]{1,2,0:T(8,128)S(1)} %copy.33), channel_id=1, source_target_pairs={{0,1},{1,2},{2,3},{3,4},{4,5},{5,6},{6,7},{7,8},{8,9},{9,10},{10,1... | collective-permute-start | bytes 130568 | tf_op jit(solution)/shard_map/ppermute | solution.py:25
  23.0 1.3 collective-permute-start.2
  24.3 3.6 %collective-permute-done.2 = f32[5,272,8]{1,2,0:T(8,128)S(1)} collective-permute-done((f32[5,272,8]{1,2,0:T(8,128)S(1)}, f32[5,272,8]{1,2,0:T(8,128)S(1)}, u32[]{:S(2)}, u32[]{:S(2)}) %collective-permute-start.2) | collective-permute-done | bytes 43552 | tf_op jit(solution)/shard_map/ppermute | solution.py:25
  29.2 2.4 %slice_bitcast_fusion.19 = (f32[271,1040]{1,0:T(8,128)S(1)}, f32[271,1040]{1,0:T(8,128)S(1)}, f32[271,1040]{1,0:T(8,128)S(1)}) fusion(f32[5,272,1040]{2,1,0:T(8,128)} %constant_dynamic-update-slice_fusion), kind=kLoop, calls=%fused_computation.72 | loop fusion | bytes 6764160 | tf_op jit(solution)/shard_map/slice | solution.py:44
  31.7 1.5 %copy-done.1 = f32[5,272,1040]{2,1,0:T(8,128)S(1)} copy-done((f32[5,272,1040]{2,1,0:T(8,128)S(1)}, f32[5,272,1040]{2,1,0:T(8,128)}, u32[]{:S(2)}) %copy-start.1) | copy-done | bytes 5657624
  37.9 2.6 %fusion.1 = (f32[2,272,1040]{2,1,0:T(8,128)}, f32[2,272,1040]{2,1,0:T(8,128)S(1)}) fusion(f32[1,272,1040]{2,1,0:T(8,128)S(1)} %get-tuple-element.18, f32[1,272,1040]{2,1,0:T(8,128)S(1)} %get-tuple-element.13, f32[1,272,1040]{2,1,0:T(8,128)S(1)} %get-tuple-element.48, f32[1,272,1040]{2,1,0:T(8,128)S(1)} %get-tuple-element.47, ...), kind=kLoop, calls=%fused_computation.8 | loop fusion | flops 10749440 | bytes 15841280 | tf_op jit(solution)/shard_map/jit(_where)/select_n | solution.py:165
  48.0 17.9 %shard_map.76.refs_3_ = f32[8,128]{1,0:T(8,128)} custom-call(f32[8,128]{1,0:T(8,128)} %bitcast_reduce_fusion.7.refs_0_, f32[8,128]{1,0:T(8,128)} %bitcast_reduce_fusion.6.refs_1_, f32[8,128]{1,0:T(8,128)} %broadcast_in_dim.13.refs_2_, f32[8,128]{1,0:T(8,128)} %iota.7.refs_3_), custom_call_target="tpu_custom_call" | custom-call | tf_op jit(solution)/shard_map/pallas_call | solution.py:129
  65.9 1.2 slice.305
  67.2 4.2 %multiply_subtract_fusion.1 = f32[2,272,1040]{2,1,0:T(8,128)S(1)} fusion(f32[2,272,1040]{2,1,0:T(8,128)S(1)} %get-tuple-element.35, f32[]{:T(128)} %bitcast.30, f32[1,272,1040]{2,1,0:T(8,128)} %copy-done.15, f32[1,272,1040]{2,1,0:T(8,128)} %copy-done.14, f32[1,272,1040]{2,1,0:T(8,128)} %copy-done.9, f32[1,272,1040]{2,1,0:T(8,128)} %copy-done.11, ...), kind=kLoop, calls=%fused_computation.23 | loop fusion | flops 7354880 | bytes 11315204 | tf_op jit(solution)/shard_map/sub | solution.py:179
  74.0 1.1 copy-done.7
  81.3 13.1 %shard_map.77.refs_3_ = f32[8,128]{1,0:T(8,128)} custom-call(f32[8,128]{1,0:T(8,128)} %bitcast_reduce_fusion.5.refs_0_, f32[8,128]{1,0:T(8,128)} %bitcast_reduce_fusion.4.refs_1_, f32[8,128]{1,0:T(8,128)} %bitcast_reduce_fusion.3.refs_2_, f32[8,128]{1,0:T(8,128)} %shard_map.76.refs_3_), custom_call_target="tpu_custom_call" | custom-call | tf_op jit(solution)/shard_map/pallas_call | solution.py:129
  94.4 1.3 fusion.28
  95.7 6.9 %multiply_subtract_fusion = (f32[2,272,1040]{2,1,0:T(8,128)S(1)}, f32[2,272,1040]{2,1,0:T(8,128)S(1)}) fusion(f32[2,272,1040]{2,1,0:T(8,128)} %copy-done.2, f32[]{:T(128)} %bitcast.36, f32[]{:T(128)} %bitcast.37, f32[1,272,1040]{2,1,0:T(8,128)} %copy-done.21, f32[1,272,1040]{2,1,0:T(8,128)} %copy-done.20, f32[1,272,1040]{2,1,0:T(8,128)} %copy-done.9, ...), kind=kLoop, calls=%fused_computation.21 | loop fusion | flops 10749440 | bytes 18104328 | tf_op jit(solution)/shard_map/sub | solution.py:179
  110.0 13.6 %shard_map.78 = f32[8,128]{1,0:T(8,128)} custom-call(f32[8,128]{1,0:T(8,128)} %bitcast_reduce_fusion.2.refs_0_, f32[8,128]{1,0:T(8,128)} %bitcast_reduce_fusion.1.refs_1_, f32[8,128]{1,0:T(8,128)} %bitcast_reduce_fusion.refs_2_, f32[8,128]{1,0:T(8,128)} %shard_map.77.refs_3_), custom_call_target="tpu_custom_call" | custom-call | tf_op jit(solution)/shard_map/pallas_call | solution.py:129
  123.6 1.3 fusion.27
  124.9 9.3 %multiply_add_fusion = f32[2,272,1040]{2,1,0:T(8,128)S(1)} fusion(f32[2,272,1040]{2,1,0:T(8,128)} %copy-done.2, f32[2,272,1040]{2,1,0:T(8,128)S(1)} %get-tuple-element.35, f32[]{:T(128)} %bitcast.44, f32[]{:T(128)} %bitcast.43, f32[]{:T(128)} %bitcast.37, f32[]{:T(128)} %bitcast.36, f32[]{:T(128)} %bitcast.30, f32[2,272,1040]{2,1,0:T(8,128)} %copy-done.13, ...), kind=kLoop, calls=%fused_computation.20 | loop fusion | flops 10749440 | bytes 18104340 | tf_op jit(solution)/shard_map/add | solution.py:176
  134.3 1.6 %slice_bitcast_fusion.24 = (f32[256,1024]{1,0:T(8,128)}, f32[256,1024]{1,0:T(8,128)}) fusion(f32[2,272,1040]{2,1,0:T(8,128)S(1)} %multiply_add_fusion), kind=kLoop, calls=%fused_computation.100 | loop fusion | bytes 4194304 | tf_op jit(solution)/shard_map/squeeze | solution.py:187
  136.2 1.0 copy-done.23
  137.2 1.4 %slice_subtract_fusion.1 = f32[256,1024]{1,0:T(8,128)} fusion(f32[272,1040]{1,0:T(8,128)S(1)} %copy-done.23, f32[271,1040]{1,0:T(8,128)S(1)} %slice_bitcast_fusion, f32[272,1040]{1,0:T(8,128)S(1)} %get-tuple-element.30, f32[272,1040]{1,0:T(8,128)S(1)} %get-tuple-element.29, f32[272,1039]{1,0:T(8,128)S(1)} %bitcast.170, f32[272,1]{1,0:T(8,128)S(1)} %slice.402), kind=kLoop, calls=%fused_computation.102 | loop fusion | flops 1572864 | bytes 6453184 | tf_op jit(solution)/shard_map/sub | solution.py:185
  (127 shorter events, 33.3 us)
Async XLA Ops:
  0.6 1.8 %copy-start.26 = (s32[256,1024]{1,0:T(8,128)S(1)}, s32[256,1024]{1,0:T(8,128)}, u32[]{:S(2)}) copy-start(s32[256,1024]{1,0:T(8,128)} %param.7) | copy-start | bytes 3145732
  3.9 7.2 %collective-permute-start = (f32[5,8,1024]{2,1,0:T(8,128)S(1)}, f32[5,8,1024]{2,1,0:T(8,128)S(1)}, u32[]{:S(2)}, u32[]{:S(2)}) collective-permute-start(f32[5,8,1024]{2,1,0:T(8,128)S(1)} %get-tuple-element.25), channel_id=1, source_target_pairs={{0,16},{16,32},{32,48},{48,64},{64,80},{80,96},{96,112},{1,17},{17... | collective-permute-start | bytes 491528 | tf_op jit(solution)/shard_map/ppermute | solution.py:25
  8.8 6.6 %collective-permute-start.1 = (f32[5,8,1024]{2,1,0:T(8,128)S(1)}, f32[5,8,1024]{2,1,0:T(8,128)S(1)}, u32[]{:S(2)}, u32[]{:S(2)}) collective-permute-start(f32[5,8,1024]{2,1,0:T(8,128)S(1)} %get-tuple-element.26), channel_id=1, source_target_pairs={{16,0},{32,16},{48,32},{64,48},{80,64},{96,80},{112,96},{17,1},{33... | collective-permute-start | bytes 491528 | tf_op jit(solution)/shard_map/ppermute | solution.py:25
  16.3 2.6 %copy-start = (f32[5,272,1040]{2,1,0:T(8,128)}, f32[5,272,1040]{2,1,0:T(8,128)S(1)}, u32[]{:S(2)}) copy-start(f32[5,272,1040]{2,1,0:T(8,128)S(1)} %select_maximum_fusion) | copy-start | bytes 16972804
  19.8 4.5 %collective-permute-start.3 = (f32[5,272,8]{1,2,0:T(8,128)S(1)}, f32[5,272,8]{1,2,0:T(8,128)S(1)}, u32[]{:S(2)}, u32[]{:S(2)}) collective-permute-start(f32[5,272,8]{1,2,0:T(8,128)S(1)} %copy.33), channel_id=1, source_target_pairs={{0,1},{1,2},{2,3},{3,4},{4,5},{5,6},{6,7},{7,8},{8,9},{9,10},{10,1... | collective-permute-start | bytes 130568 | tf_op jit(solution)/shard_map/ppermute | solution.py:25
  23.0 5.0 %collective-permute-start.2 = (f32[5,272,8]{1,2,0:T(8,128)S(1)}, f32[5,272,8]{1,2,0:T(8,128)S(1)}, u32[]{:S(2)}, u32[]{:S(2)}) collective-permute-start(f32[5,272,8]{1,2,0:T(8,128)S(1)} %copy.32), channel_id=1, source_target_pairs={{1,0},{2,1},{3,2},{4,3},{5,4},{6,5},{7,6},{8,7},{9,8},{10,9},{11,1... | collective-permute-start | bytes 130568 | tf_op jit(solution)/shard_map/ppermute | solution.py:25
  29.2 3.9 %copy-start.1 = (f32[5,272,1040]{2,1,0:T(8,128)S(1)}, f32[5,272,1040]{2,1,0:T(8,128)}, u32[]{:S(2)}) copy-start(f32[5,272,1040]{2,1,0:T(8,128)} %constant_dynamic-update-slice_fusion) | copy-start | bytes 16972804
  35.0 2.9 %copy-start.16 = (f32[1,272,1040]{2,1,0:T(8,128)}, f32[1,272,1040]{2,1,0:T(8,128)S(1)}, u32[]{:S(2)}) copy-start(f32[1,272,1040]{2,1,0:T(8,128)S(1)} %get-tuple-element.19) | copy-start | bytes 3394564
  35.0 7.0 %copy-start.3 = (f32[1,272,1040]{2,1,0:T(8,128)}, f32[1,272,1040]{2,1,0:T(8,128)S(1)}, u32[]{:S(2)}) copy-start(f32[1,272,1040]{2,1,0:T(8,128)S(1)} %get-tuple-element.17) | copy-start | bytes 3394564
  35.0 7.0 %copy-start.9 = (f32[1,272,1040]{2,1,0:T(8,128)}, f32[1,272,1040]{2,1,0:T(8,128)S(1)}, u32[]{:S(2)}) copy-start(f32[1,272,1040]{2,1,0:T(8,128)S(1)} %get-tuple-element.18) | copy-start | bytes 3394564
  35.5 2.3 %copy-start.17 = (f32[1,272,1040]{2,1,0:T(8,128)}, f32[1,272,1040]{2,1,0:T(8,128)S(1)}, u32[]{:S(2)}) copy-start(f32[1,272,1040]{2,1,0:T(8,128)S(1)} %get-tuple-element.12) | copy-start | bytes 3394564
  35.5 6.5 %copy-start.6 = (f32[1,272,1040]{2,1,0:T(8,128)}, f32[1,272,1040]{2,1,0:T(8,128)S(1)}, u32[]{:S(2)}) copy-start(f32[1,272,1040]{2,1,0:T(8,128)S(1)} %get-tuple-element.11) | copy-start | bytes 3394564
  35.6 6.5 %copy-start.11 = (f32[1,272,1040]{2,1,0:T(8,128)}, f32[1,272,1040]{2,1,0:T(8,128)S(1)}, u32[]{:S(2)}) copy-start(f32[1,272,1040]{2,1,0:T(8,128)S(1)} %get-tuple-element.13) | copy-start | bytes 3394564
  43.5 1.5 %copy-start.18 = (f32[2,272,1040]{2,1,0:T(8,128)}, f32[2,272,1040]{2,1,0:T(8,128)S(1)}, u32[]{:S(2)}) copy-start(f32[2,272,1040]{2,1,0:T(8,128)S(1)} %fusion.5) | copy-start | bytes 6789124
  71.4 5.4 %copy-start.2 = (f32[2,272,1040]{2,1,0:T(8,128)}, f32[2,272,1040]{2,1,0:T(8,128)S(1)}, u32[]{:S(2)}) copy-start(f32[2,272,1040]{2,1,0:T(8,128)S(1)} %multiply_subtract_fusion.1) | copy-start | bytes 6789124
  72.7 2.4 %copy-start.7 = (f32[1,272,1040]{2,1,0:T(8,128)S(1)}, f32[1,272,1040]{2,1,0:T(8,128)}, u32[]{:S(2)}) copy-start(f32[1,272,1040]{2,1,0:T(8,128)} %copy-done.6) | copy-start | bytes 3394564
  72.7 2.9 %copy-start.10 = (f32[1,272,1040]{2,1,0:T(8,128)S(1)}, f32[1,272,1040]{2,1,0:T(8,128)}, u32[]{:S(2)}) copy-start(f32[1,272,1040]{2,1,0:T(8,128)} %copy-done.9) | copy-start | bytes 3394564
  72.7 3.3 %copy-start.12 = (f32[1,272,1040]{2,1,0:T(8,128)S(1)}, f32[1,272,1040]{2,1,0:T(8,128)}, u32[]{:S(2)}) copy-start(f32[1,272,1040]{2,1,0:T(8,128)} %copy-done.11) | copy-start | bytes 3394564
  73.1 3.7 %copy-start.20 = (f32[1,272,1040]{2,1,0:T(8,128)}, f32[1,272,1040]{2,1,0:T(8,128)S(1)}, u32[]{:S(2)}) copy-start(f32[1,272,1040]{2,1,0:T(8,128)S(1)} %get-tuple-element.43) | copy-start | bytes 3394564
  73.1 3.7 %copy-start.21 = (f32[1,272,1040]{2,1,0:T(8,128)}, f32[1,272,1040]{2,1,0:T(8,128)S(1)}, u32[]{:S(2)}) copy-start(f32[1,272,1040]{2,1,0:T(8,128)S(1)} %get-tuple-element.44) | copy-start | bytes 3394564
  76.0 1.7 %copy-start.19 = (f32[2,272,1040]{2,1,0:T(8,128)S(1)}, f32[2,272,1040]{2,1,0:T(8,128)}, u32[]{:S(2)}) copy-start(f32[2,272,1040]{2,1,0:T(8,128)} %copy-done.18) | copy-start | bytes 6789124
  102.6 1.6 %copy-start.13 = (f32[2,272,1040]{2,1,0:T(8,128)}, f32[2,272,1040]{2,1,0:T(8,128)S(1)}, u32[]{:S(2)}) copy-start(f32[2,272,1040]{2,1,0:T(8,128)S(1)} %get-tuple-element.10) | copy-start | bytes 6789124
  103.9 1.7 %copy-start.8 = (f32[1,272,1040]{2,1,0:T(8,128)S(1)}, f32[1,272,1040]{2,1,0:T(8,128)}, u32[]{:S(2)}) copy-start(f32[1,272,1040]{2,1,0:T(8,128)} %copy-done.6) | copy-start | bytes 3394564
  103.9 2.5 %copy-start.24 = (f32[2,272,1040]{2,1,0:T(8,128)S(1)}, f32[2,272,1040]{2,1,0:T(8,128)}, u32[]{:S(2)}) copy-start(f32[2,272,1040]{2,1,0:T(8,128)} %get-tuple-element.34) | copy-start | bytes 6789124
  (9 other events, 11.8 us)

commit v14 on v12

--- a/solution.py
+++ b/solution.py
@@ -12,6 +12,7 @@
 ITERS = 3
 MARGIN_ROWS = 8
 MARGIN_COLS = 8
+SENT = 4
 
 
 courant = -0.4
@@ -83,16 +84,16 @@
             greeted += 1
     pl.semaphore_wait(barrier, greeted)
 
-    value = local_ref[...]
+    value = local_ref[0:SENT]
     for stage, (axis, stride, members) in enumerate(stages):
-        parts[stage] = value
-        got[stage, 0] = value
+        parts[stage, 0:SENT] = value
+        got[stage, 0, 0:SENT] = value
         copies = []
         for offset in range(1, members):
             slot = members - offset
             copy = pltpu.make_async_remote_copy(
-                src_ref=parts.at[stage],
-                dst_ref=got.at[stage, slot],
+                src_ref=parts.at[stage, pl.ds(0, SENT)],
+                dst_ref=got.at[stage, slot, pl.ds(0, SENT)],
                 send_sem=send_sem.at[stage, offset],
                 recv_sem=recv_sem.at[stage, slot],
                 device_id=partner(axis, stride, members, offset),
@@ -103,14 +104,14 @@
         for copy in copies:
             copy.wait()
         digit = (me[axis] // stride) % members
-        ordered = [got[stage, (member - digit) % members] for member in range(members)]
+        ordered = [got[stage, (member - digit) % members, 0:SENT] for member in range(members)]
         while len(ordered) > 1:
             ordered = [ordered[k] + ordered[k + 1] for k in range(0, len(ordered), 2)]
         value = ordered[0]
     norm, r_ar, r_ap = value[0:1], value[1:2], value[2:3]
     beta = norm / prev_ref[2:3]
     curve = r_ar + 2.0 * beta * r_ap + beta * beta * prev_ref[3:4]
-    out_ref[...] = jnp.zeros_like(value)
+    out_ref[...] = jnp.zeros(out_ref.shape, out_ref.dtype)
     out_ref[0:1] = norm / curve
     out_ref[1:2] = beta
     out_ref[2:3] = norm

time: 139 us -> 138 us (level)
  no operation moved by 1% of the time
where the time goes in v14:
time: 138 us
  Pallas kernels  43.7 us (32%)
  other arithmetic  42.7 us (31%)
  local copies, waits for them, and re-layouts  30.2 us (22%)
  starting transfers between devices  11.4 us (8%)
  waiting for transfers between devices  8.34 us (6%)
    pallas_call x3, Pallas kernels, cg_scalars(): pl.pallas_call(functools.partial(reduce_kernel, stages), out_shape=jax.Sh...  43.7 us
    unnamed x61, local copies, waits for them, and re-layouts  14.8 us
    ppermute x4, starting transfers between devices, from_behind(): lax.ppermute(value, axis, [(source, source + steps) for source in range(l...  11.4 us
    sub x2, other arithmetic, per_device(): residual = residual - alpha * image  10.8 us
    add x1, other arithmetic, per_device(): solution = solution + alpha * direction  9.23 us
    ppermute x4, waiting for transfers between devices, from_behind(): lax.ppermute(value, axis, [(source, source + steps) for source in range(l...  8.34 us
    select_n x6, other arithmetic, cg_scalars(): tile = jnp.where(rows == k, local[k], tile)  7.2 us
    reduce_sum x3, other arithmetic, dots(): return jnp.stack([jnp.sum(interior(x) * interior(y)) for x, y in pairs])  4.22 us
  transfers between devices with their start and end apart: 4, of which 3 were waited for; matrix products, arithmetic and copies ran while one was open for 0% of the time, Pallas kernels for 0%

profile of v14, /device:TPU:1, one launch (start us, length us, event | category | flops | bytes accessed | tf_op | source)
XLA Modules:
  0.0 137.7 jit_solution(9849242536861793056)
XLA Ops:
  0.7 1.4 %bitcast_dynamic-update-slice_fusion.4 = f32[5,256,1024]{2,1,0:T(8,128)S(1)} fusion(f32[256,1024]{1,0:T(8,128)} %param.5), kind=kLoop, calls=%fused_computation.107 | loop fusion | bytes 2097152
  3.9 4.9 %collective-permute-start = (f32[5,8,1024]{2,1,0:T(8,128)S(1)}, f32[5,8,1024]{2,1,0:T(8,128)S(1)}, u32[]{:S(2)}, u32[]{:S(2)}) collective-permute-start(f32[5,8,1024]{2,1,0:T(8,128)S(1)} %get-tuple-element.30), channel_id=1, source_target_pairs={{0,16},{16,32},{32,48},{48,64},{64,80},{80,96},{96,112},{1,17},{17... | collective-permute-start | bytes 491528 | tf_op jit(solution)/shard_map/ppermute | solution.py:26
  8.8 1.9 %collective-permute-start.1 = (f32[5,8,1024]{2,1,0:T(8,128)S(1)}, f32[5,8,1024]{2,1,0:T(8,128)S(1)}, u32[]{:S(2)}, u32[]{:S(2)}) collective-permute-start(f32[5,8,1024]{2,1,0:T(8,128)S(1)} %get-tuple-element.31), channel_id=1, source_target_pairs={{16,0},{32,16},{48,32},{64,48},{80,64},{96,80},{112,96},{17,1},{33... | collective-permute-start | bytes 491528 | tf_op jit(solution)/shard_map/ppermute | solution.py:26
  11.1 4.4 %collective-permute-done.1 = f32[5,8,1024]{2,1,0:T(8,128)S(1)} collective-permute-done((f32[5,8,1024]{2,1,0:T(8,128)S(1)}, f32[5,8,1024]{2,1,0:T(8,128)S(1)}, u32[]{:S(2)}, u32[]{:S(2)}) %collective-permute-start.1) | collective-permute-done | bytes 163872 | tf_op jit(solution)/shard_map/ppermute | solution.py:26
  16.3 2.6 %copy-done = f32[5,272,1040]{2,1,0:T(8,128)} copy-done((f32[5,272,1040]{2,1,0:T(8,128)}, f32[5,272,1040]{2,1,0:T(8,128)S(1)}, u32[]{:S(2)}) %copy-start) | copy-done | bytes 5657624
  19.8 3.2 %collective-permute-start.3 = (f32[5,272,8]{1,2,0:T(8,128)S(1)}, f32[5,272,8]{1,2,0:T(8,128)S(1)}, u32[]{:S(2)}, u32[]{:S(2)}) collective-permute-start(f32[5,272,8]{1,2,0:T(8,128)S(1)} %copy.17), channel_id=1, source_target_pairs={{0,1},{1,2},{2,3},{3,4},{4,5},{5,6},{6,7},{7,8},{8,9},{9,10},{10,1... | collective-permute-start | bytes 130568 | tf_op jit(solution)/shard_map/ppermute | solution.py:26
  24.3 3.6 %collective-permute-done.2 = f32[5,272,8]{1,2,0:T(8,128)S(1)} collective-permute-done((f32[5,272,8]{1,2,0:T(8,128)S(1)}, f32[5,272,8]{1,2,0:T(8,128)S(1)}, u32[]{:S(2)}, u32[]{:S(2)}) %collective-permute-start.2) | collective-permute-done | bytes 43552 | tf_op jit(solution)/shard_map/ppermute | solution.py:26
  29.2 2.4 %slice_bitcast_fusion.19 = (f32[271,1040]{1,0:T(8,128)S(1)}, f32[271,1040]{1,0:T(8,128)S(1)}, f32[271,1040]{1,0:T(8,128)S(1)}) fusion(f32[5,272,1040]{2,1,0:T(8,128)} %constant_dynamic-update-slice_fusion), kind=kLoop, calls=%fused_computation.67 | loop fusion | bytes 6764160 | tf_op jit(solution)/shard_map/slice | solution.py:45
  31.7 1.5 %copy-done.1 = f32[5,272,1040]{2,1,0:T(8,128)S(1)} copy-done((f32[5,272,1040]{2,1,0:T(8,128)S(1)}, f32[5,272,1040]{2,1,0:T(8,128)}, u32[]{:S(2)}) %copy-start.1) | copy-done | bytes 5657624
  37.9 2.6 %fusion.1 = (f32[2,272,1040]{2,1,0:T(8,128)}, f32[2,272,1040]{2,1,0:T(8,128)S(1)}) fusion(f32[1,272,1040]{2,1,0:T(8,128)S(1)} %get-tuple-element.23, f32[1,272,1040]{2,1,0:T(8,128)S(1)} %get-tuple-element.18, f32[1,272,1040]{2,1,0:T(8,128)S(1)} %get-tuple-element.45, f32[1,272,1040]{2,1,0:T(8,128)S(1)} %get-tuple-element.44, ...), kind=kLoop, calls=%fused_computation.8 | loop fusion | flops 10749440 | bytes 15841280 | tf_op jit(solution)/shard_map/jit(_where)/select_n | solution.py:161
  43.4 1.4 %multiply_reduce_fusion.4 = (f32[]{:T(128)}, f32[]{:T(128)}) fusion(f32[2,272,1040]{2,1,0:T(8,128)S(1)} %fusion.5, f32[2,272,1040]{2,1,0:T(8,128)S(1)} %get-tuple-element.37), kind=kLoop, calls=%fused_computation.39 | loop fusion | flops 2097150 | bytes 4194312 | tf_op jit(solution)/shard_map/reduce_sum | solution.py:150
  45.6 1.3 broadcast_select_fusion.local_ref
  47.6 17.7 %shard_map.76.prev_ref = f32[8,128]{1,0:T(8,128)} custom-call(f32[8,128]{1,0:T(8,128)} %broadcast_select_fusion.local_ref, f32[8,128]{1,0:T(8,128)} %iota.49.prev_ref), custom_call_target="tpu_custom_call" | custom-call | tf_op jit(solution)/shard_map/pallas_call | solution.py:129
  66.5 4.2 %multiply_subtract_fusion.1 = f32[2,272,1040]{2,1,0:T(8,128)S(1)} fusion(f32[2,272,1040]{2,1,0:T(8,128)S(1)} %get-tuple-element.37, f32[]{:T(128)} %bitcast.30, f32[1,272,1040]{2,1,0:T(8,128)} %copy-done.15, f32[1,272,1040]{2,1,0:T(8,128)} %copy-done.14, f32[1,272,1040]{2,1,0:T(8,128)} %copy-done.9, f32[1,272,1040]{2,1,0:T(8,128)} %copy-done.11, ...), kind=kLoop, calls=%fused_computation.23 | loop fusion | flops 7354880 | bytes 11315204 | tf_op jit(solution)/shard_map/sub | solution.py:175
  79.0 2.0 %select_select_fusion.1.local_ref = f32[8,128]{1,0:T(8,128)} fusion(f32[8]{0:T(128)S(1)} %fusion.29, f32[]{:T(128)} %get-tuple-element.10, f32[]{:T(128)} %get-tuple-element.9, pred[8]{0:T(512)(128)(4,1)S(1)} %get-tuple-element.54, pred[8]{0:T(512)(128)(4,1)S(1)} %get-tuple-element.55), kind=kLoop, calls=%fused_computation.113 | loop fusion | flops 2048 | bytes 4152 | tf_op jit(solution)/shard_map/jit(_where)/select_n | solution.py:128
  81.0 12.7 %shard_map.77.prev_ref = f32[8,128]{1,0:T(8,128)} custom-call(f32[8,128]{1,0:T(8,128)} %select_select_fusion.1.local_ref, f32[8,128]{1,0:T(8,128)} %shard_map.76.prev_ref), custom_call_target="tpu_custom_call" | custom-call | tf_op jit(solution)/shard_map/pallas_call | solution.py:129
  93.7 1.3 fusion.34
  95.0 6.5 %multiply_subtract_fusion = (f32[2,272,1040]{2,1,0:T(8,128)S(1)}, f32[2,272,1040]{2,1,0:T(8,128)S(1)}) fusion(f32[2,272,1040]{2,1,0:T(8,128)} %copy-done.2, f32[]{:T(128)} %bitcast.36, f32[]{:T(128)} %bitcast.37, f32[1,272,1040]{2,1,0:T(8,128)} %copy-done.21, f32[1,272,1040]{2,1,0:T(8,128)} %copy-done.20, f32[1,272,1040]{2,1,0:T(8,128)} %copy-done.9, ...), kind=kLoop, calls=%fused_computation.21 | loop fusion | flops 10749440 | bytes 18104328 | tf_op jit(solution)/shard_map/sub | solution.py:175
  105.3 1.5 %fusion.12 = (f32[]{:T(128)}, f32[]{:T(128)}, f32[]{:T(128)}) fusion(f32[2,272,1040]{2,1,0:T(8,128)S(1)} %get-tuple-element.15, f32[2,272,1040]{2,1,0:T(8,128)S(1)} %get-tuple-element.14, f32[1,272,1040]{2,1,0:T(8,128)S(1)} %get-tuple-element.39, f32[1,272,1040]{2,1,0:T(8,128)S(1)} %get-tuple-element.38, f32[2,272,1040]{2,1,0:T(8,128)S(1)} %copy-done.24, ...), kind=kLoop, calls=%fused_computation.32 | loop fusion | flops 5767165 | bytes 10817548 | tf_op jit(solution)/shard_map/reduce_sum | solution.py:150
  107.5 2.0 %select_select_fusion.local_ref = f32[8,128]{1,0:T(8,128)} fusion(f32[8]{0:T(128)S(1)} %fusion.28, f32[]{:T(128)} %get-tuple-element.8, f32[]{:T(128)} %get-tuple-element.6, pred[8]{0:T(512)(128)(4,1)S(1)} %get-tuple-element.54, pred[8]{0:T(512)(128)(4,1)S(1)} %get-tuple-element.55), kind=kLoop, calls=%fused_computation.112 | loop fusion | flops 2048 | bytes 4152 | tf_op jit(solution)/shard_map/jit(_where)/select_n | solution.py:128
  109.4 13.3 %shard_map.78 = f32[8,128]{1,0:T(8,128)} custom-call(f32[8,128]{1,0:T(8,128)} %select_select_fusion.local_ref, f32[8,128]{1,0:T(8,128)} %shard_map.77.prev_ref), custom_call_target="tpu_custom_call" | custom-call | tf_op jit(solution)/shard_map/pallas_call | solution.py:129
  124.0 9.2 %multiply_add_fusion = f32[2,272,1040]{2,1,0:T(8,128)S(1)} fusion(f32[2,272,1040]{2,1,0:T(8,128)} %copy-done.2, f32[2,272,1040]{2,1,0:T(8,128)S(1)} %get-tuple-element.37, f32[]{:T(128)} %bitcast.44, f32[]{:T(128)} %bitcast.43, f32[]{:T(128)} %bitcast.37, f32[]{:T(128)} %bitcast.36, f32[]{:T(128)} %bitcast.30, f32[2,272,1040]{2,1,0:T(8,128)} %copy-done.13, ...), kind=kLoop, calls=%fused_computation.20 | loop fusion | flops 10749440 | bytes 18104340 | tf_op jit(solution)/shard_map/add | solution.py:172
  133.3 1.6 %slice_bitcast_fusion.24 = (f32[256,1024]{1,0:T(8,128)}, f32[256,1024]{1,0:T(8,128)}) fusion(f32[2,272,1040]{2,1,0:T(8,128)S(1)} %multiply_add_fusion), kind=kLoop, calls=%fused_computation.95 | loop fusion | bytes 4194304 | tf_op jit(solution)/shard_map/squeeze | solution.py:183
  136.2 1.4 %slice_subtract_fusion.1 = f32[256,1024]{1,0:T(8,128)} fusion(f32[272,1040]{1,0:T(8,128)S(1)} %copy-done.23, f32[271,1040]{1,0:T(8,128)S(1)} %slice_bitcast_fusion, f32[272,1040]{1,0:T(8,128)S(1)} %get-tuple-element.35, f32[272,1040]{1,0:T(8,128)S(1)} %get-tuple-element.34, f32[272,1039]{1,0:T(8,128)S(1)} %bitcast.130, f32[272,1]{1,0:T(8,128)S(1)} %slice.402), kind=kLoop, calls=%fused_computation.97 | loop fusion | flops 1572864 | bytes 6453184 | tf_op jit(solution)/shard_map/sub | solution.py:181
  (125 shorter events, 31.4 us)
Async XLA Ops:
  0.6 1.5 %copy-start.25 = (f32[256,1024]{1,0:T(8,128)S(1)}, f32[256,1024]{1,0:T(8,128)}, u32[]{:S(2)}) copy-start(f32[256,1024]{1,0:T(8,128)} %param.6) | copy-start | bytes 3145732
  0.6 1.8 %copy-start.26 = (s32[256,1024]{1,0:T(8,128)S(1)}, s32[256,1024]{1,0:T(8,128)}, u32[]{:S(2)}) copy-start(s32[256,1024]{1,0:T(8,128)} %param.7) | copy-start | bytes 3145732
  3.9 7.2 %collective-permute-start = (f32[5,8,1024]{2,1,0:T(8,128)S(1)}, f32[5,8,1024]{2,1,0:T(8,128)S(1)}, u32[]{:S(2)}, u32[]{:S(2)}) collective-permute-start(f32[5,8,1024]{2,1,0:T(8,128)S(1)} %get-tuple-element.30), channel_id=1, source_target_pairs={{0,16},{16,32},{32,48},{48,64},{64,80},{80,96},{96,112},{1,17},{17... | collective-permute-start | bytes 491528 | tf_op jit(solution)/shard_map/ppermute | solution.py:26
  8.8 6.6 %collective-permute-start.1 = (f32[5,8,1024]{2,1,0:T(8,128)S(1)}, f32[5,8,1024]{2,1,0:T(8,128)S(1)}, u32[]{:S(2)}, u32[]{:S(2)}) collective-permute-start(f32[5,8,1024]{2,1,0:T(8,128)S(1)} %get-tuple-element.31), channel_id=1, source_target_pairs={{16,0},{32,16},{48,32},{64,48},{80,64},{96,80},{112,96},{17,1},{33... | collective-permute-start | bytes 491528 | tf_op jit(solution)/shard_map/ppermute | solution.py:26
  16.3 2.6 %copy-start = (f32[5,272,1040]{2,1,0:T(8,128)}, f32[5,272,1040]{2,1,0:T(8,128)S(1)}, u32[]{:S(2)}) copy-start(f32[5,272,1040]{2,1,0:T(8,128)S(1)} %select_maximum_fusion) | copy-start | bytes 16972804
  19.8 4.5 %collective-permute-start.3 = (f32[5,272,8]{1,2,0:T(8,128)S(1)}, f32[5,272,8]{1,2,0:T(8,128)S(1)}, u32[]{:S(2)}, u32[]{:S(2)}) collective-permute-start(f32[5,272,8]{1,2,0:T(8,128)S(1)} %copy.17), channel_id=1, source_target_pairs={{0,1},{1,2},{2,3},{3,4},{4,5},{5,6},{6,7},{7,8},{8,9},{9,10},{10,1... | collective-permute-start | bytes 130568 | tf_op jit(solution)/shard_map/ppermute | solution.py:26
  23.0 5.0 %collective-permute-start.2 = (f32[5,272,8]{1,2,0:T(8,128)S(1)}, f32[5,272,8]{1,2,0:T(8,128)S(1)}, u32[]{:S(2)}, u32[]{:S(2)}) collective-permute-start(f32[5,272,8]{1,2,0:T(8,128)S(1)} %copy.16), channel_id=1, source_target_pairs={{1,0},{2,1},{3,2},{4,3},{5,4},{6,5},{7,6},{8,7},{9,8},{10,9},{11,1... | collective-permute-start | bytes 130568 | tf_op jit(solution)/shard_map/ppermute | solution.py:26
  29.2 3.9 %copy-start.1 = (f32[5,272,1040]{2,1,0:T(8,128)S(1)}, f32[5,272,1040]{2,1,0:T(8,128)}, u32[]{:S(2)}) copy-start(f32[5,272,1040]{2,1,0:T(8,128)} %constant_dynamic-update-slice_fusion) | copy-start | bytes 16972804
  35.0 2.9 %copy-start.16 = (f32[1,272,1040]{2,1,0:T(8,128)}, f32[1,272,1040]{2,1,0:T(8,128)S(1)}, u32[]{:S(2)}) copy-start(f32[1,272,1040]{2,1,0:T(8,128)S(1)} %get-tuple-element.24) | copy-start | bytes 3394564
  35.0 7.0 %copy-start.3 = (f32[1,272,1040]{2,1,0:T(8,128)}, f32[1,272,1040]{2,1,0:T(8,128)S(1)}, u32[]{:S(2)}) copy-start(f32[1,272,1040]{2,1,0:T(8,128)S(1)} %get-tuple-element.22) | copy-start | bytes 3394564
  35.0 7.0 %copy-start.9 = (f32[1,272,1040]{2,1,0:T(8,128)}, f32[1,272,1040]{2,1,0:T(8,128)S(1)}, u32[]{:S(2)}) copy-start(f32[1,272,1040]{2,1,0:T(8,128)S(1)} %get-tuple-element.23) | copy-start | bytes 3394564
  35.5 2.3 %copy-start.17 = (f32[1,272,1040]{2,1,0:T(8,128)}, f32[1,272,1040]{2,1,0:T(8,128)S(1)}, u32[]{:S(2)}) copy-start(f32[1,272,1040]{2,1,0:T(8,128)S(1)} %get-tuple-element.17) | copy-start | bytes 3394564
  35.5 6.5 %copy-start.6 = (f32[1,272,1040]{2,1,0:T(8,128)}, f32[1,272,1040]{2,1,0:T(8,128)S(1)}, u32[]{:S(2)}) copy-start(f32[1,272,1040]{2,1,0:T(8,128)S(1)} %get-tuple-element.16) | copy-start | bytes 3394564
  35.5 6.5 %copy-start.11 = (f32[1,272,1040]{2,1,0:T(8,128)}, f32[1,272,1040]{2,1,0:T(8,128)S(1)}, u32[]{:S(2)}) copy-start(f32[1,272,1040]{2,1,0:T(8,128)S(1)} %get-tuple-element.18) | copy-start | bytes 3394564
  70.7 5.4 %copy-start.2 = (f32[2,272,1040]{2,1,0:T(8,128)}, f32[2,272,1040]{2,1,0:T(8,128)S(1)}, u32[]{:S(2)}) copy-start(f32[2,272,1040]{2,1,0:T(8,128)S(1)} %multiply_subtract_fusion.1) | copy-start | bytes 6789124
  72.0 2.4 %copy-start.7 = (f32[1,272,1040]{2,1,0:T(8,128)S(1)}, f32[1,272,1040]{2,1,0:T(8,128)}, u32[]{:S(2)}) copy-start(f32[1,272,1040]{2,1,0:T(8,128)} %copy-done.6) | copy-start | bytes 3394564
  72.0 2.9 %copy-start.10 = (f32[1,272,1040]{2,1,0:T(8,128)S(1)}, f32[1,272,1040]{2,1,0:T(8,128)}, u32[]{:S(2)}) copy-start(f32[1,272,1040]{2,1,0:T(8,128)} %copy-done.9) | copy-start | bytes 3394564
  72.0 3.3 %copy-start.12 = (f32[1,272,1040]{2,1,0:T(8,128)S(1)}, f32[1,272,1040]{2,1,0:T(8,128)}, u32[]{:S(2)}) copy-start(f32[1,272,1040]{2,1,0:T(8,128)} %copy-done.11) | copy-start | bytes 3394564
  72.4 3.7 %copy-start.20 = (f32[1,272,1040]{2,1,0:T(8,128)}, f32[1,272,1040]{2,1,0:T(8,128)S(1)}, u32[]{:S(2)}) copy-start(f32[1,272,1040]{2,1,0:T(8,128)S(1)} %get-tuple-element.40) | copy-start | bytes 3394564
  72.5 3.7 %copy-start.21 = (f32[1,272,1040]{2,1,0:T(8,128)}, f32[1,272,1040]{2,1,0:T(8,128)S(1)}, u32[]{:S(2)}) copy-start(f32[1,272,1040]{2,1,0:T(8,128)S(1)} %get-tuple-element.41) | copy-start | bytes 3394564
  75.3 1.7 %copy-start.19 = (f32[2,272,1040]{2,1,0:T(8,128)S(1)}, f32[2,272,1040]{2,1,0:T(8,128)}, u32[]{:S(2)}) copy-start(f32[2,272,1040]{2,1,0:T(8,128)} %copy-done.18) | copy-start | bytes 6789124
  101.6 1.6 %copy-start.13 = (f32[2,272,1040]{2,1,0:T(8,128)}, f32[2,272,1040]{2,1,0:T(8,128)S(1)}, u32[]{:S(2)}) copy-start(f32[2,272,1040]{2,1,0:T(8,128)S(1)} %get-tuple-element.15) | copy-start | bytes 6789124
  102.8 1.7 %copy-start.8 = (f32[1,272,1040]{2,1,0:T(8,128)S(1)}, f32[1,272,1040]{2,1,0:T(8,128)}, u32[]{:S(2)}) copy-start(f32[1,272,1040]{2,1,0:T(8,128)} %copy-done.6) | copy-start | bytes 3394564
  102.8 2.5 %copy-start.24 = (f32[2,272,1040]{2,1,0:T(8,128)S(1)}, f32[2,272,1040]{2,1,0:T(8,128)}, u32[]{:S(2)}) copy-start(f32[2,272,1040]{2,1,0:T(8,128)} %get-tuple-element.36) | copy-start | bytes 6789124
  (9 other events, 11.8 us)

commit v15 on v14

--- a/solution.py
+++ b/solution.py
@@ -85,6 +85,7 @@
     pl.semaphore_wait(barrier, greeted)
 
     value = local_ref[0:SENT]
+    sent = []
     for stage, (axis, stride, members) in enumerate(stages):
         parts[stage, 0:SENT] = value
         got[stage, 0, 0:SENT] = value
@@ -102,7 +103,8 @@
             copy.start()
             copies.append(copy)
         for copy in copies:
-            copy.wait()
+            copy.wait_recv()
+        sent.extend(copies)
         digit = (me[axis] // stride) % members
         ordered = [got[stage, (member - digit) % members, 0:SENT] for member in range(members)]
         while len(ordered) > 1:
@@ -111,6 +113,8 @@
     norm, r_ar, r_ap = value[0:1], value[1:2], value[2:3]
     beta = norm / prev_ref[2:3]
     curve = r_ar + 2.0 * beta * r_ap + beta * beta * prev_ref[3:4]
+    for copy in sent:
+        copy.wait_send()
     out_ref[...] = jnp.zeros(out_ref.shape, out_ref.dtype)
     out_ref[0:1] = norm / curve
     out_ref[1:2] = beta

time: 138 us -> 138 us (level)
  no operation moved by 1% of the time
where the time goes in v15:
time: 138 us
  Pallas kernels  43.7 us (32%)
  other arithmetic  42.7 us (31%)
  local copies, waits for them, and re-layouts  30.2 us (22%)
  starting transfers between devices  11.4 us (8%)
  waiting for transfers between devices  8.34 us (6%)
    pallas_call x3, Pallas kernels, cg_scalars(): pl.pallas_call(functools.partial(reduce_kernel, stages), out_shape=jax.Sh...  43.7 us
    unnamed x61, local copies, waits for them, and re-layouts  14.8 us
    ppermute x4, starting transfers between devices, from_behind(): lax.ppermute(value, axis, [(source, source + steps) for source in range(l...  11.4 us
    sub x2, other arithmetic, per_device(): residual = residual - alpha * image  10.8 us
    add x1, other arithmetic, per_device(): solution = solution + alpha * direction  9.23 us
    ppermute x4, waiting for transfers between devices, from_behind(): lax.ppermute(value, axis, [(source, source + steps) for source in range(l...  8.34 us
    select_n x6, other arithmetic, cg_scalars(): tile = jnp.where(rows == k, local[k], tile)  7.2 us
    reduce_sum x3, other arithmetic, dots(): return jnp.stack([jnp.sum(interior(x) * interior(y)) for x, y in pairs])  4.22 us
  transfers between devices with their start and end apart: 4, of which 3 were waited for; matrix products, arithmetic and copies ran while one was open for 0% of the time, Pallas kernels for 0%

profile of v15, /device:TPU:1, one launch (start us, length us, event | category | flops | bytes accessed | tf_op | source)
XLA Modules:
  0.0 137.7 jit_solution(14878050020572911575)
XLA Ops:
  0.7 1.4 %bitcast_dynamic-update-slice_fusion.4 = f32[5,256,1024]{2,1,0:T(8,128)S(1)} fusion(f32[256,1024]{1,0:T(8,128)} %param.5), kind=kLoop, calls=%fused_computation.107 | loop fusion | bytes 2097152
  3.9 4.9 %collective-permute-start = (f32[5,8,1024]{2,1,0:T(8,128)S(1)}, f32[5,8,1024]{2,1,0:T(8,128)S(1)}, u32[]{:S(2)}, u32[]{:S(2)}) collective-permute-start(f32[5,8,1024]{2,1,0:T(8,128)S(1)} %get-tuple-element.30), channel_id=1, source_target_pairs={{0,16},{16,32},{32,48},{48,64},{64,80},{80,96},{96,112},{1,17},{17... | collective-permute-start | bytes 491528 | tf_op jit(solution)/shard_map/ppermute | solution.py:26
  8.8 1.9 %collective-permute-start.1 = (f32[5,8,1024]{2,1,0:T(8,128)S(1)}, f32[5,8,1024]{2,1,0:T(8,128)S(1)}, u32[]{:S(2)}, u32[]{:S(2)}) collective-permute-start(f32[5,8,1024]{2,1,0:T(8,128)S(1)} %get-tuple-element.31), channel_id=1, source_target_pairs={{16,0},{32,16},{48,32},{64,48},{80,64},{96,80},{112,96},{17,1},{33... | collective-permute-start | bytes 491528 | tf_op jit(solution)/shard_map/ppermute | solution.py:26
  11.1 4.4 %collective-permute-done.1 = f32[5,8,1024]{2,1,0:T(8,128)S(1)} collective-permute-done((f32[5,8,1024]{2,1,0:T(8,128)S(1)}, f32[5,8,1024]{2,1,0:T(8,128)S(1)}, u32[]{:S(2)}, u32[]{:S(2)}) %collective-permute-start.1) | collective-permute-done | bytes 163872 | tf_op jit(solution)/shard_map/ppermute | solution.py:26
  16.3 2.6 %copy-done = f32[5,272,1040]{2,1,0:T(8,128)} copy-done((f32[5,272,1040]{2,1,0:T(8,128)}, f32[5,272,1040]{2,1,0:T(8,128)S(1)}, u32[]{:S(2)}) %copy-start) | copy-done | bytes 5657624
  19.8 3.2 %collective-permute-start.3 = (f32[5,272,8]{1,2,0:T(8,128)S(1)}, f32[5,272,8]{1,2,0:T(8,128)S(1)}, u32[]{:S(2)}, u32[]{:S(2)}) collective-permute-start(f32[5,272,8]{1,2,0:T(8,128)S(1)} %copy.17), channel_id=1, source_target_pairs={{0,1},{1,2},{2,3},{3,4},{4,5},{5,6},{6,7},{7,8},{8,9},{9,10},{10,1... | collective-permute-start | bytes 130568 | tf_op jit(solution)/shard_map/ppermute | solution.py:26
  24.3 3.6 %collective-permute-done.2 = f32[5,272,8]{1,2,0:T(8,128)S(1)} collective-permute-done((f32[5,272,8]{1,2,0:T(8,128)S(1)}, f32[5,272,8]{1,2,0:T(8,128)S(1)}, u32[]{:S(2)}, u32[]{:S(2)}) %collective-permute-start.2) | collective-permute-done | bytes 43552 | tf_op jit(solution)/shard_map/ppermute | solution.py:26
  29.2 2.4 %slice_bitcast_fusion.19 = (f32[271,1040]{1,0:T(8,128)S(1)}, f32[271,1040]{1,0:T(8,128)S(1)}, f32[271,1040]{1,0:T(8,128)S(1)}) fusion(f32[5,272,1040]{2,1,0:T(8,128)} %constant_dynamic-update-slice_fusion), kind=kLoop, calls=%fused_computation.67 | loop fusion | bytes 6764160 | tf_op jit(solution)/shard_map/slice | solution.py:45
  31.7 1.5 %copy-done.1 = f32[5,272,1040]{2,1,0:T(8,128)S(1)} copy-done((f32[5,272,1040]{2,1,0:T(8,128)S(1)}, f32[5,272,1040]{2,1,0:T(8,128)}, u32[]{:S(2)}) %copy-start.1) | copy-done | bytes 5657624
  37.9 2.6 %fusion.1 = (f32[2,272,1040]{2,1,0:T(8,128)}, f32[2,272,1040]{2,1,0:T(8,128)S(1)}) fusion(f32[1,272,1040]{2,1,0:T(8,128)S(1)} %get-tuple-element.23, f32[1,272,1040]{2,1,0:T(8,128)S(1)} %get-tuple-element.18, f32[1,272,1040]{2,1,0:T(8,128)S(1)} %get-tuple-element.45, f32[1,272,1040]{2,1,0:T(8,128)S(1)} %get-tuple-element.44, ...), kind=kLoop, calls=%fused_computation.8 | loop fusion | flops 10749440 | bytes 15841280 | tf_op jit(solution)/shard_map/jit(_where)/select_n | solution.py:165
  43.4 1.4 %multiply_reduce_fusion.4 = (f32[]{:T(128)}, f32[]{:T(128)}) fusion(f32[2,272,1040]{2,1,0:T(8,128)S(1)} %fusion.5, f32[2,272,1040]{2,1,0:T(8,128)S(1)} %get-tuple-element.37), kind=kLoop, calls=%fused_computation.39 | loop fusion | flops 2097150 | bytes 4194312 | tf_op jit(solution)/shard_map/reduce_sum | solution.py:154
  45.6 1.3 broadcast_select_fusion.local_ref
  47.6 17.7 %shard_map.76.prev_ref = f32[8,128]{1,0:T(8,128)} custom-call(f32[8,128]{1,0:T(8,128)} %broadcast_select_fusion.local_ref, f32[8,128]{1,0:T(8,128)} %iota.49.prev_ref), custom_call_target="tpu_custom_call" | custom-call | tf_op jit(solution)/shard_map/pallas_call | solution.py:133
  66.5 4.2 %multiply_subtract_fusion.1 = f32[2,272,1040]{2,1,0:T(8,128)S(1)} fusion(f32[2,272,1040]{2,1,0:T(8,128)S(1)} %get-tuple-element.37, f32[]{:T(128)} %bitcast.30, f32[1,272,1040]{2,1,0:T(8,128)} %copy-done.15, f32[1,272,1040]{2,1,0:T(8,128)} %copy-done.14, f32[1,272,1040]{2,1,0:T(8,128)} %copy-done.9, f32[1,272,1040]{2,1,0:T(8,128)} %copy-done.11, ...), kind=kLoop, calls=%fused_computation.23 | loop fusion | flops 7354880 | bytes 11315204 | tf_op jit(solution)/shard_map/sub | solution.py:179
  79.0 2.0 %select_select_fusion.1.local_ref = f32[8,128]{1,0:T(8,128)} fusion(f32[8]{0:T(128)S(1)} %fusion.29, f32[]{:T(128)} %get-tuple-element.10, f32[]{:T(128)} %get-tuple-element.9, pred[8]{0:T(512)(128)(4,1)S(1)} %get-tuple-element.54, pred[8]{0:T(512)(128)(4,1)S(1)} %get-tuple-element.55), kind=kLoop, calls=%fused_computation.113 | loop fusion | flops 2048 | bytes 4152 | tf_op jit(solution)/shard_map/jit(_where)/select_n | solution.py:132
  81.0 12.8 %shard_map.77.prev_ref = f32[8,128]{1,0:T(8,128)} custom-call(f32[8,128]{1,0:T(8,128)} %select_select_fusion.1.local_ref, f32[8,128]{1,0:T(8,128)} %shard_map.76.prev_ref), custom_call_target="tpu_custom_call" | custom-call | tf_op jit(solution)/shard_map/pallas_call | solution.py:133
  93.7 1.3 fusion.34
  95.1 6.5 %multiply_subtract_fusion = (f32[2,272,1040]{2,1,0:T(8,128)S(1)}, f32[2,272,1040]{2,1,0:T(8,128)S(1)}) fusion(f32[2,272,1040]{2,1,0:T(8,128)} %copy-done.2, f32[]{:T(128)} %bitcast.36, f32[]{:T(128)} %bitcast.37, f32[1,272,1040]{2,1,0:T(8,128)} %copy-done.21, f32[1,272,1040]{2,1,0:T(8,128)} %copy-done.20, f32[1,272,1040]{2,1,0:T(8,128)} %copy-done.9, ...), kind=kLoop, calls=%fused_computation.21 | loop fusion | flops 10749440 | bytes 18104328 | tf_op jit(solution)/shard_map/sub | solution.py:179
  105.3 1.5 %fusion.12 = (f32[]{:T(128)}, f32[]{:T(128)}, f32[]{:T(128)}) fusion(f32[2,272,1040]{2,1,0:T(8,128)S(1)} %get-tuple-element.15, f32[2,272,1040]{2,1,0:T(8,128)S(1)} %get-tuple-element.14, f32[1,272,1040]{2,1,0:T(8,128)S(1)} %get-tuple-element.39, f32[1,272,1040]{2,1,0:T(8,128)S(1)} %get-tuple-element.38, f32[2,272,1040]{2,1,0:T(8,128)S(1)} %copy-done.24, ...), kind=kLoop, calls=%fused_computation.32 | loop fusion | flops 5767165 | bytes 10817548 | tf_op jit(solution)/shard_map/reduce_sum | solution.py:154
  107.5 2.0 %select_select_fusion.local_ref = f32[8,128]{1,0:T(8,128)} fusion(f32[8]{0:T(128)S(1)} %fusion.28, f32[]{:T(128)} %get-tuple-element.8, f32[]{:T(128)} %get-tuple-element.6, pred[8]{0:T(512)(128)(4,1)S(1)} %get-tuple-element.54, pred[8]{0:T(512)(128)(4,1)S(1)} %get-tuple-element.55), kind=kLoop, calls=%fused_computation.112 | loop fusion | flops 2048 | bytes 4152 | tf_op jit(solution)/shard_map/jit(_where)/select_n | solution.py:132
  109.4 13.2 %shard_map.78 = f32[8,128]{1,0:T(8,128)} custom-call(f32[8,128]{1,0:T(8,128)} %select_select_fusion.local_ref, f32[8,128]{1,0:T(8,128)} %shard_map.77.prev_ref), custom_call_target="tpu_custom_call" | custom-call | tf_op jit(solution)/shard_map/pallas_call | solution.py:133
  124.0 9.2 %multiply_add_fusion = f32[2,272,1040]{2,1,0:T(8,128)S(1)} fusion(f32[2,272,1040]{2,1,0:T(8,128)} %copy-done.2, f32[2,272,1040]{2,1,0:T(8,128)S(1)} %get-tuple-element.37, f32[]{:T(128)} %bitcast.44, f32[]{:T(128)} %bitcast.43, f32[]{:T(128)} %bitcast.37, f32[]{:T(128)} %bitcast.36, f32[]{:T(128)} %bitcast.30, f32[2,272,1040]{2,1,0:T(8,128)} %copy-done.13, ...), kind=kLoop, calls=%fused_computation.20 | loop fusion | flops 10749440 | bytes 18104340 | tf_op jit(solution)/shard_map/add | solution.py:176
  133.3 1.6 %slice_bitcast_fusion.24 = (f32[256,1024]{1,0:T(8,128)}, f32[256,1024]{1,0:T(8,128)}) fusion(f32[2,272,1040]{2,1,0:T(8,128)S(1)} %multiply_add_fusion), kind=kLoop, calls=%fused_computation.95 | loop fusion | bytes 4194304 | tf_op jit(solution)/shard_map/squeeze | solution.py:187
  136.2 1.4 %slice_subtract_fusion.1 = f32[256,1024]{1,0:T(8,128)} fusion(f32[272,1040]{1,0:T(8,128)S(1)} %copy-done.23, f32[271,1040]{1,0:T(8,128)S(1)} %slice_bitcast_fusion, f32[272,1040]{1,0:T(8,128)S(1)} %get-tuple-element.35, f32[272,1040]{1,0:T(8,128)S(1)} %get-tuple-element.34, f32[272,1039]{1,0:T(8,128)S(1)} %bitcast.130, f32[272,1]{1,0:T(8,128)S(1)} %slice.402), kind=kLoop, calls=%fused_computation.97 | loop fusion | flops 1572864 | bytes 6453184 | tf_op jit(solution)/shard_map/sub | solution.py:185
  (125 shorter events, 31.4 us)
Async XLA Ops:
  0.6 1.5 %copy-start.25 = (f32[256,1024]{1,0:T(8,128)S(1)}, f32[256,1024]{1,0:T(8,128)}, u32[]{:S(2)}) copy-start(f32[256,1024]{1,0:T(8,128)} %param.6) | copy-start | bytes 3145732
  0.6 1.8 %copy-start.26 = (s32[256,1024]{1,0:T(8,128)S(1)}, s32[256,1024]{1,0:T(8,128)}, u32[]{:S(2)}) copy-start(s32[256,1024]{1,0:T(8,128)} %param.7) | copy-start | bytes 3145732
  3.9 7.2 %collective-permute-start = (f32[5,8,1024]{2,1,0:T(8,128)S(1)}, f32[5,8,1024]{2,1,0:T(8,128)S(1)}, u32[]{:S(2)}, u32[]{:S(2)}) collective-permute-start(f32[5,8,1024]{2,1,0:T(8,128)S(1)} %get-tuple-element.30), channel_id=1, source_target_pairs={{0,16},{16,32},{32,48},{48,64},{64,80},{80,96},{96,112},{1,17},{17... | collective-permute-start | bytes 491528 | tf_op jit(solution)/shard_map/ppermute | solution.py:26
  8.8 6.6 %collective-permute-start.1 = (f32[5,8,1024]{2,1,0:T(8,128)S(1)}, f32[5,8,1024]{2,1,0:T(8,128)S(1)}, u32[]{:S(2)}, u32[]{:S(2)}) collective-permute-start(f32[5,8,1024]{2,1,0:T(8,128)S(1)} %get-tuple-element.31), channel_id=1, source_target_pairs={{16,0},{32,16},{48,32},{64,48},{80,64},{96,80},{112,96},{17,1},{33... | collective-permute-start | bytes 491528 | tf_op jit(solution)/shard_map/ppermute | solution.py:26
  16.3 2.6 %copy-start = (f32[5,272,1040]{2,1,0:T(8,128)}, f32[5,272,1040]{2,1,0:T(8,128)S(1)}, u32[]{:S(2)}) copy-start(f32[5,272,1040]{2,1,0:T(8,128)S(1)} %select_maximum_fusion) | copy-start | bytes 16972804
  19.8 4.5 %collective-permute-start.3 = (f32[5,272,8]{1,2,0:T(8,128)S(1)}, f32[5,272,8]{1,2,0:T(8,128)S(1)}, u32[]{:S(2)}, u32[]{:S(2)}) collective-permute-start(f32[5,272,8]{1,2,0:T(8,128)S(1)} %copy.17), channel_id=1, source_target_pairs={{0,1},{1,2},{2,3},{3,4},{4,5},{5,6},{6,7},{7,8},{8,9},{9,10},{10,1... | collective-permute-start | bytes 130568 | tf_op jit(solution)/shard_map/ppermute | solution.py:26
  23.0 5.0 %collective-permute-start.2 = (f32[5,272,8]{1,2,0:T(8,128)S(1)}, f32[5,272,8]{1,2,0:T(8,128)S(1)}, u32[]{:S(2)}, u32[]{:S(2)}) collective-permute-start(f32[5,272,8]{1,2,0:T(8,128)S(1)} %copy.16), channel_id=1, source_target_pairs={{1,0},{2,1},{3,2},{4,3},{5,4},{6,5},{7,6},{8,7},{9,8},{10,9},{11,1... | collective-permute-start | bytes 130568 | tf_op jit(solution)/shard_map/ppermute | solution.py:26
  29.2 3.9 %copy-start.1 = (f32[5,272,1040]{2,1,0:T(8,128)S(1)}, f32[5,272,1040]{2,1,0:T(8,128)}, u32[]{:S(2)}) copy-start(f32[5,272,1040]{2,1,0:T(8,128)} %constant_dynamic-update-slice_fusion) | copy-start | bytes 16972804
  35.0 2.9 %copy-start.16 = (f32[1,272,1040]{2,1,0:T(8,128)}, f32[1,272,1040]{2,1,0:T(8,128)S(1)}, u32[]{:S(2)}) copy-start(f32[1,272,1040]{2,1,0:T(8,128)S(1)} %get-tuple-element.24) | copy-start | bytes 3394564
  35.0 7.0 %copy-start.3 = (f32[1,272,1040]{2,1,0:T(8,128)}, f32[1,272,1040]{2,1,0:T(8,128)S(1)}, u32[]{:S(2)}) copy-start(f32[1,272,1040]{2,1,0:T(8,128)S(1)} %get-tuple-element.22) | copy-start | bytes 3394564
  35.0 7.0 %copy-start.9 = (f32[1,272,1040]{2,1,0:T(8,128)}, f32[1,272,1040]{2,1,0:T(8,128)S(1)}, u32[]{:S(2)}) copy-start(f32[1,272,1040]{2,1,0:T(8,128)S(1)} %get-tuple-element.23) | copy-start | bytes 3394564
  35.5 2.3 %copy-start.17 = (f32[1,272,1040]{2,1,0:T(8,128)}, f32[1,272,1040]{2,1,0:T(8,128)S(1)}, u32[]{:S(2)}) copy-start(f32[1,272,1040]{2,1,0:T(8,128)S(1)} %get-tuple-element.17) | copy-start | bytes 3394564
  35.5 6.5 %copy-start.6 = (f32[1,272,1040]{2,1,0:T(8,128)}, f32[1,272,1040]{2,1,0:T(8,128)S(1)}, u32[]{:S(2)}) copy-start(f32[1,272,1040]{2,1,0:T(8,128)S(1)} %get-tuple-element.16) | copy-start | bytes 3394564
  35.5 6.5 %copy-start.11 = (f32[1,272,1040]{2,1,0:T(8,128)}, f32[1,272,1040]{2,1,0:T(8,128)S(1)}, u32[]{:S(2)}) copy-start(f32[1,272,1040]{2,1,0:T(8,128)S(1)} %get-tuple-element.18) | copy-start | bytes 3394564
  70.7 5.4 %copy-start.2 = (f32[2,272,1040]{2,1,0:T(8,128)}, f32[2,272,1040]{2,1,0:T(8,128)S(1)}, u32[]{:S(2)}) copy-start(f32[2,272,1040]{2,1,0:T(8,128)S(1)} %multiply_subtract_fusion.1) | copy-start | bytes 6789124
  72.0 2.4 %copy-start.7 = (f32[1,272,1040]{2,1,0:T(8,128)S(1)}, f32[1,272,1040]{2,1,0:T(8,128)}, u32[]{:S(2)}) copy-start(f32[1,272,1040]{2,1,0:T(8,128)} %copy-done.6) | copy-start | bytes 3394564
  72.0 2.9 %copy-start.10 = (f32[1,272,1040]{2,1,0:T(8,128)S(1)}, f32[1,272,1040]{2,1,0:T(8,128)}, u32[]{:S(2)}) copy-start(f32[1,272,1040]{2,1,0:T(8,128)} %copy-done.9) | copy-start | bytes 3394564
  72.0 3.3 %copy-start.12 = (f32[1,272,1040]{2,1,0:T(8,128)S(1)}, f32[1,272,1040]{2,1,0:T(8,128)}, u32[]{:S(2)}) copy-start(f32[1,272,1040]{2,1,0:T(8,128)} %copy-done.11) | copy-start | bytes 3394564
  72.4 3.7 %copy-start.20 = (f32[1,272,1040]{2,1,0:T(8,128)}, f32[1,272,1040]{2,1,0:T(8,128)S(1)}, u32[]{:S(2)}) copy-start(f32[1,272,1040]{2,1,0:T(8,128)S(1)} %get-tuple-element.40) | copy-start | bytes 3394564
  72.5 3.7 %copy-start.21 = (f32[1,272,1040]{2,1,0:T(8,128)}, f32[1,272,1040]{2,1,0:T(8,128)S(1)}, u32[]{:S(2)}) copy-start(f32[1,272,1040]{2,1,0:T(8,128)S(1)} %get-tuple-element.41) | copy-start | bytes 3394564
  75.3 1.7 %copy-start.19 = (f32[2,272,1040]{2,1,0:T(8,128)S(1)}, f32[2,272,1040]{2,1,0:T(8,128)}, u32[]{:S(2)}) copy-start(f32[2,272,1040]{2,1,0:T(8,128)} %copy-done.18) | copy-start | bytes 6789124
  101.6 1.6 %copy-start.13 = (f32[2,272,1040]{2,1,0:T(8,128)}, f32[2,272,1040]{2,1,0:T(8,128)S(1)}, u32[]{:S(2)}) copy-start(f32[2,272,1040]{2,1,0:T(8,128)S(1)} %get-tuple-element.15) | copy-start | bytes 6789124
  102.9 1.7 %copy-start.8 = (f32[1,272,1040]{2,1,0:T(8,128)S(1)}, f32[1,272,1040]{2,1,0:T(8,128)}, u32[]{:S(2)}) copy-start(f32[1,272,1040]{2,1,0:T(8,128)} %copy-done.6) | copy-start | bytes 3394564
  102.9 2.5 %copy-start.24 = (f32[2,272,1040]{2,1,0:T(8,128)S(1)}, f32[2,272,1040]{2,1,0:T(8,128)}, u32[]{:S(2)}) copy-start(f32[2,272,1040]{2,1,0:T(8,128)} %get-tuple-element.36) | copy-start | bytes 6789124
  (9 other events, 11.8 us)

commit v16 on v14

--- a/solution.py
+++ b/solution.py
@@ -12,7 +12,7 @@
 ITERS = 3
 MARGIN_ROWS = 8
 MARGIN_COLS = 8
-SENT = 4
+SENT = 1
 
 
 courant = -0.4
@@ -108,9 +108,10 @@
         while len(ordered) > 1:
             ordered = [ordered[k] + ordered[k + 1] for k in range(0, len(ordered), 2)]
         value = ordered[0]
-    norm, r_ar, r_ap = value[0:1], value[1:2], value[2:3]
-    beta = norm / prev_ref[2:3]
-    curve = r_ar + 2.0 * beta * r_ap + beta * beta * prev_ref[3:4]
+    norm, r_ar, r_ap = value[:, 0:1], value[:, 1:2], value[:, 2:3]
+    beta = jnp.broadcast_to(norm / prev_ref[2:3, 0:1], (1, 128))
+    curve = jnp.broadcast_to(r_ar + 2.0 * beta[:, 0:1] * r_ap + beta[:, 0:1] * beta[:, 0:1] * prev_ref[3:4, 0:1], (1, 128))
+    norm = jnp.broadcast_to(norm, (1, 128))
     out_ref[...] = jnp.zeros(out_ref.shape, out_ref.dtype)
     out_ref[0:1] = norm / curve
     out_ref[1:2] = beta
@@ -123,9 +124,10 @@
     stages = stages_of(sizes)
     widest = max(members for _, _, members in stages)
     rows = lax.broadcasted_iota(jnp.int32, (8, 128), 0)
+    lanes = lax.broadcasted_iota(jnp.int32, (8, 128), 1)
     tile = jnp.zeros((8, 128), jnp.float32)
     for k in range(local.shape[0]):
-        tile = jnp.where(rows == k, local[k], tile)
+        tile = jnp.where((rows == 0) & (lanes == k), local[k], tile)
     return pl.pallas_call(
         functools.partial(reduce_kernel, stages),
         out_shape=jax.ShapeDtypeStruct((8, 128), jnp.float32),

time: 138 us -> 138 us (level)
    select_n x6 -> x3, other arithmetic: 7.2 us -> 7.1 us  [cg_scalars(): tile = jnp.where((rows == 0) & (lanes == k), local[k], tile)]
where the time goes in v16:
time: 138 us; the launch traced here: 137 us
  Pallas kernels  43.6 us (32%)
  other arithmetic  42.6 us (31%)
  local copies, waits for them, and re-layouts  30.2 us (22%)
  starting transfers between devices  11.4 us (8%)
  waiting for transfers between devices  8.32 us (6%)
    pallas_call x3, Pallas kernels, cg_scalars(): pl.pallas_call(functools.partial(reduce_kernel, stages), out_shape=jax.Sh...  43.6 us
    unnamed x61, local copies, waits for them, and re-layouts  14.9 us
    ppermute x4, starting transfers between devices, from_behind(): lax.ppermute(value, axis, [(source, source + steps) for source in range(l...  11.4 us
    sub x2, other arithmetic, per_device(): residual = residual - alpha * image  10.8 us
    add x1, other arithmetic, per_device(): solution = solution + alpha * direction  9.23 us
    ppermute x4, waiting for transfers between devices, from_behind(): lax.ppermute(value, axis, [(source, source + steps) for source in range(l...  8.32 us
    select_n x3, other arithmetic, cg_scalars(): tile = jnp.where((rows == 0) & (lanes == k), local[k], tile)  7.1 us
    reduce_sum x3, other arithmetic, dots(): return jnp.stack([jnp.sum(interior(x) * interior(y)) for x, y in pairs])  4.22 us
  transfers between devices with their start and end apart: 4, of which 3 were waited for; matrix products, arithmetic and copies ran while one was open for 0% of the time, Pallas kernels for 0%

profile of v16, /device:TPU:1, one launch (start us, length us, event | category | flops | bytes accessed | tf_op | source)
XLA Modules:
  0.0 137.4 jit_solution(1412610228263337503)
XLA Ops:
  0.7 1.4 %bitcast_dynamic-update-slice_fusion.4 = f32[5,256,1024]{2,1,0:T(8,128)S(1)} fusion(f32[256,1024]{1,0:T(8,128)} %param.5), kind=kLoop, calls=%fused_computation.107 | loop fusion | bytes 2097152
  3.9 4.9 %collective-permute-start = (f32[5,8,1024]{2,1,0:T(8,128)S(1)}, f32[5,8,1024]{2,1,0:T(8,128)S(1)}, u32[]{:S(2)}, u32[]{:S(2)}) collective-permute-start(f32[5,8,1024]{2,1,0:T(8,128)S(1)} %get-tuple-element.30), channel_id=1, source_target_pairs={{0,16},{16,32},{32,48},{48,64},{64,80},{80,96},{96,112},{1,17},{17... | collective-permute-start | bytes 491528 | tf_op jit(solution)/shard_map/ppermute | solution.py:26
  8.8 1.9 %collective-permute-start.1 = (f32[5,8,1024]{2,1,0:T(8,128)S(1)}, f32[5,8,1024]{2,1,0:T(8,128)S(1)}, u32[]{:S(2)}, u32[]{:S(2)}) collective-permute-start(f32[5,8,1024]{2,1,0:T(8,128)S(1)} %get-tuple-element.31), channel_id=1, source_target_pairs={{16,0},{32,16},{48,32},{64,48},{80,64},{96,80},{112,96},{17,1},{33... | collective-permute-start | bytes 491528 | tf_op jit(solution)/shard_map/ppermute | solution.py:26
  11.1 4.4 %collective-permute-done.1 = f32[5,8,1024]{2,1,0:T(8,128)S(1)} collective-permute-done((f32[5,8,1024]{2,1,0:T(8,128)S(1)}, f32[5,8,1024]{2,1,0:T(8,128)S(1)}, u32[]{:S(2)}, u32[]{:S(2)}) %collective-permute-start.1) | collective-permute-done | bytes 163872 | tf_op jit(solution)/shard_map/ppermute | solution.py:26
  16.3 2.6 %copy-done = f32[5,272,1040]{2,1,0:T(8,128)} copy-done((f32[5,272,1040]{2,1,0:T(8,128)}, f32[5,272,1040]{2,1,0:T(8,128)S(1)}, u32[]{:S(2)}) %copy-start) | copy-done | bytes 5657624
  19.7 3.2 %collective-permute-start.3 = (f32[5,272,8]{1,2,0:T(8,128)S(1)}, f32[5,272,8]{1,2,0:T(8,128)S(1)}, u32[]{:S(2)}, u32[]{:S(2)}) collective-permute-start(f32[5,272,8]{1,2,0:T(8,128)S(1)} %copy.17), channel_id=1, source_target_pairs={{0,1},{1,2},{2,3},{3,4},{4,5},{5,6},{6,7},{7,8},{8,9},{9,10},{10,1... | collective-permute-start | bytes 130568 | tf_op jit(solution)/shard_map/ppermute | solution.py:26
  24.3 3.6 %collective-permute-done.2 = f32[5,272,8]{1,2,0:T(8,128)S(1)} collective-permute-done((f32[5,272,8]{1,2,0:T(8,128)S(1)}, f32[5,272,8]{1,2,0:T(8,128)S(1)}, u32[]{:S(2)}, u32[]{:S(2)}) %collective-permute-start.2) | collective-permute-done | bytes 43552 | tf_op jit(solution)/shard_map/ppermute | solution.py:26
  29.2 2.4 %slice_bitcast_fusion.19 = (f32[271,1040]{1,0:T(8,128)S(1)}, f32[271,1040]{1,0:T(8,128)S(1)}, f32[271,1040]{1,0:T(8,128)S(1)}) fusion(f32[5,272,1040]{2,1,0:T(8,128)} %constant_dynamic-update-slice_fusion), kind=kLoop, calls=%fused_computation.67 | loop fusion | bytes 6764160 | tf_op jit(solution)/shard_map/slice | solution.py:45
  31.6 1.5 %copy-done.1 = f32[5,272,1040]{2,1,0:T(8,128)S(1)} copy-done((f32[5,272,1040]{2,1,0:T(8,128)S(1)}, f32[5,272,1040]{2,1,0:T(8,128)}, u32[]{:S(2)}) %copy-start.1) | copy-done | bytes 5657624
  37.8 2.6 %fusion.1 = (f32[2,272,1040]{2,1,0:T(8,128)}, f32[2,272,1040]{2,1,0:T(8,128)S(1)}) fusion(f32[1,272,1040]{2,1,0:T(8,128)S(1)} %get-tuple-element.23, f32[1,272,1040]{2,1,0:T(8,128)S(1)} %get-tuple-element.18, f32[1,272,1040]{2,1,0:T(8,128)S(1)} %get-tuple-element.45, f32[1,272,1040]{2,1,0:T(8,128)S(1)} %get-tuple-element.44, ...), kind=kLoop, calls=%fused_computation.8 | loop fusion | flops 10749440 | bytes 15841280 | tf_op jit(solution)/shard_map/jit(_where)/select_n | solution.py:163
  43.4 1.4 %multiply_reduce_fusion.4 = (f32[]{:T(128)}, f32[]{:T(128)}) fusion(f32[2,272,1040]{2,1,0:T(8,128)S(1)} %fusion.5, f32[2,272,1040]{2,1,0:T(8,128)S(1)} %get-tuple-element.37), kind=kLoop, calls=%fused_computation.39 | loop fusion | flops 2097150 | bytes 4194312 | tf_op jit(solution)/shard_map/reduce_sum | solution.py:152
  44.9 2.0 %and_select_fusion.5.local_ref = f32[8,128]{1,0:T(8,128)} fusion(f32[]{:T(128)} %get-tuple-element.13, f32[]{:T(128)} %get-tuple-element.12, pred[128]{0:T(512)(128)(4,1)S(1)} %get-tuple-element.54, pred[128]{0:T(512)(128)(4,1)S(1)} %get-tuple-element.55, pred[8]{0:T(512)(128)(4,1)S(1)} %iota_compare_fusion.4), kind=kLoop, calls=%fused_computation.117 | loop fusion | flops 4096 | bytes 4368 | tf_op jit(solution)/shard_map/jit(_where)/select_n | solution.py:130
  47.5 17.6 %shard_map.76.prev_ref = f32[8,128]{1,0:T(8,128)} custom-call(f32[8,128]{1,0:T(8,128)} %and_select_fusion.5.local_ref, f32[8,128]{1,0:T(8,128)} %iota.89.prev_ref), custom_call_target="tpu_custom_call" | custom-call | tf_op jit(solution)/shard_map/pallas_call | solution.py:131
  66.3 4.2 %multiply_subtract_fusion.1 = f32[2,272,1040]{2,1,0:T(8,128)S(1)} fusion(f32[2,272,1040]{2,1,0:T(8,128)S(1)} %get-tuple-element.37, f32[]{:T(128)} %bitcast.30, f32[1,272,1040]{2,1,0:T(8,128)} %copy-done.15, f32[1,272,1040]{2,1,0:T(8,128)} %copy-done.14, f32[1,272,1040]{2,1,0:T(8,128)} %copy-done.9, f32[1,272,1040]{2,1,0:T(8,128)} %copy-done.11, ...), kind=kLoop, calls=%fused_computation.23 | loop fusion | flops 7354880 | bytes 11315204 | tf_op jit(solution)/shard_map/sub | solution.py:177
  78.2 2.6 %and_select_fusion.7.local_ref = f32[8,128]{1,0:T(8,128)} fusion(f32[]{:T(128)} %get-tuple-element.11, f32[]{:T(128)} %get-tuple-element.10, f32[]{:T(128)} %get-tuple-element.9, pred[128]{0:T(512)(128)(4,1)S(1)} %iota_compare_fusion.1, pred[128]{0:T(512)(128)(4,1)S(1)} %get-tuple-element.54, pred[128]{0:T(512)(128)(4,1)S(1)} %get-tuple-element.55, ...), kind=kLoop, calls=%fused_computation.119 | loop fusion | flops 6144 | bytes 4500 | tf_op jit(solution)/shard_map/jit(_where)/select_n | solution.py:130
  80.8 12.7 %shard_map.77.prev_ref = f32[8,128]{1,0:T(8,128)} custom-call(f32[8,128]{1,0:T(8,128)} %and_select_fusion.7.local_ref, f32[8,128]{1,0:T(8,128)} %shard_map.76.prev_ref), custom_call_target="tpu_custom_call" | custom-call | tf_op jit(solution)/shard_map/pallas_call | solution.py:131
  93.5 1.3 fusion.31
  94.8 6.5 %multiply_subtract_fusion = (f32[2,272,1040]{2,1,0:T(8,128)S(1)}, f32[2,272,1040]{2,1,0:T(8,128)S(1)}) fusion(f32[2,272,1040]{2,1,0:T(8,128)} %copy-done.2, f32[]{:T(128)} %bitcast.36, f32[]{:T(128)} %bitcast.37, f32[1,272,1040]{2,1,0:T(8,128)} %copy-done.21, f32[1,272,1040]{2,1,0:T(8,128)} %copy-done.20, f32[1,272,1040]{2,1,0:T(8,128)} %copy-done.9, ...), kind=kLoop, calls=%fused_computation.21 | loop fusion | flops 10749440 | bytes 18104328 | tf_op jit(solution)/shard_map/sub | solution.py:177
  105.1 1.5 %fusion.12 = (f32[]{:T(128)}, f32[]{:T(128)}, f32[]{:T(128)}) fusion(f32[2,272,1040]{2,1,0:T(8,128)S(1)} %get-tuple-element.15, f32[2,272,1040]{2,1,0:T(8,128)S(1)} %get-tuple-element.14, f32[1,272,1040]{2,1,0:T(8,128)S(1)} %get-tuple-element.39, f32[1,272,1040]{2,1,0:T(8,128)S(1)} %get-tuple-element.38, f32[2,272,1040]{2,1,0:T(8,128)S(1)} %copy-done.24, ...), kind=kLoop, calls=%fused_computation.32 | loop fusion | flops 5767165 | bytes 10817548 | tf_op jit(solution)/shard_map/reduce_sum | solution.py:152
  106.6 2.5 %and_select_fusion.6.local_ref = f32[8,128]{1,0:T(8,128)} fusion(f32[]{:T(128)} %get-tuple-element.7, f32[]{:T(128)} %get-tuple-element.8, f32[]{:T(128)} %get-tuple-element.6, pred[128]{0:T(512)(128)(4,1)S(1)} %iota_compare_fusion.1, pred[128]{0:T(512)(128)(4,1)S(1)} %get-tuple-element.54, pred[128]{0:T(512)(128)(4,1)S(1)} %get-tuple-element.55, ...), kind=kLoop, calls=%fused_computation.118 | loop fusion | flops 6144 | bytes 4500 | tf_op jit(solution)/shard_map/jit(_where)/select_n | solution.py:130
  109.1 13.3 %shard_map.78 = f32[8,128]{1,0:T(8,128)} custom-call(f32[8,128]{1,0:T(8,128)} %and_select_fusion.6.local_ref, f32[8,128]{1,0:T(8,128)} %shard_map.77.prev_ref), custom_call_target="tpu_custom_call" | custom-call | tf_op jit(solution)/shard_map/pallas_call | solution.py:131
  123.7 9.2 %multiply_add_fusion = f32[2,272,1040]{2,1,0:T(8,128)S(1)} fusion(f32[2,272,1040]{2,1,0:T(8,128)} %copy-done.2, f32[2,272,1040]{2,1,0:T(8,128)S(1)} %get-tuple-element.37, f32[]{:T(128)} %bitcast.44, f32[]{:T(128)} %bitcast.43, f32[]{:T(128)} %bitcast.37, f32[]{:T(128)} %bitcast.36, f32[]{:T(128)} %bitcast.30, f32[2,272,1040]{2,1,0:T(8,128)} %copy-done.13, ...), kind=kLoop, calls=%fused_computation.20 | loop fusion | flops 10749440 | bytes 18104340 | tf_op jit(solution)/shard_map/add | solution.py:174
  133.1 1.6 %slice_bitcast_fusion.24 = (f32[256,1024]{1,0:T(8,128)}, f32[256,1024]{1,0:T(8,128)}) fusion(f32[2,272,1040]{2,1,0:T(8,128)S(1)} %multiply_add_fusion), kind=kLoop, calls=%fused_computation.95 | loop fusion | bytes 4194304 | tf_op jit(solution)/shard_map/squeeze | solution.py:185
  136.0 1.5 %slice_subtract_fusion.1 = f32[256,1024]{1,0:T(8,128)} fusion(f32[272,1040]{1,0:T(8,128)S(1)} %copy-done.23, f32[271,1040]{1,0:T(8,128)S(1)} %slice_bitcast_fusion, f32[272,1040]{1,0:T(8,128)S(1)} %get-tuple-element.35, f32[272,1040]{1,0:T(8,128)S(1)} %get-tuple-element.34, f32[272,1039]{1,0:T(8,128)S(1)} %bitcast.130, f32[272,1]{1,0:T(8,128)S(1)} %slice.402), kind=kLoop, calls=%fused_computation.97 | loop fusion | flops 1572864 | bytes 6453184 | tf_op jit(solution)/shard_map/sub | solution.py:183
  (124 shorter events, 29.4 us)
Async XLA Ops:
  0.6 1.5 %copy-start.25 = (f32[256,1024]{1,0:T(8,128)S(1)}, f32[256,1024]{1,0:T(8,128)}, u32[]{:S(2)}) copy-start(f32[256,1024]{1,0:T(8,128)} %param.6) | copy-start | bytes 3145732
  0.6 1.8 %copy-start.26 = (s32[256,1024]{1,0:T(8,128)S(1)}, s32[256,1024]{1,0:T(8,128)}, u32[]{:S(2)}) copy-start(s32[256,1024]{1,0:T(8,128)} %param.7) | copy-start | bytes 3145732
  3.9 7.2 %collective-permute-start = (f32[5,8,1024]{2,1,0:T(8,128)S(1)}, f32[5,8,1024]{2,1,0:T(8,128)S(1)}, u32[]{:S(2)}, u32[]{:S(2)}) collective-permute-start(f32[5,8,1024]{2,1,0:T(8,128)S(1)} %get-tuple-element.30), channel_id=1, source_target_pairs={{0,16},{16,32},{32,48},{48,64},{64,80},{80,96},{96,112},{1,17},{17... | collective-permute-start | bytes 491528 | tf_op jit(solution)/shard_map/ppermute | solution.py:26
  8.8 6.6 %collective-permute-start.1 = (f32[5,8,1024]{2,1,0:T(8,128)S(1)}, f32[5,8,1024]{2,1,0:T(8,128)S(1)}, u32[]{:S(2)}, u32[]{:S(2)}) collective-permute-start(f32[5,8,1024]{2,1,0:T(8,128)S(1)} %get-tuple-element.31), channel_id=1, source_target_pairs={{16,0},{32,16},{48,32},{64,48},{80,64},{96,80},{112,96},{17,1},{33... | collective-permute-start | bytes 491528 | tf_op jit(solution)/shard_map/ppermute | solution.py:26
  16.3 2.6 %copy-start = (f32[5,272,1040]{2,1,0:T(8,128)}, f32[5,272,1040]{2,1,0:T(8,128)S(1)}, u32[]{:S(2)}) copy-start(f32[5,272,1040]{2,1,0:T(8,128)S(1)} %select_maximum_fusion) | copy-start | bytes 16972804
  19.7 4.5 %collective-permute-start.3 = (f32[5,272,8]{1,2,0:T(8,128)S(1)}, f32[5,272,8]{1,2,0:T(8,128)S(1)}, u32[]{:S(2)}, u32[]{:S(2)}) collective-permute-start(f32[5,272,8]{1,2,0:T(8,128)S(1)} %copy.17), channel_id=1, source_target_pairs={{0,1},{1,2},{2,3},{3,4},{4,5},{5,6},{6,7},{7,8},{8,9},{9,10},{10,1... | collective-permute-start | bytes 130568 | tf_op jit(solution)/shard_map/ppermute | solution.py:26
  23.0 5.0 %collective-permute-start.2 = (f32[5,272,8]{1,2,0:T(8,128)S(1)}, f32[5,272,8]{1,2,0:T(8,128)S(1)}, u32[]{:S(2)}, u32[]{:S(2)}) collective-permute-start(f32[5,272,8]{1,2,0:T(8,128)S(1)} %copy.16), channel_id=1, source_target_pairs={{1,0},{2,1},{3,2},{4,3},{5,4},{6,5},{7,6},{8,7},{9,8},{10,9},{11,1... | collective-permute-start | bytes 130568 | tf_op jit(solution)/shard_map/ppermute | solution.py:26
  29.2 3.9 %copy-start.1 = (f32[5,272,1040]{2,1,0:T(8,128)S(1)}, f32[5,272,1040]{2,1,0:T(8,128)}, u32[]{:S(2)}) copy-start(f32[5,272,1040]{2,1,0:T(8,128)} %constant_dynamic-update-slice_fusion) | copy-start | bytes 16972804
  35.0 2.9 %copy-start.16 = (f32[1,272,1040]{2,1,0:T(8,128)}, f32[1,272,1040]{2,1,0:T(8,128)S(1)}, u32[]{:S(2)}) copy-start(f32[1,272,1040]{2,1,0:T(8,128)S(1)} %get-tuple-element.24) | copy-start | bytes 3394564
  35.0 7.0 %copy-start.3 = (f32[1,272,1040]{2,1,0:T(8,128)}, f32[1,272,1040]{2,1,0:T(8,128)S(1)}, u32[]{:S(2)}) copy-start(f32[1,272,1040]{2,1,0:T(8,128)S(1)} %get-tuple-element.22) | copy-start | bytes 3394564
  35.0 7.0 %copy-start.9 = (f32[1,272,1040]{2,1,0:T(8,128)}, f32[1,272,1040]{2,1,0:T(8,128)S(1)}, u32[]{:S(2)}) copy-start(f32[1,272,1040]{2,1,0:T(8,128)S(1)} %get-tuple-element.23) | copy-start | bytes 3394564
  35.5 2.3 %copy-start.17 = (f32[1,272,1040]{2,1,0:T(8,128)}, f32[1,272,1040]{2,1,0:T(8,128)S(1)}, u32[]{:S(2)}) copy-start(f32[1,272,1040]{2,1,0:T(8,128)S(1)} %get-tuple-element.17) | copy-start | bytes 3394564
  35.5 6.5 %copy-start.6 = (f32[1,272,1040]{2,1,0:T(8,128)}, f32[1,272,1040]{2,1,0:T(8,128)S(1)}, u32[]{:S(2)}) copy-start(f32[1,272,1040]{2,1,0:T(8,128)S(1)} %get-tuple-element.16) | copy-start | bytes 3394564
  35.5 6.5 %copy-start.11 = (f32[1,272,1040]{2,1,0:T(8,128)}, f32[1,272,1040]{2,1,0:T(8,128)S(1)}, u32[]{:S(2)}) copy-start(f32[1,272,1040]{2,1,0:T(8,128)S(1)} %get-tuple-element.18) | copy-start | bytes 3394564
  70.6 5.4 %copy-start.2 = (f32[2,272,1040]{2,1,0:T(8,128)}, f32[2,272,1040]{2,1,0:T(8,128)S(1)}, u32[]{:S(2)}) copy-start(f32[2,272,1040]{2,1,0:T(8,128)S(1)} %multiply_subtract_fusion.1) | copy-start | bytes 6789124
  71.8 2.4 %copy-start.7 = (f32[1,272,1040]{2,1,0:T(8,128)S(1)}, f32[1,272,1040]{2,1,0:T(8,128)}, u32[]{:S(2)}) copy-start(f32[1,272,1040]{2,1,0:T(8,128)} %copy-done.6) | copy-start | bytes 3394564
  71.9 2.9 %copy-start.10 = (f32[1,272,1040]{2,1,0:T(8,128)S(1)}, f32[1,272,1040]{2,1,0:T(8,128)}, u32[]{:S(2)}) copy-start(f32[1,272,1040]{2,1,0:T(8,128)} %copy-done.9) | copy-start | bytes 3394564
  71.9 3.3 %copy-start.12 = (f32[1,272,1040]{2,1,0:T(8,128)S(1)}, f32[1,272,1040]{2,1,0:T(8,128)}, u32[]{:S(2)}) copy-start(f32[1,272,1040]{2,1,0:T(8,128)} %copy-done.11) | copy-start | bytes 3394564
  72.3 3.7 %copy-start.20 = (f32[1,272,1040]{2,1,0:T(8,128)}, f32[1,272,1040]{2,1,0:T(8,128)S(1)}, u32[]{:S(2)}) copy-start(f32[1,272,1040]{2,1,0:T(8,128)S(1)} %get-tuple-element.40) | copy-start | bytes 3394564
  72.3 3.7 %copy-start.21 = (f32[1,272,1040]{2,1,0:T(8,128)}, f32[1,272,1040]{2,1,0:T(8,128)S(1)}, u32[]{:S(2)}) copy-start(f32[1,272,1040]{2,1,0:T(8,128)S(1)} %get-tuple-element.41) | copy-start | bytes 3394564
  75.2 1.7 %copy-start.19 = (f32[2,272,1040]{2,1,0:T(8,128)S(1)}, f32[2,272,1040]{2,1,0:T(8,128)}, u32[]{:S(2)}) copy-start(f32[2,272,1040]{2,1,0:T(8,128)} %copy-done.18) | copy-start | bytes 6789124
  101.4 1.6 %copy-start.13 = (f32[2,272,1040]{2,1,0:T(8,128)}, f32[2,272,1040]{2,1,0:T(8,128)S(1)}, u32[]{:S(2)}) copy-start(f32[2,272,1040]{2,1,0:T(8,128)S(1)} %get-tuple-element.15) | copy-start | bytes 6789124
  102.6 1.7 %copy-start.8 = (f32[1,272,1040]{2,1,0:T(8,128)S(1)}, f32[1,272,1040]{2,1,0:T(8,128)}, u32[]{:S(2)}) copy-start(f32[1,272,1040]{2,1,0:T(8,128)} %copy-done.6) | copy-start | bytes 3394564
  102.6 2.5 %copy-start.24 = (f32[2,272,1040]{2,1,0:T(8,128)S(1)}, f32[2,272,1040]{2,1,0:T(8,128)}, u32[]{:S(2)}) copy-start(f32[2,272,1040]{2,1,0:T(8,128)} %get-tuple-element.36) | copy-start | bytes 6789124
  (9 other events, 11.8 us)

commit v17 on v14

--- a/solution.py
+++ b/solution.py
@@ -1,4 +1,6 @@
 import functools
+
+import numpy as np
 
 import jax
 import jax.numpy as jnp
@@ -163,8 +165,9 @@
     solution = start
     residual = right_side - operate(start, wet, inverse)
     applied = operate(residual, wet, inverse)
-    rows = lax.broadcasted_iota(jnp.int32, (8, 128), 0)
-    previous = jnp.where(rows == 2, jnp.inf, 0.0).astype(jnp.float32)
+    previous = np.zeros((8, 128), np.float32)
+    previous[2] = np.inf
+    previous = jnp.asarray(previous)
     stats = cg_scalars(dots((residual, residual), (residual, applied)), previous)
     direction, image = residual, applied
     for step in range(ITERS):

time: 138 us -> 138 us (level)
  no operation moved by 1% of the time
where the time goes in v17:
time: 138 us; the launch traced here: 137 us
  Pallas kernels  43.7 us (32%)
  other arithmetic  42.7 us (31%)
  local copies, waits for them, and re-layouts  29.5 us (21%)
  starting transfers between devices  11.4 us (8%)
  waiting for transfers between devices  8.35 us (6%)
    pallas_call x3, Pallas kernels, cg_scalars(): pl.pallas_call(functools.partial(reduce_kernel, stages), out_shape=jax.Sh...  43.7 us
    unnamed x61, local copies, waits for them, and re-layouts  14.8 us
    ppermute x4, starting transfers between devices, from_behind(): lax.ppermute(value, axis, [(source, source + steps) for source in range(l...  11.4 us
    sub x2, other arithmetic, per_device(): residual = residual - alpha * image  10.8 us
    add x1, other arithmetic, per_device(): solution = solution + alpha * direction  9.23 us
    ppermute x4, waiting for transfers between devices, from_behind(): lax.ppermute(value, axis, [(source, source + steps) for source in range(l...  8.35 us
    select_n x6, other arithmetic, cg_scalars(): tile = jnp.where(rows == k, local[k], tile)  7.2 us
    reduce_sum x3, other arithmetic, dots(): return jnp.stack([jnp.sum(interior(x) * interior(y)) for x, y in pairs])  4.22 us
  transfers between devices with their start and end apart: 4, of which 3 were waited for; matrix products, arithmetic and copies ran while one was open for 0% of the time, Pallas kernels for 0%

profile of v17, /device:TPU:1, one launch (start us, length us, event | category | flops | bytes accessed | tf_op | source)
XLA Modules:
  0.0 137.0 jit_solution(18393610671898783030)
XLA Ops:
  0.7 1.4 %bitcast_dynamic-update-slice_fusion.4 = f32[5,256,1024]{2,1,0:T(8,128)S(1)} fusion(f32[256,1024]{1,0:T(8,128)} %param.6), kind=kLoop, calls=%fused_computation.107 | loop fusion | bytes 2097152
  3.9 4.9 %collective-permute-start = (f32[5,8,1024]{2,1,0:T(8,128)S(1)}, f32[5,8,1024]{2,1,0:T(8,128)S(1)}, u32[]{:S(2)}, u32[]{:S(2)}) collective-permute-start(f32[5,8,1024]{2,1,0:T(8,128)S(1)} %get-tuple-element.30), channel_id=1, source_target_pairs={{0,16},{16,32},{32,48},{48,64},{64,80},{80,96},{96,112},{1,17},{17... | collective-permute-start | bytes 491528 | tf_op jit(solution)/shard_map/ppermute | solution.py:28
  8.8 1.9 %collective-permute-start.1 = (f32[5,8,1024]{2,1,0:T(8,128)S(1)}, f32[5,8,1024]{2,1,0:T(8,128)S(1)}, u32[]{:S(2)}, u32[]{:S(2)}) collective-permute-start(f32[5,8,1024]{2,1,0:T(8,128)S(1)} %get-tuple-element.31), channel_id=1, source_target_pairs={{16,0},{32,16},{48,32},{64,48},{80,64},{96,80},{112,96},{17,1},{33... | collective-permute-start | bytes 491528 | tf_op jit(solution)/shard_map/ppermute | solution.py:28
  11.1 4.4 %collective-permute-done.1 = f32[5,8,1024]{2,1,0:T(8,128)S(1)} collective-permute-done((f32[5,8,1024]{2,1,0:T(8,128)S(1)}, f32[5,8,1024]{2,1,0:T(8,128)S(1)}, u32[]{:S(2)}, u32[]{:S(2)}) %collective-permute-start.1) | collective-permute-done | bytes 163872 | tf_op jit(solution)/shard_map/ppermute | solution.py:28
  16.3 2.6 %copy-done = f32[5,272,1040]{2,1,0:T(8,128)} copy-done((f32[5,272,1040]{2,1,0:T(8,128)}, f32[5,272,1040]{2,1,0:T(8,128)S(1)}, u32[]{:S(2)}) %copy-start) | copy-done | bytes 5657624
  19.8 3.2 %collective-permute-start.3 = (f32[5,272,8]{1,2,0:T(8,128)S(1)}, f32[5,272,8]{1,2,0:T(8,128)S(1)}, u32[]{:S(2)}, u32[]{:S(2)}) collective-permute-start(f32[5,272,8]{1,2,0:T(8,128)S(1)} %copy.18), channel_id=1, source_target_pairs={{0,1},{1,2},{2,3},{3,4},{4,5},{5,6},{6,7},{7,8},{8,9},{9,10},{10,1... | collective-permute-start | bytes 130568 | tf_op jit(solution)/shard_map/ppermute | solution.py:28
  24.3 3.6 %collective-permute-done.2 = f32[5,272,8]{1,2,0:T(8,128)S(1)} collective-permute-done((f32[5,272,8]{1,2,0:T(8,128)S(1)}, f32[5,272,8]{1,2,0:T(8,128)S(1)}, u32[]{:S(2)}, u32[]{:S(2)}) %collective-permute-start.2) | collective-permute-done | bytes 43552 | tf_op jit(solution)/shard_map/ppermute | solution.py:28
  29.2 2.4 %slice_bitcast_fusion.19 = (f32[271,1040]{1,0:T(8,128)S(1)}, f32[271,1040]{1,0:T(8,128)S(1)}, f32[271,1040]{1,0:T(8,128)S(1)}) fusion(f32[5,272,1040]{2,1,0:T(8,128)} %constant_dynamic-update-slice_fusion), kind=kLoop, calls=%fused_computation.67 | loop fusion | bytes 6764160 | tf_op jit(solution)/shard_map/slice | solution.py:47
  31.7 1.5 %copy-done.1 = f32[5,272,1040]{2,1,0:T(8,128)S(1)} copy-done((f32[5,272,1040]{2,1,0:T(8,128)S(1)}, f32[5,272,1040]{2,1,0:T(8,128)}, u32[]{:S(2)}) %copy-start.1) | copy-done | bytes 5657624
  37.9 2.6 %fusion.1 = (f32[2,272,1040]{2,1,0:T(8,128)}, f32[2,272,1040]{2,1,0:T(8,128)S(1)}) fusion(f32[1,272,1040]{2,1,0:T(8,128)S(1)} %get-tuple-element.23, f32[1,272,1040]{2,1,0:T(8,128)S(1)} %get-tuple-element.18, f32[1,272,1040]{2,1,0:T(8,128)S(1)} %get-tuple-element.45, f32[1,272,1040]{2,1,0:T(8,128)S(1)} %get-tuple-element.44, ...), kind=kLoop, calls=%fused_computation.8 | loop fusion | flops 10749440 | bytes 15841280 | tf_op jit(solution)/shard_map/jit(_where)/select_n | solution.py:163
  43.4 1.4 %multiply_reduce_fusion.4 = (f32[]{:T(128)}, f32[]{:T(128)}) fusion(f32[2,272,1040]{2,1,0:T(8,128)S(1)} %fusion.5, f32[2,272,1040]{2,1,0:T(8,128)S(1)} %get-tuple-element.37), kind=kLoop, calls=%fused_computation.39 | loop fusion | flops 2097150 | bytes 4194312 | tf_op jit(solution)/shard_map/reduce_sum | solution.py:152
  45.6 1.3 broadcast_select_fusion.local_ref
  46.9 17.7 %shard_map.85.prev_ref = f32[8,128]{1,0:T(8,128)} custom-call(f32[8,128]{1,0:T(8,128)} %broadcast_select_fusion.local_ref, f32[8,128]{1,0:T(8,128)} %constant.9.clone.prev_ref), custom_call_target="tpu_custom_call" | custom-call | tf_op jit(solution)/shard_map/pallas_call | solution.py:131
  65.8 4.2 %multiply_subtract_fusion.1 = f32[2,272,1040]{2,1,0:T(8,128)S(1)} fusion(f32[2,272,1040]{2,1,0:T(8,128)S(1)} %get-tuple-element.37, f32[]{:T(128)} %bitcast.30, f32[1,272,1040]{2,1,0:T(8,128)} %copy-done.15, f32[1,272,1040]{2,1,0:T(8,128)} %copy-done.14, f32[1,272,1040]{2,1,0:T(8,128)} %copy-done.9, f32[1,272,1040]{2,1,0:T(8,128)} %copy-done.11, ...), kind=kLoop, calls=%fused_computation.23 | loop fusion | flops 7354880 | bytes 11315204 | tf_op jit(solution)/shard_map/sub | solution.py:178
  78.3 2.0 %select_select_fusion.1.local_ref = f32[8,128]{1,0:T(8,128)} fusion(f32[8]{0:T(128)S(1)} %fusion.29, f32[]{:T(128)} %get-tuple-element.10, f32[]{:T(128)} %get-tuple-element.9, pred[8]{0:T(512)(128)(4,1)S(1)} %get-tuple-element.54, pred[8]{0:T(512)(128)(4,1)S(1)} %get-tuple-element.55), kind=kLoop, calls=%fused_computation.113 | loop fusion | flops 2048 | bytes 4152 | tf_op jit(solution)/shard_map/jit(_where)/select_n | solution.py:130
  80.3 12.7 %shard_map.86.prev_ref = f32[8,128]{1,0:T(8,128)} custom-call(f32[8,128]{1,0:T(8,128)} %select_select_fusion.1.local_ref, f32[8,128]{1,0:T(8,128)} %shard_map.85.prev_ref), custom_call_target="tpu_custom_call" | custom-call | tf_op jit(solution)/shard_map/pallas_call | solution.py:131
  93.0 1.3 fusion.34
  94.4 6.5 %multiply_subtract_fusion = (f32[2,272,1040]{2,1,0:T(8,128)S(1)}, f32[2,272,1040]{2,1,0:T(8,128)S(1)}) fusion(f32[2,272,1040]{2,1,0:T(8,128)} %copy-done.2, f32[]{:T(128)} %bitcast.36, f32[]{:T(128)} %bitcast.37, f32[1,272,1040]{2,1,0:T(8,128)} %copy-done.21, f32[1,272,1040]{2,1,0:T(8,128)} %copy-done.20, f32[1,272,1040]{2,1,0:T(8,128)} %copy-done.9, ...), kind=kLoop, calls=%fused_computation.21 | loop fusion | flops 10749440 | bytes 18104328 | tf_op jit(solution)/shard_map/sub | solution.py:178
  104.6 1.5 %fusion.12 = (f32[]{:T(128)}, f32[]{:T(128)}, f32[]{:T(128)}) fusion(f32[2,272,1040]{2,1,0:T(8,128)S(1)} %get-tuple-element.15, f32[2,272,1040]{2,1,0:T(8,128)S(1)} %get-tuple-element.14, f32[1,272,1040]{2,1,0:T(8,128)S(1)} %get-tuple-element.39, f32[1,272,1040]{2,1,0:T(8,128)S(1)} %get-tuple-element.38, f32[2,272,1040]{2,1,0:T(8,128)S(1)} %copy-done.24, ...), kind=kLoop, calls=%fused_computation.32 | loop fusion | flops 5767165 | bytes 10817548 | tf_op jit(solution)/shard_map/reduce_sum | solution.py:152
  106.8 2.0 %select_select_fusion.local_ref = f32[8,128]{1,0:T(8,128)} fusion(f32[8]{0:T(128)S(1)} %fusion.28, f32[]{:T(128)} %get-tuple-element.8, f32[]{:T(128)} %get-tuple-element.6, pred[8]{0:T(512)(128)(4,1)S(1)} %get-tuple-element.54, pred[8]{0:T(512)(128)(4,1)S(1)} %get-tuple-element.55), kind=kLoop, calls=%fused_computation.112 | loop fusion | flops 2048 | bytes 4152 | tf_op jit(solution)/shard_map/jit(_where)/select_n | solution.py:130
  108.8 13.3 %shard_map.87 = f32[8,128]{1,0:T(8,128)} custom-call(f32[8,128]{1,0:T(8,128)} %select_select_fusion.local_ref, f32[8,128]{1,0:T(8,128)} %shard_map.86.prev_ref), custom_call_target="tpu_custom_call" | custom-call | tf_op jit(solution)/shard_map/pallas_call | solution.py:131
  123.3 9.2 %multiply_add_fusion = f32[2,272,1040]{2,1,0:T(8,128)S(1)} fusion(f32[2,272,1040]{2,1,0:T(8,128)} %copy-done.2, f32[2,272,1040]{2,1,0:T(8,128)S(1)} %get-tuple-element.37, f32[]{:T(128)} %bitcast.44, f32[]{:T(128)} %bitcast.43, f32[]{:T(128)} %bitcast.37, f32[]{:T(128)} %bitcast.36, f32[]{:T(128)} %bitcast.30, f32[2,272,1040]{2,1,0:T(8,128)} %copy-done.13, ...), kind=kLoop, calls=%fused_computation.20 | loop fusion | flops 10749440 | bytes 18104340 | tf_op jit(solution)/shard_map/add | solution.py:175
  132.7 1.6 %slice_bitcast_fusion.24 = (f32[256,1024]{1,0:T(8,128)}, f32[256,1024]{1,0:T(8,128)}) fusion(f32[2,272,1040]{2,1,0:T(8,128)S(1)} %multiply_add_fusion), kind=kLoop, calls=%fused_computation.95 | loop fusion | bytes 4194304 | tf_op jit(solution)/shard_map/squeeze | solution.py:186
  135.5 1.4 %slice_subtract_fusion.1 = f32[256,1024]{1,0:T(8,128)} fusion(f32[272,1040]{1,0:T(8,128)S(1)} %copy-done.23, f32[271,1040]{1,0:T(8,128)S(1)} %slice_bitcast_fusion, f32[272,1040]{1,0:T(8,128)S(1)} %get-tuple-element.35, f32[272,1040]{1,0:T(8,128)S(1)} %get-tuple-element.34, f32[272,1039]{1,0:T(8,128)S(1)} %bitcast.130, f32[272,1]{1,0:T(8,128)S(1)} %slice.402), kind=kLoop, calls=%fused_computation.97 | loop fusion | flops 1572864 | bytes 6453184 | tf_op jit(solution)/shard_map/sub | solution.py:184
  (123 shorter events, 30.7 us)
Async XLA Ops:
  0.6 1.5 %copy-start.25 = (f32[256,1024]{1,0:T(8,128)S(1)}, f32[256,1024]{1,0:T(8,128)}, u32[]{:S(2)}) copy-start(f32[256,1024]{1,0:T(8,128)} %param.7) | copy-start | bytes 3145732
  0.6 1.8 %copy-start.26 = (s32[256,1024]{1,0:T(8,128)S(1)}, s32[256,1024]{1,0:T(8,128)}, u32[]{:S(2)}) copy-start(s32[256,1024]{1,0:T(8,128)} %param.8) | copy-start | bytes 3145732
  3.9 7.2 %collective-permute-start = (f32[5,8,1024]{2,1,0:T(8,128)S(1)}, f32[5,8,1024]{2,1,0:T(8,128)S(1)}, u32[]{:S(2)}, u32[]{:S(2)}) collective-permute-start(f32[5,8,1024]{2,1,0:T(8,128)S(1)} %get-tuple-element.30), channel_id=1, source_target_pairs={{0,16},{16,32},{32,48},{48,64},{64,80},{80,96},{96,112},{1,17},{17... | collective-permute-start | bytes 491528 | tf_op jit(solution)/shard_map/ppermute | solution.py:28
  8.8 6.6 %collective-permute-start.1 = (f32[5,8,1024]{2,1,0:T(8,128)S(1)}, f32[5,8,1024]{2,1,0:T(8,128)S(1)}, u32[]{:S(2)}, u32[]{:S(2)}) collective-permute-start(f32[5,8,1024]{2,1,0:T(8,128)S(1)} %get-tuple-element.31), channel_id=1, source_target_pairs={{16,0},{32,16},{48,32},{64,48},{80,64},{96,80},{112,96},{17,1},{33... | collective-permute-start | bytes 491528 | tf_op jit(solution)/shard_map/ppermute | solution.py:28
  16.3 2.6 %copy-start = (f32[5,272,1040]{2,1,0:T(8,128)}, f32[5,272,1040]{2,1,0:T(8,128)S(1)}, u32[]{:S(2)}) copy-start(f32[5,272,1040]{2,1,0:T(8,128)S(1)} %select_maximum_fusion) | copy-start | bytes 16972804
  19.8 4.5 %collective-permute-start.3 = (f32[5,272,8]{1,2,0:T(8,128)S(1)}, f32[5,272,8]{1,2,0:T(8,128)S(1)}, u32[]{:S(2)}, u32[]{:S(2)}) collective-permute-start(f32[5,272,8]{1,2,0:T(8,128)S(1)} %copy.18), channel_id=1, source_target_pairs={{0,1},{1,2},{2,3},{3,4},{4,5},{5,6},{6,7},{7,8},{8,9},{9,10},{10,1... | collective-permute-start | bytes 130568 | tf_op jit(solution)/shard_map/ppermute | solution.py:28
  23.0 5.0 %collective-permute-start.2 = (f32[5,272,8]{1,2,0:T(8,128)S(1)}, f32[5,272,8]{1,2,0:T(8,128)S(1)}, u32[]{:S(2)}, u32[]{:S(2)}) collective-permute-start(f32[5,272,8]{1,2,0:T(8,128)S(1)} %copy.17), channel_id=1, source_target_pairs={{1,0},{2,1},{3,2},{4,3},{5,4},{6,5},{7,6},{8,7},{9,8},{10,9},{11,1... | collective-permute-start | bytes 130568 | tf_op jit(solution)/shard_map/ppermute | solution.py:28
  29.2 3.9 %copy-start.1 = (f32[5,272,1040]{2,1,0:T(8,128)S(1)}, f32[5,272,1040]{2,1,0:T(8,128)}, u32[]{:S(2)}) copy-start(f32[5,272,1040]{2,1,0:T(8,128)} %constant_dynamic-update-slice_fusion) | copy-start | bytes 16972804
  35.0 2.9 %copy-start.16 = (f32[1,272,1040]{2,1,0:T(8,128)}, f32[1,272,1040]{2,1,0:T(8,128)S(1)}, u32[]{:S(2)}) copy-start(f32[1,272,1040]{2,1,0:T(8,128)S(1)} %get-tuple-element.24) | copy-start | bytes 3394564
  35.0 7.0 %copy-start.3 = (f32[1,272,1040]{2,1,0:T(8,128)}, f32[1,272,1040]{2,1,0:T(8,128)S(1)}, u32[]{:S(2)}) copy-start(f32[1,272,1040]{2,1,0:T(8,128)S(1)} %get-tuple-element.22) | copy-start | bytes 3394564
  35.0 7.0 %copy-start.9 = (f32[1,272,1040]{2,1,0:T(8,128)}, f32[1,272,1040]{2,1,0:T(8,128)S(1)}, u32[]{:S(2)}) copy-start(f32[1,272,1040]{2,1,0:T(8,128)S(1)} %get-tuple-element.23) | copy-start | bytes 3394564
  35.5 2.3 %copy-start.17 = (f32[1,272,1040]{2,1,0:T(8,128)}, f32[1,272,1040]{2,1,0:T(8,128)S(1)}, u32[]{:S(2)}) copy-start(f32[1,272,1040]{2,1,0:T(8,128)S(1)} %get-tuple-element.17) | copy-start | bytes 3394564
  35.5 6.5 %copy-start.6 = (f32[1,272,1040]{2,1,0:T(8,128)}, f32[1,272,1040]{2,1,0:T(8,128)S(1)}, u32[]{:S(2)}) copy-start(f32[1,272,1040]{2,1,0:T(8,128)S(1)} %get-tuple-element.16) | copy-start | bytes 3394564
  35.5 6.5 %copy-start.11 = (f32[1,272,1040]{2,1,0:T(8,128)}, f32[1,272,1040]{2,1,0:T(8,128)S(1)}, u32[]{:S(2)}) copy-start(f32[1,272,1040]{2,1,0:T(8,128)S(1)} %get-tuple-element.18) | copy-start | bytes 3394564
  70.1 5.4 %copy-start.2 = (f32[2,272,1040]{2,1,0:T(8,128)}, f32[2,272,1040]{2,1,0:T(8,128)S(1)}, u32[]{:S(2)}) copy-start(f32[2,272,1040]{2,1,0:T(8,128)S(1)} %multiply_subtract_fusion.1) | copy-start | bytes 6789124
  71.3 2.4 %copy-start.7 = (f32[1,272,1040]{2,1,0:T(8,128)S(1)}, f32[1,272,1040]{2,1,0:T(8,128)}, u32[]{:S(2)}) copy-start(f32[1,272,1040]{2,1,0:T(8,128)} %copy-done.6) | copy-start | bytes 3394564
  71.4 2.9 %copy-start.10 = (f32[1,272,1040]{2,1,0:T(8,128)S(1)}, f32[1,272,1040]{2,1,0:T(8,128)}, u32[]{:S(2)}) copy-start(f32[1,272,1040]{2,1,0:T(8,128)} %copy-done.9) | copy-start | bytes 3394564
  71.4 3.3 %copy-start.12 = (f32[1,272,1040]{2,1,0:T(8,128)S(1)}, f32[1,272,1040]{2,1,0:T(8,128)}, u32[]{:S(2)}) copy-start(f32[1,272,1040]{2,1,0:T(8,128)} %copy-done.11) | copy-start | bytes 3394564
  71.8 3.7 %copy-start.20 = (f32[1,272,1040]{2,1,0:T(8,128)}, f32[1,272,1040]{2,1,0:T(8,128)S(1)}, u32[]{:S(2)}) copy-start(f32[1,272,1040]{2,1,0:T(8,128)S(1)} %get-tuple-element.40) | copy-start | bytes 3394564
  71.8 3.7 %copy-start.21 = (f32[1,272,1040]{2,1,0:T(8,128)}, f32[1,272,1040]{2,1,0:T(8,128)S(1)}, u32[]{:S(2)}) copy-start(f32[1,272,1040]{2,1,0:T(8,128)S(1)} %get-tuple-element.41) | copy-start | bytes 3394564
  74.7 1.7 %copy-start.19 = (f32[2,272,1040]{2,1,0:T(8,128)S(1)}, f32[2,272,1040]{2,1,0:T(8,128)}, u32[]{:S(2)}) copy-start(f32[2,272,1040]{2,1,0:T(8,128)} %copy-done.18) | copy-start | bytes 6789124
  100.9 1.6 %copy-start.13 = (f32[2,272,1040]{2,1,0:T(8,128)}, f32[2,272,1040]{2,1,0:T(8,128)S(1)}, u32[]{:S(2)}) copy-start(f32[2,272,1040]{2,1,0:T(8,128)S(1)} %get-tuple-element.15) | copy-start | bytes 6789124
  102.2 1.7 %copy-start.8 = (f32[1,272,1040]{2,1,0:T(8,128)S(1)}, f32[1,272,1040]{2,1,0:T(8,128)}, u32[]{:S(2)}) copy-start(f32[1,272,1040]{2,1,0:T(8,128)} %copy-done.6) | copy-start | bytes 3394564
  102.2 2.5 %copy-start.24 = (f32[2,272,1040]{2,1,0:T(8,128)S(1)}, f32[2,272,1040]{2,1,0:T(8,128)}, u32[]{:S(2)}) copy-start(f32[2,272,1040]{2,1,0:T(8,128)} %get-tuple-element.36) | copy-start | bytes 6789124
  (9 other events, 11.8 us)
